TPU v7x, 32 devices: a whole 2x2x4 slice. The times are simulated.
32 devices in a mesh: row: 4 (over y, x), col: 4 (over z), layer: 2 (over core).
Axes of the slice: x: 2, y: 2, z: 4, core: 2. Of those that a mesh axis runs over, the one named last changes fastest.
Arguments:
- x_blocks: bfloat16 [4, 4, 28, 128, 128], P('col', 'row'), may hold values from -1.75 to 1.75
- slot_rows: int32 [4, 4, 28], replicated, may hold values from 0 to 27, as said below
- slot_cols: int32 [4, 4, 28], replicated, may hold values from 0 to 27, as said below
Outputs:
- c_blocks: bfloat16 [4, 4, 28, 128, 128], P('col', 'row', 'layer')
Inputs may be any that keep to these rules, and one draw needn't show every extreme that they name: In every tile the pairs (slot_rows, slot_cols) are distinct; exactly 7 local rows hold 2 stored blocks, 14 local rows hold one, the others none. slot_cols[a, b, s] is slot_rows[a, b, s] or slot_rows[a, b, s] + 1, modulo 28; a row with two stored blocks has both.
All inputs are finite; a program needn't handle non-finite values.
Results may differ from a plain program's by a relative error of at most 0.001.
Values may be sent and summed in bfloat16 or wider, within the bound.
No kernel may reach another device: no remote copies, remote signals or barrier semaphores. Data moves between devices by JAX's collectives and lax.ppermute only.
A program may use at most 64 MiB of HBM per device.

v0:
```python
import functools

import jax
import jax.numpy as jnp
from jax import lax
from jax.experimental import pallas as pl
from jax.experimental.pallas import tpu as pltpu
from jax.sharding import PartitionSpec as P

TB = 28
GROUP = 4
LANES = 128
GRANT = 16 << 20
CHUNKS = 2
JOIN = 3


class Plan:
    def __init__(self, mesh):
        self.grid = mesh.shape["row"]
        self.half = min(6, self.grid) // 2
        self.whole = 2 * self.half == self.grid
        self.stages = self.grid - 1 if self.whole else self.half

    def shift(self, a, l):
        if self.whole:
            return l - a
        mid = self.grid // 2
        k = (l - a + mid) % self.grid - mid
        return k if -self.half <= k < self.half else None

    def hop_pairs(self, stage):
        pairs = []
        for source in range(self.grid):
            for layer, step in ((0, 1), (1, -1)):
                target = source + step
                origin = target - step * stage
                if self.whole and not (0 <= target < self.grid and 0 <= origin < self.grid):
                    continue
                target %= self.grid
                if self.shift(target, origin % self.grid) == -step * stage:
                    pairs.append((source * 2 + layer, target * 2 + layer))
        return pairs

    def row_pairs(self, by, held=0):
        pairs = []
        for r in range(self.grid):
            for a in range(self.grid):
                k = self.shift(a, r)
                if k is not None:
                    layer = int(k > 0)
                    pairs.append(
                        tuple(
                            (p * self.grid + a) * 2 + layer
                            for p in (r ^ held, r ^ held ^ by)
                        )
                    )
        return pairs

    def taken(self, a, layer, stage):
        l = jnp.where(layer == 0, a - stage, a + stage)
        if self.whole:
            valid = (l >= 0) & (l < self.grid)
        else:
            valid = jnp.where(layer == 0, stage <= self.half, stage < self.half)
        if stage == 0:
            valid = valid & (layer == 0)
        l = jnp.where(l < 0, l + self.grid, l)
        return jnp.where(l >= self.grid, l - self.grid, l), valid


def place():
    return tuple(lax.axis_index(n) for n in ("col", "row", "layer"))


def list_kernel(plan, bounds, rows_in, cols_in, pairs, rows, cols, keys, codes, sem):
    slots = rows.shape[2]
    stages = plan.stages + 1
    inputs = [
        pltpu.make_async_copy(rows_in, rows, sem.at[0]),
        pltpu.make_async_copy(cols_in, cols, sem.at[1]),
    ]
    for copy in inputs:
        copy.start()
    a, b, layer = place()
    lane = lax.broadcasted_iota(jnp.int32, (1, LANES), 1)
    down = lax.broadcasted_iota(jnp.int32, (LANES, LANES), 0)
    across = lax.broadcasted_iota(jnp.int32, (LANES, LANES), 1)

    def key_of(i, j):
        r, c = rows[i, pl.ds(j, 1), :], cols[i, pl.ds(j, 1), :]
        return 2 * r + (c != r).astype(jnp.int32)

    keys[...] = jnp.full_like(keys, -1)
    for copy in inputs:
        copy.wait()
    taken = []
    for stage in range(stages):
        l, valid = plan.taken(a, layer, stage)
        taken.append(valid)
        l = jnp.clip(l, 0, plan.grid - 1)
        keys[pl.ds(stage, 1), 0:slots] = key_of(a, l)
        keys[pl.ds(stages + stage, 1), 0:slots] = key_of(l, b)
    keys[pl.ds(2 * stages, 1), 0:slots] = key_of(a, b)
    out = keys[pl.ds(2 * stages, 1), :]
    out = jnp.where(lane < LANES // 2, out, pltpu.roll(out, LANES // 2, 1))
    slot = lane % (LANES // 2)
    r, d = out // 2, out % 2
    after = jnp.where(r + 1 == TB, 0, r + 1)
    second = lane >= LANES // 2
    left_key = jnp.where(second, 2 * r + 1, 2 * r)
    right_key = jnp.where(second, jnp.where(d == 1, 2 * after, -2), out)
    wanted = slot < slots
    left_key = jnp.where(wanted, left_key, -2)
    right_key = jnp.where(wanted, right_key, -2)
    columns = keys[...].T

    def find(column, key):
        hit = columns[:, column : column + 1] == key
        return jnp.sum(jnp.where(hit, down + 1, 0), axis=0, keepdims=True)

    codes[...] = jnp.zeros_like(codes)
    for stage in range(stages):
        left, right = find(stage, left_key), find(stages + stage, right_key)
        good = (left > 0) & (right > 0) & taken[stage]
        code = jnp.where(good, ((left - 1) * 64 + (right - 1)) * 64 + slot + 1, 0)
        if stage < plan.stages:
            codes[pl.ds(stage, 1), :] = code
        else:
            for j, (low, high) in enumerate(zip(bounds[:-1], bounds[1:])):
                here = (right > low) & (right <= high)
                codes[pl.ds(stage + j, 1), :] = jnp.where(here, code, 0)
    found = codes[...] > 0
    ahead = jnp.dot(
        found.astype(jnp.float32),
        (down < across).astype(jnp.float32),
        preferred_element_type=jnp.float32,
    ).astype(jnp.int32)
    order = jnp.where(found, ahead, -1).T
    entries = codes[...].T
    for stage in range(pairs.shape[0]):
        hit = order[:, stage : stage + 1] == across
        entry = jnp.where(hit, entries[:, stage : stage + 1], 0)
        entry = jnp.sum(entry, axis=0, keepdims=True)
        count = jnp.sum(
            found[stage : stage + 1].astype(jnp.int32), axis=1, keepdims=True
        )
        entry = jnp.where(lane < count, entry - 1, slots)
        pairs[pl.ds(stage, 1), :] = jnp.where(lane == LANES - 1, count, entry)


def add_products(count, pairs, row, left, right, acc, low=0):
    def step(i, carry):
        codes = [pairs[row, i * GROUP + j] for j in range(GROUP)]
        products = [
            jnp.dot(
                left[code // 4096],
                right[jnp.maximum((code // 64) % 64 - low, 0)],
                preferred_element_type=jnp.float32,
            )
            for code in codes
        ]
        for code, product in zip(codes, products):
            acc[code % 64] += product
        return carry

    lax.fori_loop(0, (count + GROUP - 1) // GROUP, step, 0)


def fetch(copies, buffer, sem):
    at = 0
    for j, ref in enumerate(copies):
        pltpu.make_async_copy(
            ref, buffer.at[pl.ds(at, ref.shape[0])], sem.at[j]
        ).start()
        at += ref.shape[0]


def fetched(copies, buffer, sem):
    at = 0
    for j, ref in enumerate(copies):
        pltpu.make_async_copy(
            ref, buffer.at[pl.ds(at, ref.shape[0])], sem.at[j]
        ).wait()
        at += ref.shape[0]


def fetch_left(lefts, by, buffer, sem):
    for n, ref in lefts.items():

        @pl.when(by == n)
        def _(ref=ref):
            pltpu.make_async_copy(ref, buffer, sem).start()


def early_kernel(plan, parts, pairs, *refs):
    far = plan.grid - 1
    lefts = dict(enumerate(refs[:far]))
    refs = refs[far:]
    rights = []
    for n in parts:
        rights.append(refs[:n])
        refs = refs[n:]
    acc, left, right, left_sem, right_sem = refs
    a, b, layer = place()
    last = pairs.shape[1] - 1
    jobs = []
    for stage in range(plan.stages):
        l, _ = plan.taken(a, layer, stage)
        by = b ^ l
        count = jnp.where(by == far, 0, pairs[stage, last])
        jobs.append((stage, by, count))

        @pl.when(count > 0)
        def _(stage=stage, by=by):
            fetch(rights[stage], right.at[stage], right_sem.at[stage])
            fetch_left(lefts, by, left.at[stage], left_sem.at[stage])

    acc[...] = jnp.zeros_like(acc)
    for stage, by, count in jobs:

        @pl.when(count > 0)
        def _(stage=stage, count=count):
            pltpu.make_async_copy(
                lefts[0], left.at[stage], left_sem.at[stage]
            ).wait()
            fetched(rights[stage], right.at[stage], right_sem.at[stage])
            add_products(
                count, pairs, stage, left.at[stage], right.at[stage], acc
            )


def middle_kernel(plan, parts, pairs, total, *refs):
    del total
    lefts = dict(enumerate(refs[: plan.grid - 1]))
    refs = refs[plan.grid - 1 :]
    far_parts, refs = refs[:2], refs[2:]
    rights = []
    for n in parts[:-1]:
        rights.append(refs[:n])
        refs = refs[n:]
    first, acc, left_last, left, right, left_sem, right_sem = refs
    far, end, last = plan.grid - 1, plan.stages, pairs.shape[1] - 1
    a, b, layer = place()
    l, _ = plan.taken(a, layer, end)
    end_by = b ^ l

    @pl.when(end_by == far)
    def _():
        fetch(far_parts, left_last, left_sem.at[1])

    fetch_left(lefts, end_by, left_last, left_sem.at[1, 0])
    for stage in range(end):
        l, _ = plan.taken(a, layer, stage)
        count = jnp.where(b ^ l == far, pairs[stage, last], 0)

        @pl.when(count > 0)
        def _(stage=stage, count=count):
            fetch(rights[stage], right, right_sem)
            fetch(far_parts, left, left_sem.at[0])
            fetched(rights[stage], right, right_sem)
            fetched(far_parts, left, left_sem.at[0])
            add_products(count, pairs, stage, left, right, acc)

    @pl.when(end_by == far)
    def _():
        fetched(far_parts, left_last, left_sem.at[1])

    @pl.when((end_by >= 0) & (end_by < far))
    def _():
        pltpu.make_async_copy(lefts[0], left_last, left_sem.at[1, 0]).wait()

    add_products(pairs[end, last], pairs, end, left_last, first, acc)


def last_kernel(plan, bounds, pairs, total, left_last, *refs):
    del total
    refs, (acc, mine, other) = refs[:-3], refs[-3:]
    last = pairs.shape[1] - 1
    for j, part in enumerate(refs):
        row = plan.stages + 1 + j
        add_products(pairs[row, last], pairs, row, left_last, part, acc, bounds[1 + j])
    layer = lax.axis_index("layer")
    share = mine.shape[0]
    mine[...] = acc[pl.ds(layer * share, share)]
    other[...] = acc[pl.ds((1 - layer) * share, share)]


def on_device(plan, x_blocks, slot_rows, slot_cols):
    own = x_blocks[0, 0]
    slots, size = own.shape[0], own.shape[1]
    share = slots // 2
    bounds = [slots * i // CHUNKS for i in range(CHUNKS + 1)]
    held = [
        (lax.optimization_barrier(own) if i else own)[i:j]
        for i, j in zip(bounds[:-1], bounds[1:])
    ]
    anywhere = pl.BlockSpec(memory_space=pl.ANY)
    scalars = pl.BlockSpec(memory_space=pltpu.SMEM)
    vmem = pl.BlockSpec(memory_space=pltpu.VMEM)
    compiler_params = pltpu.CompilerParams(vmem_limit_bytes=GRANT)
    tile_bytes = own.size * 2

    def cost(products, tiles):
        return pl.CostEstimate(
            flops=2 * size**3 * products,
            bytes_accessed=tiles * tile_bytes,
            transcendentals=0,
        )

    lists = pl.pallas_call(
        functools.partial(list_kernel, plan, bounds),
        out_shape=jax.ShapeDtypeStruct((plan.stages + CHUNKS, LANES), jnp.int32),
        in_specs=[anywhere] * 2,
        out_specs=vmem,
        scratch_shapes=[pltpu.VMEM(slot_rows.shape, jnp.int32)] * 2
        + [pltpu.VMEM((LANES, LANES), jnp.int32)] * 2
        + [pltpu.SemaphoreType.DMA((2,))],
        compiler_params=compiler_params,
        cost_estimate=cost(0, 2),
        name="list_products",
    )(slot_rows, slot_cols)
    rights = [[own]]
    for stage in range(1, plan.stages + 1):
        pairs = plan.hop_pairs(stage)
        if stage == JOIN:
            held[0], lists = lax.optimization_barrier((held[0], lists))
        arrived = []
        for part in held:
            arrived.append(lax.ppermute(part, ("col", "layer"), pairs))
        rights.append(arrived)
        held = list(arrived)
    everywhere = ("row", "col", "layer")
    far = plan.grid - 1
    lefts = [own]
    for by in range(1, far):
        lefts.append(lax.ppermute(own, everywhere, plan.row_pairs(by)))
    far_parts = []
    for by, part in ((1, lefts[1][:share]), (2, lefts[2][share:])):
        far_parts.append(lax.ppermute(part, everywhere, plan.row_pairs(far ^ by, by)))
    parts = [len(r) for r in rights]
    running = jax.ShapeDtypeStruct((slots + 1, size, size), jnp.float32)
    before = [part for stage in rights[:-1] for part in stage]
    total = pl.pallas_call(
        functools.partial(early_kernel, plan, parts[:-1]),
        out_shape=running,
        in_specs=[scalars] + [anywhere] * (len(lefts) + len(before)),
        out_specs=vmem,
        scratch_shapes=[
            pltpu.VMEM((plan.stages, *own.shape), own.dtype),
            pltpu.VMEM((plan.stages, *own.shape), own.dtype),
            pltpu.SemaphoreType.DMA((plan.stages,)),
            pltpu.SemaphoreType.DMA((plan.stages, CHUNKS)),
        ],
        compiler_params=compiler_params,
        cost_estimate=cost(slots * plan.stages, 2 * plan.stages),
        name="early_products",
    )(lists, *lefts, *before)
    first, *rest = rights[-1]
    total, left_last = pl.pallas_call(
        functools.partial(middle_kernel, plan, parts),
        out_shape=(running, jax.ShapeDtypeStruct(own.shape, own.dtype)),
        in_specs=[scalars, vmem]
        + [anywhere] * (len(lefts) + len(far_parts) + len(before))
        + [vmem],
        out_specs=(vmem, vmem),
        input_output_aliases={1: 0},
        scratch_shapes=[
            pltpu.VMEM(own.shape, own.dtype),
            pltpu.VMEM(own.shape, own.dtype),
            pltpu.SemaphoreType.DMA((2, 2)),
            pltpu.SemaphoreType.DMA((CHUNKS,)),
        ],
        compiler_params=compiler_params,
        cost_estimate=cost(slots, 4),
        name="middle_products",
    )(lists, total, *lefts, *far_parts, *before, first)
    half = jax.ShapeDtypeStruct((share, size, size), jnp.float32)
    _, mine, other = pl.pallas_call(
        functools.partial(last_kernel, plan, bounds),
        out_shape=(running, half, half),
        in_specs=[scalars] + [vmem] * (2 + len(rest)),
        out_specs=(vmem, vmem, vmem),
        input_output_aliases={1: 0},
        compiler_params=compiler_params,
        cost_estimate=cost(slots // 2, 4),
        name="last_products",
    )(lists, total, left_last, *rest)
    received = lax.ppermute(other, "layer", [(0, 1), (1, 0)])
    return (mine + received).astype(jnp.bfloat16)[None, None]


def solution(mesh):
    plan = Plan(mesh)

    def body(*args):
        return on_device(plan, *args)

    in_specs = (P("col", "row", None, None, None), P(), P())
    out_specs = P("col", "row", "layer", None, None)
    return jax.shard_map(
        body, mesh=mesh, in_specs=in_specs, out_specs=out_specs, check_vma=False
    )
```

profile of v0, /device:TPU:31, one launch (start us, length us, event | category | flops | bytes accessed | tf_op | source)
XLA Modules:
  0.0 51.5 jit_solution(18112315854467269748)
XLA Ops:
  0.0 1.1 %slice_bitcast_fusion = bf16[14,128,128]{2,1,0:T(8,128)(2,1)S(1)} fusion(bf16[1,1,28,128,128]{4,3,2,1,0:T(8,128)(2,1)} %param.3), kind=kLoop, calls=%fused_computation.2 | loop fusion | bytes 917504 | tf_op jit(solution)/shard_map/slice | solution.py:295
  1.1 2.1 %collective-permute-start = (bf16[14,128,128]{2,1,0:T(8,128)(2,1)S(1)}, bf16[14,128,128]{2,1,0:T(8,128)(2,1)S(1)}, u32[]{:S(2)}, u32[]{:S(2)}) collective-permute-start(bf16[14,128,128]{2,1,0:T(8,128)(2,1)S(1)} %slice_bitcast_fusion), channel_id=1, source_target_pairs={{0,2},{2,4},{3,1},{4,6},{5,3},{7,5},{8,10},{10,12},{11,9},{12,14},... | collective-permute-start | bytes 1376264 | tf_op jit(solution)/shard_map/ppermute | solution.py:330
  3.2 0.7 %collective-permute-start.2 = (bf16[28,128,128]{2,1,0:T(8,128)(2,1)}, bf16[28,128,128]{2,1,0:T(8,128)(2,1)S(1)}, u32[]{:S(2)}, u32[]{:S(2)}) collective-permute-start(bf16[28,128,128]{2,1,0:T(8,128)(2,1)} %bitcast.5), channel_id=1, source_target_pairs={{0,8},{2,10},{4,12},{6,14},{9,1},{10,2},{12,4},{14,6},{17,25},{19,... | collective-permute-start | bytes 2752520 | tf_op jit(solution)/shard_map/ppermute | solution.py:337
  4.0 0.7 %collective-permute-start.3 = (bf16[28,128,128]{2,1,0:T(8,128)(2,1)}, bf16[28,128,128]{2,1,0:T(8,128)(2,1)S(1)}, u32[]{:S(2)}, u32[]{:S(2)}) collective-permute-start(bf16[28,128,128]{2,1,0:T(8,128)(2,1)} %bitcast.6), channel_id=1, source_target_pairs={{0,16},{2,18},{4,20},{6,22},{9,25},{10,26},{12,28},{14,30},{17,1},... | collective-permute-start | bytes 2752520 | tf_op jit(solution)/shard_map/ppermute | solution.py:337
  4.7 1.1 %slice.20 = bf16[14,128,128]{2,1,0:T(8,128)(2,1)S(1)} slice(bf16[28,128,128]{2,1,0:T(8,128)(2,1)} %bitcast.7), slice={[14:28], [0:128], [0:128]} | slice | bytes 917504 | tf_op jit(solution)/shard_map/slice | solution.py:295
  5.8 4.2 %collective-permute-start.4 = (bf16[14,128,128]{2,1,0:T(8,128)(2,1)S(1)}, bf16[14,128,128]{2,1,0:T(8,128)(2,1)S(1)}, u32[]{:S(2)}, u32[]{:S(2)}) collective-permute-start(bf16[14,128,128]{2,1,0:T(8,128)(2,1)S(1)} %slice.20), channel_id=1, source_target_pairs={{0,2},{2,4},{3,1},{4,6},{5,3},{7,5},{8,10},{10,12},{11,9},{12,14},... | collective-permute-start | bytes 1376264 | tf_op jit(solution)/shard_map/ppermute | solution.py:330
  10.0 0.0 collective-permute-done.refs_4_.refs_6_
  10.0 0.7 %collective-permute-start.1 = (bf16[14,128,128]{2,1,0:T(8,128)(2,1)S(1)}, bf16[14,128,128]{2,1,0:T(8,128)(2,1)S(1)}, u32[]{:S(2)}, u32[]{:S(2)}) collective-permute-start(bf16[14,128,128]{2,1,0:T(8,128)(2,1)S(1)} %collective-permute-done.refs_4_.refs_6_), channel_id=1, source_target_pairs={{2,4},{3,1},{4,6},{5,3},{10,12},{11,9},{12,14},{13,11},{18,20},{19... | collective-permute-start | bytes 1376264 | tf_op jit(solution)/shard_map/ppermute | solution.py:330
  10.7 4.7 %collective-permute-done.4.refs_5_.refs_7_ = bf16[14,128,128]{2,1,0:T(8,128)(2,1)S(1)} collective-permute-done((bf16[14,128,128]{2,1,0:T(8,128)(2,1)S(1)}, bf16[14,128,128]{2,1,0:T(8,128)(2,1)S(1)}, u32[]{:S(2)}, u32[]{:S(2)}) %collective-permute-start.4) | collective-permute-done | bytes 458784 | tf_op jit(solution)/shard_map/ppermute | solution.py:330
  15.4 0.7 %collective-permute-start.5 = (bf16[14,128,128]{2,1,0:T(8,128)(2,1)S(1)}, bf16[14,128,128]{2,1,0:T(8,128)(2,1)S(1)}, u32[]{:S(2)}, u32[]{:S(2)}) collective-permute-start(bf16[14,128,128]{2,1,0:T(8,128)(2,1)S(1)} %collective-permute-done.4.refs_5_.refs_7_), channel_id=1, source_target_pairs={{2,4},{3,1},{4,6},{5,3},{10,12},{11,9},{12,14},{13,11},{18,20},{19... | collective-permute-start | bytes 1376264 | tf_op jit(solution)/shard_map/ppermute | solution.py:330
  16.0 0.0 copy-start.1
  16.1 0.7 %copy-done.1 = s32[4,4,28]{2,1,0:T(4,128)S(1)} copy-done((s32[4,4,28]{2,1,0:T(4,128)S(1)}, s32[4,4,28]{2,1,0:T(4,128)}, u32[]{:S(2)}) %copy-start.1) | copy-done | bytes 1816
  16.7 0.7 %copy-done.2 = s32[4,4,28]{2,1,0:T(4,128)S(1)} copy-done((s32[4,4,28]{2,1,0:T(4,128)S(1)}, s32[4,4,28]{2,1,0:T(4,128)}, u32[]{:S(2)}) %copy-start.2) | copy-done | bytes 1816
  17.4 1.0 %list_products.1.pairs = s32[5,128]{1,0:T(8,128)S(1)} custom-call(s32[4,4,28]{2,1,0:T(4,128)S(1)} %copy-done.1, s32[4,4,28]{2,1,0:T(4,128)S(1)} %copy-done.2), custom_call_target="tpu_custom_call" | custom-call | bytes 1835008 | tf_op jit(solution)/shard_map/list_products/pallas_call | solution.py:311
  18.4 0.0 collective-permute-done.1.refs_6_.refs_8_
  18.4 0.0 collective-permute-done.2.refs_1_
  18.5 0.7 %collective-permute-start.6 = (bf16[14,128,128]{2,1,0:T(8,128)(2,1)S(1)}, bf16[14,128,128]{2,1,0:T(8,128)(2,1)S(1)}, u32[]{:S(2)}, u32[]{:S(2)}) collective-permute-start(bf16[14,128,128]{2,1,0:T(8,128)(2,1)S(1)} %slice.21), channel_id=1, source_target_pairs={{8,24},{10,26},{12,28},{14,30},{1,17},{2,18},{4,20},{6,22},{25,9},... | collective-permute-start | bytes 1376264 | tf_op jit(solution)/shard_map/ppermute | solution.py:340
  19.2 0.0 collective-permute-done.3.refs_2_
  19.2 0.7 %collective-permute-start.7 = (bf16[14,128,128]{2,1,0:T(8,128)(2,1)S(1)}, bf16[14,128,128]{2,1,0:T(8,128)(2,1)S(1)}, u32[]{:S(2)}, u32[]{:S(2)}) collective-permute-start(bf16[14,128,128]{2,1,0:T(8,128)(2,1)S(1)} %slice.22), channel_id=1, source_target_pairs={{16,24},{18,26},{20,28},{22,30},{25,17},{26,18},{28,20},{30,22},{1... | collective-permute-start | bytes 1376264 | tf_op jit(solution)/shard_map/ppermute | solution.py:340
  19.9 0.7 %collective-permute-start.8 = (bf16[14,128,128]{2,1,0:T(8,128)(2,1)S(1)}, bf16[14,128,128]{2,1,0:T(8,128)(2,1)S(1)}, u32[]{:S(2)}, u32[]{:S(2)}) collective-permute-start(bf16[14,128,128]{2,1,0:T(8,128)(2,1)S(1)} %collective-permute-done.1.refs_6_.refs_8_), channel_id=1, source_target_pairs={{3,1},{4,6},{11,9},{12,14},{19,17},{20,22},{27,25},{28,30}} | collective-permute-start | bytes 1376264 | tf_op jit(solution)/shard_map/ppermute | solution.py:330
  20.6 0.0 collective-permute-done.5.refs_7_.refs_9_
  20.6 0.7 %collective-permute-start.9 = (bf16[14,128,128]{2,1,0:T(8,128)(2,1)S(1)}, bf16[14,128,128]{2,1,0:T(8,128)(2,1)S(1)}, u32[]{:S(2)}, u32[]{:S(2)}) collective-permute-start(bf16[14,128,128]{2,1,0:T(8,128)(2,1)S(1)} %collective-permute-done.5.refs_7_.refs_9_), channel_id=1, source_target_pairs={{3,1},{4,6},{11,9},{12,14},{19,17},{20,22},{27,25},{28,30}} | collective-permute-start | bytes 1376264 | tf_op jit(solution)/shard_map/ppermute | solution.py:330
  21.4 0.9 %early_products.1.total = f32[29,128,128]{2,1,0:T(8,128)S(1)} custom-call(s32[5,128]{1,0:T(8,128)S(1)} %list_products.1.pairs, bf16[28,128,128]{2,1,0:T(8,128)(2,1)S(1)} %bitcast.8, bf16[28,128,128]{2,1,0:T(8,128)(2,1)S(1)} %collective-permute-done.2.refs_1_, bf16[28,128,128]{2,1,0:T(8,128)(2,1)S(1)} %collective-permute-done.3.refs_2_, ...), custom_call_target="tpu_custom_call" | custom-call | flops 352321536 | bytes 5505024 | tf_op jit(solution)/shard_map/early_products/pallas_call | solution.py:344
  22.2 0.0 collective-permute-done.6.refs_3_
  22.2 0.0 collective-permute-done.7.refs_4_
  22.2 0.0 collective-permute-done.8.refs_10_
  22.3 1.0 %middle_products.1 = (f32[29,128,128]{2,1,0:T(8,128)S(1)}, bf16[28,128,128]{2,1,0:T(8,128)(2,1)S(1)}) custom-call(s32[5,128]{1,0:T(8,128)S(1)} %list_products.1.pairs, f32[29,128,128]{2,1,0:T(8,128)S(1)} %early_products.1.total, bf16[28,128,128]{2,1,0:T(8,128)(2,1)S(1)} %bitcast.10, ...), custom_call_target="tpu_custom_call", output_to_operand_aliasing={{0}: (1, {})} | custom-call | flops 117440512 | bytes 3670016 | tf_op jit(solution)/shard_map/middle_products/pallas_call | solution.py:360
  23.2 0.0 collective-permute-done.9.refs_0_
  23.2 0.7 %last_products.1 = (f32[29,128,128]{2,1,0:T(8,128)S(1)}, f32[14,128,128]{2,1,0:T(8,128)S(1)}, f32[14,128,128]{2,1,0:T(8,128)S(1)}) custom-call(s32[5,128]{1,0:T(8,128)S(1)} %list_products.1.pairs, f32[29,128,128]{2,1,0:T(8,128)S(1)} %get-tuple-element.13.total, ...), custom_call_target="tpu_custom_call", output_to_operand_aliasing={{0}: (1, {})} | custom-call | flops 58720256 | bytes 3670016 | tf_op jit(solution)/shard_map/last_products/pallas_call | solution.py:379
  24.0 24.5 %collective-permute-start.10 = (f32[14,128,128]{2,1,0:T(8,128)S(1)}, f32[14,128,128]{2,1,0:T(8,128)S(1)}, u32[]{:S(2)}, u32[]{:S(2)}) collective-permute-start(f32[14,128,128]{2,1,0:T(8,128)S(1)} %get-tuple-element.16), channel_id=1, source_target_pairs={{0,1},{1,0},{2,3},{3,2},{4,5},{5,4},{6,7},{7,6},{8,9},{9,8},{10,11... | collective-permute-start | bytes 2752520 | tf_op jit(solution)/shard_map/ppermute | solution.py:389
  48.5 2.1 %collective-permute-done.10 = f32[14,128,128]{2,1,0:T(8,128)S(1)} collective-permute-done((f32[14,128,128]{2,1,0:T(8,128)S(1)}, f32[14,128,128]{2,1,0:T(8,128)S(1)}, u32[]{:S(2)}, u32[]{:S(2)}) %collective-permute-start.10) | collective-permute-done | bytes 917536 | tf_op jit(solution)/shard_map/ppermute | solution.py:389
  50.6 0.9 %fusion = bf16[1,1,14,128,128]{4,3,2,1,0:T(8,128)(2,1)} fusion(f32[14,128,128]{2,1,0:T(8,128)S(1)} %get-tuple-element.15, f32[14,128,128]{2,1,0:T(8,128)S(1)} %collective-permute-done.10), kind=kLoop, calls=%fused_computation.1 | loop fusion | flops 458752 | bytes 2293760 | tf_op jit(solution)/shard_map/broadcast_in_dim | solution.py:390
  (5 shorter events, 0.1 us)
Async XLA Ops:
  0.0 21.3 %copy-start = (bf16[1,1,28,128,128]{4,3,2,1,0:T(8,128)(2,1)S(1)}, bf16[1,1,28,128,128]{4,3,2,1,0:T(8,128)(2,1)}, u32[]{:S(2)}) copy-start(bf16[1,1,28,128,128]{4,3,2,1,0:T(8,128)(2,1)} %param.3) | copy-start | bytes 2752516
  1.1 8.8 %collective-permute-start = (bf16[14,128,128]{2,1,0:T(8,128)(2,1)S(1)}, bf16[14,128,128]{2,1,0:T(8,128)(2,1)S(1)}, u32[]{:S(2)}, u32[]{:S(2)}) collective-permute-start(bf16[14,128,128]{2,1,0:T(8,128)(2,1)S(1)} %slice_bitcast_fusion), channel_id=1, source_target_pairs={{0,2},{2,4},{3,1},{4,6},{5,3},{7,5},{8,10},{10,12},{11,9},{12,14},... | collective-permute-start | bytes 1376264 | tf_op jit(solution)/shard_map/ppermute | solution.py:330
  3.2 15.2 %collective-permute-start.2 = (bf16[28,128,128]{2,1,0:T(8,128)(2,1)}, bf16[28,128,128]{2,1,0:T(8,128)(2,1)S(1)}, u32[]{:S(2)}, u32[]{:S(2)}) collective-permute-start(bf16[28,128,128]{2,1,0:T(8,128)(2,1)} %bitcast.5), channel_id=1, source_target_pairs={{0,8},{2,10},{4,12},{6,14},{9,1},{10,2},{12,4},{14,6},{17,25},{19,... | collective-permute-start | bytes 2752520 | tf_op jit(solution)/shard_map/ppermute | solution.py:337
  4.0 15.2 %collective-permute-start.3 = (bf16[28,128,128]{2,1,0:T(8,128)(2,1)}, bf16[28,128,128]{2,1,0:T(8,128)(2,1)S(1)}, u32[]{:S(2)}, u32[]{:S(2)}) collective-permute-start(bf16[28,128,128]{2,1,0:T(8,128)(2,1)} %bitcast.6), channel_id=1, source_target_pairs={{0,16},{2,18},{4,20},{6,22},{9,25},{10,26},{12,28},{14,30},{17,1},... | collective-permute-start | bytes 2752520 | tf_op jit(solution)/shard_map/ppermute | solution.py:337
  5.8 9.6 %collective-permute-start.4 = (bf16[14,128,128]{2,1,0:T(8,128)(2,1)S(1)}, bf16[14,128,128]{2,1,0:T(8,128)(2,1)S(1)}, u32[]{:S(2)}, u32[]{:S(2)}) collective-permute-start(bf16[14,128,128]{2,1,0:T(8,128)(2,1)S(1)} %slice.20), channel_id=1, source_target_pairs={{0,2},{2,4},{3,1},{4,6},{5,3},{7,5},{8,10},{10,12},{11,9},{12,14},... | collective-permute-start | bytes 1376264 | tf_op jit(solution)/shard_map/ppermute | solution.py:330
  10.0 8.4 %collective-permute-start.1 = (bf16[14,128,128]{2,1,0:T(8,128)(2,1)S(1)}, bf16[14,128,128]{2,1,0:T(8,128)(2,1)S(1)}, u32[]{:S(2)}, u32[]{:S(2)}) collective-permute-start(bf16[14,128,128]{2,1,0:T(8,128)(2,1)S(1)} %collective-permute-done.refs_4_.refs_6_), channel_id=1, source_target_pairs={{2,4},{3,1},{4,6},{5,3},{10,12},{11,9},{12,14},{13,11},{18,20},{19... | collective-permute-start | bytes 1376264 | tf_op jit(solution)/shard_map/ppermute | solution.py:330
  15.4 5.3 %collective-permute-start.5 = (bf16[14,128,128]{2,1,0:T(8,128)(2,1)S(1)}, bf16[14,128,128]{2,1,0:T(8,128)(2,1)S(1)}, u32[]{:S(2)}, u32[]{:S(2)}) collective-permute-start(bf16[14,128,128]{2,1,0:T(8,128)(2,1)S(1)} %collective-permute-done.4.refs_5_.refs_7_), channel_id=1, source_target_pairs={{2,4},{3,1},{4,6},{5,3},{10,12},{11,9},{12,14},{13,11},{18,20},{19... | collective-permute-start | bytes 1376264 | tf_op jit(solution)/shard_map/ppermute | solution.py:330
  16.0 0.7 %copy-start.1 = (s32[4,4,28]{2,1,0:T(4,128)S(1)}, s32[4,4,28]{2,1,0:T(4,128)}, u32[]{:S(2)}) copy-start(s32[4,4,28]{2,1,0:T(4,128)} %rows_in.1) | copy-start | bytes 5380
  16.7 0.7 %copy-start.2 = (s32[4,4,28]{2,1,0:T(4,128)S(1)}, s32[4,4,28]{2,1,0:T(4,128)}, u32[]{:S(2)}) copy-start(s32[4,4,28]{2,1,0:T(4,128)} %cols_in.1) | copy-start | bytes 5380
  18.5 3.7 %collective-permute-start.6 = (bf16[14,128,128]{2,1,0:T(8,128)(2,1)S(1)}, bf16[14,128,128]{2,1,0:T(8,128)(2,1)S(1)}, u32[]{:S(2)}, u32[]{:S(2)}) collective-permute-start(bf16[14,128,128]{2,1,0:T(8,128)(2,1)S(1)} %slice.21), channel_id=1, source_target_pairs={{8,24},{10,26},{12,28},{14,30},{1,17},{2,18},{4,20},{6,22},{25,9},... | collective-permute-start | bytes 1376264 | tf_op jit(solution)/shard_map/ppermute | solution.py:340
  19.2 3.0 %collective-permute-start.7 = (bf16[14,128,128]{2,1,0:T(8,128)(2,1)S(1)}, bf16[14,128,128]{2,1,0:T(8,128)(2,1)S(1)}, u32[]{:S(2)}, u32[]{:S(2)}) collective-permute-start(bf16[14,128,128]{2,1,0:T(8,128)(2,1)S(1)} %slice.22), channel_id=1, source_target_pairs={{16,24},{18,26},{20,28},{22,30},{25,17},{26,18},{28,20},{30,22},{1... | collective-permute-start | bytes 1376264 | tf_op jit(solution)/shard_map/ppermute | solution.py:340
  19.9 2.3 %collective-permute-start.8 = (bf16[14,128,128]{2,1,0:T(8,128)(2,1)S(1)}, bf16[14,128,128]{2,1,0:T(8,128)(2,1)S(1)}, u32[]{:S(2)}, u32[]{:S(2)}) collective-permute-start(bf16[14,128,128]{2,1,0:T(8,128)(2,1)S(1)} %collective-permute-done.1.refs_6_.refs_8_), channel_id=1, source_target_pairs={{3,1},{4,6},{11,9},{12,14},{19,17},{20,22},{27,25},{28,30}} | collective-permute-start | bytes 1376264 | tf_op jit(solution)/shard_map/ppermute | solution.py:330
  20.6 2.6 %collective-permute-start.9 = (bf16[14,128,128]{2,1,0:T(8,128)(2,1)S(1)}, bf16[14,128,128]{2,1,0:T(8,128)(2,1)S(1)}, u32[]{:S(2)}, u32[]{:S(2)}) collective-permute-start(bf16[14,128,128]{2,1,0:T(8,128)(2,1)S(1)} %collective-permute-done.5.refs_7_.refs_9_), channel_id=1, source_target_pairs={{3,1},{4,6},{11,9},{12,14},{19,17},{20,22},{27,25},{28,30}} | collective-permute-start | bytes 1376264 | tf_op jit(solution)/shard_map/ppermute | solution.py:330
  24.0 26.6 %collective-permute-start.10 = (f32[14,128,128]{2,1,0:T(8,128)S(1)}, f32[14,128,128]{2,1,0:T(8,128)S(1)}, u32[]{:S(2)}, u32[]{:S(2)}) collective-permute-start(f32[14,128,128]{2,1,0:T(8,128)S(1)} %get-tuple-element.16), channel_id=1, source_target_pairs={{0,1},{1,0},{2,3},{3,2},{4,5},{5,4},{6,7},{7,6},{8,9},{9,8},{10,11... | collective-permute-start | bytes 2752520 | tf_op jit(solution)/shard_map/ppermute | solution.py:389
where the time goes:
time: 51.9 us; the launch traced here: 51.5 us
  starting transfers between devices  36.4 us (70%)
  waiting for transfers between devices  6.79 us (13%)
  local copies, waits for them, and re-layouts  3.64 us (7%)
  Pallas kernels  3.56 us (7%)
  other arithmetic  0.9 us (2%)
    ppermute x1, starting transfers between devices, on_device(): received = lax.ppermute(other, 'layer', [(0, 1), (1, 0)])  24.5 us
    ppermute x6, starting transfers between devices, on_device(): arrived.append(lax.ppermute(part, ('col', 'layer'), pairs))  9.06 us
    ppermute x6, waiting for transfers between devices, on_device(): arrived.append(lax.ppermute(part, ('col', 'layer'), pairs))  4.68 us
    slice x2, local copies, waits for them, and re-layouts, on_device(): (lax.optimization_barrier(own) if i else own)[i:j]  2.18 us
    ppermute x1, waiting for transfers between devices, on_device(): received = lax.ppermute(other, 'layer', [(0, 1), (1, 0)])  2.1 us
    ppermute x2, starting transfers between devices, on_device(): lefts.append(lax.ppermute(own, everywhere, plan.row_pairs(by)))  1.44 us
    unnamed x6, local copies, waits for them, and re-layouts  1.39 us
    ppermute x2, starting transfers between devices, on_device(): lax.ppermute(part, everywhere, plan.row_pairs(far ^ by, by))  1.38 us
  transfers between devices with their start and end apart: 11, of which 2 were waited for; matrix products, arithmetic and copies ran while one was open for 2% of the time, Pallas kernels for 5%

commit v1 on v0

--- a/solution.py
+++ b/solution.py
@@ -8,11 +8,10 @@
 from jax.sharding import PartitionSpec as P
 
 TB = 28
-GROUP = 4
+GROUP = 8
 LANES = 128
 GRANT = 16 << 20
 CHUNKS = 2
-JOIN = 3
 
 
 class Plan:
@@ -42,7 +41,7 @@
                     pairs.append((source * 2 + layer, target * 2 + layer))
         return pairs
 
-    def row_pairs(self, by, held=0):
+    def row_pairs(self, by):
         pairs = []
         for r in range(self.grid):
             for a in range(self.grid):
@@ -50,10 +49,7 @@
                 if k is not None:
                     layer = int(k > 0)
                     pairs.append(
-                        tuple(
-                            (p * self.grid + a) * 2 + layer
-                            for p in (r ^ held, r ^ held ^ by)
-                        )
+                        tuple((p * self.grid + a) * 2 + layer for p in (r, r ^ by))
                     )
         return pairs
 
@@ -232,45 +228,35 @@
 
 def middle_kernel(plan, parts, pairs, total, *refs):
     del total
-    lefts = dict(enumerate(refs[: plan.grid - 1]))
-    refs = refs[plan.grid - 1 :]
-    far_parts, refs = refs[:2], refs[2:]
+    lefts = dict(enumerate(refs[: plan.grid]))
+    refs = refs[plan.grid :]
     rights = []
     for n in parts[:-1]:
         rights.append(refs[:n])
         refs = refs[n:]
-    first, acc, left_last, left, right, left_sem, right_sem = refs
+    first, acc, left_last, right, left_sem, right_sem = refs
     far, end, last = plan.grid - 1, plan.stages, pairs.shape[1] - 1
     a, b, layer = place()
     l, _ = plan.taken(a, layer, end)
-    end_by = b ^ l
-
-    @pl.when(end_by == far)
-    def _():
-        fetch(far_parts, left_last, left_sem.at[1])
-
-    fetch_left(lefts, end_by, left_last, left_sem.at[1, 0])
+    fetch_left(lefts, b ^ l, left_last, left_sem)
+    counts = []
     for stage in range(end):
         l, _ = plan.taken(a, layer, stage)
         count = jnp.where(b ^ l == far, pairs[stage, last], 0)
+        counts.append(count)
+
+        @pl.when(count > 0)
+        def _(stage=stage):
+            fetch(rights[stage], right, right_sem)
+
+    pltpu.make_async_copy(lefts[0], left_last, left_sem).wait()
+    add_products(pairs[end, last], pairs, end, left_last, first, acc)
+    for stage, count in enumerate(counts):
 
         @pl.when(count > 0)
         def _(stage=stage, count=count):
-            fetch(rights[stage], right, right_sem)
-            fetch(far_parts, left, left_sem.at[0])
             fetched(rights[stage], right, right_sem)
-            fetched(far_parts, left, left_sem.at[0])
-            add_products(count, pairs, stage, left, right, acc)
-
-    @pl.when(end_by == far)
-    def _():
-        fetched(far_parts, left_last, left_sem.at[1])
-
-    @pl.when((end_by >= 0) & (end_by < far))
-    def _():
-        pltpu.make_async_copy(lefts[0], left_last, left_sem.at[1, 0]).wait()
-
-    add_products(pairs[end, last], pairs, end, left_last, first, acc)
+            add_products(count, pairs, stage, lefts[far], right, acc)
 
 
 def last_kernel(plan, bounds, pairs, total, left_last, *refs):
@@ -311,7 +297,7 @@
     lists = pl.pallas_call(
         functools.partial(list_kernel, plan, bounds),
         out_shape=jax.ShapeDtypeStruct((plan.stages + CHUNKS, LANES), jnp.int32),
-        in_specs=[anywhere] * 2,
+        in_specs=[pl.BlockSpec(memory_space=pltpu.HBM)] * 2,
         out_specs=vmem,
         scratch_shapes=[pltpu.VMEM(slot_rows.shape, jnp.int32)] * 2
         + [pltpu.VMEM((LANES, LANES), jnp.int32)] * 2
@@ -323,28 +309,23 @@
     rights = [[own]]
     for stage in range(1, plan.stages + 1):
         pairs = plan.hop_pairs(stage)
-        if stage == JOIN:
-            held[0], lists = lax.optimization_barrier((held[0], lists))
         arrived = []
         for part in held:
             arrived.append(lax.ppermute(part, ("col", "layer"), pairs))
         rights.append(arrived)
         held = list(arrived)
     everywhere = ("row", "col", "layer")
-    far = plan.grid - 1
     lefts = [own]
-    for by in range(1, far):
+    for by in range(1, plan.grid):
         lefts.append(lax.ppermute(own, everywhere, plan.row_pairs(by)))
-    far_parts = []
-    for by, part in ((1, lefts[1][:share]), (2, lefts[2][share:])):
-        far_parts.append(lax.ppermute(part, everywhere, plan.row_pairs(far ^ by, by)))
+    *near, far = lefts
     parts = [len(r) for r in rights]
     running = jax.ShapeDtypeStruct((slots + 1, size, size), jnp.float32)
     before = [part for stage in rights[:-1] for part in stage]
     total = pl.pallas_call(
         functools.partial(early_kernel, plan, parts[:-1]),
         out_shape=running,
-        in_specs=[scalars] + [anywhere] * (len(lefts) + len(before)),
+        in_specs=[scalars] + [anywhere] * (len(near) + len(before)),
         out_specs=vmem,
         scratch_shapes=[
             pltpu.VMEM((plan.stages, *own.shape), own.dtype),
@@ -355,26 +336,27 @@
         compiler_params=compiler_params,
         cost_estimate=cost(slots * plan.stages, 2 * plan.stages),
         name="early_products",
-    )(lists, *lefts, *before)
+    )(lists, *near, *before)
     first, *rest = rights[-1]
     total, left_last = pl.pallas_call(
         functools.partial(middle_kernel, plan, parts),
         out_shape=(running, jax.ShapeDtypeStruct(own.shape, own.dtype)),
         in_specs=[scalars, vmem]
-        + [anywhere] * (len(lefts) + len(far_parts) + len(before))
+        + [anywhere] * len(near)
+        + [vmem]
+        + [anywhere] * len(before)
         + [vmem],
         out_specs=(vmem, vmem),
         input_output_aliases={1: 0},
         scratch_shapes=[
             pltpu.VMEM(own.shape, own.dtype),
-            pltpu.VMEM(own.shape, own.dtype),
-            pltpu.SemaphoreType.DMA((2, 2)),
+            pltpu.SemaphoreType.DMA,
             pltpu.SemaphoreType.DMA((CHUNKS,)),
         ],
         compiler_params=compiler_params,
         cost_estimate=cost(slots, 4),
         name="middle_products",
-    )(lists, total, *lefts, *far_parts, *before, first)
+    )(lists, total, *near, far, *before, first)
     half = jax.ShapeDtypeStruct((share, size, size), jnp.float32)
     _, mine, other = pl.pallas_call(
         functools.partial(last_kernel, plan, bounds),

time: 51.9 us -> 47.2 us (0.909)
  the two profiles are of different devices: /device:TPU:31 before, /device:TPU:17 now
where the time goes in v1:
time: 47.2 us; the launch traced here: 46.8 us
  starting transfers between devices  21.9 us (46%)
  waiting for transfers between devices  15.9 us (34%)
  Pallas kernels  4.34 us (9%)
  local copies, waits for them, and re-layouts  3.57 us (8%)
  other arithmetic  0.9 us (2%)
    ppermute x1, starting transfers between devices, on_device(): received = lax.ppermute(other, 'layer', [(0, 1), (1, 0)])  9.65 us
    ppermute x6, starting transfers between devices, on_device(): arrived.append(lax.ppermute(part, ('col', 'layer'), pairs))  9.54 us
    ppermute x6, waiting for transfers between devices, on_device(): arrived.append(lax.ppermute(part, ('col', 'layer'), pairs))  9.53 us
    ppermute x3, waiting for transfers between devices, on_device(): lefts.append(lax.ppermute(own, everywhere, plan.row_pairs(by)))  4.27 us
    ppermute x3, starting transfers between devices, on_device(): lefts.append(lax.ppermute(own, everywhere, plan.row_pairs(by)))  2.73 us
    slice x2, local copies, waits for them, and re-layouts, on_device(): (lax.optimization_barrier(own) if i else own)[i:j]  2.18 us
    ppermute x1, waiting for transfers between devices, on_device(): received = lax.ppermute(other, 'layer', [(0, 1), (1, 0)])  2.1 us
    pallas_call x1, Pallas kernels, on_device(): pl.pallas_call(functools.partial(middle_kernel, plan, parts), out_shape=(...  1.76 us
  transfers between devices with their start and end apart: 10, of which 6 were waited for; matrix products, arithmetic and copies ran while one was open for 2% of the time, Pallas kernels for 8%

profile of v1, /device:TPU:17, one launch (start us, length us, event | category | flops | bytes accessed | tf_op | source)
XLA Modules:
  0.0 46.8 jit_solution(9118105261916825552)
XLA Ops:
  0.0 0.0 copy-start
  0.0 1.1 %slice_bitcast_fusion = bf16[14,128,128]{2,1,0:T(8,128)(2,1)S(1)} fusion(bf16[1,1,28,128,128]{4,3,2,1,0:T(8,128)(2,1)} %param.3), kind=kLoop, calls=%fused_computation.2 | loop fusion | bytes 917504 | tf_op jit(solution)/shard_map/slice | solution.py:281
  1.1 2.1 %collective-permute-start.2 = (bf16[14,128,128]{2,1,0:T(8,128)(2,1)S(1)}, bf16[14,128,128]{2,1,0:T(8,128)(2,1)S(1)}, u32[]{:S(2)}, u32[]{:S(2)}) collective-permute-start(bf16[14,128,128]{2,1,0:T(8,128)(2,1)S(1)} %slice_bitcast_fusion), channel_id=1, source_target_pairs={{0,2},{2,4},{3,1},{4,6},{5,3},{7,5},{8,10},{10,12},{11,9},{12,14},... | collective-permute-start | bytes 1376264 | tf_op jit(solution)/shard_map/ppermute | solution.py:314
  3.2 1.1 %slice.12 = bf16[14,128,128]{2,1,0:T(8,128)(2,1)S(1)} slice(bf16[28,128,128]{2,1,0:T(8,128)(2,1)} %bitcast.5), slice={[14:28], [0:128], [0:128]} | slice | bytes 917504 | tf_op jit(solution)/shard_map/slice | solution.py:281
  4.3 1.9 %collective-permute-start.3 = (bf16[14,128,128]{2,1,0:T(8,128)(2,1)S(1)}, bf16[14,128,128]{2,1,0:T(8,128)(2,1)S(1)}, u32[]{:S(2)}, u32[]{:S(2)}) collective-permute-start(bf16[14,128,128]{2,1,0:T(8,128)(2,1)S(1)} %slice.12), channel_id=1, source_target_pairs={{0,2},{2,4},{3,1},{4,6},{5,3},{7,5},{8,10},{10,12},{11,9},{12,14},... | collective-permute-start | bytes 1376264 | tf_op jit(solution)/shard_map/ppermute | solution.py:314
  6.2 0.7 %collective-permute-start = (bf16[28,128,128]{2,1,0:T(8,128)(2,1)}, bf16[28,128,128]{2,1,0:T(8,128)(2,1)S(1)}, u32[]{:S(2)}, u32[]{:S(2)}) collective-permute-start(bf16[28,128,128]{2,1,0:T(8,128)(2,1)} %bitcast.6), channel_id=1, source_target_pairs={{0,8},{2,10},{4,12},{6,14},{9,1},{10,2},{12,4},{14,6},{17,25},{19,... | collective-permute-start | bytes 2752520 | tf_op jit(solution)/shard_map/ppermute | solution.py:320
  6.9 0.7 %collective-permute-start.1 = (bf16[28,128,128]{2,1,0:T(8,128)(2,1)}, bf16[28,128,128]{2,1,0:T(8,128)(2,1)S(1)}, u32[]{:S(2)}, u32[]{:S(2)}) collective-permute-start(bf16[28,128,128]{2,1,0:T(8,128)(2,1)} %bitcast.7), channel_id=1, source_target_pairs={{0,16},{2,18},{4,20},{6,22},{9,25},{10,26},{12,28},{14,30},{17,1},... | collective-permute-start | bytes 2752520 | tf_op jit(solution)/shard_map/ppermute | solution.py:320
  7.7 1.3 %collective-permute-start.6 = (bf16[28,128,128]{2,1,0:T(8,128)(2,1)}, bf16[28,128,128]{2,1,0:T(8,128)(2,1)S(1)}, u32[]{:S(2)}, u32[]{:S(2)}) collective-permute-start(bf16[28,128,128]{2,1,0:T(8,128)(2,1)} %bitcast.8), channel_id=1, source_target_pairs={{0,24},{2,26},{4,28},{6,30},{9,17},{10,18},{12,20},{14,22},{17,9},... | collective-permute-start | bytes 2752520 | tf_op jit(solution)/shard_map/ppermute | solution.py:320
  9.0 1.7 %collective-permute-done.2.refs_4_.refs_5_ = bf16[14,128,128]{2,1,0:T(8,128)(2,1)S(1)} collective-permute-done((bf16[14,128,128]{2,1,0:T(8,128)(2,1)S(1)}, bf16[14,128,128]{2,1,0:T(8,128)(2,1)S(1)}, u32[]{:S(2)}, u32[]{:S(2)}) %collective-permute-start.2) | collective-permute-done | bytes 458784 | tf_op jit(solution)/shard_map/ppermute | solution.py:314
  10.7 2.1 %collective-permute-start.4 = (bf16[14,128,128]{2,1,0:T(8,128)(2,1)S(1)}, bf16[14,128,128]{2,1,0:T(8,128)(2,1)S(1)}, u32[]{:S(2)}, u32[]{:S(2)}) collective-permute-start(bf16[14,128,128]{2,1,0:T(8,128)(2,1)S(1)} %collective-permute-done.2.refs_4_.refs_5_), channel_id=1, source_target_pairs={{2,4},{3,1},{4,6},{5,3},{10,12},{11,9},{12,14},{13,11},{18,20},{19... | collective-permute-start | bytes 1376264 | tf_op jit(solution)/shard_map/ppermute | solution.py:314
  12.8 2.8 %collective-permute-done.3.refs_5_.refs_6_ = bf16[14,128,128]{2,1,0:T(8,128)(2,1)S(1)} collective-permute-done((bf16[14,128,128]{2,1,0:T(8,128)(2,1)S(1)}, bf16[14,128,128]{2,1,0:T(8,128)(2,1)S(1)}, u32[]{:S(2)}, u32[]{:S(2)}) %collective-permute-start.3) | collective-permute-done | bytes 458784 | tf_op jit(solution)/shard_map/ppermute | solution.py:314
  15.6 2.1 %collective-permute-start.5 = (bf16[14,128,128]{2,1,0:T(8,128)(2,1)S(1)}, bf16[14,128,128]{2,1,0:T(8,128)(2,1)S(1)}, u32[]{:S(2)}, u32[]{:S(2)}) collective-permute-start(bf16[14,128,128]{2,1,0:T(8,128)(2,1)S(1)} %collective-permute-done.3.refs_5_.refs_6_), channel_id=1, source_target_pairs={{2,4},{3,1},{4,6},{5,3},{10,12},{11,9},{12,14},{13,11},{18,20},{19... | collective-permute-start | bytes 1376264 | tf_op jit(solution)/shard_map/ppermute | solution.py:314
  17.7 0.8 %collective-permute-done.4.refs_6_.refs_7_ = bf16[14,128,128]{2,1,0:T(8,128)(2,1)S(1)} collective-permute-done((bf16[14,128,128]{2,1,0:T(8,128)(2,1)S(1)}, bf16[14,128,128]{2,1,0:T(8,128)(2,1)S(1)}, u32[]{:S(2)}, u32[]{:S(2)}) %collective-permute-start.4) | collective-permute-done | bytes 458784 | tf_op jit(solution)/shard_map/ppermute | solution.py:314
  18.5 0.7 %collective-permute-start.7 = (bf16[14,128,128]{2,1,0:T(8,128)(2,1)S(1)}, bf16[14,128,128]{2,1,0:T(8,128)(2,1)S(1)}, u32[]{:S(2)}, u32[]{:S(2)}) collective-permute-start(bf16[14,128,128]{2,1,0:T(8,128)(2,1)S(1)} %collective-permute-done.4.refs_6_.refs_7_), channel_id=1, source_target_pairs={{3,1},{4,6},{11,9},{12,14},{19,17},{20,22},{27,25},{28,30}} | collective-permute-start | bytes 1376264 | tf_op jit(solution)/shard_map/ppermute | solution.py:314
  19.1 4.2 %collective-permute-done.5.refs_7_.refs_8_ = bf16[14,128,128]{2,1,0:T(8,128)(2,1)S(1)} collective-permute-done((bf16[14,128,128]{2,1,0:T(8,128)(2,1)S(1)}, bf16[14,128,128]{2,1,0:T(8,128)(2,1)S(1)}, u32[]{:S(2)}, u32[]{:S(2)}) %collective-permute-start.5) | collective-permute-done | bytes 458784 | tf_op jit(solution)/shard_map/ppermute | solution.py:314
  23.4 0.7 %collective-permute-start.8 = (bf16[14,128,128]{2,1,0:T(8,128)(2,1)S(1)}, bf16[14,128,128]{2,1,0:T(8,128)(2,1)S(1)}, u32[]{:S(2)}, u32[]{:S(2)}) collective-permute-start(bf16[14,128,128]{2,1,0:T(8,128)(2,1)S(1)} %collective-permute-done.5.refs_7_.refs_8_), channel_id=1, source_target_pairs={{3,1},{4,6},{11,9},{12,14},{19,17},{20,22},{27,25},{28,30}} | collective-permute-start | bytes 1376264 | tf_op jit(solution)/shard_map/ppermute | solution.py:314
  24.1 0.0 copy-start.1
  24.1 0.7 %copy-done.1 = s32[4,4,28]{2,1,0:T(4,128)S(1)} copy-done((s32[4,4,28]{2,1,0:T(4,128)S(1)}, s32[4,4,28]{2,1,0:T(4,128)}, u32[]{:S(2)}) %copy-start.1) | copy-done | bytes 1816
  24.8 0.7 %copy-done.2 = s32[4,4,28]{2,1,0:T(4,128)S(1)} copy-done((s32[4,4,28]{2,1,0:T(4,128)S(1)}, s32[4,4,28]{2,1,0:T(4,128)}, u32[]{:S(2)}) %copy-start.2) | copy-done | bytes 1816
  25.5 1.0 %list_products.1.pairs = s32[5,128]{1,0:T(8,128)S(1)} custom-call(s32[4,4,28]{2,1,0:T(4,128)S(1)} %copy-done.1, s32[4,4,28]{2,1,0:T(4,128)S(1)} %copy-done.2), custom_call_target="tpu_custom_call" | custom-call | bytes 1835008 | tf_op jit(solution)/shard_map/list_products/pallas_call | solution.py:297
  26.4 0.0 collective-permute-done.refs_1_
  26.5 0.0 collective-permute-done.1.refs_2_
  26.5 0.0 copy-done
  26.5 0.9 %early_products.1.total = f32[29,128,128]{2,1,0:T(8,128)S(1)} custom-call(s32[5,128]{1,0:T(8,128)S(1)} %list_products.1.pairs, bf16[28,128,128]{2,1,0:T(8,128)(2,1)S(1)} %bitcast.9, bf16[28,128,128]{2,1,0:T(8,128)(2,1)S(1)} %collective-permute-done.refs_1_, bf16[28,128,128]{2,1,0:T(8,128)(2,1)S(1)} %collective-permute-done.1.refs_2_, ...), custom_call_target="tpu_custom_call" | custom-call | flops 352321536 | bytes 5505024 | tf_op jit(solution)/shard_map/early_products/pallas_call | solution.py:325
  27.3 4.3 %collective-permute-done.6.refs_3_ = bf16[28,128,128]{2,1,0:T(8,128)(2,1)S(1)} collective-permute-done((bf16[28,128,128]{2,1,0:T(8,128)(2,1)}, bf16[28,128,128]{2,1,0:T(8,128)(2,1)S(1)}, u32[]{:S(2)}, u32[]{:S(2)}) %collective-permute-start.6) | collective-permute-done | bytes 917536 | tf_op jit(solution)/shard_map/ppermute | solution.py:320
  31.6 0.0 collective-permute-done.7.refs_9_
  31.6 1.8 %middle_products.1 = (f32[29,128,128]{2,1,0:T(8,128)S(1)}, bf16[28,128,128]{2,1,0:T(8,128)(2,1)S(1)}) custom-call(s32[5,128]{1,0:T(8,128)S(1)} %list_products.1.pairs, f32[29,128,128]{2,1,0:T(8,128)S(1)} %early_products.1.total, bf16[28,128,128]{2,1,0:T(8,128)(2,1)S(1)} %bitcast.11, ...), custom_call_target="tpu_custom_call", output_to_operand_aliasing={{0}: (1, {})} | custom-call | flops 117440512 | bytes 3670016 | tf_op jit(solution)/shard_map/middle_products/pallas_call | solution.py:341
  33.4 0.0 collective-permute-done.8.refs_0_
  33.4 0.7 %last_products.1 = (f32[29,128,128]{2,1,0:T(8,128)S(1)}, f32[14,128,128]{2,1,0:T(8,128)S(1)}, f32[14,128,128]{2,1,0:T(8,128)S(1)}) custom-call(s32[5,128]{1,0:T(8,128)S(1)} %list_products.1.pairs, f32[29,128,128]{2,1,0:T(8,128)S(1)} %get-tuple-element.9.total, ...), custom_call_target="tpu_custom_call", output_to_operand_aliasing={{0}: (1, {})} | custom-call | flops 58720256 | bytes 3670016 | tf_op jit(solution)/shard_map/last_products/pallas_call | solution.py:361
  34.1 9.6 %collective-permute-start.9 = (f32[14,128,128]{2,1,0:T(8,128)S(1)}, f32[14,128,128]{2,1,0:T(8,128)S(1)}, u32[]{:S(2)}, u32[]{:S(2)}) collective-permute-start(f32[14,128,128]{2,1,0:T(8,128)S(1)} %get-tuple-element.12), channel_id=1, source_target_pairs={{0,1},{1,0},{2,3},{3,2},{4,5},{5,4},{6,7},{7,6},{8,9},{9,8},{10,11... | collective-permute-start | bytes 2752520 | tf_op jit(solution)/shard_map/ppermute | solution.py:371
  43.8 2.1 %collective-permute-done.9 = f32[14,128,128]{2,1,0:T(8,128)S(1)} collective-permute-done((f32[14,128,128]{2,1,0:T(8,128)S(1)}, f32[14,128,128]{2,1,0:T(8,128)S(1)}, u32[]{:S(2)}, u32[]{:S(2)}) %collective-permute-start.9) | collective-permute-done | bytes 917536 | tf_op jit(solution)/shard_map/ppermute | solution.py:371
  45.9 0.9 %fusion = bf16[1,1,14,128,128]{4,3,2,1,0:T(8,128)(2,1)} fusion(f32[14,128,128]{2,1,0:T(8,128)S(1)} %get-tuple-element.11, f32[14,128,128]{2,1,0:T(8,128)S(1)} %collective-permute-done.9), kind=kLoop, calls=%fused_computation.1 | loop fusion | flops 458752 | bytes 2293760 | tf_op jit(solution)/shard_map/broadcast_in_dim | solution.py:372
  (1 shorter events, 0.0 us)
Async XLA Ops:
  0.0 26.5 %copy-start = (bf16[1,1,28,128,128]{4,3,2,1,0:T(8,128)(2,1)S(1)}, bf16[1,1,28,128,128]{4,3,2,1,0:T(8,128)(2,1)}, u32[]{:S(2)}) copy-start(bf16[1,1,28,128,128]{4,3,2,1,0:T(8,128)(2,1)} %param.3) | copy-start | bytes 2752516
  1.1 9.5 %collective-permute-start.2 = (bf16[14,128,128]{2,1,0:T(8,128)(2,1)S(1)}, bf16[14,128,128]{2,1,0:T(8,128)(2,1)S(1)}, u32[]{:S(2)}, u32[]{:S(2)}) collective-permute-start(bf16[14,128,128]{2,1,0:T(8,128)(2,1)S(1)} %slice_bitcast_fusion), channel_id=1, source_target_pairs={{0,2},{2,4},{3,1},{4,6},{5,3},{7,5},{8,10},{10,12},{11,9},{12,14},... | collective-permute-start | bytes 1376264 | tf_op jit(solution)/shard_map/ppermute | solution.py:314
  4.3 11.3 %collective-permute-start.3 = (bf16[14,128,128]{2,1,0:T(8,128)(2,1)S(1)}, bf16[14,128,128]{2,1,0:T(8,128)(2,1)S(1)}, u32[]{:S(2)}, u32[]{:S(2)}) collective-permute-start(bf16[14,128,128]{2,1,0:T(8,128)(2,1)S(1)} %slice.12), channel_id=1, source_target_pairs={{0,2},{2,4},{3,1},{4,6},{5,3},{7,5},{8,10},{10,12},{11,9},{12,14},... | collective-permute-start | bytes 1376264 | tf_op jit(solution)/shard_map/ppermute | solution.py:314
  6.2 20.2 %collective-permute-start = (bf16[28,128,128]{2,1,0:T(8,128)(2,1)}, bf16[28,128,128]{2,1,0:T(8,128)(2,1)S(1)}, u32[]{:S(2)}, u32[]{:S(2)}) collective-permute-start(bf16[28,128,128]{2,1,0:T(8,128)(2,1)} %bitcast.6), channel_id=1, source_target_pairs={{0,8},{2,10},{4,12},{6,14},{9,1},{10,2},{12,4},{14,6},{17,25},{19,... | collective-permute-start | bytes 2752520 | tf_op jit(solution)/shard_map/ppermute | solution.py:320
  6.9 19.5 %collective-permute-start.1 = (bf16[28,128,128]{2,1,0:T(8,128)(2,1)}, bf16[28,128,128]{2,1,0:T(8,128)(2,1)S(1)}, u32[]{:S(2)}, u32[]{:S(2)}) collective-permute-start(bf16[28,128,128]{2,1,0:T(8,128)(2,1)} %bitcast.7), channel_id=1, source_target_pairs={{0,16},{2,18},{4,20},{6,22},{9,25},{10,26},{12,28},{14,30},{17,1},... | collective-permute-start | bytes 2752520 | tf_op jit(solution)/shard_map/ppermute | solution.py:320
  7.7 23.9 %collective-permute-start.6 = (bf16[28,128,128]{2,1,0:T(8,128)(2,1)}, bf16[28,128,128]{2,1,0:T(8,128)(2,1)S(1)}, u32[]{:S(2)}, u32[]{:S(2)}) collective-permute-start(bf16[28,128,128]{2,1,0:T(8,128)(2,1)} %bitcast.8), channel_id=1, source_target_pairs={{0,24},{2,26},{4,28},{6,30},{9,17},{10,18},{12,20},{14,22},{17,9},... | collective-permute-start | bytes 2752520 | tf_op jit(solution)/shard_map/ppermute | solution.py:320
  10.7 7.8 %collective-permute-start.4 = (bf16[14,128,128]{2,1,0:T(8,128)(2,1)S(1)}, bf16[14,128,128]{2,1,0:T(8,128)(2,1)S(1)}, u32[]{:S(2)}, u32[]{:S(2)}) collective-permute-start(bf16[14,128,128]{2,1,0:T(8,128)(2,1)S(1)} %collective-permute-done.2.refs_4_.refs_5_), channel_id=1, source_target_pairs={{2,4},{3,1},{4,6},{5,3},{10,12},{11,9},{12,14},{13,11},{18,20},{19... | collective-permute-start | bytes 1376264 | tf_op jit(solution)/shard_map/ppermute | solution.py:314
  15.6 7.8 %collective-permute-start.5 = (bf16[14,128,128]{2,1,0:T(8,128)(2,1)S(1)}, bf16[14,128,128]{2,1,0:T(8,128)(2,1)S(1)}, u32[]{:S(2)}, u32[]{:S(2)}) collective-permute-start(bf16[14,128,128]{2,1,0:T(8,128)(2,1)S(1)} %collective-permute-done.3.refs_5_.refs_6_), channel_id=1, source_target_pairs={{2,4},{3,1},{4,6},{5,3},{10,12},{11,9},{12,14},{13,11},{18,20},{19... | collective-permute-start | bytes 1376264 | tf_op jit(solution)/shard_map/ppermute | solution.py:314
  18.5 13.2 %collective-permute-start.7 = (bf16[14,128,128]{2,1,0:T(8,128)(2,1)S(1)}, bf16[14,128,128]{2,1,0:T(8,128)(2,1)S(1)}, u32[]{:S(2)}, u32[]{:S(2)}) collective-permute-start(bf16[14,128,128]{2,1,0:T(8,128)(2,1)S(1)} %collective-permute-done.4.refs_6_.refs_7_), channel_id=1, source_target_pairs={{3,1},{4,6},{11,9},{12,14},{19,17},{20,22},{27,25},{28,30}} | collective-permute-start | bytes 1376264 | tf_op jit(solution)/shard_map/ppermute | solution.py:314
  23.4 10.0 %collective-permute-start.8 = (bf16[14,128,128]{2,1,0:T(8,128)(2,1)S(1)}, bf16[14,128,128]{2,1,0:T(8,128)(2,1)S(1)}, u32[]{:S(2)}, u32[]{:S(2)}) collective-permute-start(bf16[14,128,128]{2,1,0:T(8,128)(2,1)S(1)} %collective-permute-done.5.refs_7_.refs_8_), channel_id=1, source_target_pairs={{3,1},{4,6},{11,9},{12,14},{19,17},{20,22},{27,25},{28,30}} | collective-permute-start | bytes 1376264 | tf_op jit(solution)/shard_map/ppermute | solution.py:314
  24.1 0.7 %copy-start.1 = (s32[4,4,28]{2,1,0:T(4,128)S(1)}, s32[4,4,28]{2,1,0:T(4,128)}, u32[]{:S(2)}) copy-start(s32[4,4,28]{2,1,0:T(4,128)} %rows_in.1) | copy-start | bytes 5380
  24.8 0.7 %copy-start.2 = (s32[4,4,28]{2,1,0:T(4,128)S(1)}, s32[4,4,28]{2,1,0:T(4,128)}, u32[]{:S(2)}) copy-start(s32[4,4,28]{2,1,0:T(4,128)} %cols_in.1) | copy-start | bytes 5380
  34.1 11.7 %collective-permute-start.9 = (f32[14,128,128]{2,1,0:T(8,128)S(1)}, f32[14,128,128]{2,1,0:T(8,128)S(1)}, u32[]{:S(2)}, u32[]{:S(2)}) collective-permute-start(f32[14,128,128]{2,1,0:T(8,128)S(1)} %get-tuple-element.12), channel_id=1, source_target_pairs={{0,1},{1,0},{2,3},{3,2},{4,5},{5,4},{6,7},{7,6},{8,9},{9,8},{10,11... | collective-permute-start | bytes 2752520 | tf_op jit(solution)/shard_map/ppermute | solution.py:371

commit v2 on v1

--- a/solution.py
+++ b/solution.py
@@ -41,16 +41,17 @@
                     pairs.append((source * 2 + layer, target * 2 + layer))
         return pairs
 
-    def row_pairs(self, by):
+    def row_pairs(self, bys):
         pairs = []
         for r in range(self.grid):
             for a in range(self.grid):
-                k = self.shift(a, r)
-                if k is not None:
-                    layer = int(k > 0)
-                    pairs.append(
-                        tuple((p * self.grid + a) * 2 + layer for p in (r, r ^ by))
-                    )
+                if self.shift(a, r) is not None:
+                    for layer, by in enumerate(bys):
+                        pairs.append(
+                            tuple(
+                                (p * self.grid + a) * 2 + layer for p in (r, r ^ by)
+                            )
+                        )
         return pairs
 
     def taken(self, a, layer, stage):
@@ -69,35 +70,23 @@
     return tuple(lax.axis_index(n) for n in ("col", "row", "layer"))
 
 
-def list_kernel(plan, bounds, rows_in, cols_in, pairs, rows, cols, keys, codes, sem):
-    slots = rows.shape[2]
+def list_kernel(plan, bounds, slot_keys, pairs, keys, codes):
+    slots = slot_keys.shape[2]
     stages = plan.stages + 1
-    inputs = [
-        pltpu.make_async_copy(rows_in, rows, sem.at[0]),
-        pltpu.make_async_copy(cols_in, cols, sem.at[1]),
-    ]
-    for copy in inputs:
-        copy.start()
     a, b, layer = place()
     lane = lax.broadcasted_iota(jnp.int32, (1, LANES), 1)
     down = lax.broadcasted_iota(jnp.int32, (LANES, LANES), 0)
     across = lax.broadcasted_iota(jnp.int32, (LANES, LANES), 1)
 
-    def key_of(i, j):
-        r, c = rows[i, pl.ds(j, 1), :], cols[i, pl.ds(j, 1), :]
-        return 2 * r + (c != r).astype(jnp.int32)
-
     keys[...] = jnp.full_like(keys, -1)
-    for copy in inputs:
-        copy.wait()
     taken = []
     for stage in range(stages):
         l, valid = plan.taken(a, layer, stage)
         taken.append(valid)
         l = jnp.clip(l, 0, plan.grid - 1)
-        keys[pl.ds(stage, 1), 0:slots] = key_of(a, l)
-        keys[pl.ds(stages + stage, 1), 0:slots] = key_of(l, b)
-    keys[pl.ds(2 * stages, 1), 0:slots] = key_of(a, b)
+        keys[pl.ds(stage, 1), 0:slots] = slot_keys[a, pl.ds(l, 1), :]
+        keys[pl.ds(stages + stage, 1), 0:slots] = slot_keys[l, pl.ds(b, 1), :]
+    keys[pl.ds(2 * stages, 1), 0:slots] = slot_keys[a, pl.ds(b, 1), :]
     out = keys[pl.ds(2 * stages, 1), :]
     out = jnp.where(lane < LANES // 2, out, pltpu.roll(out, LANES // 2, 1))
     slot = lane % (LANES // 2)
@@ -181,18 +170,35 @@
         at += ref.shape[0]
 
 
-def fetch_left(lefts, by, buffer, sem):
-    for n, ref in lefts.items():
-
-        @pl.when(by == n)
-        def _(ref=ref):
-            pltpu.make_async_copy(ref, buffer, sem).start()
+def fetch_left(lefts, by, layer, buffer, sem):
+    own, near, swapped = lefts
+    at = 2 * by + layer
+
+    @pl.when(by == 0)
+    def _():
+        pltpu.make_async_copy(own, buffer, sem).start()
+
+    for k in range(len(near)):
+
+        @pl.when((at == 4 * k + 2) | (at == 4 * k + 5))
+        def _(k=k):
+            pltpu.make_async_copy(near[k], buffer, sem).start()
+
+        @pl.when((at == 4 * k + 3) | (at == 4 * k + 4))
+        def _(k=k):
+            pltpu.make_async_copy(swapped[k], buffer, sem).start()
+
+
+def split_lefts(plan, refs):
+    near = plan.grid // 2 - 1
+    return (refs[0], refs[1 : 1 + near], refs[1 + near : 1 + 2 * near]), refs[
+        1 + 2 * near :
+    ]
 
 
 def early_kernel(plan, parts, pairs, *refs):
     far = plan.grid - 1
-    lefts = dict(enumerate(refs[:far]))
-    refs = refs[far:]
+    lefts, refs = split_lefts(plan, refs)
     rights = []
     for n in parts:
         rights.append(refs[:n])
@@ -210,7 +216,7 @@
         @pl.when(count > 0)
         def _(stage=stage, by=by):
             fetch(rights[stage], right.at[stage], right_sem.at[stage])
-            fetch_left(lefts, by, left.at[stage], left_sem.at[stage])
+            fetch_left(lefts, by, layer, left.at[stage], left_sem.at[stage])
 
     acc[...] = jnp.zeros_like(acc)
     for stage, by, count in jobs:
@@ -228,17 +234,34 @@
 
 def middle_kernel(plan, parts, pairs, total, *refs):
     del total
-    lefts = dict(enumerate(refs[: plan.grid]))
-    refs = refs[plan.grid :]
+    lefts, refs = split_lefts(plan, refs)
+    halves, refs = refs[:2], refs[2:]
     rights = []
     for n in parts[:-1]:
         rights.append(refs[:n])
         refs = refs[n:]
-    first, acc, left_last, right, left_sem, right_sem = refs
+    first, acc, left_last, left, right, left_sem, far_sem, right_sem = refs
     far, end, last = plan.grid - 1, plan.stages, pairs.shape[1] - 1
     a, b, layer = place()
+    share = halves[0].shape[0]
+
+    def far_copies(buffer):
+        return [
+            pltpu.make_async_copy(
+                half, buffer.at[pl.ds(jnp.abs(layer - j) * share, share)], far_sem.at[j]
+            )
+            for j, half in enumerate(halves)
+        ]
+
     l, _ = plan.taken(a, layer, end)
-    fetch_left(lefts, b ^ l, left_last, left_sem)
+    end_by = b ^ l
+    fetch_left(lefts, end_by, layer, left_last, left_sem)
+
+    @pl.when(end_by == far)
+    def _():
+        for copy in far_copies(left_last):
+            copy.start()
+
     counts = []
     for stage in range(end):
         l, _ = plan.taken(a, layer, stage)
@@ -248,15 +271,27 @@
         @pl.when(count > 0)
         def _(stage=stage):
             fetch(rights[stage], right, right_sem)
-
-    pltpu.make_async_copy(lefts[0], left_last, left_sem).wait()
+            for copy in far_copies(left):
+                copy.start()
+
+    @pl.when(end_by == far)
+    def _():
+        for copy in far_copies(left_last):
+            copy.wait()
+
+    @pl.when(end_by != far)
+    def _():
+        pltpu.make_async_copy(lefts[0], left_last, left_sem).wait()
+
     add_products(pairs[end, last], pairs, end, left_last, first, acc)
     for stage, count in enumerate(counts):
 
         @pl.when(count > 0)
         def _(stage=stage, count=count):
             fetched(rights[stage], right, right_sem)
-            add_products(count, pairs, stage, lefts[far], right, acc)
+            for copy in far_copies(left):
+                copy.wait()
+            add_products(count, pairs, stage, left, right, acc)
 
 
 def last_kernel(plan, bounds, pairs, total, left_last, *refs):
@@ -297,15 +332,14 @@
     lists = pl.pallas_call(
         functools.partial(list_kernel, plan, bounds),
         out_shape=jax.ShapeDtypeStruct((plan.stages + CHUNKS, LANES), jnp.int32),
-        in_specs=[pl.BlockSpec(memory_space=pltpu.HBM)] * 2,
+        in_specs=[vmem],
         out_specs=vmem,
-        scratch_shapes=[pltpu.VMEM(slot_rows.shape, jnp.int32)] * 2
-        + [pltpu.VMEM((LANES, LANES), jnp.int32)] * 2
-        + [pltpu.SemaphoreType.DMA((2,))],
+        scratch_shapes=[pltpu.VMEM((LANES, LANES), jnp.int32)] * 2,
         compiler_params=compiler_params,
         cost_estimate=cost(0, 2),
         name="list_products",
-    )(slot_rows, slot_cols)
+    )(2 * slot_rows + (slot_cols != slot_rows))
+    halves = list(held)
     rights = [[own]]
     for stage in range(1, plan.stages + 1):
         pairs = plan.hop_pairs(stage)
@@ -315,17 +349,26 @@
         rights.append(arrived)
         held = list(arrived)
     everywhere = ("row", "col", "layer")
-    lefts = [own]
-    for by in range(1, plan.grid):
-        lefts.append(lax.ppermute(own, everywhere, plan.row_pairs(by)))
-    *near, far = lefts
+    swap = [(0, 1), (1, 0)]
+    far = plan.grid - 1
+    near, swapped = [], []
+    for k in range(plan.grid // 2 - 1):
+        bys = (2 * k + 1, 2 * k + 2)
+        near.append(lax.ppermute(own, everywhere, plan.row_pairs(bys)))
+        swapped.append(lax.ppermute(near[-1], "layer", swap))
+    sent = jnp.where(
+        lax.axis_index("layer") == 0, *lax.optimization_barrier(halves)
+    )
+    far_half = lax.ppermute(sent, everywhere, plan.row_pairs((far, far)))
+    far_swapped = lax.ppermute(far_half, "layer", swap)
+    lefts = [own, *near, *swapped]
     parts = [len(r) for r in rights]
     running = jax.ShapeDtypeStruct((slots + 1, size, size), jnp.float32)
     before = [part for stage in rights[:-1] for part in stage]
     total = pl.pallas_call(
         functools.partial(early_kernel, plan, parts[:-1]),
         out_shape=running,
-        in_specs=[scalars] + [anywhere] * (len(near) + len(before)),
+        in_specs=[scalars] + [anywhere] * (len(lefts) + len(before)),
         out_specs=vmem,
         scratch_shapes=[
             pltpu.VMEM((plan.stages, *own.shape), own.dtype),
@@ -336,27 +379,27 @@
         compiler_params=compiler_params,
         cost_estimate=cost(slots * plan.stages, 2 * plan.stages),
         name="early_products",
-    )(lists, *near, *before)
+    )(lists, *lefts, *before)
     first, *rest = rights[-1]
     total, left_last = pl.pallas_call(
         functools.partial(middle_kernel, plan, parts),
         out_shape=(running, jax.ShapeDtypeStruct(own.shape, own.dtype)),
         in_specs=[scalars, vmem]
-        + [anywhere] * len(near)
-        + [vmem]
-        + [anywhere] * len(before)
+        + [anywhere] * (len(lefts) + 2 + len(before))
         + [vmem],
         out_specs=(vmem, vmem),
         input_output_aliases={1: 0},
         scratch_shapes=[
             pltpu.VMEM(own.shape, own.dtype),
+            pltpu.VMEM(own.shape, own.dtype),
             pltpu.SemaphoreType.DMA,
+            pltpu.SemaphoreType.DMA((2,)),
             pltpu.SemaphoreType.DMA((CHUNKS,)),
         ],
         compiler_params=compiler_params,
         cost_estimate=cost(slots, 4),
         name="middle_products",
-    )(lists, total, *near, far, *before, first)
+    )(lists, total, *lefts, far_half, far_swapped, *before, first)
     half = jax.ShapeDtypeStruct((share, size, size), jnp.float32)
     _, mine, other = pl.pallas_call(
         functools.partial(last_kernel, plan, bounds),
@@ -368,7 +411,7 @@
         cost_estimate=cost(slots // 2, 4),
         name="last_products",
     )(lists, total, left_last, *rest)
-    received = lax.ppermute(other, "layer", [(0, 1), (1, 0)])
+    received = lax.ppermute(other, "layer", swap)
     return (mine + received).astype(jnp.bfloat16)[None, None]
 
 

time: 47.2 us -> 48.2 us (1.021)
  the two profiles are of different devices: /device:TPU:17 before, /device:TPU:0 now
where the time goes in v2:
time: 48.2 us; the launch traced here: 47.6 us
  starting transfers between devices  25 us (52%)
  waiting for transfers between devices  12.6 us (26%)
  Pallas kernels  4.99 us (10%)
  local copies, waits for them, and re-layouts  2.92 us (6%)
  other arithmetic  1.98 us (4%)
    ppermute x6, starting transfers between devices, on_device(): arrived.append(lax.ppermute(part, ('col', 'layer'), pairs))  9.71 us
    ppermute x1, starting transfers between devices, on_device(): received = lax.ppermute(other, 'layer', swap)  9.22 us
    ppermute x1, waiting for transfers between devices, on_device(): far_half = lax.ppermute(sent, everywhere, plan.row_pairs((far, far)))  8.75 us
    ppermute x1, starting transfers between devices, on_device(): far_half = lax.ppermute(sent, everywhere, plan.row_pairs((far, far)))  3.04 us
    ppermute x1, starting transfers between devices, on_device(): near.append(lax.ppermute(own, everywhere, plan.row_pairs(bys)))  3.03 us
    slice x2, local copies, waits for them, and re-layouts, on_device(): (lax.optimization_barrier(own) if i else own)[i:j]  2.91 us
    pallas_call x1, Pallas kernels, on_device(): pl.pallas_call(functools.partial(early_kernel, plan, parts[:-1]), out_sha...  2.32 us
    ppermute x1, waiting for transfers between devices, on_device(): received = lax.ppermute(other, 'layer', swap)  2.1 us
  transfers between devices with their start and end apart: 11, of which 3 were waited for; matrix products, arithmetic and copies ran while one was open for 8% of the time, Pallas kernels for 9%

profile of v2, /device:TPU:0, one launch (start us, length us, event | category | flops | bytes accessed | tf_op | source)
XLA Modules:
  0.0 47.6 jit_solution(8223861492305906083)
XLA Ops:
  0.0 3.0 %collective-permute-start = (bf16[28,128,128]{2,1,0:T(8,128)(2,1)}, bf16[28,128,128]{2,1,0:T(8,128)(2,1)S(1)}, u32[]{:S(2)}, u32[]{:S(2)}) collective-permute-start(bf16[28,128,128]{2,1,0:T(8,128)(2,1)} %bitcast.5), channel_id=1, source_target_pairs={{0,8},{1,17},{2,10},{3,19},{4,12},{5,21},{6,14},{7,23},{8,0},{9,25... | collective-permute-start | bytes 2752520 | tf_op jit(solution)/shard_map/ppermute | solution.py:357
  3.0 1.9 %slice_bitcast_fusion = bf16[14,128,128]{2,1,0:T(8,128)(2,1)} fusion(bf16[1,1,28,128,128]{4,3,2,1,0:T(8,128)(2,1)} %param.3), kind=kLoop, calls=%fused_computation.2 | loop fusion | bytes 917504 | tf_op jit(solution)/shard_map/slice | solution.py:316
  4.9 3.5 %collective-permute-start.2 = (bf16[14,128,128]{2,1,0:T(8,128)(2,1)}, bf16[14,128,128]{2,1,0:T(8,128)(2,1)S(1)}, u32[]{:S(2)}, u32[]{:S(2)}) collective-permute-start(bf16[14,128,128]{2,1,0:T(8,128)(2,1)} %slice_bitcast_fusion), channel_id=1, source_target_pairs={{0,2},{2,4},{3,1},{4,6},{5,3},{7,5},{8,10},{10,12},{11,9},{12,14},... | collective-permute-start | bytes 1376264 | tf_op jit(solution)/shard_map/ppermute | solution.py:348
  8.4 1.1 %slice.12 = bf16[14,128,128]{2,1,0:T(8,128)(2,1)S(1)} slice(bf16[28,128,128]{2,1,0:T(8,128)(2,1)} %bitcast.6), slice={[14:28], [0:128], [0:128]} | slice | bytes 917504 | tf_op jit(solution)/shard_map/slice | solution.py:316
  9.5 3.5 %collective-permute-start.3 = (bf16[14,128,128]{2,1,0:T(8,128)(2,1)S(1)}, bf16[14,128,128]{2,1,0:T(8,128)(2,1)S(1)}, u32[]{:S(2)}, u32[]{:S(2)}) collective-permute-start(bf16[14,128,128]{2,1,0:T(8,128)(2,1)S(1)} %slice.12), channel_id=1, source_target_pairs={{0,2},{2,4},{3,1},{4,6},{5,3},{7,5},{8,10},{10,12},{11,9},{12,14},... | collective-permute-start | bytes 1376264 | tf_op jit(solution)/shard_map/ppermute | solution.py:348
  13.0 1.7 %collective-permute-done.refs_1_ = bf16[28,128,128]{2,1,0:T(8,128)(2,1)S(1)} collective-permute-done((bf16[28,128,128]{2,1,0:T(8,128)(2,1)}, bf16[28,128,128]{2,1,0:T(8,128)(2,1)S(1)}, u32[]{:S(2)}, u32[]{:S(2)}) %collective-permute-start) | collective-permute-done | bytes 917536 | tf_op jit(solution)/shard_map/ppermute | solution.py:357
  14.6 0.0 collective-permute-start.1
  14.6 1.1 %broadcast_select_fusion = bf16[14,128,128]{2,1,0:T(8,128)(2,1)S(1)} fusion(bf16[14,128,128]{2,1,0:T(8,128)(2,1)} %slice_bitcast_fusion, bf16[14,128,128]{2,1,0:T(8,128)(2,1)S(1)} %slice.12, pred[]{:T(512)S(6)} %eq.3), kind=kLoop, calls=%fused_computation.3 | loop fusion | flops 229376 | bytes 1376257 | tf_op jit(solution)/shard_map/jit(_where)/select_n | solution.py:359
  15.7 3.0 %collective-permute-start.6 = (bf16[14,128,128]{2,1,0:T(8,128)(2,1)S(1)}, bf16[14,128,128]{2,1,0:T(8,128)(2,1)S(1)}, u32[]{:S(2)}, u32[]{:S(2)}) collective-permute-start(bf16[14,128,128]{2,1,0:T(8,128)(2,1)S(1)} %broadcast_select_fusion), channel_id=1, source_target_pairs={{0,24},{1,25},{2,26},{3,27},{4,28},{5,29},{6,30},{7,31},{8,16},{9,... | collective-permute-start | bytes 1376264 | tf_op jit(solution)/shard_map/ppermute | solution.py:362
  18.7 0.0 collective-permute-done.2.refs_4_.refs_6_
  18.7 0.7 %collective-permute-start.4 = (bf16[14,128,128]{2,1,0:T(8,128)(2,1)S(1)}, bf16[14,128,128]{2,1,0:T(8,128)(2,1)S(1)}, u32[]{:S(2)}, u32[]{:S(2)}) collective-permute-start(bf16[14,128,128]{2,1,0:T(8,128)(2,1)S(1)} %collective-permute-done.2.refs_4_.refs_6_), channel_id=1, source_target_pairs={{2,4},{3,1},{4,6},{5,3},{10,12},{11,9},{12,14},{13,11},{18,20},{19... | collective-permute-start | bytes 1376264 | tf_op jit(solution)/shard_map/ppermute | solution.py:348
  19.4 0.0 collective-permute-done.3.refs_5_.refs_7_
  19.5 0.7 %collective-permute-start.5 = (bf16[14,128,128]{2,1,0:T(8,128)(2,1)S(1)}, bf16[14,128,128]{2,1,0:T(8,128)(2,1)S(1)}, u32[]{:S(2)}, u32[]{:S(2)}) collective-permute-start(bf16[14,128,128]{2,1,0:T(8,128)(2,1)S(1)} %collective-permute-done.3.refs_5_.refs_7_), channel_id=1, source_target_pairs={{2,4},{3,1},{4,6},{5,3},{10,12},{11,9},{12,14},{13,11},{18,20},{19... | collective-permute-start | bytes 1376264 | tf_op jit(solution)/shard_map/ppermute | solution.py:348
  20.2 8.8 %collective-permute-done.6.refs_3_ = bf16[14,128,128]{2,1,0:T(8,128)(2,1)S(1)} collective-permute-done((bf16[14,128,128]{2,1,0:T(8,128)(2,1)S(1)}, bf16[14,128,128]{2,1,0:T(8,128)(2,1)S(1)}, u32[]{:S(2)}, u32[]{:S(2)}) %collective-permute-start.6) | collective-permute-done | bytes 458784 | tf_op jit(solution)/shard_map/ppermute | solution.py:362
  28.9 0.0 collective-permute-start.7
  28.9 0.0 collective-permute-done.4.refs_6_.refs_8_
  28.9 0.7 %collective-permute-start.8 = (bf16[14,128,128]{2,1,0:T(8,128)(2,1)S(1)}, bf16[14,128,128]{2,1,0:T(8,128)(2,1)S(1)}, u32[]{:S(2)}, u32[]{:S(2)}) collective-permute-start(bf16[14,128,128]{2,1,0:T(8,128)(2,1)S(1)} %collective-permute-done.4.refs_6_.refs_8_), channel_id=1, source_target_pairs={{3,1},{4,6},{11,9},{12,14},{19,17},{20,22},{27,25},{28,30}} | collective-permute-start | bytes 1376264 | tf_op jit(solution)/shard_map/ppermute | solution.py:348
  29.6 0.0 collective-permute-done.5.refs_7_.refs_9_
  29.6 0.7 %collective-permute-start.9 = (bf16[14,128,128]{2,1,0:T(8,128)(2,1)S(1)}, bf16[14,128,128]{2,1,0:T(8,128)(2,1)S(1)}, u32[]{:S(2)}, u32[]{:S(2)}) collective-permute-start(bf16[14,128,128]{2,1,0:T(8,128)(2,1)S(1)} %collective-permute-done.5.refs_7_.refs_9_), channel_id=1, source_target_pairs={{3,1},{4,6},{11,9},{12,14},{19,17},{20,22},{27,25},{28,30}} | collective-permute-start | bytes 1376264 | tf_op jit(solution)/shard_map/ppermute | solution.py:348
  30.3 0.0 copy-done.1
  30.4 1.0 %list_products.1.pairs = s32[5,128]{1,0:T(8,128)S(1)} custom-call(s32[4,4,28]{2,1,0:T(4,128)S(1)} %convert_add_fusion.slot_keys), custom_call_target="tpu_custom_call" | custom-call | bytes 1835008 | tf_op jit(solution)/shard_map/list_products/pallas_call | solution.py:332
  31.3 0.0 collective-permute-done.1.refs_2_
  31.3 0.0 copy-done
  31.3 2.3 %early_products.1.total = f32[29,128,128]{2,1,0:T(8,128)S(1)} custom-call(s32[5,128]{1,0:T(8,128)S(1)} %list_products.1.pairs, bf16[28,128,128]{2,1,0:T(8,128)(2,1)S(1)} %bitcast.7, bf16[28,128,128]{2,1,0:T(8,128)(2,1)S(1)} %collective-permute-done.refs_1_, bf16[28,128,128]{2,1,0:T(8,128)(2,1)S(1)} %collective-permute-done.1.refs_2_, ...), custom_call_target="tpu_custom_call" | custom-call | flops 352321536 | bytes 5505024 | tf_op jit(solution)/shard_map/early_products/pallas_call | solution.py:368
  33.7 0.0 collective-permute-done.7.refs_4_
  33.7 0.0 collective-permute-done.8.refs_10_
  33.7 1.0 %middle_products.1 = (f32[29,128,128]{2,1,0:T(8,128)S(1)}, bf16[28,128,128]{2,1,0:T(8,128)(2,1)S(1)}) custom-call(s32[5,128]{1,0:T(8,128)S(1)} %list_products.1.pairs, f32[29,128,128]{2,1,0:T(8,128)S(1)} %early_products.1.total, bf16[28,128,128]{2,1,0:T(8,128)(2,1)S(1)} %bitcast.9, ...), custom_call_target="tpu_custom_call", output_to_operand_aliasing={{0}: (1, {})} | custom-call | flops 117440512 | bytes 3670016 | tf_op jit(solution)/shard_map/middle_products/pallas_call | solution.py:384
  34.7 0.0 collective-permute-done.9.refs_0_
  34.7 0.7 %last_products.1 = (f32[29,128,128]{2,1,0:T(8,128)S(1)}, f32[14,128,128]{2,1,0:T(8,128)S(1)}, f32[14,128,128]{2,1,0:T(8,128)S(1)}) custom-call(s32[5,128]{1,0:T(8,128)S(1)} %list_products.1.pairs, f32[29,128,128]{2,1,0:T(8,128)S(1)} %get-tuple-element.13.total, ...), custom_call_target="tpu_custom_call", output_to_operand_aliasing={{0}: (1, {})} | custom-call | flops 58720256 | bytes 3670016 | tf_op jit(solution)/shard_map/last_products/pallas_call | solution.py:404
  35.4 9.2 %collective-permute-start.10 = (f32[14,128,128]{2,1,0:T(8,128)S(1)}, f32[14,128,128]{2,1,0:T(8,128)S(1)}, u32[]{:S(2)}, u32[]{:S(2)}) collective-permute-start(f32[14,128,128]{2,1,0:T(8,128)S(1)} %get-tuple-element.16), channel_id=1, source_target_pairs={{0,1},{1,0},{2,3},{3,2},{4,5},{5,4},{6,7},{7,6},{8,9},{9,8},{10,11... | collective-permute-start | bytes 2752520 | tf_op jit(solution)/shard_map/ppermute | solution.py:414
  44.6 2.1 %collective-permute-done.10 = f32[14,128,128]{2,1,0:T(8,128)S(1)} collective-permute-done((f32[14,128,128]{2,1,0:T(8,128)S(1)}, f32[14,128,128]{2,1,0:T(8,128)S(1)}, u32[]{:S(2)}, u32[]{:S(2)}) %collective-permute-start.10) | collective-permute-done | bytes 917536 | tf_op jit(solution)/shard_map/ppermute | solution.py:414
  46.7 0.9 %fusion = bf16[1,1,14,128,128]{4,3,2,1,0:T(8,128)(2,1)} fusion(f32[14,128,128]{2,1,0:T(8,128)S(1)} %get-tuple-element.15, f32[14,128,128]{2,1,0:T(8,128)S(1)} %collective-permute-done.10), kind=kLoop, calls=%fused_computation.1 | loop fusion | flops 458752 | bytes 2293760 | tf_op jit(solution)/shard_map/broadcast_in_dim | solution.py:415
  (5 shorter events, 0.0 us)
Async XLA Ops:
  0.0 31.3 %copy-start = (bf16[1,1,28,128,128]{4,3,2,1,0:T(8,128)(2,1)S(1)}, bf16[1,1,28,128,128]{4,3,2,1,0:T(8,128)(2,1)}, u32[]{:S(2)}) copy-start(bf16[1,1,28,128,128]{4,3,2,1,0:T(8,128)(2,1)} %param.3) | copy-start | bytes 2752516
  0.0 30.3 %copy-start.1 = (s32[4,4,28]{2,1,0:T(4,128)S(1)}, s32[4,4,28]{2,1,0:T(4,128)}, u32[]{:S(2)}) copy-start(s32[4,4,28]{2,1,0:T(4,128)} %param.4) | copy-start | bytes 5380
  0.0 30.3 %copy-start.2 = (s32[4,4,28]{2,1,0:T(4,128)S(1)}, s32[4,4,28]{2,1,0:T(4,128)}, u32[]{:S(2)}) copy-start(s32[4,4,28]{2,1,0:T(4,128)} %param.5) | copy-start | bytes 5380
  0.0 14.6 %collective-permute-start = (bf16[28,128,128]{2,1,0:T(8,128)(2,1)}, bf16[28,128,128]{2,1,0:T(8,128)(2,1)S(1)}, u32[]{:S(2)}, u32[]{:S(2)}) collective-permute-start(bf16[28,128,128]{2,1,0:T(8,128)(2,1)} %bitcast.5), channel_id=1, source_target_pairs={{0,8},{1,17},{2,10},{3,19},{4,12},{5,21},{6,14},{7,23},{8,0},{9,25... | collective-permute-start | bytes 2752520 | tf_op jit(solution)/shard_map/ppermute | solution.py:357
  4.9 13.8 %collective-permute-start.2 = (bf16[14,128,128]{2,1,0:T(8,128)(2,1)}, bf16[14,128,128]{2,1,0:T(8,128)(2,1)S(1)}, u32[]{:S(2)}, u32[]{:S(2)}) collective-permute-start(bf16[14,128,128]{2,1,0:T(8,128)(2,1)} %slice_bitcast_fusion), channel_id=1, source_target_pairs={{0,2},{2,4},{3,1},{4,6},{5,3},{7,5},{8,10},{10,12},{11,9},{12,14},... | collective-permute-start | bytes 1376264 | tf_op jit(solution)/shard_map/ppermute | solution.py:348
  9.5 10.0 %collective-permute-start.3 = (bf16[14,128,128]{2,1,0:T(8,128)(2,1)S(1)}, bf16[14,128,128]{2,1,0:T(8,128)(2,1)S(1)}, u32[]{:S(2)}, u32[]{:S(2)}) collective-permute-start(bf16[14,128,128]{2,1,0:T(8,128)(2,1)S(1)} %slice.12), channel_id=1, source_target_pairs={{0,2},{2,4},{3,1},{4,6},{5,3},{7,5},{8,10},{10,12},{11,9},{12,14},... | collective-permute-start | bytes 1376264 | tf_op jit(solution)/shard_map/ppermute | solution.py:348
  14.6 16.7 %collective-permute-start.1 = (bf16[28,128,128]{2,1,0:T(8,128)(2,1)S(1)}, bf16[28,128,128]{2,1,0:T(8,128)(2,1)S(1)}, u32[]{:S(2)}, u32[]{:S(2)}) collective-permute-start(bf16[28,128,128]{2,1,0:T(8,128)(2,1)S(1)} %collective-permute-done.refs_1_), channel_id=1, source_target_pairs={{0,1},{1,0},{2,3},{3,2},{4,5},{5,4},{6,7},{7,6},{8,9},{9,8},{10,11... | collective-permute-start | bytes 2752520 | tf_op jit(solution)/shard_map/ppermute | solution.py:358
  15.7 13.2 %collective-permute-start.6 = (bf16[14,128,128]{2,1,0:T(8,128)(2,1)S(1)}, bf16[14,128,128]{2,1,0:T(8,128)(2,1)S(1)}, u32[]{:S(2)}, u32[]{:S(2)}) collective-permute-start(bf16[14,128,128]{2,1,0:T(8,128)(2,1)S(1)} %broadcast_select_fusion), channel_id=1, source_target_pairs={{0,24},{1,25},{2,26},{3,27},{4,28},{5,29},{6,30},{7,31},{8,16},{9,... | collective-permute-start | bytes 1376264 | tf_op jit(solution)/shard_map/ppermute | solution.py:362
  18.7 10.2 %collective-permute-start.4 = (bf16[14,128,128]{2,1,0:T(8,128)(2,1)S(1)}, bf16[14,128,128]{2,1,0:T(8,128)(2,1)S(1)}, u32[]{:S(2)}, u32[]{:S(2)}) collective-permute-start(bf16[14,128,128]{2,1,0:T(8,128)(2,1)S(1)} %collective-permute-done.2.refs_4_.refs_6_), channel_id=1, source_target_pairs={{2,4},{3,1},{4,6},{5,3},{10,12},{11,9},{12,14},{13,11},{18,20},{19... | collective-permute-start | bytes 1376264 | tf_op jit(solution)/shard_map/ppermute | solution.py:348
  19.5 10.1 %collective-permute-start.5 = (bf16[14,128,128]{2,1,0:T(8,128)(2,1)S(1)}, bf16[14,128,128]{2,1,0:T(8,128)(2,1)S(1)}, u32[]{:S(2)}, u32[]{:S(2)}) collective-permute-start(bf16[14,128,128]{2,1,0:T(8,128)(2,1)S(1)} %collective-permute-done.3.refs_5_.refs_7_), channel_id=1, source_target_pairs={{2,4},{3,1},{4,6},{5,3},{10,12},{11,9},{12,14},{13,11},{18,20},{19... | collective-permute-start | bytes 1376264 | tf_op jit(solution)/shard_map/ppermute | solution.py:348
  28.9 4.7 %collective-permute-start.7 = (bf16[14,128,128]{2,1,0:T(8,128)(2,1)S(1)}, bf16[14,128,128]{2,1,0:T(8,128)(2,1)S(1)}, u32[]{:S(2)}, u32[]{:S(2)}) collective-permute-start(bf16[14,128,128]{2,1,0:T(8,128)(2,1)S(1)} %collective-permute-done.6.refs_3_), channel_id=1, source_target_pairs={{0,1},{1,0},{2,3},{3,2},{4,5},{5,4},{6,7},{7,6},{8,9},{9,8},{10,11... | collective-permute-start | bytes 1376264 | tf_op jit(solution)/shard_map/ppermute | solution.py:363
  28.9 4.7 %collective-permute-start.8 = (bf16[14,128,128]{2,1,0:T(8,128)(2,1)S(1)}, bf16[14,128,128]{2,1,0:T(8,128)(2,1)S(1)}, u32[]{:S(2)}, u32[]{:S(2)}) collective-permute-start(bf16[14,128,128]{2,1,0:T(8,128)(2,1)S(1)} %collective-permute-done.4.refs_6_.refs_8_), channel_id=1, source_target_pairs={{3,1},{4,6},{11,9},{12,14},{19,17},{20,22},{27,25},{28,30}} | collective-permute-start | bytes 1376264 | tf_op jit(solution)/shard_map/ppermute | solution.py:348
  29.6 5.0 %collective-permute-start.9 = (bf16[14,128,128]{2,1,0:T(8,128)(2,1)S(1)}, bf16[14,128,128]{2,1,0:T(8,128)(2,1)S(1)}, u32[]{:S(2)}, u32[]{:S(2)}) collective-permute-start(bf16[14,128,128]{2,1,0:T(8,128)(2,1)S(1)} %collective-permute-done.5.refs_7_.refs_9_), channel_id=1, source_target_pairs={{3,1},{4,6},{11,9},{12,14},{19,17},{20,22},{27,25},{28,30}} | collective-permute-start | bytes 1376264 | tf_op jit(solution)/shard_map/ppermute | solution.py:348
  35.4 11.3 %collective-permute-start.10 = (f32[14,128,128]{2,1,0:T(8,128)S(1)}, f32[14,128,128]{2,1,0:T(8,128)S(1)}, u32[]{:S(2)}, u32[]{:S(2)}) collective-permute-start(f32[14,128,128]{2,1,0:T(8,128)S(1)} %get-tuple-element.16), channel_id=1, source_target_pairs={{0,1},{1,0},{2,3},{3,2},{4,5},{5,4},{6,7},{7,6},{8,9},{9,8},{10,11... | collective-permute-start | bytes 2752520 | tf_op jit(solution)/shard_map/ppermute | solution.py:414

commit v3 on v2

--- a/solution.py
+++ b/solution.py
@@ -41,7 +41,7 @@
                     pairs.append((source * 2 + layer, target * 2 + layer))
         return pairs
 
-    def row_pairs(self, bys):
+    def near_pairs(self, bys):
         pairs = []
         for r in range(self.grid):
             for a in range(self.grid):
@@ -52,6 +52,20 @@
                                 (p * self.grid + a) * 2 + layer for p in (r, r ^ by)
                             )
                         )
+        return pairs
+
+    def far_pairs(self):
+        pairs = []
+        for r in range(self.grid):
+            for a in range(self.grid):
+                k = self.shift(a, r)
+                if k is not None:
+                    pairs.append(
+                        tuple(
+                            (p * self.grid + a) * 2 + int(k > 0)
+                            for p in (r, r ^ (self.grid - 1))
+                        )
+                    )
         return pairs
 
     def taken(self, a, layer, stage):
@@ -235,32 +249,21 @@
 def middle_kernel(plan, parts, pairs, total, *refs):
     del total
     lefts, refs = split_lefts(plan, refs)
-    halves, refs = refs[:2], refs[2:]
+    far_tile, *refs = refs
     rights = []
     for n in parts[:-1]:
         rights.append(refs[:n])
         refs = refs[n:]
-    first, acc, left_last, left, right, left_sem, far_sem, right_sem = refs
+    first, acc, left_last, right, left_sem, right_sem = refs
     far, end, last = plan.grid - 1, plan.stages, pairs.shape[1] - 1
     a, b, layer = place()
-    share = halves[0].shape[0]
-
-    def far_copies(buffer):
-        return [
-            pltpu.make_async_copy(
-                half, buffer.at[pl.ds(jnp.abs(layer - j) * share, share)], far_sem.at[j]
-            )
-            for j, half in enumerate(halves)
-        ]
-
     l, _ = plan.taken(a, layer, end)
     end_by = b ^ l
     fetch_left(lefts, end_by, layer, left_last, left_sem)
 
     @pl.when(end_by == far)
     def _():
-        for copy in far_copies(left_last):
-            copy.start()
+        pltpu.make_async_copy(far_tile, left_last, left_sem).start()
 
     counts = []
     for stage in range(end):
@@ -271,27 +274,15 @@
         @pl.when(count > 0)
         def _(stage=stage):
             fetch(rights[stage], right, right_sem)
-            for copy in far_copies(left):
-                copy.start()
-
-    @pl.when(end_by == far)
-    def _():
-        for copy in far_copies(left_last):
-            copy.wait()
-
-    @pl.when(end_by != far)
-    def _():
-        pltpu.make_async_copy(lefts[0], left_last, left_sem).wait()
-
+
+    pltpu.make_async_copy(far_tile, left_last, left_sem).wait()
     add_products(pairs[end, last], pairs, end, left_last, first, acc)
     for stage, count in enumerate(counts):
 
         @pl.when(count > 0)
         def _(stage=stage, count=count):
             fetched(rights[stage], right, right_sem)
-            for copy in far_copies(left):
-                copy.wait()
-            add_products(count, pairs, stage, left, right, acc)
+            add_products(count, pairs, stage, far_tile, right, acc)
 
 
 def last_kernel(plan, bounds, pairs, total, left_last, *refs):
@@ -339,7 +330,6 @@
         cost_estimate=cost(0, 2),
         name="list_products",
     )(2 * slot_rows + (slot_cols != slot_rows))
-    halves = list(held)
     rights = [[own]]
     for stage in range(1, plan.stages + 1):
         pairs = plan.hop_pairs(stage)
@@ -350,17 +340,12 @@
         held = list(arrived)
     everywhere = ("row", "col", "layer")
     swap = [(0, 1), (1, 0)]
-    far = plan.grid - 1
     near, swapped = [], []
     for k in range(plan.grid // 2 - 1):
         bys = (2 * k + 1, 2 * k + 2)
-        near.append(lax.ppermute(own, everywhere, plan.row_pairs(bys)))
+        near.append(lax.ppermute(own, everywhere, plan.near_pairs(bys)))
         swapped.append(lax.ppermute(near[-1], "layer", swap))
-    sent = jnp.where(
-        lax.axis_index("layer") == 0, *lax.optimization_barrier(halves)
-    )
-    far_half = lax.ppermute(sent, everywhere, plan.row_pairs((far, far)))
-    far_swapped = lax.ppermute(far_half, "layer", swap)
+    far = lax.ppermute(own, everywhere, plan.far_pairs())
     lefts = [own, *near, *swapped]
     parts = [len(r) for r in rights]
     running = jax.ShapeDtypeStruct((slots + 1, size, size), jnp.float32)
@@ -385,21 +370,21 @@
         functools.partial(middle_kernel, plan, parts),
         out_shape=(running, jax.ShapeDtypeStruct(own.shape, own.dtype)),
         in_specs=[scalars, vmem]
-        + [anywhere] * (len(lefts) + 2 + len(before))
+        + [anywhere] * len(lefts)
+        + [vmem]
+        + [anywhere] * len(before)
         + [vmem],
         out_specs=(vmem, vmem),
         input_output_aliases={1: 0},
         scratch_shapes=[
             pltpu.VMEM(own.shape, own.dtype),
-            pltpu.VMEM(own.shape, own.dtype),
             pltpu.SemaphoreType.DMA,
-            pltpu.SemaphoreType.DMA((2,)),
             pltpu.SemaphoreType.DMA((CHUNKS,)),
         ],
         compiler_params=compiler_params,
         cost_estimate=cost(slots, 4),
         name="middle_products",
-    )(lists, total, *lefts, far_half, far_swapped, *before, first)
+    )(lists, total, *lefts, far, *before, first)
     half = jax.ShapeDtypeStruct((share, size, size), jnp.float32)
     _, mine, other = pl.pallas_call(
         functools.partial(last_kernel, plan, bounds),

time: 48.2 us -> 49.3 us (1.023)
  the two profiles are of different devices: /device:TPU:0 before, /device:TPU:17 now
where the time goes in v3:
time: 49.3 us; the launch traced here: 48.9 us
  starting transfers between devices  25.7 us (52%)
  waiting for transfers between devices  15 us (30%)
  Pallas kernels  4.31 us (9%)
  local copies, waits for them, and re-layouts  2.14 us (4%)
  other arithmetic  1.62 us (3%)
    ppermute x1, starting transfers between devices, on_device(): received = lax.ppermute(other, 'layer', swap)  12.1 us
    ppermute x6, starting transfers between devices, on_device(): arrived.append(lax.ppermute(part, ('col', 'layer'), pairs))  9.53 us
    ppermute x6, waiting for transfers between devices, on_device(): arrived.append(lax.ppermute(part, ('col', 'layer'), pairs))  7.68 us
    ppermute x1, waiting for transfers between devices, on_device(): near.append(lax.ppermute(own, everywhere, plan.near_pairs(bys)))  5.2 us
    slice x2, local copies, waits for them, and re-layouts, on_device(): (lax.optimization_barrier(own) if i else own)[i:j]  2.13 us
    ppermute x1, waiting for transfers between devices, on_device(): received = lax.ppermute(other, 'layer', swap)  2.1 us
    pallas_call x1, Pallas kernels, on_device(): pl.pallas_call(functools.partial(middle_kernel, plan, parts), out_shape=(...  1.76 us
    ppermute x1, starting transfers between devices, on_device(): swapped.append(lax.ppermute(near[-1], 'layer', swap))  1.53 us
  transfers between devices with their start and end apart: 10, of which 4 were waited for; matrix products, arithmetic and copies ran while one was open for 6% of the time, Pallas kernels for 7%

profile of v3, /device:TPU:17, one launch (start us, length us, event | category | flops | bytes accessed | tf_op | source)
XLA Modules:
  0.0 48.9 jit_solution(1652485740728787909)
XLA Ops:
  0.0 0.0 copy-start
  0.0 1.2 %collective-permute-start = (bf16[28,128,128]{2,1,0:T(8,128)(2,1)}, bf16[28,128,128]{2,1,0:T(8,128)(2,1)S(1)}, u32[]{:S(2)}, u32[]{:S(2)}) collective-permute-start(bf16[28,128,128]{2,1,0:T(8,128)(2,1)} %bitcast.5), channel_id=1, source_target_pairs={{0,8},{1,17},{2,10},{3,19},{4,12},{5,21},{6,14},{7,23},{8,0},{9,25... | collective-permute-start | bytes 2752520 | tf_op jit(solution)/shard_map/ppermute | solution.py:346
  1.2 1.1 %slice_bitcast_fusion = bf16[14,128,128]{2,1,0:T(8,128)(2,1)S(1)} fusion(bf16[1,1,28,128,128]{4,3,2,1,0:T(8,128)(2,1)} %param.3), kind=kLoop, calls=%fused_computation.2 | loop fusion | bytes 917504 | tf_op jit(solution)/shard_map/slice | solution.py:307
  2.3 2.1 %collective-permute-start.2 = (bf16[14,128,128]{2,1,0:T(8,128)(2,1)S(1)}, bf16[14,128,128]{2,1,0:T(8,128)(2,1)S(1)}, u32[]{:S(2)}, u32[]{:S(2)}) collective-permute-start(bf16[14,128,128]{2,1,0:T(8,128)(2,1)S(1)} %slice_bitcast_fusion), channel_id=1, source_target_pairs={{0,2},{2,4},{3,1},{4,6},{5,3},{7,5},{8,10},{10,12},{11,9},{12,14},... | collective-permute-start | bytes 1376264 | tf_op jit(solution)/shard_map/ppermute | solution.py:338
  4.4 1.1 %slice.12 = bf16[14,128,128]{2,1,0:T(8,128)(2,1)S(1)} slice(bf16[28,128,128]{2,1,0:T(8,128)(2,1)} %bitcast.6), slice={[14:28], [0:128], [0:128]} | slice | bytes 917504 | tf_op jit(solution)/shard_map/slice | solution.py:307
  5.5 2.1 %collective-permute-start.3 = (bf16[14,128,128]{2,1,0:T(8,128)(2,1)S(1)}, bf16[14,128,128]{2,1,0:T(8,128)(2,1)S(1)}, u32[]{:S(2)}, u32[]{:S(2)}) collective-permute-start(bf16[14,128,128]{2,1,0:T(8,128)(2,1)S(1)} %slice.12), channel_id=1, source_target_pairs={{0,2},{2,4},{3,1},{4,6},{5,3},{7,5},{8,10},{10,12},{11,9},{12,14},... | collective-permute-start | bytes 1376264 | tf_op jit(solution)/shard_map/ppermute | solution.py:338
  7.6 5.2 %collective-permute-done.refs_1_ = bf16[28,128,128]{2,1,0:T(8,128)(2,1)S(1)} collective-permute-done((bf16[28,128,128]{2,1,0:T(8,128)(2,1)}, bf16[28,128,128]{2,1,0:T(8,128)(2,1)S(1)}, u32[]{:S(2)}, u32[]{:S(2)}) %collective-permute-start) | collective-permute-done | bytes 917536 | tf_op jit(solution)/shard_map/ppermute | solution.py:346
  12.8 1.5 %collective-permute-start.1 = (bf16[28,128,128]{2,1,0:T(8,128)(2,1)S(1)}, bf16[28,128,128]{2,1,0:T(8,128)(2,1)S(1)}, u32[]{:S(2)}, u32[]{:S(2)}) collective-permute-start(bf16[28,128,128]{2,1,0:T(8,128)(2,1)S(1)} %collective-permute-done.refs_1_), channel_id=1, source_target_pairs={{0,1},{1,0},{2,3},{3,2},{4,5},{5,4},{6,7},{7,6},{8,9},{9,8},{10,11... | collective-permute-start | bytes 2752520 | tf_op jit(solution)/shard_map/ppermute | solution.py:347
  14.3 1.3 %collective-permute-start.6 = (bf16[28,128,128]{2,1,0:T(8,128)(2,1)}, bf16[28,128,128]{2,1,0:T(8,128)(2,1)S(1)}, u32[]{:S(2)}, u32[]{:S(2)}) collective-permute-start(bf16[28,128,128]{2,1,0:T(8,128)(2,1)} %bitcast.7), channel_id=1, source_target_pairs={{0,24},{2,26},{4,28},{6,30},{9,17},{10,18},{12,20},{14,22},{17,9},... | collective-permute-start | bytes 2752520 | tf_op jit(solution)/shard_map/ppermute | solution.py:348
  15.6 0.0 collective-permute-done.2.refs_4_.refs_5_
  15.6 2.1 %collective-permute-start.4 = (bf16[14,128,128]{2,1,0:T(8,128)(2,1)S(1)}, bf16[14,128,128]{2,1,0:T(8,128)(2,1)S(1)}, u32[]{:S(2)}, u32[]{:S(2)}) collective-permute-start(bf16[14,128,128]{2,1,0:T(8,128)(2,1)S(1)} %collective-permute-done.2.refs_4_.refs_5_), channel_id=1, source_target_pairs={{2,4},{3,1},{4,6},{5,3},{10,12},{11,9},{12,14},{13,11},{18,20},{19... | collective-permute-start | bytes 1376264 | tf_op jit(solution)/shard_map/ppermute | solution.py:338
  17.7 0.0 collective-permute-done.3.refs_5_.refs_6_
  17.7 1.9 %collective-permute-start.5 = (bf16[14,128,128]{2,1,0:T(8,128)(2,1)S(1)}, bf16[14,128,128]{2,1,0:T(8,128)(2,1)S(1)}, u32[]{:S(2)}, u32[]{:S(2)}) collective-permute-start(bf16[14,128,128]{2,1,0:T(8,128)(2,1)S(1)} %collective-permute-done.3.refs_5_.refs_6_), channel_id=1, source_target_pairs={{2,4},{3,1},{4,6},{5,3},{10,12},{11,9},{12,14},{13,11},{18,20},{19... | collective-permute-start | bytes 1376264 | tf_op jit(solution)/shard_map/ppermute | solution.py:338
  19.6 3.4 %collective-permute-done.4.refs_6_.refs_7_ = bf16[14,128,128]{2,1,0:T(8,128)(2,1)S(1)} collective-permute-done((bf16[14,128,128]{2,1,0:T(8,128)(2,1)S(1)}, bf16[14,128,128]{2,1,0:T(8,128)(2,1)S(1)}, u32[]{:S(2)}, u32[]{:S(2)}) %collective-permute-start.4) | collective-permute-done | bytes 458784 | tf_op jit(solution)/shard_map/ppermute | solution.py:338
  23.1 0.7 %collective-permute-start.7 = (bf16[14,128,128]{2,1,0:T(8,128)(2,1)S(1)}, bf16[14,128,128]{2,1,0:T(8,128)(2,1)S(1)}, u32[]{:S(2)}, u32[]{:S(2)}) collective-permute-start(bf16[14,128,128]{2,1,0:T(8,128)(2,1)S(1)} %collective-permute-done.4.refs_6_.refs_7_), channel_id=1, source_target_pairs={{3,1},{4,6},{11,9},{12,14},{19,17},{20,22},{27,25},{28,30}} | collective-permute-start | bytes 1376264 | tf_op jit(solution)/shard_map/ppermute | solution.py:338
  23.8 4.2 %collective-permute-done.5.refs_7_.refs_8_ = bf16[14,128,128]{2,1,0:T(8,128)(2,1)S(1)} collective-permute-done((bf16[14,128,128]{2,1,0:T(8,128)(2,1)S(1)}, bf16[14,128,128]{2,1,0:T(8,128)(2,1)S(1)}, u32[]{:S(2)}, u32[]{:S(2)}) %collective-permute-start.5) | collective-permute-done | bytes 458784 | tf_op jit(solution)/shard_map/ppermute | solution.py:338
  28.0 0.7 %collective-permute-start.8 = (bf16[14,128,128]{2,1,0:T(8,128)(2,1)S(1)}, bf16[14,128,128]{2,1,0:T(8,128)(2,1)S(1)}, u32[]{:S(2)}, u32[]{:S(2)}) collective-permute-start(bf16[14,128,128]{2,1,0:T(8,128)(2,1)S(1)} %collective-permute-done.5.refs_7_.refs_8_), channel_id=1, source_target_pairs={{3,1},{4,6},{11,9},{12,14},{19,17},{20,22},{27,25},{28,30}} | collective-permute-start | bytes 1376264 | tf_op jit(solution)/shard_map/ppermute | solution.py:338
  28.7 0.7 %convert_add_fusion.slot_keys = s32[4,4,28]{2,1,0:T(4,128)S(1)} fusion(s32[4,4,28]{2,1,0:T(4,128)} %param.4, s32[4,4,28]{2,1,0:T(4,128)} %param.5), kind=kLoop, calls=%fused_computation.3 | loop fusion | flops 1792 | bytes 5376 | tf_op jit(solution)/shard_map/add | solution.py:332
  29.4 0.9 %list_products.1.pairs = s32[5,128]{1,0:T(8,128)S(1)} custom-call(s32[4,4,28]{2,1,0:T(4,128)S(1)} %convert_add_fusion.slot_keys), custom_call_target="tpu_custom_call" | custom-call | bytes 1835008 | tf_op jit(solution)/shard_map/list_products/pallas_call | solution.py:323
  30.3 0.0 collective-permute-done.1.refs_2_
  30.3 0.0 copy-done
  30.4 0.9 %early_products.1.total = f32[29,128,128]{2,1,0:T(8,128)S(1)} custom-call(s32[5,128]{1,0:T(8,128)S(1)} %list_products.1.pairs, bf16[28,128,128]{2,1,0:T(8,128)(2,1)S(1)} %bitcast.8, bf16[28,128,128]{2,1,0:T(8,128)(2,1)S(1)} %collective-permute-done.refs_1_, bf16[28,128,128]{2,1,0:T(8,128)(2,1)S(1)} %collective-permute-done.1.refs_2_, ...), custom_call_target="tpu_custom_call" | custom-call | flops 352321536 | bytes 5505024 | tf_op jit(solution)/shard_map/early_products/pallas_call | solution.py:353
  31.2 0.0 collective-permute-done.6.refs_3_
  31.2 0.0 collective-permute-done.7.refs_9_
  31.2 1.8 %middle_products.1 = (f32[29,128,128]{2,1,0:T(8,128)S(1)}, bf16[28,128,128]{2,1,0:T(8,128)(2,1)S(1)}) custom-call(s32[5,128]{1,0:T(8,128)S(1)} %list_products.1.pairs, f32[29,128,128]{2,1,0:T(8,128)S(1)} %early_products.1.total, bf16[28,128,128]{2,1,0:T(8,128)(2,1)S(1)} %bitcast.10, ...), custom_call_target="tpu_custom_call", output_to_operand_aliasing={{0}: (1, {})} | custom-call | flops 117440512 | bytes 3670016 | tf_op jit(solution)/shard_map/middle_products/pallas_call | solution.py:369
  33.0 0.0 collective-permute-done.8.refs_0_
  33.0 0.7 %last_products.1 = (f32[29,128,128]{2,1,0:T(8,128)S(1)}, f32[14,128,128]{2,1,0:T(8,128)S(1)}, f32[14,128,128]{2,1,0:T(8,128)S(1)}) custom-call(s32[5,128]{1,0:T(8,128)S(1)} %list_products.1.pairs, f32[29,128,128]{2,1,0:T(8,128)S(1)} %get-tuple-element.9.total, ...), custom_call_target="tpu_custom_call", output_to_operand_aliasing={{0}: (1, {})} | custom-call | flops 58720256 | bytes 3670016 | tf_op jit(solution)/shard_map/last_products/pallas_call | solution.py:389
  33.8 12.1 %collective-permute-start.9 = (f32[14,128,128]{2,1,0:T(8,128)S(1)}, f32[14,128,128]{2,1,0:T(8,128)S(1)}, u32[]{:S(2)}, u32[]{:S(2)}) collective-permute-start(f32[14,128,128]{2,1,0:T(8,128)S(1)} %get-tuple-element.12), channel_id=1, source_target_pairs={{0,1},{1,0},{2,3},{3,2},{4,5},{5,4},{6,7},{7,6},{8,9},{9,8},{10,11... | collective-permute-start | bytes 2752520 | tf_op jit(solution)/shard_map/ppermute | solution.py:399
  45.9 2.1 %collective-permute-done.9 = f32[14,128,128]{2,1,0:T(8,128)S(1)} collective-permute-done((f32[14,128,128]{2,1,0:T(8,128)S(1)}, f32[14,128,128]{2,1,0:T(8,128)S(1)}, u32[]{:S(2)}, u32[]{:S(2)}) %collective-permute-start.9) | collective-permute-done | bytes 917536 | tf_op jit(solution)/shard_map/ppermute | solution.py:399
  48.0 0.9 %fusion = bf16[1,1,14,128,128]{4,3,2,1,0:T(8,128)(2,1)} fusion(f32[14,128,128]{2,1,0:T(8,128)S(1)} %get-tuple-element.11, f32[14,128,128]{2,1,0:T(8,128)S(1)} %collective-permute-done.9), kind=kLoop, calls=%fused_computation.1 | loop fusion | flops 458752 | bytes 2293760 | tf_op jit(solution)/shard_map/broadcast_in_dim | solution.py:400
Async XLA Ops:
  0.0 30.3 %copy-start = (bf16[1,1,28,128,128]{4,3,2,1,0:T(8,128)(2,1)S(1)}, bf16[1,1,28,128,128]{4,3,2,1,0:T(8,128)(2,1)}, u32[]{:S(2)}) copy-start(bf16[1,1,28,128,128]{4,3,2,1,0:T(8,128)(2,1)} %param.3) | copy-start | bytes 2752516
  0.0 12.8 %collective-permute-start = (bf16[28,128,128]{2,1,0:T(8,128)(2,1)}, bf16[28,128,128]{2,1,0:T(8,128)(2,1)S(1)}, u32[]{:S(2)}, u32[]{:S(2)}) collective-permute-start(bf16[28,128,128]{2,1,0:T(8,128)(2,1)} %bitcast.5), channel_id=1, source_target_pairs={{0,8},{1,17},{2,10},{3,19},{4,12},{5,21},{6,14},{7,23},{8,0},{9,25... | collective-permute-start | bytes 2752520 | tf_op jit(solution)/shard_map/ppermute | solution.py:346
  2.3 13.2 %collective-permute-start.2 = (bf16[14,128,128]{2,1,0:T(8,128)(2,1)S(1)}, bf16[14,128,128]{2,1,0:T(8,128)(2,1)S(1)}, u32[]{:S(2)}, u32[]{:S(2)}) collective-permute-start(bf16[14,128,128]{2,1,0:T(8,128)(2,1)S(1)} %slice_bitcast_fusion), channel_id=1, source_target_pairs={{0,2},{2,4},{3,1},{4,6},{5,3},{7,5},{8,10},{10,12},{11,9},{12,14},... | collective-permute-start | bytes 1376264 | tf_op jit(solution)/shard_map/ppermute | solution.py:338
  5.5 12.2 %collective-permute-start.3 = (bf16[14,128,128]{2,1,0:T(8,128)(2,1)S(1)}, bf16[14,128,128]{2,1,0:T(8,128)(2,1)S(1)}, u32[]{:S(2)}, u32[]{:S(2)}) collective-permute-start(bf16[14,128,128]{2,1,0:T(8,128)(2,1)S(1)} %slice.12), channel_id=1, source_target_pairs={{0,2},{2,4},{3,1},{4,6},{5,3},{7,5},{8,10},{10,12},{11,9},{12,14},... | collective-permute-start | bytes 1376264 | tf_op jit(solution)/shard_map/ppermute | solution.py:338
  12.8 17.6 %collective-permute-start.1 = (bf16[28,128,128]{2,1,0:T(8,128)(2,1)S(1)}, bf16[28,128,128]{2,1,0:T(8,128)(2,1)S(1)}, u32[]{:S(2)}, u32[]{:S(2)}) collective-permute-start(bf16[28,128,128]{2,1,0:T(8,128)(2,1)S(1)} %collective-permute-done.refs_1_), channel_id=1, source_target_pairs={{0,1},{1,0},{2,3},{3,2},{4,5},{5,4},{6,7},{7,6},{8,9},{9,8},{10,11... | collective-permute-start | bytes 2752520 | tf_op jit(solution)/shard_map/ppermute | solution.py:347
  14.3 16.9 %collective-permute-start.6 = (bf16[28,128,128]{2,1,0:T(8,128)(2,1)}, bf16[28,128,128]{2,1,0:T(8,128)(2,1)S(1)}, u32[]{:S(2)}, u32[]{:S(2)}) collective-permute-start(bf16[28,128,128]{2,1,0:T(8,128)(2,1)} %bitcast.7), channel_id=1, source_target_pairs={{0,24},{2,26},{4,28},{6,30},{9,17},{10,18},{12,20},{14,22},{17,9},... | collective-permute-start | bytes 2752520 | tf_op jit(solution)/shard_map/ppermute | solution.py:348
  15.6 7.5 %collective-permute-start.4 = (bf16[14,128,128]{2,1,0:T(8,128)(2,1)S(1)}, bf16[14,128,128]{2,1,0:T(8,128)(2,1)S(1)}, u32[]{:S(2)}, u32[]{:S(2)}) collective-permute-start(bf16[14,128,128]{2,1,0:T(8,128)(2,1)S(1)} %collective-permute-done.2.refs_4_.refs_5_), channel_id=1, source_target_pairs={{2,4},{3,1},{4,6},{5,3},{10,12},{11,9},{12,14},{13,11},{18,20},{19... | collective-permute-start | bytes 1376264 | tf_op jit(solution)/shard_map/ppermute | solution.py:338
  17.7 10.3 %collective-permute-start.5 = (bf16[14,128,128]{2,1,0:T(8,128)(2,1)S(1)}, bf16[14,128,128]{2,1,0:T(8,128)(2,1)S(1)}, u32[]{:S(2)}, u32[]{:S(2)}) collective-permute-start(bf16[14,128,128]{2,1,0:T(8,128)(2,1)S(1)} %collective-permute-done.3.refs_5_.refs_6_), channel_id=1, source_target_pairs={{2,4},{3,1},{4,6},{5,3},{10,12},{11,9},{12,14},{13,11},{18,20},{19... | collective-permute-start | bytes 1376264 | tf_op jit(solution)/shard_map/ppermute | solution.py:338
  23.1 8.2 %collective-permute-start.7 = (bf16[14,128,128]{2,1,0:T(8,128)(2,1)S(1)}, bf16[14,128,128]{2,1,0:T(8,128)(2,1)S(1)}, u32[]{:S(2)}, u32[]{:S(2)}) collective-permute-start(bf16[14,128,128]{2,1,0:T(8,128)(2,1)S(1)} %collective-permute-done.4.refs_6_.refs_7_), channel_id=1, source_target_pairs={{3,1},{4,6},{11,9},{12,14},{19,17},{20,22},{27,25},{28,30}} | collective-permute-start | bytes 1376264 | tf_op jit(solution)/shard_map/ppermute | solution.py:338
  28.0 5.0 %collective-permute-start.8 = (bf16[14,128,128]{2,1,0:T(8,128)(2,1)S(1)}, bf16[14,128,128]{2,1,0:T(8,128)(2,1)S(1)}, u32[]{:S(2)}, u32[]{:S(2)}) collective-permute-start(bf16[14,128,128]{2,1,0:T(8,128)(2,1)S(1)} %collective-permute-done.5.refs_7_.refs_8_), channel_id=1, source_target_pairs={{3,1},{4,6},{11,9},{12,14},{19,17},{20,22},{27,25},{28,30}} | collective-permute-start | bytes 1376264 | tf_op jit(solution)/shard_map/ppermute | solution.py:338
  33.8 14.2 %collective-permute-start.9 = (f32[14,128,128]{2,1,0:T(8,128)S(1)}, f32[14,128,128]{2,1,0:T(8,128)S(1)}, u32[]{:S(2)}, u32[]{:S(2)}) collective-permute-start(f32[14,128,128]{2,1,0:T(8,128)S(1)} %get-tuple-element.12), channel_id=1, source_target_pairs={{0,1},{1,0},{2,3},{3,2},{4,5},{5,4},{6,7},{7,6},{8,9},{9,8},{10,11... | collective-permute-start | bytes 2752520 | tf_op jit(solution)/shard_map/ppermute | solution.py:399

commit v4 on v3

--- a/solution.py
+++ b/solution.py
@@ -10,7 +10,7 @@
 TB = 28
 GROUP = 8
 LANES = 128
-GRANT = 16 << 20
+GRANT = 8 << 20
 CHUNKS = 2
 
 
@@ -55,17 +55,18 @@
         return pairs
 
     def far_pairs(self):
+        far = self.grid - 1
         pairs = []
         for r in range(self.grid):
             for a in range(self.grid):
-                k = self.shift(a, r)
-                if k is not None:
-                    pairs.append(
-                        tuple(
-                            (p * self.grid + a) * 2 + int(k > 0)
-                            for p in (r, r ^ (self.grid - 1))
+                if self.shift(a, r) is not None:
+                    for layer, by in enumerate((1, 2)):
+                        pairs.append(
+                            tuple(
+                                (p * self.grid + a) * 2 + layer
+                                for p in (r ^ by, r ^ far)
+                            )
                         )
-                    )
         return pairs
 
     def taken(self, a, layer, stage):
@@ -184,105 +185,119 @@
         at += ref.shape[0]
 
 
-def fetch_left(lefts, by, layer, buffer, sem):
-    own, near, swapped = lefts
-    at = 2 * by + layer
-
-    @pl.when(by == 0)
-    def _():
-        pltpu.make_async_copy(own, buffer, sem).start()
-
-    for k in range(len(near)):
-
-        @pl.when((at == 4 * k + 2) | (at == 4 * k + 5))
-        def _(k=k):
-            pltpu.make_async_copy(near[k], buffer, sem).start()
-
-        @pl.when((at == 4 * k + 3) | (at == 4 * k + 4))
-        def _(k=k):
-            pltpu.make_async_copy(swapped[k], buffer, sem).start()
-
-
-def split_lefts(plan, refs):
-    near = plan.grid // 2 - 1
-    return (refs[0], refs[1 : 1 + near], refs[1 + near : 1 + 2 * near]), refs[
-        1 + 2 * near :
-    ]
-
-
-def early_kernel(plan, parts, pairs, *refs):
-    far = plan.grid - 1
-    lefts, refs = split_lefts(plan, refs)
-    rights = []
-    for n in parts:
-        rights.append(refs[:n])
-        refs = refs[n:]
-    acc, left, right, left_sem, right_sem = refs
-    a, b, layer = place()
-    last = pairs.shape[1] - 1
-    jobs = []
-    for stage in range(plan.stages):
-        l, _ = plan.taken(a, layer, stage)
-        by = b ^ l
-        count = jnp.where(by == far, 0, pairs[stage, last])
-        jobs.append((stage, by, count))
-
-        @pl.when(count > 0)
-        def _(stage=stage, by=by):
-            fetch(rights[stage], right.at[stage], right_sem.at[stage])
-            fetch_left(lefts, by, layer, left.at[stage], left_sem.at[stage])
-
-    acc[...] = jnp.zeros_like(acc)
-    for stage, by, count in jobs:
-
-        @pl.when(count > 0)
-        def _(stage=stage, count=count):
-            pltpu.make_async_copy(
-                lefts[0], left.at[stage], left_sem.at[stage]
-            ).wait()
-            fetched(rights[stage], right.at[stage], right_sem.at[stage])
-            add_products(
-                count, pairs, stage, left.at[stage], right.at[stage], acc
-            )
-
-
-def middle_kernel(plan, parts, pairs, total, *refs):
-    del total
-    lefts, refs = split_lefts(plan, refs)
-    far_tile, *refs = refs
+class Lefts:
+    def __init__(self, plan, refs, late):
+        near = plan.grid // 2 - 1
+        self.far = plan.grid - 1
+        self.own, self.near = refs[0], refs[1 : 1 + near]
+        self.late = late
+        if late:
+            self.swapped = refs[1 + near : 1 + 2 * near]
+            self.halves = refs[1 + 2 * near : 3 + 2 * near]
+
+    @staticmethod
+    def number(plan, late):
+        near = plan.grid // 2 - 1
+        return 3 + 2 * near if late else 1 + near
+
+    def direct(self, by, layer):
+        found = by == 0
+        for k in range(len(self.near)):
+            found |= by == 2 * k + 1 + layer
+        return found & (by != self.far)
+
+    def fetch(self, by, layer, buffer, sem):
+        @pl.when(by == 0)
+        def _():
+            pltpu.make_async_copy(self.own, buffer, sem).start()
+
+        for k in range(len(self.near)):
+
+            @pl.when(by == 2 * k + 1 + layer)
+            def _(k=k):
+                pltpu.make_async_copy(self.near[k], buffer, sem).start()
+
+            if self.late:
+
+                @pl.when(by == 2 * k + 2 - layer)
+                def _(k=k):
+                    pltpu.make_async_copy(self.swapped[k], buffer, sem).start()
+
+        if self.late:
+
+            @pl.when(by == self.far)
+            def _():
+                share = self.halves[0].shape[0]
+                for j, half in enumerate(self.halves):
+                    at = jnp.abs(layer - j) * share
+                    pltpu.make_async_copy(
+                        half, buffer.at[pl.ds(at, share)], sem
+                    ).start()
+
+    def fetched(self, buffer, sem):
+        pltpu.make_async_copy(self.own, buffer, sem).wait()
+
+
+def stages_of(parts, refs):
     rights = []
     for n in parts[:-1]:
         rights.append(refs[:n])
         refs = refs[n:]
-    first, acc, left_last, right, left_sem, right_sem = refs
-    far, end, last = plan.grid - 1, plan.stages, pairs.shape[1] - 1
+    return rights, refs
+
+
+def start_jobs(plan, lefts, rights, pairs, left, right, left_sem, right_sem, late):
+    a, b, layer = place()
+    counts = []
+    for stage in range(plan.stages):
+        l, _ = plan.taken(a, layer, stage)
+        by = b ^ l
+        here = lefts.direct(by, layer) != late
+        count = jnp.where(here, pairs[stage, pairs.shape[1] - 1], 0)
+        counts.append(count)
+
+        @pl.when(count > 0)
+        def _(stage=stage, by=by):
+            fetch(rights[stage], right.at[stage], right_sem.at[stage])
+            lefts.fetch(by, layer, left.at[stage], left_sem.at[stage])
+
+    return counts
+
+
+def finish_jobs(counts, lefts, rights, pairs, left, right, left_sem, right_sem, acc):
+    for stage, count in enumerate(counts):
+
+        @pl.when(count > 0)
+        def _(stage=stage, count=count):
+            lefts.fetched(left.at[stage], left_sem.at[stage])
+            fetched(rights[stage], right.at[stage], right_sem.at[stage])
+            add_products(count, pairs, stage, left.at[stage], right.at[stage], acc)
+
+
+def early_kernel(plan, parts, pairs, *refs):
+    n = Lefts.number(plan, False)
+    lefts = Lefts(plan, refs[:n], False)
+    rights, refs = stages_of(parts, refs[n:])
+    acc, *buffers = refs
+    counts = start_jobs(plan, lefts, rights, pairs, *buffers, False)
+    acc[...] = jnp.zeros_like(acc)
+    finish_jobs(counts, lefts, rights, pairs, *buffers, acc)
+
+
+def middle_kernel(plan, parts, pairs, total, *refs):
+    del total
+    n = Lefts.number(plan, True)
+    lefts = Lefts(plan, refs[:n], True)
+    rights, refs = stages_of(parts, refs[n:])
+    first, acc, left_last, *buffers, last_sem = refs
+    end = plan.stages
     a, b, layer = place()
     l, _ = plan.taken(a, layer, end)
-    end_by = b ^ l
-    fetch_left(lefts, end_by, layer, left_last, left_sem)
-
-    @pl.when(end_by == far)
-    def _():
-        pltpu.make_async_copy(far_tile, left_last, left_sem).start()
-
-    counts = []
-    for stage in range(end):
-        l, _ = plan.taken(a, layer, stage)
-        count = jnp.where(b ^ l == far, pairs[stage, last], 0)
-        counts.append(count)
-
-        @pl.when(count > 0)
-        def _(stage=stage):
-            fetch(rights[stage], right, right_sem)
-
-    pltpu.make_async_copy(far_tile, left_last, left_sem).wait()
-    add_products(pairs[end, last], pairs, end, left_last, first, acc)
-    for stage, count in enumerate(counts):
-
-        @pl.when(count > 0)
-        def _(stage=stage, count=count):
-            fetched(rights[stage], right, right_sem)
-            add_products(count, pairs, stage, far_tile, right, acc)
+    counts = start_jobs(plan, lefts, rights, pairs, *buffers, True)
+    lefts.fetch(b ^ l, layer, left_last, last_sem)
+    finish_jobs(counts, lefts, rights, pairs, *buffers, acc)
+    lefts.fetched(left_last, last_sem)
+    add_products(pairs[end, pairs.shape[1] - 1], pairs, end, left_last, first, acc)
 
 
 def last_kernel(plan, bounds, pairs, total, left_last, *refs):
@@ -345,46 +360,46 @@
         bys = (2 * k + 1, 2 * k + 2)
         near.append(lax.ppermute(own, everywhere, plan.near_pairs(bys)))
         swapped.append(lax.ppermute(near[-1], "layer", swap))
-    far = lax.ppermute(own, everywhere, plan.far_pairs())
-    lefts = [own, *near, *swapped]
+    sent = jnp.where(
+        lax.axis_index("layer") == 0, near[0][:share], near[0][share:]
+    )
+    far = lax.ppermute(sent, everywhere, plan.far_pairs())
+    far_swapped = lax.ppermute(far, "layer", swap)
+    direct = [own, *near]
+    lefts = [*direct, *swapped, far, far_swapped]
     parts = [len(r) for r in rights]
     running = jax.ShapeDtypeStruct((slots + 1, size, size), jnp.float32)
     before = [part for stage in rights[:-1] for part in stage]
+    buffers = [
+        pltpu.VMEM((plan.stages, *own.shape), own.dtype),
+        pltpu.VMEM((plan.stages, *own.shape), own.dtype),
+        pltpu.SemaphoreType.DMA((plan.stages,)),
+        pltpu.SemaphoreType.DMA((plan.stages, CHUNKS)),
+    ]
     total = pl.pallas_call(
-        functools.partial(early_kernel, plan, parts[:-1]),
+        functools.partial(early_kernel, plan, parts),
         out_shape=running,
-        in_specs=[scalars] + [anywhere] * (len(lefts) + len(before)),
+        in_specs=[scalars] + [anywhere] * (len(direct) + len(before)),
         out_specs=vmem,
-        scratch_shapes=[
-            pltpu.VMEM((plan.stages, *own.shape), own.dtype),
-            pltpu.VMEM((plan.stages, *own.shape), own.dtype),
-            pltpu.SemaphoreType.DMA((plan.stages,)),
-            pltpu.SemaphoreType.DMA((plan.stages, CHUNKS)),
-        ],
+        scratch_shapes=buffers,
         compiler_params=compiler_params,
         cost_estimate=cost(slots * plan.stages, 2 * plan.stages),
         name="early_products",
-    )(lists, *lefts, *before)
+    )(lists, *direct, *before)
     first, *rest = rights[-1]
     total, left_last = pl.pallas_call(
         functools.partial(middle_kernel, plan, parts),
         out_shape=(running, jax.ShapeDtypeStruct(own.shape, own.dtype)),
         in_specs=[scalars, vmem]
-        + [anywhere] * len(lefts)
-        + [vmem]
-        + [anywhere] * len(before)
+        + [anywhere] * (len(lefts) + len(before))
         + [vmem],
         out_specs=(vmem, vmem),
         input_output_aliases={1: 0},
-        scratch_shapes=[
-            pltpu.VMEM(own.shape, own.dtype),
-            pltpu.SemaphoreType.DMA,
-            pltpu.SemaphoreType.DMA((CHUNKS,)),
-        ],
+        scratch_shapes=buffers + [pltpu.SemaphoreType.DMA],
         compiler_params=compiler_params,
-        cost_estimate=cost(slots, 4),
+        cost_estimate=cost(slots * plan.stages, 2 * plan.stages),
         name="middle_products",
-    )(lists, total, *lefts, far, *before, first)
+    )(lists, total, *lefts, *before, first)
     half = jax.ShapeDtypeStruct((share, size, size), jnp.float32)
     _, mine, other = pl.pallas_call(
         functools.partial(last_kernel, plan, bounds),

time: 49.3 us -> 44.9 us (0.911)
  the two profiles are of different devices: /device:TPU:17 before, /device:TPU:0 now
where the time goes in v4:
time: 44.9 us; the launch traced here: 44.1 us
  starting transfers between devices  25.6 us (57%)
  waiting for transfers between devices  9.39 us (21%)
  Pallas kernels  5.03 us (11%)
  local copies, waits for them, and re-layouts  2.92 us (7%)
  other arithmetic  0.94 us (2%)
    ppermute x1, starting transfers between devices, on_device(): received = lax.ppermute(other, 'layer', swap)  9.88 us
    ppermute x6, starting transfers between devices, on_device(): arrived.append(lax.ppermute(part, ('col', 'layer'), pairs))  9.71 us
    ppermute x6, waiting for transfers between devices, on_device(): arrived.append(lax.ppermute(part, ('col', 'layer'), pairs))  4.19 us
    ppermute x1, waiting for transfers between devices, on_device(): far = lax.ppermute(sent, everywhere, plan.far_pairs())  3.09 us
    ppermute x1, starting transfers between devices, on_device(): near.append(lax.ppermute(own, everywhere, plan.near_pairs(bys)))  3.03 us
    slice x2, local copies, waits for them, and re-layouts, on_device(): (lax.optimization_barrier(own) if i else own)[i:j]  2.91 us
    pallas_call x1, Pallas kernels, on_device(): pl.pallas_call(functools.partial(early_kernel, plan, parts), out_shape=ru...  2.32 us
    ppermute x1, waiting for transfers between devices, on_device(): received = lax.ppermute(other, 'layer', swap)  2.1 us
  transfers between devices with their start and end apart: 11, of which 4 were waited for; matrix products, arithmetic and copies ran while one was open for 7% of the time, Pallas kernels for 10%

profile of v4, /device:TPU:0, one launch (start us, length us, event | category | flops | bytes accessed | tf_op | source)
XLA Modules:
  0.0 44.1 jit_solution(9325392197526603551)
XLA Ops:
  0.0 3.0 %collective-permute-start = (bf16[28,128,128]{2,1,0:T(8,128)(2,1)}, bf16[28,128,128]{2,1,0:T(8,128)(2,1)S(1)}, u32[]{:S(2)}, u32[]{:S(2)}) collective-permute-start(bf16[28,128,128]{2,1,0:T(8,128)(2,1)} %bitcast.5), channel_id=1, source_target_pairs={{0,8},{1,17},{2,10},{3,19},{4,12},{5,21},{6,14},{7,23},{8,0},{9,25... | collective-permute-start | bytes 2752520 | tf_op jit(solution)/shard_map/ppermute | solution.py:361
  3.0 1.9 %slice_bitcast_fusion = bf16[14,128,128]{2,1,0:T(8,128)(2,1)} fusion(bf16[1,1,28,128,128]{4,3,2,1,0:T(8,128)(2,1)} %param.3), kind=kLoop, calls=%fused_computation.3 | loop fusion | bytes 917504 | tf_op jit(solution)/shard_map/slice | solution.py:322
  4.9 3.5 %collective-permute-start.1 = (bf16[14,128,128]{2,1,0:T(8,128)(2,1)}, bf16[14,128,128]{2,1,0:T(8,128)(2,1)S(1)}, u32[]{:S(2)}, u32[]{:S(2)}) collective-permute-start(bf16[14,128,128]{2,1,0:T(8,128)(2,1)} %slice_bitcast_fusion), channel_id=1, source_target_pairs={{0,2},{2,4},{3,1},{4,6},{5,3},{7,5},{8,10},{10,12},{11,9},{12,14},... | collective-permute-start | bytes 1376264 | tf_op jit(solution)/shard_map/ppermute | solution.py:353
  8.4 1.1 %slice.20 = bf16[14,128,128]{2,1,0:T(8,128)(2,1)S(1)} slice(bf16[28,128,128]{2,1,0:T(8,128)(2,1)} %bitcast.6), slice={[14:28], [0:128], [0:128]} | slice | bytes 917504 | tf_op jit(solution)/shard_map/slice | solution.py:322
  9.5 3.5 %collective-permute-start.2 = (bf16[14,128,128]{2,1,0:T(8,128)(2,1)S(1)}, bf16[14,128,128]{2,1,0:T(8,128)(2,1)S(1)}, u32[]{:S(2)}, u32[]{:S(2)}) collective-permute-start(bf16[14,128,128]{2,1,0:T(8,128)(2,1)S(1)} %slice.20), channel_id=1, source_target_pairs={{0,2},{2,4},{3,1},{4,6},{5,3},{7,5},{8,10},{10,12},{11,9},{12,14},... | collective-permute-start | bytes 1376264 | tf_op jit(solution)/shard_map/ppermute | solution.py:353
  13.0 1.7 %collective-permute-done.1.refs_3_.refs_6_ = bf16[14,128,128]{2,1,0:T(8,128)(2,1)S(1)} collective-permute-done((bf16[14,128,128]{2,1,0:T(8,128)(2,1)}, bf16[14,128,128]{2,1,0:T(8,128)(2,1)S(1)}, u32[]{:S(2)}, u32[]{:S(2)}) %collective-permute-start.1) | collective-permute-done | bytes 458784 | tf_op jit(solution)/shard_map/ppermute | solution.py:353
  14.7 0.7 %collective-permute-start.3 = (bf16[14,128,128]{2,1,0:T(8,128)(2,1)S(1)}, bf16[14,128,128]{2,1,0:T(8,128)(2,1)S(1)}, u32[]{:S(2)}, u32[]{:S(2)}) collective-permute-start(bf16[14,128,128]{2,1,0:T(8,128)(2,1)S(1)} %collective-permute-done.1.refs_3_.refs_6_), channel_id=1, source_target_pairs={{2,4},{3,1},{4,6},{5,3},{10,12},{11,9},{12,14},{13,11},{18,20},{19... | collective-permute-start | bytes 1376264 | tf_op jit(solution)/shard_map/ppermute | solution.py:353
  15.4 0.0 collective-permute-done.refs_1_
  15.4 0.1 slice_select_fusion
  15.4 1.6 %collective-permute-start.6 = (bf16[14,128,128]{2,1,0:T(8,128)(2,1)S(1)}, bf16[14,128,128]{2,1,0:T(8,128)(2,1)S(1)}, u32[]{:S(2)}, u32[]{:S(2)}) collective-permute-start(bf16[14,128,128]{2,1,0:T(8,128)(2,1)S(1)} %slice_select_fusion), channel_id=1, source_target_pairs={{8,24},{17,25},{10,26},{19,27},{12,28},{21,29},{14,30},{23,31},{0,... | collective-permute-start | bytes 1376264 | tf_op jit(solution)/shard_map/ppermute | solution.py:366
  17.0 0.0 collective-permute-start.5
  17.0 2.5 %collective-permute-done.2.refs_4_.refs_7_ = bf16[14,128,128]{2,1,0:T(8,128)(2,1)S(1)} collective-permute-done((bf16[14,128,128]{2,1,0:T(8,128)(2,1)S(1)}, bf16[14,128,128]{2,1,0:T(8,128)(2,1)S(1)}, u32[]{:S(2)}, u32[]{:S(2)}) %collective-permute-start.2) | collective-permute-done | bytes 458784 | tf_op jit(solution)/shard_map/ppermute | solution.py:353
  19.5 0.7 %collective-permute-start.4 = (bf16[14,128,128]{2,1,0:T(8,128)(2,1)S(1)}, bf16[14,128,128]{2,1,0:T(8,128)(2,1)S(1)}, u32[]{:S(2)}, u32[]{:S(2)}) collective-permute-start(bf16[14,128,128]{2,1,0:T(8,128)(2,1)S(1)} %collective-permute-done.2.refs_4_.refs_7_), channel_id=1, source_target_pairs={{2,4},{3,1},{4,6},{5,3},{10,12},{11,9},{12,14},{13,11},{18,20},{19... | collective-permute-start | bytes 1376264 | tf_op jit(solution)/shard_map/ppermute | solution.py:353
  20.2 0.0 collective-permute-done.3.refs_5_.refs_8_
  20.2 0.7 %collective-permute-start.8 = (bf16[14,128,128]{2,1,0:T(8,128)(2,1)S(1)}, bf16[14,128,128]{2,1,0:T(8,128)(2,1)S(1)}, u32[]{:S(2)}, u32[]{:S(2)}) collective-permute-start(bf16[14,128,128]{2,1,0:T(8,128)(2,1)S(1)} %collective-permute-done.3.refs_5_.refs_8_), channel_id=1, source_target_pairs={{3,1},{4,6},{11,9},{12,14},{19,17},{20,22},{27,25},{28,30}} | collective-permute-start | bytes 1376264 | tf_op jit(solution)/shard_map/ppermute | solution.py:353
  20.9 3.1 %collective-permute-done.6.refs_3_ = bf16[14,128,128]{2,1,0:T(8,128)(2,1)S(1)} collective-permute-done((bf16[14,128,128]{2,1,0:T(8,128)(2,1)S(1)}, bf16[14,128,128]{2,1,0:T(8,128)(2,1)S(1)}, u32[]{:S(2)}, u32[]{:S(2)}) %collective-permute-start.6) | collective-permute-done | bytes 458784 | tf_op jit(solution)/shard_map/ppermute | solution.py:366
  24.0 1.4 %collective-permute-start.7 = (bf16[14,128,128]{2,1,0:T(8,128)(2,1)S(1)}, bf16[14,128,128]{2,1,0:T(8,128)(2,1)S(1)}, u32[]{:S(2)}, u32[]{:S(2)}) collective-permute-start(bf16[14,128,128]{2,1,0:T(8,128)(2,1)S(1)} %collective-permute-done.6.refs_3_), channel_id=1, source_target_pairs={{0,1},{1,0},{2,3},{3,2},{4,5},{5,4},{6,7},{7,6},{8,9},{9,8},{10,11... | collective-permute-start | bytes 1376264 | tf_op jit(solution)/shard_map/ppermute | solution.py:367
  25.4 0.0 collective-permute-done.4.refs_6_.refs_9_
  25.4 0.7 %collective-permute-start.9 = (bf16[14,128,128]{2,1,0:T(8,128)(2,1)S(1)}, bf16[14,128,128]{2,1,0:T(8,128)(2,1)S(1)}, u32[]{:S(2)}, u32[]{:S(2)}) collective-permute-start(bf16[14,128,128]{2,1,0:T(8,128)(2,1)S(1)} %collective-permute-done.4.refs_6_.refs_9_), channel_id=1, source_target_pairs={{3,1},{4,6},{11,9},{12,14},{19,17},{20,22},{27,25},{28,30}} | collective-permute-start | bytes 1376264 | tf_op jit(solution)/shard_map/ppermute | solution.py:353
  26.1 0.0 copy-done.1
  26.1 0.0 copy-done.2
  26.1 1.0 %list_products.1.pairs = s32[5,128]{1,0:T(8,128)S(1)} custom-call(s32[4,4,28]{2,1,0:T(4,128)S(1)} %convert_add_fusion.slot_keys), custom_call_target="tpu_custom_call" | custom-call | bytes 1835008 | tf_op jit(solution)/shard_map/list_products/pallas_call | solution.py:338
  27.1 2.3 %early_products.1.total = f32[29,128,128]{2,1,0:T(8,128)S(1)} custom-call(s32[5,128]{1,0:T(8,128)S(1)} %list_products.1.pairs, bf16[28,128,128]{2,1,0:T(8,128)(2,1)S(1)} %bitcast.7, bf16[28,128,128]{2,1,0:T(8,128)(2,1)S(1)} %collective-permute-done.refs_1_, bf16[28,128,128]{2,1,0:T(8,128)(2,1)S(1)} %bitcast.8, ...), custom_call_target="tpu_custom_call" | custom-call | flops 352321536 | bytes 5505024 | tf_op jit(solution)/shard_map/early_products/pallas_call | solution.py:379
  29.4 0.0 collective-permute-done.8.refs_10_
  29.4 0.0 collective-permute-done.7.refs_4_
  29.4 0.0 collective-permute-done.5.refs_2_
  29.4 1.0 %middle_products.1 = (f32[29,128,128]{2,1,0:T(8,128)S(1)}, bf16[28,128,128]{2,1,0:T(8,128)(2,1)S(1)}) custom-call(s32[5,128]{1,0:T(8,128)S(1)} %list_products.1.pairs, f32[29,128,128]{2,1,0:T(8,128)S(1)} %early_products.1.total, bf16[28,128,128]{2,1,0:T(8,128)(2,1)S(1)} %bitcast.9, ...), custom_call_target="tpu_custom_call", output_to_operand_aliasing={{0}: (1, {})} | custom-call | flops 352321536 | bytes 5505024 | tf_op jit(solution)/shard_map/middle_products/pallas_call | solution.py:390
  30.5 0.0 collective-permute-done.9.refs_0_
  30.5 0.7 %last_products.1 = (f32[29,128,128]{2,1,0:T(8,128)S(1)}, f32[14,128,128]{2,1,0:T(8,128)S(1)}, f32[14,128,128]{2,1,0:T(8,128)S(1)}) custom-call(s32[5,128]{1,0:T(8,128)S(1)} %list_products.1.pairs, f32[29,128,128]{2,1,0:T(8,128)S(1)} %get-tuple-element.9.total, ...), custom_call_target="tpu_custom_call", output_to_operand_aliasing={{0}: (1, {})} | custom-call | flops 58720256 | bytes 3670016 | tf_op jit(solution)/shard_map/last_products/pallas_call | solution.py:404
  31.2 9.9 %collective-permute-start.10 = (f32[14,128,128]{2,1,0:T(8,128)S(1)}, f32[14,128,128]{2,1,0:T(8,128)S(1)}, u32[]{:S(2)}, u32[]{:S(2)}) collective-permute-start(f32[14,128,128]{2,1,0:T(8,128)S(1)} %get-tuple-element.12), channel_id=1, source_target_pairs={{0,1},{1,0},{2,3},{3,2},{4,5},{5,4},{6,7},{7,6},{8,9},{9,8},{10,11... | collective-permute-start | bytes 2752520 | tf_op jit(solution)/shard_map/ppermute | solution.py:414
  41.1 2.1 %collective-permute-done.10 = f32[14,128,128]{2,1,0:T(8,128)S(1)} collective-permute-done((f32[14,128,128]{2,1,0:T(8,128)S(1)}, f32[14,128,128]{2,1,0:T(8,128)S(1)}, u32[]{:S(2)}, u32[]{:S(2)}) %collective-permute-start.10) | collective-permute-done | bytes 917536 | tf_op jit(solution)/shard_map/ppermute | solution.py:414
  43.2 0.9 %fusion = bf16[1,1,14,128,128]{4,3,2,1,0:T(8,128)(2,1)} fusion(f32[14,128,128]{2,1,0:T(8,128)S(1)} %get-tuple-element.11, f32[14,128,128]{2,1,0:T(8,128)S(1)} %collective-permute-done.10), kind=kLoop, calls=%fused_computation.1 | loop fusion | flops 458752 | bytes 2293760 | tf_op jit(solution)/shard_map/broadcast_in_dim | solution.py:415
  (5 shorter events, 0.0 us)
Async XLA Ops:
  0.0 27.1 %copy-start = (bf16[1,1,28,128,128]{4,3,2,1,0:T(8,128)(2,1)S(1)}, bf16[1,1,28,128,128]{4,3,2,1,0:T(8,128)(2,1)}, u32[]{:S(2)}) copy-start(bf16[1,1,28,128,128]{4,3,2,1,0:T(8,128)(2,1)} %param.3) | copy-start | bytes 2752516
  0.0 26.1 %copy-start.1 = (s32[4,4,28]{2,1,0:T(4,128)S(1)}, s32[4,4,28]{2,1,0:T(4,128)}, u32[]{:S(2)}) copy-start(s32[4,4,28]{2,1,0:T(4,128)} %param.4) | copy-start | bytes 5380
  0.0 26.1 %copy-start.2 = (s32[4,4,28]{2,1,0:T(4,128)S(1)}, s32[4,4,28]{2,1,0:T(4,128)}, u32[]{:S(2)}) copy-start(s32[4,4,28]{2,1,0:T(4,128)} %param.5) | copy-start | bytes 5380
  0.0 15.3 %collective-permute-start = (bf16[28,128,128]{2,1,0:T(8,128)(2,1)}, bf16[28,128,128]{2,1,0:T(8,128)(2,1)S(1)}, u32[]{:S(2)}, u32[]{:S(2)}) collective-permute-start(bf16[28,128,128]{2,1,0:T(8,128)(2,1)} %bitcast.5), channel_id=1, source_target_pairs={{0,8},{1,17},{2,10},{3,19},{4,12},{5,21},{6,14},{7,23},{8,0},{9,25... | collective-permute-start | bytes 2752520 | tf_op jit(solution)/shard_map/ppermute | solution.py:361
  4.9 9.8 %collective-permute-start.1 = (bf16[14,128,128]{2,1,0:T(8,128)(2,1)}, bf16[14,128,128]{2,1,0:T(8,128)(2,1)S(1)}, u32[]{:S(2)}, u32[]{:S(2)}) collective-permute-start(bf16[14,128,128]{2,1,0:T(8,128)(2,1)} %slice_bitcast_fusion), channel_id=1, source_target_pairs={{0,2},{2,4},{3,1},{4,6},{5,3},{7,5},{8,10},{10,12},{11,9},{12,14},... | collective-permute-start | bytes 1376264 | tf_op jit(solution)/shard_map/ppermute | solution.py:353
  9.5 10.0 %collective-permute-start.2 = (bf16[14,128,128]{2,1,0:T(8,128)(2,1)S(1)}, bf16[14,128,128]{2,1,0:T(8,128)(2,1)S(1)}, u32[]{:S(2)}, u32[]{:S(2)}) collective-permute-start(bf16[14,128,128]{2,1,0:T(8,128)(2,1)S(1)} %slice.20), channel_id=1, source_target_pairs={{0,2},{2,4},{3,1},{4,6},{5,3},{7,5},{8,10},{10,12},{11,9},{12,14},... | collective-permute-start | bytes 1376264 | tf_op jit(solution)/shard_map/ppermute | solution.py:353
  14.7 5.5 %collective-permute-start.3 = (bf16[14,128,128]{2,1,0:T(8,128)(2,1)S(1)}, bf16[14,128,128]{2,1,0:T(8,128)(2,1)S(1)}, u32[]{:S(2)}, u32[]{:S(2)}) collective-permute-start(bf16[14,128,128]{2,1,0:T(8,128)(2,1)S(1)} %collective-permute-done.1.refs_3_.refs_6_), channel_id=1, source_target_pairs={{2,4},{3,1},{4,6},{5,3},{10,12},{11,9},{12,14},{13,11},{18,20},{19... | collective-permute-start | bytes 1376264 | tf_op jit(solution)/shard_map/ppermute | solution.py:353
  15.4 8.5 %collective-permute-start.6 = (bf16[14,128,128]{2,1,0:T(8,128)(2,1)S(1)}, bf16[14,128,128]{2,1,0:T(8,128)(2,1)S(1)}, u32[]{:S(2)}, u32[]{:S(2)}) collective-permute-start(bf16[14,128,128]{2,1,0:T(8,128)(2,1)S(1)} %slice_select_fusion), channel_id=1, source_target_pairs={{8,24},{17,25},{10,26},{19,27},{12,28},{21,29},{14,30},{23,31},{0,... | collective-permute-start | bytes 1376264 | tf_op jit(solution)/shard_map/ppermute | solution.py:366
  17.0 12.4 %collective-permute-start.5 = (bf16[28,128,128]{2,1,0:T(8,128)(2,1)S(1)}, bf16[28,128,128]{2,1,0:T(8,128)(2,1)S(1)}, u32[]{:S(2)}, u32[]{:S(2)}) collective-permute-start(bf16[28,128,128]{2,1,0:T(8,128)(2,1)S(1)} %collective-permute-done.refs_1_), channel_id=1, source_target_pairs={{0,1},{1,0},{2,3},{3,2},{4,5},{5,4},{6,7},{7,6},{8,9},{9,8},{10,11... | collective-permute-start | bytes 2752520 | tf_op jit(solution)/shard_map/ppermute | solution.py:362
  19.5 5.9 %collective-permute-start.4 = (bf16[14,128,128]{2,1,0:T(8,128)(2,1)S(1)}, bf16[14,128,128]{2,1,0:T(8,128)(2,1)S(1)}, u32[]{:S(2)}, u32[]{:S(2)}) collective-permute-start(bf16[14,128,128]{2,1,0:T(8,128)(2,1)S(1)} %collective-permute-done.2.refs_4_.refs_7_), channel_id=1, source_target_pairs={{2,4},{3,1},{4,6},{5,3},{10,12},{11,9},{12,14},{13,11},{18,20},{19... | collective-permute-start | bytes 1376264 | tf_op jit(solution)/shard_map/ppermute | solution.py:353
  20.2 9.2 %collective-permute-start.8 = (bf16[14,128,128]{2,1,0:T(8,128)(2,1)S(1)}, bf16[14,128,128]{2,1,0:T(8,128)(2,1)S(1)}, u32[]{:S(2)}, u32[]{:S(2)}) collective-permute-start(bf16[14,128,128]{2,1,0:T(8,128)(2,1)S(1)} %collective-permute-done.3.refs_5_.refs_8_), channel_id=1, source_target_pairs={{3,1},{4,6},{11,9},{12,14},{19,17},{20,22},{27,25},{28,30}} | collective-permute-start | bytes 1376264 | tf_op jit(solution)/shard_map/ppermute | solution.py:353
  24.0 5.5 %collective-permute-start.7 = (bf16[14,128,128]{2,1,0:T(8,128)(2,1)S(1)}, bf16[14,128,128]{2,1,0:T(8,128)(2,1)S(1)}, u32[]{:S(2)}, u32[]{:S(2)}) collective-permute-start(bf16[14,128,128]{2,1,0:T(8,128)(2,1)S(1)} %collective-permute-done.6.refs_3_), channel_id=1, source_target_pairs={{0,1},{1,0},{2,3},{3,2},{4,5},{5,4},{6,7},{7,6},{8,9},{9,8},{10,11... | collective-permute-start | bytes 1376264 | tf_op jit(solution)/shard_map/ppermute | solution.py:367
  25.4 5.1 %collective-permute-start.9 = (bf16[14,128,128]{2,1,0:T(8,128)(2,1)S(1)}, bf16[14,128,128]{2,1,0:T(8,128)(2,1)S(1)}, u32[]{:S(2)}, u32[]{:S(2)}) collective-permute-start(bf16[14,128,128]{2,1,0:T(8,128)(2,1)S(1)} %collective-permute-done.4.refs_6_.refs_9_), channel_id=1, source_target_pairs={{3,1},{4,6},{11,9},{12,14},{19,17},{20,22},{27,25},{28,30}} | collective-permute-start | bytes 1376264 | tf_op jit(solution)/shard_map/ppermute | solution.py:353
  31.2 12.0 %collective-permute-start.10 = (f32[14,128,128]{2,1,0:T(8,128)S(1)}, f32[14,128,128]{2,1,0:T(8,128)S(1)}, u32[]{:S(2)}, u32[]{:S(2)}) collective-permute-start(f32[14,128,128]{2,1,0:T(8,128)S(1)} %get-tuple-element.12), channel_id=1, source_target_pairs={{0,1},{1,0},{2,3},{3,2},{4,5},{5,4},{6,7},{7,6},{8,9},{9,8},{10,11... | collective-permute-start | bytes 2752520 | tf_op jit(solution)/shard_map/ppermute | solution.py:414

commit v5 on v4

--- a/solution.py
+++ b/solution.py
@@ -149,13 +149,13 @@
         pairs[pl.ds(stage, 1), :] = jnp.where(lane == LANES - 1, count, entry)
 
 
-def add_products(count, pairs, row, left, right, acc, low=0):
+def add_products(count, pairs, row, left, right, acc):
     def step(i, carry):
         codes = [pairs[row, i * GROUP + j] for j in range(GROUP)]
         products = [
             jnp.dot(
-                left[code // 4096],
-                right[jnp.maximum((code // 64) % 64 - low, 0)],
+                left(code // 4096),
+                right((code // 64) % 64),
                 preferred_element_type=jnp.float32,
             )
             for code in codes
@@ -167,22 +167,20 @@
     lax.fori_loop(0, (count + GROUP - 1) // GROUP, step, 0)
 
 
-def fetch(copies, buffer, sem):
-    at = 0
-    for j, ref in enumerate(copies):
-        pltpu.make_async_copy(
-            ref, buffer.at[pl.ds(at, ref.shape[0])], sem.at[j]
-        ).start()
-        at += ref.shape[0]
-
-
-def fetched(copies, buffer, sem):
-    at = 0
-    for j, ref in enumerate(copies):
-        pltpu.make_async_copy(
-            ref, buffer.at[pl.ds(at, ref.shape[0])], sem.at[j]
-        ).wait()
-        at += ref.shape[0]
+def blocks_of(parts):
+    if len(parts) == 1:
+        return lambda slot: parts[0][slot]
+    first, second = parts
+    size = first.shape[0]
+
+    def block(slot):
+        return lax.select(
+            slot < size,
+            first[jnp.minimum(slot, size - 1)],
+            second[jnp.maximum(slot - size, 0)],
+        )
+
+    return block
 
 
 class Lefts:
@@ -190,7 +188,7 @@
         near = plan.grid // 2 - 1
         self.far = plan.grid - 1
         self.own, self.near = refs[0], refs[1 : 1 + near]
-        self.late = late
+        self.swapped = self.halves = ()
         if late:
             self.swapped = refs[1 + near : 1 + 2 * near]
             self.halves = refs[1 + 2 * near : 3 + 2 * near]
@@ -201,113 +199,83 @@
         return 3 + 2 * near if late else 1 + near
 
     def direct(self, by, layer):
-        found = by == 0
-        for k in range(len(self.near)):
-            found |= by == 2 * k + 1 + layer
-        return found & (by != self.far)
-
-    def fetch(self, by, layer, buffer, sem):
-        @pl.when(by == 0)
-        def _():
-            pltpu.make_async_copy(self.own, buffer, sem).start()
-
-        for k in range(len(self.near)):
-
-            @pl.when(by == 2 * k + 1 + layer)
-            def _(k=k):
-                pltpu.make_async_copy(self.near[k], buffer, sem).start()
-
-            if self.late:
-
-                @pl.when(by == 2 * k + 2 - layer)
-                def _(k=k):
-                    pltpu.make_async_copy(self.swapped[k], buffer, sem).start()
-
-        if self.late:
-
-            @pl.when(by == self.far)
-            def _():
-                share = self.halves[0].shape[0]
-                for j, half in enumerate(self.halves):
-                    at = jnp.abs(layer - j) * share
-                    pltpu.make_async_copy(
-                        half, buffer.at[pl.ds(at, share)], sem
-                    ).start()
-
-    def fetched(self, buffer, sem):
-        pltpu.make_async_copy(self.own, buffer, sem).wait()
+        yield by == 0, blocks_of([self.own])
+        for k, tile in enumerate(self.near):
+            yield by == 2 * k + 1 + layer, blocks_of([tile])
+
+    def indirect(self, by, layer):
+        for k, tile in enumerate(self.swapped):
+            yield by == 2 * k + 2 - layer, blocks_of([tile])
+        mine, other = self.halves
+        share = mine.shape[0]
+
+        def block(slot):
+            second = (slot >= share).astype(jnp.int32)
+            slot = slot - second * share
+            return lax.select(second == layer, mine[slot], other[slot])
+
+        yield by == self.far, block
+
+
+def run_jobs(cases, count, pairs, row, right, acc):
+    for here, left in cases:
+
+        @pl.when(here & (count > 0))
+        def _(left=left):
+            add_products(count, pairs, row, left, right, acc)
 
 
 def stages_of(parts, refs):
     rights = []
-    for n in parts[:-1]:
+    for n in parts:
         rights.append(refs[:n])
         refs = refs[n:]
     return rights, refs
 
 
-def start_jobs(plan, lefts, rights, pairs, left, right, left_sem, right_sem, late):
-    a, b, layer = place()
-    counts = []
-    for stage in range(plan.stages):
-        l, _ = plan.taken(a, layer, stage)
-        by = b ^ l
-        here = lefts.direct(by, layer) != late
-        count = jnp.where(here, pairs[stage, pairs.shape[1] - 1], 0)
-        counts.append(count)
-
-        @pl.when(count > 0)
-        def _(stage=stage, by=by):
-            fetch(rights[stage], right.at[stage], right_sem.at[stage])
-            lefts.fetch(by, layer, left.at[stage], left_sem.at[stage])
-
-    return counts
-
-
-def finish_jobs(counts, lefts, rights, pairs, left, right, left_sem, right_sem, acc):
-    for stage, count in enumerate(counts):
-
-        @pl.when(count > 0)
-        def _(stage=stage, count=count):
-            lefts.fetched(left.at[stage], left_sem.at[stage])
-            fetched(rights[stage], right.at[stage], right_sem.at[stage])
-            add_products(count, pairs, stage, left.at[stage], right.at[stage], acc)
-
-
 def early_kernel(plan, parts, pairs, *refs):
     n = Lefts.number(plan, False)
     lefts = Lefts(plan, refs[:n], False)
-    rights, refs = stages_of(parts, refs[n:])
-    acc, *buffers = refs
-    counts = start_jobs(plan, lefts, rights, pairs, *buffers, False)
+    rights, (acc,) = stages_of(parts[:-1], refs[n:])
+    a, b, layer = place()
     acc[...] = jnp.zeros_like(acc)
-    finish_jobs(counts, lefts, rights, pairs, *buffers, acc)
+    for stage, right in enumerate(rights):
+        by = b ^ plan.taken(a, layer, stage)[0]
+        count = pairs[stage, pairs.shape[1] - 1]
+        cases = lefts.direct(by, layer)
+        run_jobs(cases, count, pairs, stage, blocks_of(right), acc)
 
 
 def middle_kernel(plan, parts, pairs, total, *refs):
     del total
     n = Lefts.number(plan, True)
     lefts = Lefts(plan, refs[:n], True)
-    rights, refs = stages_of(parts, refs[n:])
-    first, acc, left_last, *buffers, last_sem = refs
-    end = plan.stages
+    rights, (first, acc) = stages_of(parts[:-1], refs[n:])
     a, b, layer = place()
-    l, _ = plan.taken(a, layer, end)
-    counts = start_jobs(plan, lefts, rights, pairs, *buffers, True)
-    lefts.fetch(b ^ l, layer, left_last, last_sem)
-    finish_jobs(counts, lefts, rights, pairs, *buffers, acc)
-    lefts.fetched(left_last, last_sem)
-    add_products(pairs[end, pairs.shape[1] - 1], pairs, end, left_last, first, acc)
-
-
-def last_kernel(plan, bounds, pairs, total, left_last, *refs):
+    last = pairs.shape[1] - 1
+    for stage, right in enumerate([*rights, [first]]):
+        by = b ^ plan.taken(a, layer, stage)[0]
+        cases = list(lefts.indirect(by, layer))
+        if stage == plan.stages:
+            cases += lefts.direct(by, layer)
+        run_jobs(cases, pairs[stage, last], pairs, stage, blocks_of(right), acc)
+
+
+def last_kernel(plan, bounds, pairs, total, *refs):
     del total
-    refs, (acc, mine, other) = refs[:-3], refs[-3:]
-    last = pairs.shape[1] - 1
+    n = Lefts.number(plan, True)
+    lefts = Lefts(plan, refs[:n], True)
+    refs, (acc, mine, other) = refs[n:-3], refs[-3:]
+    a, b, layer = place()
+    by = b ^ plan.taken(a, layer, plan.stages)[0]
     for j, part in enumerate(refs):
-        row = plan.stages + 1 + j
-        add_products(pairs[row, last], pairs, row, left_last, part, acc, bounds[1 + j])
-    layer = lax.axis_index("layer")
+        row, low = plan.stages + 1 + j, bounds[1 + j]
+        cases = [*lefts.direct(by, layer), *lefts.indirect(by, layer)]
+
+        def right(slot, part=part, low=low):
+            return part[jnp.maximum(slot - low, 0)]
+
+        run_jobs(cases, pairs[row, pairs.shape[1] - 1], pairs, row, right, acc)
     share = mine.shape[0]
     mine[...] = acc[pl.ds(layer * share, share)]
     other[...] = acc[pl.ds((1 - layer) * share, share)]
@@ -322,7 +290,6 @@
         (lax.optimization_barrier(own) if i else own)[i:j]
         for i, j in zip(bounds[:-1], bounds[1:])
     ]
-    anywhere = pl.BlockSpec(memory_space=pl.ANY)
     scalars = pl.BlockSpec(memory_space=pltpu.SMEM)
     vmem = pl.BlockSpec(memory_space=pltpu.VMEM)
     compiler_params = pltpu.CompilerParams(vmem_limit_bytes=GRANT)
@@ -370,32 +337,22 @@
     parts = [len(r) for r in rights]
     running = jax.ShapeDtypeStruct((slots + 1, size, size), jnp.float32)
     before = [part for stage in rights[:-1] for part in stage]
-    buffers = [
-        pltpu.VMEM((plan.stages, *own.shape), own.dtype),
-        pltpu.VMEM((plan.stages, *own.shape), own.dtype),
-        pltpu.SemaphoreType.DMA((plan.stages,)),
-        pltpu.SemaphoreType.DMA((plan.stages, CHUNKS)),
-    ]
     total = pl.pallas_call(
         functools.partial(early_kernel, plan, parts),
         out_shape=running,
-        in_specs=[scalars] + [anywhere] * (len(direct) + len(before)),
+        in_specs=[scalars] + [vmem] * (len(direct) + len(before)),
         out_specs=vmem,
-        scratch_shapes=buffers,
         compiler_params=compiler_params,
         cost_estimate=cost(slots * plan.stages, 2 * plan.stages),
         name="early_products",
     )(lists, *direct, *before)
     first, *rest = rights[-1]
-    total, left_last = pl.pallas_call(
+    total = pl.pallas_call(
         functools.partial(middle_kernel, plan, parts),
-        out_shape=(running, jax.ShapeDtypeStruct(own.shape, own.dtype)),
-        in_specs=[scalars, vmem]
-        + [anywhere] * (len(lefts) + len(before))
-        + [vmem],
-        out_specs=(vmem, vmem),
+        out_shape=running,
+        in_specs=[scalars] + [vmem] * (2 + len(lefts) + len(before)),
+        out_specs=vmem,
         input_output_aliases={1: 0},
-        scratch_shapes=buffers + [pltpu.SemaphoreType.DMA],
         compiler_params=compiler_params,
         cost_estimate=cost(slots * plan.stages, 2 * plan.stages),
         name="middle_products",
@@ -404,13 +361,13 @@
     _, mine, other = pl.pallas_call(
         functools.partial(last_kernel, plan, bounds),
         out_shape=(running, half, half),
-        in_specs=[scalars] + [vmem] * (2 + len(rest)),
+        in_specs=[scalars] + [vmem] * (1 + len(lefts) + len(rest)),
         out_specs=(vmem, vmem, vmem),
         input_output_aliases={1: 0},
         compiler_params=compiler_params,
         cost_estimate=cost(slots // 2, 4),
         name="last_products",
-    )(lists, total, left_last, *rest)
+    )(lists, total, *lefts, *rest)
     received = lax.ppermute(other, "layer", swap)
     return (mine + received).astype(jnp.bfloat16)[None, None]
 

time: 44.9 us -> 44.7 us (level)
  starting transfers between devices: 25.6 us -> 26.5 us
  Pallas kernels: 5.03 us -> 4.18 us
    ppermute x1, starting transfers between devices: 9.88 us -> 10.8 us  [on_device(): received = lax.ppermute(other, 'layer', swap)]
    pallas_call x1, Pallas kernels: 2.32 us -> 1.76 us  [on_device(): pl.pallas_call(functools.partial(early_kernel, plan, parts), out_shape=ru...]
  transfers between devices with their start and end apart: 11 -> 11, of which waited for: 4 -> 4; matrix products, arithmetic and copies ran while one was open for 7% -> 7% of each run, Pallas kernels for 10% -> 8%
where the time goes in v5:
time: 44.7 us; the launch traced here: 44.2 us
  starting transfers between devices  26.5 us (59%)
  waiting for transfers between devices  9.39 us (21%)
  Pallas kernels  4.18 us (9%)
  local copies, waits for them, and re-layouts  2.92 us (7%)
  other arithmetic  0.96 us (2%)
    ppermute x1, starting transfers between devices, on_device(): received = lax.ppermute(other, 'layer', swap)  10.8 us
    ppermute x6, starting transfers between devices, on_device(): arrived.append(lax.ppermute(part, ('col', 'layer'), pairs))  9.71 us
    ppermute x6, waiting for transfers between devices, on_device(): arrived.append(lax.ppermute(part, ('col', 'layer'), pairs))  4.19 us
    ppermute x1, waiting for transfers between devices, on_device(): far = lax.ppermute(sent, everywhere, plan.far_pairs())  3.09 us
    ppermute x1, starting transfers between devices, on_device(): near.append(lax.ppermute(own, everywhere, plan.near_pairs(bys)))  3.03 us
    slice x2, local copies, waits for them, and re-layouts, on_device(): (lax.optimization_barrier(own) if i else own)[i:j]  2.91 us
    ppermute x1, waiting for transfers between devices, on_device(): received = lax.ppermute(other, 'layer', swap)  2.1 us
    pallas_call x1, Pallas kernels, on_device(): pl.pallas_call(functools.partial(early_kernel, plan, parts), out_shape=ru...  1.76 us
  transfers between devices with their start and end apart: 11, of which 4 were waited for; matrix products, arithmetic and copies ran while one was open for 7% of the time, Pallas kernels for 8%

profile of v5, /device:TPU:0, one launch (start us, length us, event | category | flops | bytes accessed | tf_op | source)
XLA Modules:
  0.0 44.2 jit_solution(7315913148008261497)
XLA Ops:
  0.0 3.0 %collective-permute-start = (bf16[28,128,128]{2,1,0:T(8,128)(2,1)}, bf16[28,128,128]{2,1,0:T(8,128)(2,1)S(1)}, u32[]{:S(2)}, u32[]{:S(2)}) collective-permute-start(bf16[28,128,128]{2,1,0:T(8,128)(2,1)} %bitcast.5), channel_id=1, source_target_pairs={{0,8},{1,17},{2,10},{3,19},{4,12},{5,21},{6,14},{7,23},{8,0},{9,25... | collective-permute-start | bytes 2752520 | tf_op jit(solution)/shard_map/ppermute | solution.py:328
  3.0 1.9 %slice_bitcast_fusion = bf16[14,128,128]{2,1,0:T(8,128)(2,1)} fusion(bf16[1,1,28,128,128]{4,3,2,1,0:T(8,128)(2,1)} %param.3), kind=kLoop, calls=%fused_computation.3 | loop fusion | bytes 917504 | tf_op jit(solution)/shard_map/slice | solution.py:290
  4.9 3.5 %collective-permute-start.1 = (bf16[14,128,128]{2,1,0:T(8,128)(2,1)}, bf16[14,128,128]{2,1,0:T(8,128)(2,1)S(1)}, u32[]{:S(2)}, u32[]{:S(2)}) collective-permute-start(bf16[14,128,128]{2,1,0:T(8,128)(2,1)} %slice_bitcast_fusion), channel_id=1, source_target_pairs={{0,2},{2,4},{3,1},{4,6},{5,3},{7,5},{8,10},{10,12},{11,9},{12,14},... | collective-permute-start | bytes 1376264 | tf_op jit(solution)/shard_map/ppermute | solution.py:320
  8.4 1.1 %slice.20 = bf16[14,128,128]{2,1,0:T(8,128)(2,1)S(1)} slice(bf16[28,128,128]{2,1,0:T(8,128)(2,1)} %bitcast.6), slice={[14:28], [0:128], [0:128]} | slice | bytes 917504 | tf_op jit(solution)/shard_map/slice | solution.py:290
  9.5 3.5 %collective-permute-start.2 = (bf16[14,128,128]{2,1,0:T(8,128)(2,1)S(1)}, bf16[14,128,128]{2,1,0:T(8,128)(2,1)S(1)}, u32[]{:S(2)}, u32[]{:S(2)}) collective-permute-start(bf16[14,128,128]{2,1,0:T(8,128)(2,1)S(1)} %slice.20), channel_id=1, source_target_pairs={{0,2},{2,4},{3,1},{4,6},{5,3},{7,5},{8,10},{10,12},{11,9},{12,14},... | collective-permute-start | bytes 1376264 | tf_op jit(solution)/shard_map/ppermute | solution.py:320
  13.0 1.7 %collective-permute-done.1.refs_3_.refs_6_ = bf16[14,128,128]{2,1,0:T(8,128)(2,1)S(1)} collective-permute-done((bf16[14,128,128]{2,1,0:T(8,128)(2,1)}, bf16[14,128,128]{2,1,0:T(8,128)(2,1)S(1)}, u32[]{:S(2)}, u32[]{:S(2)}) %collective-permute-start.1) | collective-permute-done | bytes 458784 | tf_op jit(solution)/shard_map/ppermute | solution.py:320
  14.7 0.7 %collective-permute-start.3 = (bf16[14,128,128]{2,1,0:T(8,128)(2,1)S(1)}, bf16[14,128,128]{2,1,0:T(8,128)(2,1)S(1)}, u32[]{:S(2)}, u32[]{:S(2)}) collective-permute-start(bf16[14,128,128]{2,1,0:T(8,128)(2,1)S(1)} %collective-permute-done.1.refs_3_.refs_6_), channel_id=1, source_target_pairs={{2,4},{3,1},{4,6},{5,3},{10,12},{11,9},{12,14},{13,11},{18,20},{19... | collective-permute-start | bytes 1376264 | tf_op jit(solution)/shard_map/ppermute | solution.py:320
  15.4 0.0 collective-permute-done.refs_1_
  15.4 0.1 slice_select_fusion
  15.4 1.6 %collective-permute-start.6 = (bf16[14,128,128]{2,1,0:T(8,128)(2,1)S(1)}, bf16[14,128,128]{2,1,0:T(8,128)(2,1)S(1)}, u32[]{:S(2)}, u32[]{:S(2)}) collective-permute-start(bf16[14,128,128]{2,1,0:T(8,128)(2,1)S(1)} %slice_select_fusion), channel_id=1, source_target_pairs={{8,24},{17,25},{10,26},{19,27},{12,28},{21,29},{14,30},{23,31},{0,... | collective-permute-start | bytes 1376264 | tf_op jit(solution)/shard_map/ppermute | solution.py:333
  17.0 0.0 collective-permute-start.5
  17.0 2.5 %collective-permute-done.2.refs_4_.refs_7_ = bf16[14,128,128]{2,1,0:T(8,128)(2,1)S(1)} collective-permute-done((bf16[14,128,128]{2,1,0:T(8,128)(2,1)S(1)}, bf16[14,128,128]{2,1,0:T(8,128)(2,1)S(1)}, u32[]{:S(2)}, u32[]{:S(2)}) %collective-permute-start.2) | collective-permute-done | bytes 458784 | tf_op jit(solution)/shard_map/ppermute | solution.py:320
  19.5 0.7 %collective-permute-start.4 = (bf16[14,128,128]{2,1,0:T(8,128)(2,1)S(1)}, bf16[14,128,128]{2,1,0:T(8,128)(2,1)S(1)}, u32[]{:S(2)}, u32[]{:S(2)}) collective-permute-start(bf16[14,128,128]{2,1,0:T(8,128)(2,1)S(1)} %collective-permute-done.2.refs_4_.refs_7_), channel_id=1, source_target_pairs={{2,4},{3,1},{4,6},{5,3},{10,12},{11,9},{12,14},{13,11},{18,20},{19... | collective-permute-start | bytes 1376264 | tf_op jit(solution)/shard_map/ppermute | solution.py:320
  20.2 0.0 collective-permute-done.3.refs_5_.refs_8_
  20.2 0.7 %collective-permute-start.8 = (bf16[14,128,128]{2,1,0:T(8,128)(2,1)S(1)}, bf16[14,128,128]{2,1,0:T(8,128)(2,1)S(1)}, u32[]{:S(2)}, u32[]{:S(2)}) collective-permute-start(bf16[14,128,128]{2,1,0:T(8,128)(2,1)S(1)} %collective-permute-done.3.refs_5_.refs_8_), channel_id=1, source_target_pairs={{3,1},{4,6},{11,9},{12,14},{19,17},{20,22},{27,25},{28,30}} | collective-permute-start | bytes 1376264 | tf_op jit(solution)/shard_map/ppermute | solution.py:320
  20.9 3.1 %collective-permute-done.6.refs_3_ = bf16[14,128,128]{2,1,0:T(8,128)(2,1)S(1)} collective-permute-done((bf16[14,128,128]{2,1,0:T(8,128)(2,1)S(1)}, bf16[14,128,128]{2,1,0:T(8,128)(2,1)S(1)}, u32[]{:S(2)}, u32[]{:S(2)}) %collective-permute-start.6) | collective-permute-done | bytes 458784 | tf_op jit(solution)/shard_map/ppermute | solution.py:333
  24.0 1.4 %collective-permute-start.7 = (bf16[14,128,128]{2,1,0:T(8,128)(2,1)S(1)}, bf16[14,128,128]{2,1,0:T(8,128)(2,1)S(1)}, u32[]{:S(2)}, u32[]{:S(2)}) collective-permute-start(bf16[14,128,128]{2,1,0:T(8,128)(2,1)S(1)} %collective-permute-done.6.refs_3_), channel_id=1, source_target_pairs={{0,1},{1,0},{2,3},{3,2},{4,5},{5,4},{6,7},{7,6},{8,9},{9,8},{10,11... | collective-permute-start | bytes 1376264 | tf_op jit(solution)/shard_map/ppermute | solution.py:334
  25.4 0.0 collective-permute-done.4.refs_6_.refs_9_
  25.4 0.7 %collective-permute-start.9 = (bf16[14,128,128]{2,1,0:T(8,128)(2,1)S(1)}, bf16[14,128,128]{2,1,0:T(8,128)(2,1)S(1)}, u32[]{:S(2)}, u32[]{:S(2)}) collective-permute-start(bf16[14,128,128]{2,1,0:T(8,128)(2,1)S(1)} %collective-permute-done.4.refs_6_.refs_9_), channel_id=1, source_target_pairs={{3,1},{4,6},{11,9},{12,14},{19,17},{20,22},{27,25},{28,30}} | collective-permute-start | bytes 1376264 | tf_op jit(solution)/shard_map/ppermute | solution.py:320
  26.1 0.0 copy-done.1
  26.1 0.0 copy-done.2
  26.1 1.0 %list_products.1.pairs = s32[5,128]{1,0:T(8,128)S(1)} custom-call(s32[4,4,28]{2,1,0:T(4,128)S(1)} %convert_add_fusion.slot_keys), custom_call_target="tpu_custom_call" | custom-call | bytes 1835008 | tf_op jit(solution)/shard_map/list_products/pallas_call | solution.py:305
  27.1 1.8 %early_products.1.total = f32[29,128,128]{2,1,0:T(8,128)S(1)} custom-call(s32[5,128]{1,0:T(8,128)S(1)} %list_products.1.pairs, bf16[28,128,128]{2,1,0:T(8,128)(2,1)S(1)} %bitcast.7, bf16[28,128,128]{2,1,0:T(8,128)(2,1)S(1)} %collective-permute-done.refs_1_, bf16[28,128,128]{2,1,0:T(8,128)(2,1)S(1)} %bitcast.8, ...), custom_call_target="tpu_custom_call" | custom-call | flops 352321536 | bytes 5505024 | tf_op jit(solution)/shard_map/early_products/pallas_call | solution.py:340
  28.8 0.0 collective-permute-done.8.refs_10_
  28.9 0.0 collective-permute-done.7.refs_4_
  28.9 0.0 collective-permute-done.5.refs_2_
  28.9 0.7 %middle_products.1.total = f32[29,128,128]{2,1,0:T(8,128)S(1)} custom-call(s32[5,128]{1,0:T(8,128)S(1)} %list_products.1.pairs, f32[29,128,128]{2,1,0:T(8,128)S(1)} %early_products.1.total, bf16[28,128,128]{2,1,0:T(8,128)(2,1)S(1)} %bitcast.9, bf16[28,128,128]{2,1,0:T(8,128)(2,1)S(1)} %collective-permute-done.refs_1_, ...), custom_call_target="tpu_custom_call", output_to_operand_aliasing={{}: (1, {})} | custom-call | flops 352321536 | bytes 5505024 | tf_op jit(solution)/shard_map/middle_products/pallas_call | solution.py:350
  29.6 0.0 collective-permute-done.9.refs_5_
  29.6 0.8 %last_products.1 = (f32[29,128,128]{2,1,0:T(8,128)S(1)}, f32[14,128,128]{2,1,0:T(8,128)S(1)}, f32[14,128,128]{2,1,0:T(8,128)S(1)}) custom-call(s32[5,128]{1,0:T(8,128)S(1)} %list_products.1.pairs, f32[29,128,128]{2,1,0:T(8,128)S(1)} %middle_products.1.total, bf16[28,128,128]{2,1,0:T(8,128)(2,1)S(1)} %bitcast.11, ...), custom_call_target="tpu_custom_call", output_to_operand_aliasing={{0}: (1, {})} | custom-call | flops 58720256 | bytes 3670016 | tf_op jit(solution)/shard_map/last_products/pallas_call | solution.py:361
  30.4 10.8 %collective-permute-start.10 = (f32[14,128,128]{2,1,0:T(8,128)S(1)}, f32[14,128,128]{2,1,0:T(8,128)S(1)}, u32[]{:S(2)}, u32[]{:S(2)}) collective-permute-start(f32[14,128,128]{2,1,0:T(8,128)S(1)} %get-tuple-element.8), channel_id=1, source_target_pairs={{0,1},{1,0},{2,3},{3,2},{4,5},{5,4},{6,7},{7,6},{8,9},{9,8},{10,11... | collective-permute-start | bytes 2752520 | tf_op jit(solution)/shard_map/ppermute | solution.py:371
  41.2 2.1 %collective-permute-done.10 = f32[14,128,128]{2,1,0:T(8,128)S(1)} collective-permute-done((f32[14,128,128]{2,1,0:T(8,128)S(1)}, f32[14,128,128]{2,1,0:T(8,128)S(1)}, u32[]{:S(2)}, u32[]{:S(2)}) %collective-permute-start.10) | collective-permute-done | bytes 917536 | tf_op jit(solution)/shard_map/ppermute | solution.py:371
  43.3 0.9 %fusion = bf16[1,1,14,128,128]{4,3,2,1,0:T(8,128)(2,1)} fusion(f32[14,128,128]{2,1,0:T(8,128)S(1)} %get-tuple-element.7, f32[14,128,128]{2,1,0:T(8,128)S(1)} %collective-permute-done.10), kind=kLoop, calls=%fused_computation.1 | loop fusion | flops 458752 | bytes 2293760 | tf_op jit(solution)/shard_map/broadcast_in_dim | solution.py:372
  (5 shorter events, 0.0 us)
Async XLA Ops:
  0.0 27.1 %copy-start = (bf16[1,1,28,128,128]{4,3,2,1,0:T(8,128)(2,1)S(1)}, bf16[1,1,28,128,128]{4,3,2,1,0:T(8,128)(2,1)}, u32[]{:S(2)}) copy-start(bf16[1,1,28,128,128]{4,3,2,1,0:T(8,128)(2,1)} %param.3) | copy-start | bytes 2752516
  0.0 26.1 %copy-start.1 = (s32[4,4,28]{2,1,0:T(4,128)S(1)}, s32[4,4,28]{2,1,0:T(4,128)}, u32[]{:S(2)}) copy-start(s32[4,4,28]{2,1,0:T(4,128)} %param.4) | copy-start | bytes 5380
  0.0 26.1 %copy-start.2 = (s32[4,4,28]{2,1,0:T(4,128)S(1)}, s32[4,4,28]{2,1,0:T(4,128)}, u32[]{:S(2)}) copy-start(s32[4,4,28]{2,1,0:T(4,128)} %param.5) | copy-start | bytes 5380
  0.0 15.3 %collective-permute-start = (bf16[28,128,128]{2,1,0:T(8,128)(2,1)}, bf16[28,128,128]{2,1,0:T(8,128)(2,1)S(1)}, u32[]{:S(2)}, u32[]{:S(2)}) collective-permute-start(bf16[28,128,128]{2,1,0:T(8,128)(2,1)} %bitcast.5), channel_id=1, source_target_pairs={{0,8},{1,17},{2,10},{3,19},{4,12},{5,21},{6,14},{7,23},{8,0},{9,25... | collective-permute-start | bytes 2752520 | tf_op jit(solution)/shard_map/ppermute | solution.py:328
  4.9 9.8 %collective-permute-start.1 = (bf16[14,128,128]{2,1,0:T(8,128)(2,1)}, bf16[14,128,128]{2,1,0:T(8,128)(2,1)S(1)}, u32[]{:S(2)}, u32[]{:S(2)}) collective-permute-start(bf16[14,128,128]{2,1,0:T(8,128)(2,1)} %slice_bitcast_fusion), channel_id=1, source_target_pairs={{0,2},{2,4},{3,1},{4,6},{5,3},{7,5},{8,10},{10,12},{11,9},{12,14},... | collective-permute-start | bytes 1376264 | tf_op jit(solution)/shard_map/ppermute | solution.py:320
  9.5 10.0 %collective-permute-start.2 = (bf16[14,128,128]{2,1,0:T(8,128)(2,1)S(1)}, bf16[14,128,128]{2,1,0:T(8,128)(2,1)S(1)}, u32[]{:S(2)}, u32[]{:S(2)}) collective-permute-start(bf16[14,128,128]{2,1,0:T(8,128)(2,1)S(1)} %slice.20), channel_id=1, source_target_pairs={{0,2},{2,4},{3,1},{4,6},{5,3},{7,5},{8,10},{10,12},{11,9},{12,14},... | collective-permute-start | bytes 1376264 | tf_op jit(solution)/shard_map/ppermute | solution.py:320
  14.7 5.5 %collective-permute-start.3 = (bf16[14,128,128]{2,1,0:T(8,128)(2,1)S(1)}, bf16[14,128,128]{2,1,0:T(8,128)(2,1)S(1)}, u32[]{:S(2)}, u32[]{:S(2)}) collective-permute-start(bf16[14,128,128]{2,1,0:T(8,128)(2,1)S(1)} %collective-permute-done.1.refs_3_.refs_6_), channel_id=1, source_target_pairs={{2,4},{3,1},{4,6},{5,3},{10,12},{11,9},{12,14},{13,11},{18,20},{19... | collective-permute-start | bytes 1376264 | tf_op jit(solution)/shard_map/ppermute | solution.py:320
  15.4 8.5 %collective-permute-start.6 = (bf16[14,128,128]{2,1,0:T(8,128)(2,1)S(1)}, bf16[14,128,128]{2,1,0:T(8,128)(2,1)S(1)}, u32[]{:S(2)}, u32[]{:S(2)}) collective-permute-start(bf16[14,128,128]{2,1,0:T(8,128)(2,1)S(1)} %slice_select_fusion), channel_id=1, source_target_pairs={{8,24},{17,25},{10,26},{19,27},{12,28},{21,29},{14,30},{23,31},{0,... | collective-permute-start | bytes 1376264 | tf_op jit(solution)/shard_map/ppermute | solution.py:333
  17.0 11.9 %collective-permute-start.5 = (bf16[28,128,128]{2,1,0:T(8,128)(2,1)S(1)}, bf16[28,128,128]{2,1,0:T(8,128)(2,1)S(1)}, u32[]{:S(2)}, u32[]{:S(2)}) collective-permute-start(bf16[28,128,128]{2,1,0:T(8,128)(2,1)S(1)} %collective-permute-done.refs_1_), channel_id=1, source_target_pairs={{0,1},{1,0},{2,3},{3,2},{4,5},{5,4},{6,7},{7,6},{8,9},{9,8},{10,11... | collective-permute-start | bytes 2752520 | tf_op jit(solution)/shard_map/ppermute | solution.py:329
  19.5 5.9 %collective-permute-start.4 = (bf16[14,128,128]{2,1,0:T(8,128)(2,1)S(1)}, bf16[14,128,128]{2,1,0:T(8,128)(2,1)S(1)}, u32[]{:S(2)}, u32[]{:S(2)}) collective-permute-start(bf16[14,128,128]{2,1,0:T(8,128)(2,1)S(1)} %collective-permute-done.2.refs_4_.refs_7_), channel_id=1, source_target_pairs={{2,4},{3,1},{4,6},{5,3},{10,12},{11,9},{12,14},{13,11},{18,20},{19... | collective-permute-start | bytes 1376264 | tf_op jit(solution)/shard_map/ppermute | solution.py:320
  20.2 8.7 %collective-permute-start.8 = (bf16[14,128,128]{2,1,0:T(8,128)(2,1)S(1)}, bf16[14,128,128]{2,1,0:T(8,128)(2,1)S(1)}, u32[]{:S(2)}, u32[]{:S(2)}) collective-permute-start(bf16[14,128,128]{2,1,0:T(8,128)(2,1)S(1)} %collective-permute-done.3.refs_5_.refs_8_), channel_id=1, source_target_pairs={{3,1},{4,6},{11,9},{12,14},{19,17},{20,22},{27,25},{28,30}} | collective-permute-start | bytes 1376264 | tf_op jit(solution)/shard_map/ppermute | solution.py:320
  24.0 4.9 %collective-permute-start.7 = (bf16[14,128,128]{2,1,0:T(8,128)(2,1)S(1)}, bf16[14,128,128]{2,1,0:T(8,128)(2,1)S(1)}, u32[]{:S(2)}, u32[]{:S(2)}) collective-permute-start(bf16[14,128,128]{2,1,0:T(8,128)(2,1)S(1)} %collective-permute-done.6.refs_3_), channel_id=1, source_target_pairs={{0,1},{1,0},{2,3},{3,2},{4,5},{5,4},{6,7},{7,6},{8,9},{9,8},{10,11... | collective-permute-start | bytes 1376264 | tf_op jit(solution)/shard_map/ppermute | solution.py:334
  25.4 4.2 %collective-permute-start.9 = (bf16[14,128,128]{2,1,0:T(8,128)(2,1)S(1)}, bf16[14,128,128]{2,1,0:T(8,128)(2,1)S(1)}, u32[]{:S(2)}, u32[]{:S(2)}) collective-permute-start(bf16[14,128,128]{2,1,0:T(8,128)(2,1)S(1)} %collective-permute-done.4.refs_6_.refs_9_), channel_id=1, source_target_pairs={{3,1},{4,6},{11,9},{12,14},{19,17},{20,22},{27,25},{28,30}} | collective-permute-start | bytes 1376264 | tf_op jit(solution)/shard_map/ppermute | solution.py:320
  30.4 12.9 %collective-permute-start.10 = (f32[14,128,128]{2,1,0:T(8,128)S(1)}, f32[14,128,128]{2,1,0:T(8,128)S(1)}, u32[]{:S(2)}, u32[]{:S(2)}) collective-permute-start(f32[14,128,128]{2,1,0:T(8,128)S(1)} %get-tuple-element.8), channel_id=1, source_target_pairs={{0,1},{1,0},{2,3},{3,2},{4,5},{5,4},{6,7},{7,6},{8,9},{9,8},{10,11... | collective-permute-start | bytes 2752520 | tf_op jit(solution)/shard_map/ppermute | solution.py:371

commit v6 on v5

--- a/solution.py
+++ b/solution.py
@@ -81,23 +81,29 @@
         return jnp.where(l >= self.grid, l - self.grid, l), valid
 
 
+def late_core(plan, a):
+    l, valid = plan.taken(a, jnp.int32(0), plan.stages)
+    other_l, other_valid = plan.taken(a, jnp.int32(1), plan.stages)
+    late = jnp.where(valid, 0, 1)
+    return late, jnp.where(valid, l, other_l), valid | other_valid
+
+
 def place():
     return tuple(lax.axis_index(n) for n in ("col", "row", "layer"))
 
 
 def list_kernel(plan, bounds, slot_keys, pairs, keys, codes):
     slots = slot_keys.shape[2]
-    stages = plan.stages + 1
+    stages = plan.stages + 2
     a, b, layer = place()
     lane = lax.broadcasted_iota(jnp.int32, (1, LANES), 1)
     down = lax.broadcasted_iota(jnp.int32, (LANES, LANES), 0)
     across = lax.broadcasted_iota(jnp.int32, (LANES, LANES), 1)
 
     keys[...] = jnp.full_like(keys, -1)
-    taken = []
-    for stage in range(stages):
-        l, valid = plan.taken(a, layer, stage)
-        taken.append(valid)
+    jobs = [plan.taken(a, layer, stage) for stage in range(stages - 1)]
+    jobs.append(late_core(plan, a)[1:])
+    for stage, (l, valid) in enumerate(jobs):
         l = jnp.clip(l, 0, plan.grid - 1)
         keys[pl.ds(stage, 1), 0:slots] = slot_keys[a, pl.ds(l, 1), :]
         keys[pl.ds(stages + stage, 1), 0:slots] = slot_keys[l, pl.ds(b, 1), :]
@@ -120,16 +126,17 @@
         return jnp.sum(jnp.where(hit, down + 1, 0), axis=0, keepdims=True)
 
     codes[...] = jnp.zeros_like(codes)
-    for stage in range(stages):
+    share = slots // 2
+    for stage, (_, valid) in enumerate(jobs):
         left, right = find(stage, left_key), find(stages + stage, right_key)
-        good = (left > 0) & (right > 0) & taken[stage]
-        code = jnp.where(good, ((left - 1) * 64 + (right - 1)) * 64 + slot + 1, 0)
-        if stage < plan.stages:
-            codes[pl.ds(stage, 1), :] = code
-        else:
-            for j, (low, high) in enumerate(zip(bounds[:-1], bounds[1:])):
-                here = (right > low) & (right <= high)
-                codes[pl.ds(stage + j, 1), :] = jnp.where(here, code, 0)
+        good = (left > 0) & (right > 0) & valid
+        if stage == plan.stages:
+            good = good & (right <= bounds[1])
+        if stage > plan.stages:
+            low = layer * share
+            good = good & (right > bounds[1]) & (slot >= low) & (slot < low + share)
+        code = ((left - 1) * 64 + (right - 1)) * 64 + slot + 1
+        codes[pl.ds(stage, 1), :] = jnp.where(good, code, 0)
     found = codes[...] > 0
     ahead = jnp.dot(
         found.astype(jnp.float32),
@@ -149,7 +156,7 @@
         pairs[pl.ds(stage, 1), :] = jnp.where(lane == LANES - 1, count, entry)
 
 
-def add_products(count, pairs, row, left, right, acc):
+def add_products(count, pairs, row, left, right, acc, at):
     def step(i, carry):
         codes = [pairs[row, i * GROUP + j] for j in range(GROUP)]
         products = [
@@ -161,7 +168,7 @@
             for code in codes
         ]
         for code, product in zip(codes, products):
-            acc[code % 64] += product
+            acc[at(code % 64)] += product
         return carry
 
     lax.fori_loop(0, (count + GROUP - 1) // GROUP, step, 0)
@@ -217,12 +224,12 @@
         yield by == self.far, block
 
 
-def run_jobs(cases, count, pairs, row, right, acc):
+def run_jobs(cases, count, pairs, row, right, acc, at=lambda slot: slot):
     for here, left in cases:
 
         @pl.when(here & (count > 0))
         def _(left=left):
-            add_products(count, pairs, row, left, right, acc)
+            add_products(count, pairs, row, left, right, acc, at)
 
 
 def stages_of(parts, refs):
@@ -250,7 +257,7 @@
     del total
     n = Lefts.number(plan, True)
     lefts = Lefts(plan, refs[:n], True)
-    rights, (first, acc) = stages_of(parts[:-1], refs[n:])
+    rights, (first, acc, mine, other) = stages_of(parts[:-1], refs[n:])
     a, b, layer = place()
     last = pairs.shape[1] - 1
     for stage, right in enumerate([*rights, [first]]):
@@ -259,26 +266,45 @@
         if stage == plan.stages:
             cases += lefts.direct(by, layer)
         run_jobs(cases, pairs[stage, last], pairs, stage, blocks_of(right), acc)
-
-
-def last_kernel(plan, bounds, pairs, total, *refs):
-    del total
+    share = other.shape[0]
+    mine[...] = acc[pl.ds(layer * share, share)]
+    other[...] = acc[pl.ds((1 - layer) * share, share)]
+
+
+def last_kernel(plan, low, pairs, mine, received, *refs):
     n = Lefts.number(plan, True)
     lefts = Lefts(plan, refs[:n], True)
-    refs, (acc, mine, other) = refs[n:-3], refs[-3:]
+    part, part_swapped, out, acc, rounded, sem = refs[n:]
     a, b, layer = place()
-    by = b ^ plan.taken(a, layer, plan.stages)[0]
-    for j, part in enumerate(refs):
-        row, low = plan.stages + 1 + j, bounds[1 + j]
-        cases = [*lefts.direct(by, layer), *lefts.indirect(by, layer)]
-
-        def right(slot, part=part, low=low):
-            return part[jnp.maximum(slot - low, 0)]
-
-        run_jobs(cases, pairs[row, pairs.shape[1] - 1], pairs, row, right, acc)
-    share = mine.shape[0]
-    mine[...] = acc[pl.ds(layer * share, share)]
-    other[...] = acc[pl.ds((1 - layer) * share, share)]
+    share = out.shape[0]
+    acc[pl.ds(0, share)] = mine[...] + received[...]
+    late, l, _ = late_core(plan, a)
+    by = b ^ l
+    row = plan.stages + 1
+    cases = [*lefts.direct(by, layer), *lefts.indirect(by, layer)]
+
+    def right(slot):
+        slot = jnp.maximum(slot - low, 0)
+        return lax.select(late == layer, part[slot], part_swapped[slot])
+
+    count = pairs[row, pairs.shape[1] - 1]
+    run_jobs(
+        cases,
+        count,
+        pairs,
+        row,
+        right,
+        acc,
+        lambda slot: jnp.minimum(slot - layer * share, share),
+    )
+    copies = []
+    for j, (start, end) in enumerate(((0, share // 2), (share // 2, share))):
+        here = pl.ds(start, end - start)
+        rounded[here] = acc[here].astype(rounded.dtype)
+        copies.append(pltpu.make_async_copy(rounded.at[here], out.at[here], sem.at[j]))
+        copies[-1].start()
+    for copy in copies:
+        copy.wait()
 
 
 def on_device(plan, x_blocks, slot_rows, slot_cols):
@@ -346,30 +372,35 @@
         cost_estimate=cost(slots * plan.stages, 2 * plan.stages),
         name="early_products",
     )(lists, *direct, *before)
-    first, *rest = rights[-1]
-    total = pl.pallas_call(
+    first, second = rights[-1]
+    half = jax.ShapeDtypeStruct((share, size, size), jnp.float32)
+    _, mine, other = pl.pallas_call(
         functools.partial(middle_kernel, plan, parts),
-        out_shape=running,
+        out_shape=(running, half, half),
         in_specs=[scalars] + [vmem] * (2 + len(lefts) + len(before)),
-        out_specs=vmem,
+        out_specs=(vmem, vmem, vmem),
         input_output_aliases={1: 0},
         compiler_params=compiler_params,
         cost_estimate=cost(slots * plan.stages, 2 * plan.stages),
         name="middle_products",
     )(lists, total, *lefts, *before, first)
-    half = jax.ShapeDtypeStruct((share, size, size), jnp.float32)
-    _, mine, other = pl.pallas_call(
-        functools.partial(last_kernel, plan, bounds),
-        out_shape=(running, half, half),
-        in_specs=[scalars] + [vmem] * (1 + len(lefts) + len(rest)),
-        out_specs=(vmem, vmem, vmem),
-        input_output_aliases={1: 0},
+    received = lax.ppermute(other, "layer", swap)
+    second_swapped = lax.ppermute(second, "layer", swap)
+    square = pl.pallas_call(
+        functools.partial(last_kernel, plan, bounds[1]),
+        out_shape=jax.ShapeDtypeStruct((share, size, size), jnp.bfloat16),
+        in_specs=[scalars] + [vmem] * (4 + len(lefts)),
+        out_specs=pl.BlockSpec(memory_space=pl.ANY),
+        scratch_shapes=[
+            pltpu.VMEM((share + 1, size, size), jnp.float32),
+            pltpu.VMEM((share, size, size), jnp.bfloat16),
+            pltpu.SemaphoreType.DMA((2,)),
+        ],
         compiler_params=compiler_params,
         cost_estimate=cost(slots // 2, 4),
         name="last_products",
-    )(lists, total, *lefts, *rest)
-    received = lax.ppermute(other, "layer", swap)
-    return (mine + received).astype(jnp.bfloat16)[None, None]
+    )(lists, mine, received, *lefts, second, second_swapped)
+    return square[None, None]
 
 
 def solution(mesh):

time: 44.7 us -> 43.9 us (0.982)
  Pallas kernels: 4.18 us -> 5.41 us
  other arithmetic: 0.96 us -> 0.06 us
  waiting for transfers between devices: 9.39 us -> 8.74 us
  starting transfers between devices: 26.5 us -> 26 us
    ppermute x1, starting transfers between devices: 10.8 us -> 7.16 us  [on_device(): received = lax.ppermute(other, 'layer', swap)]
    ppermute x0 -> x1, starting transfers between devices: none -> 3.13 us  [on_device(): second_swapped = lax.ppermute(second, 'layer', swap)]
    ppermute x1, waiting for transfers between devices: 2.1 us -> 0.01 us  [on_device(): received = lax.ppermute(other, 'layer', swap)]
    ppermute x0 -> x1, waiting for transfers between devices: none -> 1.44 us  [on_device(): second_swapped = lax.ppermute(second, 'layer', swap)]
    pallas_call x2, Pallas kernels: 1.47 us -> 2.67 us  [the longest x1 1.84 us: on_device(): pl.pallas_call(functools.partial(last_kernel, plan, bounds[1]), out_shape...]
    broadcast_in_dim x1 -> x0, other arithmetic: 0.9 us -> none  [on_device(): return (mine + received).astype(jnp.bfloat16)[None, None]]
  transfers between devices with their start and end apart: 11 -> 12, of which waited for: 4 -> 4; matrix products, arithmetic and copies ran while one was open for 7% -> 7% of each run, Pallas kernels for 8% -> 8%
where the time goes in v6:
time: 43.9 us; the launch traced here: 43.3 us
  starting transfers between devices  26 us (59%)
  waiting for transfers between devices  8.74 us (20%)
  Pallas kernels  5.41 us (12%)
  local copies, waits for them, and re-layouts  2.92 us (7%)
    ppermute x6, starting transfers between devices, on_device(): arrived.append(lax.ppermute(part, ('col', 'layer'), pairs))  9.71 us
    ppermute x1, starting transfers between devices, on_device(): received = lax.ppermute(other, 'layer', swap)  7.16 us
    ppermute x6, waiting for transfers between devices, on_device(): arrived.append(lax.ppermute(part, ('col', 'layer'), pairs))  4.19 us
    ppermute x1, starting transfers between devices, on_device(): second_swapped = lax.ppermute(second, 'layer', swap)  3.13 us
    ppermute x1, waiting for transfers between devices, on_device(): far = lax.ppermute(sent, everywhere, plan.far_pairs())  3.09 us
    ppermute x1, starting transfers between devices, on_device(): near.append(lax.ppermute(own, everywhere, plan.near_pairs(bys)))  3.03 us
    slice x2, local copies, waits for them, and re-layouts, on_device(): (lax.optimization_barrier(own) if i else own)[i:j]  2.91 us
    pallas_call x1, Pallas kernels, on_device(): pl.pallas_call(functools.partial(last_kernel, plan, bounds[1]), out_shape...  1.84 us
  transfers between devices with their start and end apart: 12, of which 4 were waited for; matrix products, arithmetic and copies ran while one was open for 7% of the time, Pallas kernels for 8%

profile of v6, /device:TPU:0, one launch (start us, length us, event | category | flops | bytes accessed | tf_op | source)
XLA Modules:
  0.0 43.3 jit_solution(13609507140107206700)
XLA Ops:
  0.0 3.0 %collective-permute-start = (bf16[28,128,128]{2,1,0:T(8,128)(2,1)}, bf16[28,128,128]{2,1,0:T(8,128)(2,1)S(1)}, u32[]{:S(2)}, u32[]{:S(2)}) collective-permute-start(bf16[28,128,128]{2,1,0:T(8,128)(2,1)} %bitcast.4), channel_id=1, source_target_pairs={{0,8},{1,17},{2,10},{3,19},{4,12},{5,21},{6,14},{7,23},{8,0},{9,25... | collective-permute-start | bytes 2752520 | tf_op jit(solution)/shard_map/ppermute | solution.py:354
  3.0 1.9 %slice_bitcast_fusion = bf16[14,128,128]{2,1,0:T(8,128)(2,1)} fusion(bf16[1,1,28,128,128]{4,3,2,1,0:T(8,128)(2,1)} %param.3), kind=kLoop, calls=%fused_computation.1 | loop fusion | bytes 917504 | tf_op jit(solution)/shard_map/slice | solution.py:316
  4.9 3.5 %collective-permute-start.1 = (bf16[14,128,128]{2,1,0:T(8,128)(2,1)}, bf16[14,128,128]{2,1,0:T(8,128)(2,1)S(1)}, u32[]{:S(2)}, u32[]{:S(2)}) collective-permute-start(bf16[14,128,128]{2,1,0:T(8,128)(2,1)} %slice_bitcast_fusion), channel_id=1, source_target_pairs={{0,2},{2,4},{3,1},{4,6},{5,3},{7,5},{8,10},{10,12},{11,9},{12,14},... | collective-permute-start | bytes 1376264 | tf_op jit(solution)/shard_map/ppermute | solution.py:346
  8.4 1.1 %slice.20 = bf16[14,128,128]{2,1,0:T(8,128)(2,1)S(1)} slice(bf16[28,128,128]{2,1,0:T(8,128)(2,1)} %bitcast.5), slice={[14:28], [0:128], [0:128]} | slice | bytes 917504 | tf_op jit(solution)/shard_map/slice | solution.py:316
  9.5 3.5 %collective-permute-start.2 = (bf16[14,128,128]{2,1,0:T(8,128)(2,1)S(1)}, bf16[14,128,128]{2,1,0:T(8,128)(2,1)S(1)}, u32[]{:S(2)}, u32[]{:S(2)}) collective-permute-start(bf16[14,128,128]{2,1,0:T(8,128)(2,1)S(1)} %slice.20), channel_id=1, source_target_pairs={{0,2},{2,4},{3,1},{4,6},{5,3},{7,5},{8,10},{10,12},{11,9},{12,14},... | collective-permute-start | bytes 1376264 | tf_op jit(solution)/shard_map/ppermute | solution.py:346
  13.0 1.7 %collective-permute-done.1.refs_3_.refs_6_ = bf16[14,128,128]{2,1,0:T(8,128)(2,1)S(1)} collective-permute-done((bf16[14,128,128]{2,1,0:T(8,128)(2,1)}, bf16[14,128,128]{2,1,0:T(8,128)(2,1)S(1)}, u32[]{:S(2)}, u32[]{:S(2)}) %collective-permute-start.1) | collective-permute-done | bytes 458784 | tf_op jit(solution)/shard_map/ppermute | solution.py:346
  14.7 0.7 %collective-permute-start.3 = (bf16[14,128,128]{2,1,0:T(8,128)(2,1)S(1)}, bf16[14,128,128]{2,1,0:T(8,128)(2,1)S(1)}, u32[]{:S(2)}, u32[]{:S(2)}) collective-permute-start(bf16[14,128,128]{2,1,0:T(8,128)(2,1)S(1)} %collective-permute-done.1.refs_3_.refs_6_), channel_id=1, source_target_pairs={{2,4},{3,1},{4,6},{5,3},{10,12},{11,9},{12,14},{13,11},{18,20},{19... | collective-permute-start | bytes 1376264 | tf_op jit(solution)/shard_map/ppermute | solution.py:346
  15.4 0.0 collective-permute-done.refs_1_
  15.4 0.1 slice_select_fusion
  15.4 1.6 %collective-permute-start.6 = (bf16[14,128,128]{2,1,0:T(8,128)(2,1)S(1)}, bf16[14,128,128]{2,1,0:T(8,128)(2,1)S(1)}, u32[]{:S(2)}, u32[]{:S(2)}) collective-permute-start(bf16[14,128,128]{2,1,0:T(8,128)(2,1)S(1)} %slice_select_fusion), channel_id=1, source_target_pairs={{8,24},{17,25},{10,26},{19,27},{12,28},{21,29},{14,30},{23,31},{0,... | collective-permute-start | bytes 1376264 | tf_op jit(solution)/shard_map/ppermute | solution.py:359
  17.0 0.0 collective-permute-start.5
  17.0 2.5 %collective-permute-done.2.refs_4_.refs_7_ = bf16[14,128,128]{2,1,0:T(8,128)(2,1)S(1)} collective-permute-done((bf16[14,128,128]{2,1,0:T(8,128)(2,1)S(1)}, bf16[14,128,128]{2,1,0:T(8,128)(2,1)S(1)}, u32[]{:S(2)}, u32[]{:S(2)}) %collective-permute-start.2) | collective-permute-done | bytes 458784 | tf_op jit(solution)/shard_map/ppermute | solution.py:346
  19.5 0.7 %collective-permute-start.4 = (bf16[14,128,128]{2,1,0:T(8,128)(2,1)S(1)}, bf16[14,128,128]{2,1,0:T(8,128)(2,1)S(1)}, u32[]{:S(2)}, u32[]{:S(2)}) collective-permute-start(bf16[14,128,128]{2,1,0:T(8,128)(2,1)S(1)} %collective-permute-done.2.refs_4_.refs_7_), channel_id=1, source_target_pairs={{2,4},{3,1},{4,6},{5,3},{10,12},{11,9},{12,14},{13,11},{18,20},{19... | collective-permute-start | bytes 1376264 | tf_op jit(solution)/shard_map/ppermute | solution.py:346
  20.2 0.0 collective-permute-done.3.refs_5_.refs_8_
  20.2 0.7 %collective-permute-start.8 = (bf16[14,128,128]{2,1,0:T(8,128)(2,1)S(1)}, bf16[14,128,128]{2,1,0:T(8,128)(2,1)S(1)}, u32[]{:S(2)}, u32[]{:S(2)}) collective-permute-start(bf16[14,128,128]{2,1,0:T(8,128)(2,1)S(1)} %collective-permute-done.3.refs_5_.refs_8_), channel_id=1, source_target_pairs={{3,1},{4,6},{11,9},{12,14},{19,17},{20,22},{27,25},{28,30}} | collective-permute-start | bytes 1376264 | tf_op jit(solution)/shard_map/ppermute | solution.py:346
  20.9 3.1 %collective-permute-done.6.refs_3_ = bf16[14,128,128]{2,1,0:T(8,128)(2,1)S(1)} collective-permute-done((bf16[14,128,128]{2,1,0:T(8,128)(2,1)S(1)}, bf16[14,128,128]{2,1,0:T(8,128)(2,1)S(1)}, u32[]{:S(2)}, u32[]{:S(2)}) %collective-permute-start.6) | collective-permute-done | bytes 458784 | tf_op jit(solution)/shard_map/ppermute | solution.py:359
  24.0 1.4 %collective-permute-start.7 = (bf16[14,128,128]{2,1,0:T(8,128)(2,1)S(1)}, bf16[14,128,128]{2,1,0:T(8,128)(2,1)S(1)}, u32[]{:S(2)}, u32[]{:S(2)}) collective-permute-start(bf16[14,128,128]{2,1,0:T(8,128)(2,1)S(1)} %collective-permute-done.6.refs_3_), channel_id=1, source_target_pairs={{0,1},{1,0},{2,3},{3,2},{4,5},{5,4},{6,7},{7,6},{8,9},{9,8},{10,11... | collective-permute-start | bytes 1376264 | tf_op jit(solution)/shard_map/ppermute | solution.py:360
  25.4 0.0 copy-done.1
  25.4 1.0 %list_products.1.pairs = s32[5,128]{1,0:T(8,128)S(1)} custom-call(s32[4,4,28]{2,1,0:T(4,128)S(1)} %convert_add_fusion.slot_keys), custom_call_target="tpu_custom_call" | custom-call | bytes 1835008 | tf_op jit(solution)/shard_map/list_products/pallas_call | solution.py:331
  26.4 0.0 collective-permute-done.4.refs_6_.refs_9_
  26.4 0.7 %collective-permute-start.10 = (bf16[14,128,128]{2,1,0:T(8,128)(2,1)S(1)}, bf16[14,128,128]{2,1,0:T(8,128)(2,1)S(1)}, u32[]{:S(2)}, u32[]{:S(2)}) collective-permute-start(bf16[14,128,128]{2,1,0:T(8,128)(2,1)S(1)} %collective-permute-done.4.refs_6_.refs_9_), channel_id=1, source_target_pairs={{3,1},{4,6},{11,9},{12,14},{19,17},{20,22},{27,25},{28,30}} | collective-permute-start | bytes 1376264 | tf_op jit(solution)/shard_map/ppermute | solution.py:346
  27.1 1.8 %early_products.1.total = f32[29,128,128]{2,1,0:T(8,128)S(1)} custom-call(s32[5,128]{1,0:T(8,128)S(1)} %list_products.1.pairs, bf16[28,128,128]{2,1,0:T(8,128)(2,1)S(1)} %bitcast.6, bf16[28,128,128]{2,1,0:T(8,128)(2,1)S(1)} %collective-permute-done.refs_1_, bf16[28,128,128]{2,1,0:T(8,128)(2,1)S(1)} %bitcast.7, ...), custom_call_target="tpu_custom_call" | custom-call | flops 352321536 | bytes 5505024 | tf_op jit(solution)/shard_map/early_products/pallas_call | solution.py:366
  28.9 0.0 collective-permute-done.8.refs_10_
  28.9 0.0 collective-permute-done.7.refs_4_
  28.9 0.0 collective-permute-done.5.refs_2_
  28.9 0.8 %middle_products.1 = (f32[29,128,128]{2,1,0:T(8,128)S(1)}, f32[14,128,128]{2,1,0:T(8,128)S(1)}, f32[14,128,128]{2,1,0:T(8,128)S(1)}) custom-call(s32[5,128]{1,0:T(8,128)S(1)} %list_products.1.pairs, f32[29,128,128]{2,1,0:T(8,128)S(1)} %early_products.1.total, bf16[28,128,128]{2,1,0:T(8,128)(2,1)S(1)} %bitcast.8, ...), custom_call_target="tpu_custom_call", output_to_operand_aliasing={{0}: (1, {})} | custom-call | flops 352321536 | bytes 5505024 | tf_op jit(solution)/shard_map/middle_products/pallas_call | solution.py:377
  29.7 7.2 %collective-permute-start.9 = (f32[14,128,128]{2,1,0:T(8,128)S(1)}, f32[14,128,128]{2,1,0:T(8,128)S(1)}, u32[]{:S(2)}, u32[]{:S(2)}) collective-permute-start(f32[14,128,128]{2,1,0:T(8,128)S(1)} %get-tuple-element.8), channel_id=1, source_target_pairs={{0,1},{1,0},{2,3},{3,2},{4,5},{5,4},{6,7},{7,6},{8,9},{9,8},{10,11... | collective-permute-start | bytes 2752520 | tf_op jit(solution)/shard_map/ppermute | solution.py:387
  36.9 0.0 collective-permute-done.10.refs_5_
  36.9 3.1 %collective-permute-start.11 = (bf16[14,128,128]{2,1,0:T(8,128)(2,1)S(1)}, bf16[14,128,128]{2,1,0:T(8,128)(2,1)S(1)}, u32[]{:S(2)}, u32[]{:S(2)}) collective-permute-start(bf16[14,128,128]{2,1,0:T(8,128)(2,1)S(1)} %collective-permute-done.10.refs_5_), channel_id=1, source_target_pairs={{0,1},{1,0},{2,3},{3,2},{4,5},{5,4},{6,7},{7,6},{8,9},{9,8},{10,11... | collective-permute-start | bytes 1376264 | tf_op jit(solution)/shard_map/ppermute | solution.py:388
  40.0 1.4 %collective-permute-done.11.refs_6_ = bf16[14,128,128]{2,1,0:T(8,128)(2,1)S(1)} collective-permute-done((bf16[14,128,128]{2,1,0:T(8,128)(2,1)S(1)}, bf16[14,128,128]{2,1,0:T(8,128)(2,1)S(1)}, u32[]{:S(2)}, u32[]{:S(2)}) %collective-permute-start.11) | collective-permute-done | bytes 458784 | tf_op jit(solution)/shard_map/ppermute | solution.py:388
  41.5 0.0 collective-permute-done.9.received
  41.5 1.8 %last_products.1 = bf16[14,128,128]{2,1,0:T(8,128)(2,1)} custom-call(s32[5,128]{1,0:T(8,128)S(1)} %list_products.1.pairs, f32[14,128,128]{2,1,0:T(8,128)S(1)} %get-tuple-element.7.mine, f32[14,128,128]{2,1,0:T(8,128)S(1)} %collective-permute-done.9.received, bf16[28,128,128]{2,1,0:T(8,128)(2,1)S(1)} %bitcast.10, ...), custom_call_target="tpu_custom_call" | custom-call | flops 58720256 | bytes 3670016 | tf_op jit(solution)/shard_map/last_products/pallas_call | solution.py:389
  (6 shorter events, 0.0 us)
Async XLA Ops:
  0.0 27.1 %copy-start = (bf16[1,1,28,128,128]{4,3,2,1,0:T(8,128)(2,1)S(1)}, bf16[1,1,28,128,128]{4,3,2,1,0:T(8,128)(2,1)}, u32[]{:S(2)}) copy-start(bf16[1,1,28,128,128]{4,3,2,1,0:T(8,128)(2,1)} %param.3) | copy-start | bytes 2752516
  0.0 25.4 %copy-start.1 = (s32[4,4,28]{2,1,0:T(4,128)S(1)}, s32[4,4,28]{2,1,0:T(4,128)}, u32[]{:S(2)}) copy-start(s32[4,4,28]{2,1,0:T(4,128)} %param.4) | copy-start | bytes 5380
  0.0 25.4 %copy-start.2 = (s32[4,4,28]{2,1,0:T(4,128)S(1)}, s32[4,4,28]{2,1,0:T(4,128)}, u32[]{:S(2)}) copy-start(s32[4,4,28]{2,1,0:T(4,128)} %param.5) | copy-start | bytes 5380
  0.0 15.3 %collective-permute-start = (bf16[28,128,128]{2,1,0:T(8,128)(2,1)}, bf16[28,128,128]{2,1,0:T(8,128)(2,1)S(1)}, u32[]{:S(2)}, u32[]{:S(2)}) collective-permute-start(bf16[28,128,128]{2,1,0:T(8,128)(2,1)} %bitcast.4), channel_id=1, source_target_pairs={{0,8},{1,17},{2,10},{3,19},{4,12},{5,21},{6,14},{7,23},{8,0},{9,25... | collective-permute-start | bytes 2752520 | tf_op jit(solution)/shard_map/ppermute | solution.py:354
  4.9 9.8 %collective-permute-start.1 = (bf16[14,128,128]{2,1,0:T(8,128)(2,1)}, bf16[14,128,128]{2,1,0:T(8,128)(2,1)S(1)}, u32[]{:S(2)}, u32[]{:S(2)}) collective-permute-start(bf16[14,128,128]{2,1,0:T(8,128)(2,1)} %slice_bitcast_fusion), channel_id=1, source_target_pairs={{0,2},{2,4},{3,1},{4,6},{5,3},{7,5},{8,10},{10,12},{11,9},{12,14},... | collective-permute-start | bytes 1376264 | tf_op jit(solution)/shard_map/ppermute | solution.py:346
  9.5 10.0 %collective-permute-start.2 = (bf16[14,128,128]{2,1,0:T(8,128)(2,1)S(1)}, bf16[14,128,128]{2,1,0:T(8,128)(2,1)S(1)}, u32[]{:S(2)}, u32[]{:S(2)}) collective-permute-start(bf16[14,128,128]{2,1,0:T(8,128)(2,1)S(1)} %slice.20), channel_id=1, source_target_pairs={{0,2},{2,4},{3,1},{4,6},{5,3},{7,5},{8,10},{10,12},{11,9},{12,14},... | collective-permute-start | bytes 1376264 | tf_op jit(solution)/shard_map/ppermute | solution.py:346
  14.7 5.5 %collective-permute-start.3 = (bf16[14,128,128]{2,1,0:T(8,128)(2,1)S(1)}, bf16[14,128,128]{2,1,0:T(8,128)(2,1)S(1)}, u32[]{:S(2)}, u32[]{:S(2)}) collective-permute-start(bf16[14,128,128]{2,1,0:T(8,128)(2,1)S(1)} %collective-permute-done.1.refs_3_.refs_6_), channel_id=1, source_target_pairs={{2,4},{3,1},{4,6},{5,3},{10,12},{11,9},{12,14},{13,11},{18,20},{19... | collective-permute-start | bytes 1376264 | tf_op jit(solution)/shard_map/ppermute | solution.py:346
  15.4 8.5 %collective-permute-start.6 = (bf16[14,128,128]{2,1,0:T(8,128)(2,1)S(1)}, bf16[14,128,128]{2,1,0:T(8,128)(2,1)S(1)}, u32[]{:S(2)}, u32[]{:S(2)}) collective-permute-start(bf16[14,128,128]{2,1,0:T(8,128)(2,1)S(1)} %slice_select_fusion), channel_id=1, source_target_pairs={{8,24},{17,25},{10,26},{19,27},{12,28},{21,29},{14,30},{23,31},{0,... | collective-permute-start | bytes 1376264 | tf_op jit(solution)/shard_map/ppermute | solution.py:359
  17.0 11.9 %collective-permute-start.5 = (bf16[28,128,128]{2,1,0:T(8,128)(2,1)S(1)}, bf16[28,128,128]{2,1,0:T(8,128)(2,1)S(1)}, u32[]{:S(2)}, u32[]{:S(2)}) collective-permute-start(bf16[28,128,128]{2,1,0:T(8,128)(2,1)S(1)} %collective-permute-done.refs_1_), channel_id=1, source_target_pairs={{0,1},{1,0},{2,3},{3,2},{4,5},{5,4},{6,7},{7,6},{8,9},{9,8},{10,11... | collective-permute-start | bytes 2752520 | tf_op jit(solution)/shard_map/ppermute | solution.py:355
  19.5 6.9 %collective-permute-start.4 = (bf16[14,128,128]{2,1,0:T(8,128)(2,1)S(1)}, bf16[14,128,128]{2,1,0:T(8,128)(2,1)S(1)}, u32[]{:S(2)}, u32[]{:S(2)}) collective-permute-start(bf16[14,128,128]{2,1,0:T(8,128)(2,1)S(1)} %collective-permute-done.2.refs_4_.refs_7_), channel_id=1, source_target_pairs={{2,4},{3,1},{4,6},{5,3},{10,12},{11,9},{12,14},{13,11},{18,20},{19... | collective-permute-start | bytes 1376264 | tf_op jit(solution)/shard_map/ppermute | solution.py:346
  20.2 8.7 %collective-permute-start.8 = (bf16[14,128,128]{2,1,0:T(8,128)(2,1)S(1)}, bf16[14,128,128]{2,1,0:T(8,128)(2,1)S(1)}, u32[]{:S(2)}, u32[]{:S(2)}) collective-permute-start(bf16[14,128,128]{2,1,0:T(8,128)(2,1)S(1)} %collective-permute-done.3.refs_5_.refs_8_), channel_id=1, source_target_pairs={{3,1},{4,6},{11,9},{12,14},{19,17},{20,22},{27,25},{28,30}} | collective-permute-start | bytes 1376264 | tf_op jit(solution)/shard_map/ppermute | solution.py:346
  24.0 4.9 %collective-permute-start.7 = (bf16[14,128,128]{2,1,0:T(8,128)(2,1)S(1)}, bf16[14,128,128]{2,1,0:T(8,128)(2,1)S(1)}, u32[]{:S(2)}, u32[]{:S(2)}) collective-permute-start(bf16[14,128,128]{2,1,0:T(8,128)(2,1)S(1)} %collective-permute-done.6.refs_3_), channel_id=1, source_target_pairs={{0,1},{1,0},{2,3},{3,2},{4,5},{5,4},{6,7},{7,6},{8,9},{9,8},{10,11... | collective-permute-start | bytes 1376264 | tf_op jit(solution)/shard_map/ppermute | solution.py:360
  26.4 10.5 %collective-permute-start.10 = (bf16[14,128,128]{2,1,0:T(8,128)(2,1)S(1)}, bf16[14,128,128]{2,1,0:T(8,128)(2,1)S(1)}, u32[]{:S(2)}, u32[]{:S(2)}) collective-permute-start(bf16[14,128,128]{2,1,0:T(8,128)(2,1)S(1)} %collective-permute-done.4.refs_6_.refs_9_), channel_id=1, source_target_pairs={{3,1},{4,6},{11,9},{12,14},{19,17},{20,22},{27,25},{28,30}} | collective-permute-start | bytes 1376264 | tf_op jit(solution)/shard_map/ppermute | solution.py:346
  29.7 11.7 %collective-permute-start.9 = (f32[14,128,128]{2,1,0:T(8,128)S(1)}, f32[14,128,128]{2,1,0:T(8,128)S(1)}, u32[]{:S(2)}, u32[]{:S(2)}) collective-permute-start(f32[14,128,128]{2,1,0:T(8,128)S(1)} %get-tuple-element.8), channel_id=1, source_target_pairs={{0,1},{1,0},{2,3},{3,2},{4,5},{5,4},{6,7},{7,6},{8,9},{9,8},{10,11... | collective-permute-start | bytes 2752520 | tf_op jit(solution)/shard_map/ppermute | solution.py:387
  36.9 4.6 %collective-permute-start.11 = (bf16[14,128,128]{2,1,0:T(8,128)(2,1)S(1)}, bf16[14,128,128]{2,1,0:T(8,128)(2,1)S(1)}, u32[]{:S(2)}, u32[]{:S(2)}) collective-permute-start(bf16[14,128,128]{2,1,0:T(8,128)(2,1)S(1)} %collective-permute-done.10.refs_5_), channel_id=1, source_target_pairs={{0,1},{1,0},{2,3},{3,2},{4,5},{5,4},{6,7},{7,6},{8,9},{9,8},{10,11... | collective-permute-start | bytes 1376264 | tf_op jit(solution)/shard_map/ppermute | solution.py:388

commit v7 on v6

--- a/solution.py
+++ b/solution.py
@@ -191,19 +191,17 @@
 
 
 class Lefts:
-    def __init__(self, plan, refs, late):
+    def __init__(self, plan, refs):
         near = plan.grid // 2 - 1
         self.far = plan.grid - 1
         self.own, self.near = refs[0], refs[1 : 1 + near]
-        self.swapped = self.halves = ()
-        if late:
-            self.swapped = refs[1 + near : 1 + 2 * near]
-            self.halves = refs[1 + 2 * near : 3 + 2 * near]
-
-    @staticmethod
-    def number(plan, late):
-        near = plan.grid // 2 - 1
-        return 3 + 2 * near if late else 1 + near
+        self.swapped = refs[1 + near : 1 + 2 * near]
+        self.halves = refs[1 + 2 * near :]
+
+    def all(self, by, layer):
+        yield from self.direct(by, layer)
+        yield from self.indirect(by, layer)
+        yield from self.opposite(by, layer)
 
     def direct(self, by, layer):
         yield by == 0, blocks_of([self.own])
@@ -213,6 +211,8 @@
     def indirect(self, by, layer):
         for k, tile in enumerate(self.swapped):
             yield by == 2 * k + 2 - layer, blocks_of([tile])
+
+    def opposite(self, by, layer):
         mine, other = self.halves
         share = mine.shape[0]
 
@@ -240,9 +240,8 @@
     return rights, refs
 
 
-def early_kernel(plan, parts, pairs, *refs):
-    n = Lefts.number(plan, False)
-    lefts = Lefts(plan, refs[:n], False)
+def early_kernel(plan, n, parts, pairs, *refs):
+    lefts = Lefts(plan, refs[:n])
     rights, (acc,) = stages_of(parts[:-1], refs[n:])
     a, b, layer = place()
     acc[...] = jnp.zeros_like(acc)
@@ -253,27 +252,40 @@
         run_jobs(cases, count, pairs, stage, blocks_of(right), acc)
 
 
-def middle_kernel(plan, parts, pairs, total, *refs):
+def second_kernel(plan, n, parts, pairs, total, *refs):
     del total
-    n = Lefts.number(plan, True)
-    lefts = Lefts(plan, refs[:n], True)
+    lefts = Lefts(plan, refs[:n])
+    rights, (acc,) = stages_of(parts[:-1], refs[n:])
+    a, b, layer = place()
+    for stage, right in enumerate(rights):
+        by = b ^ plan.taken(a, layer, stage)[0]
+        count = pairs[stage, pairs.shape[1] - 1]
+        cases = lefts.indirect(by, layer)
+        run_jobs(cases, count, pairs, stage, blocks_of(right), acc)
+
+
+def pick_kernel(tile, half):
+    share = half.shape[0]
+    half[...] = tile[pl.ds(lax.axis_index("layer") * share, share)]
+
+
+def middle_kernel(plan, n, parts, pairs, total, *refs):
+    del total
+    lefts = Lefts(plan, refs[:n])
     rights, (first, acc, mine, other) = stages_of(parts[:-1], refs[n:])
     a, b, layer = place()
     last = pairs.shape[1] - 1
     for stage, right in enumerate([*rights, [first]]):
         by = b ^ plan.taken(a, layer, stage)[0]
-        cases = list(lefts.indirect(by, layer))
-        if stage == plan.stages:
-            cases += lefts.direct(by, layer)
+        cases = (lefts.all if stage == plan.stages else lefts.opposite)(by, layer)
         run_jobs(cases, pairs[stage, last], pairs, stage, blocks_of(right), acc)
     share = other.shape[0]
     mine[...] = acc[pl.ds(layer * share, share)]
     other[...] = acc[pl.ds((1 - layer) * share, share)]
 
 
-def last_kernel(plan, low, pairs, mine, received, *refs):
-    n = Lefts.number(plan, True)
-    lefts = Lefts(plan, refs[:n], True)
+def last_kernel(plan, n, low, pairs, mine, received, *refs):
+    lefts = Lefts(plan, refs[:n])
     part, part_swapped, out, acc, rounded, sem = refs[n:]
     a, b, layer = place()
     share = out.shape[0]
@@ -281,7 +293,7 @@
     late, l, _ = late_core(plan, a)
     by = b ^ l
     row = plan.stages + 1
-    cases = [*lefts.direct(by, layer), *lefts.indirect(by, layer)]
+    cases = lefts.all(by, layer)
 
     def right(slot):
         slot = jnp.maximum(slot - low, 0)
@@ -353,9 +365,15 @@
         bys = (2 * k + 1, 2 * k + 2)
         near.append(lax.ppermute(own, everywhere, plan.near_pairs(bys)))
         swapped.append(lax.ppermute(near[-1], "layer", swap))
-    sent = jnp.where(
-        lax.axis_index("layer") == 0, near[0][:share], near[0][share:]
-    )
+    sent = pl.pallas_call(
+        pick_kernel,
+        out_shape=jax.ShapeDtypeStruct((share, size, size), own.dtype),
+        in_specs=[vmem],
+        out_specs=vmem,
+        compiler_params=compiler_params,
+        cost_estimate=cost(0, 1),
+        name="pick_half",
+    )(near[0])
     far = lax.ppermute(sent, everywhere, plan.far_pairs())
     far_swapped = lax.ppermute(far, "layer", swap)
     direct = [own, *near]
@@ -364,7 +382,7 @@
     running = jax.ShapeDtypeStruct((slots + 1, size, size), jnp.float32)
     before = [part for stage in rights[:-1] for part in stage]
     total = pl.pallas_call(
-        functools.partial(early_kernel, plan, parts),
+        functools.partial(early_kernel, plan, len(direct), parts),
         out_shape=running,
         in_specs=[scalars] + [vmem] * (len(direct) + len(before)),
         out_specs=vmem,
@@ -372,10 +390,21 @@
         cost_estimate=cost(slots * plan.stages, 2 * plan.stages),
         name="early_products",
     )(lists, *direct, *before)
+    total = pl.pallas_call(
+        functools.partial(second_kernel, plan, len(direct) + len(swapped), parts),
+        out_shape=running,
+        in_specs=[scalars]
+        + [vmem] * (1 + len(direct) + len(swapped) + len(before)),
+        out_specs=vmem,
+        input_output_aliases={1: 0},
+        compiler_params=compiler_params,
+        cost_estimate=cost(slots, 2),
+        name="second_products",
+    )(lists, total, *direct, *swapped, *before)
     first, second = rights[-1]
     half = jax.ShapeDtypeStruct((share, size, size), jnp.float32)
     _, mine, other = pl.pallas_call(
-        functools.partial(middle_kernel, plan, parts),
+        functools.partial(middle_kernel, plan, len(lefts), parts),
         out_shape=(running, half, half),
         in_specs=[scalars] + [vmem] * (2 + len(lefts) + len(before)),
         out_specs=(vmem, vmem, vmem),
@@ -387,7 +416,7 @@
     received = lax.ppermute(other, "layer", swap)
     second_swapped = lax.ppermute(second, "layer", swap)
     square = pl.pallas_call(
-        functools.partial(last_kernel, plan, bounds[1]),
+        functools.partial(last_kernel, plan, len(lefts), bounds[1]),
         out_shape=jax.ShapeDtypeStruct((share, size, size), jnp.bfloat16),
         in_specs=[scalars] + [vmem] * (4 + len(lefts)),
         out_specs=pl.BlockSpec(memory_space=pl.ANY),

time: 43.9 us -> 43.6 us (level)
  local copies, waits for them, and re-layouts: 2.92 us -> 2.15 us
  Pallas kernels: 5.41 us -> 6.11 us
  starting transfers between devices: 26 us -> 25.4 us
    ppermute x6, waiting for transfers between devices: 4.19 us -> 1.04 us  [on_device(): arrived.append(lax.ppermute(part, ('col', 'layer'), pairs))]
    ppermute x1, starting transfers between devices: 7.16 us -> 4.64 us  [on_device(): received = lax.ppermute(other, 'layer', swap)]
    ppermute x1, waiting for transfers between devices: 0.01 us -> 2.43 us  [on_device(): near.append(lax.ppermute(own, everywhere, plan.near_pairs(bys)))]
    ppermute x1, waiting for transfers between devices: 3.09 us -> 4.03 us  [on_device(): far = lax.ppermute(sent, everywhere, plan.far_pairs())]
    slice x2, local copies, waits for them, and re-layouts: 2.91 us -> 2.13 us  [on_device(): (lax.optimization_barrier(own) if i else own)[i:j]]
    ppermute x1, starting transfers between devices: 1.42 us -> 2.15 us  [on_device(): far_swapped = lax.ppermute(far, 'layer', swap)]
    pallas_call x3 -> x5, Pallas kernels: 4.43 us -> 5.13 us  [the longest x1 1.85 us: on_device(): pl.pallas_call(functools.partial(last_kernel, plan, len(lefts), bounds[1]...]
    ppermute x1, starting transfers between devices: 3.13 us -> 3.74 us  [on_device(): second_swapped = lax.ppermute(second, 'layer', swap)]
  transfers between devices with their start and end apart: 12 -> 12, of which waited for: 4 -> 4; matrix products, arithmetic and copies ran while one was open for 7% -> 5% of each run, Pallas kernels for 8% -> 10%
where the time goes in v7:
time: 43.6 us; the launch traced here: 42.8 us
  starting transfers between devices  25.4 us (58%)
  waiting for transfers between devices  8.95 us (21%)
  Pallas kernels  6.11 us (14%)
  local copies, waits for them, and re-layouts  2.15 us (5%)
    ppermute x6, starting transfers between devices, on_device(): arrived.append(lax.ppermute(part, ('col', 'layer'), pairs))  9.73 us
    ppermute x1, starting transfers between devices, on_device(): received = lax.ppermute(other, 'layer', swap)  4.64 us
    ppermute x1, waiting for transfers between devices, on_device(): far = lax.ppermute(sent, everywhere, plan.far_pairs())  4.03 us
    ppermute x1, starting transfers between devices, on_device(): second_swapped = lax.ppermute(second, 'layer', swap)  3.74 us
    ppermute x1, starting transfers between devices, on_device(): near.append(lax.ppermute(own, everywhere, plan.near_pairs(bys)))  3.03 us
    ppermute x1, waiting for transfers between devices, on_device(): near.append(lax.ppermute(own, everywhere, plan.near_pairs(bys)))  2.43 us
    ppermute x1, starting transfers between devices, on_device(): far_swapped = lax.ppermute(far, 'layer', swap)  2.15 us
    slice x2, local copies, waits for them, and re-layouts, on_device(): (lax.optimization_barrier(own) if i else own)[i:j]  2.13 us
  transfers between devices with their start and end apart: 12, of which 4 were waited for; matrix products, arithmetic and copies ran while one was open for 5% of the time, Pallas kernels for 10%

profile of v7, /device:TPU:0, one launch (start us, length us, event | category | flops | bytes accessed | tf_op | source)
XLA Modules:
  0.0 42.8 jit_solution(13798594168174738217)
XLA Ops:
  0.0 3.0 %collective-permute-start = (bf16[28,128,128]{2,1,0:T(8,128)(2,1)}, bf16[28,128,128]{2,1,0:T(8,128)(2,1)S(1)}, u32[]{:S(2)}, u32[]{:S(2)}) collective-permute-start(bf16[28,128,128]{2,1,0:T(8,128)(2,1)} %bitcast.4), channel_id=1, source_target_pairs={{0,8},{1,17},{2,10},{3,19},{4,12},{5,21},{6,14},{7,23},{8,0},{9,25... | collective-permute-start | bytes 2752520 | tf_op jit(solution)/shard_map/ppermute | solution.py:366
  3.0 1.1 %slice_bitcast_fusion = bf16[14,128,128]{2,1,0:T(8,128)(2,1)S(1)} fusion(bf16[1,1,28,128,128]{4,3,2,1,0:T(8,128)(2,1)} %param.3), kind=kLoop, calls=%fused_computation | loop fusion | bytes 917504 | tf_op jit(solution)/shard_map/slice | solution.py:328
  4.1 3.5 %collective-permute-start.1 = (bf16[14,128,128]{2,1,0:T(8,128)(2,1)S(1)}, bf16[14,128,128]{2,1,0:T(8,128)(2,1)S(1)}, u32[]{:S(2)}, u32[]{:S(2)}) collective-permute-start(bf16[14,128,128]{2,1,0:T(8,128)(2,1)S(1)} %slice_bitcast_fusion), channel_id=1, source_target_pairs={{0,2},{2,4},{3,1},{4,6},{5,3},{7,5},{8,10},{10,12},{11,9},{12,14},... | collective-permute-start | bytes 1376264 | tf_op jit(solution)/shard_map/ppermute | solution.py:358
  7.6 1.1 %slice.12 = bf16[14,128,128]{2,1,0:T(8,128)(2,1)S(1)} slice(bf16[28,128,128]{2,1,0:T(8,128)(2,1)} %bitcast.5), slice={[14:28], [0:128], [0:128]} | slice | bytes 917504 | tf_op jit(solution)/shard_map/slice | solution.py:328
  8.7 3.5 %collective-permute-start.2 = (bf16[14,128,128]{2,1,0:T(8,128)(2,1)S(1)}, bf16[14,128,128]{2,1,0:T(8,128)(2,1)S(1)}, u32[]{:S(2)}, u32[]{:S(2)}) collective-permute-start(bf16[14,128,128]{2,1,0:T(8,128)(2,1)S(1)} %slice.12), channel_id=1, source_target_pairs={{0,2},{2,4},{3,1},{4,6},{5,3},{7,5},{8,10},{10,12},{11,9},{12,14},... | collective-permute-start | bytes 1376264 | tf_op jit(solution)/shard_map/ppermute | solution.py:358
  12.2 2.4 %collective-permute-done.refs_1_.tile = bf16[28,128,128]{2,1,0:T(8,128)(2,1)S(1)} collective-permute-done((bf16[28,128,128]{2,1,0:T(8,128)(2,1)}, bf16[28,128,128]{2,1,0:T(8,128)(2,1)S(1)}, u32[]{:S(2)}, u32[]{:S(2)}) %collective-permute-start) | collective-permute-done | bytes 917536 | tf_op jit(solution)/shard_map/ppermute | solution.py:366
  14.6 0.0 collective-permute-start.5
  14.6 0.0 collective-permute-done.1.refs_3_.refs_4_.refs_6_
  14.6 0.7 %collective-permute-start.3 = (bf16[14,128,128]{2,1,0:T(8,128)(2,1)S(1)}, bf16[14,128,128]{2,1,0:T(8,128)(2,1)S(1)}, u32[]{:S(2)}, u32[]{:S(2)}) collective-permute-start(bf16[14,128,128]{2,1,0:T(8,128)(2,1)S(1)} %collective-permute-done.1.refs_3_.refs_4_.refs_6_), channel_id=1, source_target_pairs={{2,4},{3,1},{4,6},{5,3},{10,12},{11,9},{12,14},{13,11},{18,20},{19... | collective-permute-start | bytes 1376264 | tf_op jit(solution)/shard_map/ppermute | solution.py:358
  15.4 2.1 %collective-permute-start.6 = (bf16[14,128,128]{2,1,0:T(8,128)(2,1)S(1)}, bf16[14,128,128]{2,1,0:T(8,128)(2,1)S(1)}, u32[]{:S(2)}, u32[]{:S(2)}) collective-permute-start(bf16[14,128,128]{2,1,0:T(8,128)(2,1)S(1)} %pick_half.1), channel_id=1, source_target_pairs={{8,24},{17,25},{10,26},{19,27},{12,28},{21,29},{14,30},{23,31},{0,... | collective-permute-start | bytes 1376264 | tf_op jit(solution)/shard_map/ppermute | solution.py:377
  17.5 1.0 %collective-permute-done.2.refs_4_.refs_5_.refs_7_ = bf16[14,128,128]{2,1,0:T(8,128)(2,1)S(1)} collective-permute-done((bf16[14,128,128]{2,1,0:T(8,128)(2,1)S(1)}, bf16[14,128,128]{2,1,0:T(8,128)(2,1)S(1)}, u32[]{:S(2)}, u32[]{:S(2)}) %collective-permute-start.2) | collective-permute-done | bytes 458784 | tf_op jit(solution)/shard_map/ppermute | solution.py:358
  18.5 0.7 %collective-permute-start.4 = (bf16[14,128,128]{2,1,0:T(8,128)(2,1)S(1)}, bf16[14,128,128]{2,1,0:T(8,128)(2,1)S(1)}, u32[]{:S(2)}, u32[]{:S(2)}) collective-permute-start(bf16[14,128,128]{2,1,0:T(8,128)(2,1)S(1)} %collective-permute-done.2.refs_4_.refs_5_.refs_7_), channel_id=1, source_target_pairs={{2,4},{3,1},{4,6},{5,3},{10,12},{11,9},{12,14},{13,11},{18,20},{19... | collective-permute-start | bytes 1376264 | tf_op jit(solution)/shard_map/ppermute | solution.py:358
  19.2 0.0 collective-permute-done.3.refs_5_.refs_6_.refs_8_
  19.2 0.7 %collective-permute-start.8 = (bf16[14,128,128]{2,1,0:T(8,128)(2,1)S(1)}, bf16[14,128,128]{2,1,0:T(8,128)(2,1)S(1)}, u32[]{:S(2)}, u32[]{:S(2)}) collective-permute-start(bf16[14,128,128]{2,1,0:T(8,128)(2,1)S(1)} %collective-permute-done.3.refs_5_.refs_6_.refs_8_), channel_id=1, source_target_pairs={{3,1},{4,6},{11,9},{12,14},{19,17},{20,22},{27,25},{28,30}} | collective-permute-start | bytes 1376264 | tf_op jit(solution)/shard_map/ppermute | solution.py:358
  19.9 4.0 %collective-permute-done.6.refs_3_ = bf16[14,128,128]{2,1,0:T(8,128)(2,1)S(1)} collective-permute-done((bf16[14,128,128]{2,1,0:T(8,128)(2,1)S(1)}, bf16[14,128,128]{2,1,0:T(8,128)(2,1)S(1)}, u32[]{:S(2)}, u32[]{:S(2)}) %collective-permute-start.6) | collective-permute-done | bytes 458784 | tf_op jit(solution)/shard_map/ppermute | solution.py:377
  23.9 2.1 %collective-permute-start.7 = (bf16[14,128,128]{2,1,0:T(8,128)(2,1)S(1)}, bf16[14,128,128]{2,1,0:T(8,128)(2,1)S(1)}, u32[]{:S(2)}, u32[]{:S(2)}) collective-permute-start(bf16[14,128,128]{2,1,0:T(8,128)(2,1)S(1)} %collective-permute-done.6.refs_3_), channel_id=1, source_target_pairs={{0,1},{1,0},{2,3},{3,2},{4,5},{5,4},{6,7},{7,6},{8,9},{9,8},{10,11... | collective-permute-start | bytes 1376264 | tf_op jit(solution)/shard_map/ppermute | solution.py:378
  26.1 0.0 copy-done.2
  26.1 1.0 %list_products.1.pairs = s32[5,128]{1,0:T(8,128)S(1)} custom-call(s32[4,4,28]{2,1,0:T(4,128)S(1)} %convert_add_fusion.slot_keys), custom_call_target="tpu_custom_call" | custom-call | bytes 1835008 | tf_op jit(solution)/shard_map/list_products/pallas_call | solution.py:343
  27.1 0.0 collective-permute-done.4.refs_6_.refs_7_.refs_9_
  27.1 0.7 %collective-permute-start.10 = (bf16[14,128,128]{2,1,0:T(8,128)(2,1)S(1)}, bf16[14,128,128]{2,1,0:T(8,128)(2,1)S(1)}, u32[]{:S(2)}, u32[]{:S(2)}) collective-permute-start(bf16[14,128,128]{2,1,0:T(8,128)(2,1)S(1)} %collective-permute-done.4.refs_6_.refs_7_.refs_9_), channel_id=1, source_target_pairs={{3,1},{4,6},{11,9},{12,14},{19,17},{20,22},{27,25},{28,30}} | collective-permute-start | bytes 1376264 | tf_op jit(solution)/shard_map/ppermute | solution.py:358
  27.8 1.8 %early_products.1.total = f32[29,128,128]{2,1,0:T(8,128)S(1)} custom-call(s32[5,128]{1,0:T(8,128)S(1)} %list_products.1.pairs, bf16[28,128,128]{2,1,0:T(8,128)(2,1)S(1)} %bitcast.6, bf16[28,128,128]{2,1,0:T(8,128)(2,1)S(1)} %collective-permute-done.refs_1_.tile, bf16[28,128,128]{2,1,0:T(8,128)(2,1)S(1)} %bitcast.7, ...), custom_call_target="tpu_custom_call" | custom-call | flops 352321536 | bytes 5505024 | tf_op jit(solution)/shard_map/early_products/pallas_call | solution.py:384
  29.6 0.0 collective-permute-done.5.refs_2_
  29.6 0.7 %second_products.1.total = f32[29,128,128]{2,1,0:T(8,128)S(1)} custom-call(s32[5,128]{1,0:T(8,128)S(1)} %list_products.1.pairs, f32[29,128,128]{2,1,0:T(8,128)S(1)} %early_products.1.total, bf16[28,128,128]{2,1,0:T(8,128)(2,1)S(1)} %bitcast.8, bf16[28,128,128]{2,1,0:T(8,128)(2,1)S(1)} %collective-permute-done.refs_1_.tile, ...), custom_call_target="tpu_custom_call", output_to_operand_aliasing={{}: (1, {})} | custom-call | flops 117440512 | bytes 1835008 | tf_op jit(solution)/shard_map/second_products/pallas_call | solution.py:393
  30.2 0.0 collective-permute-done.8.refs_10_
  30.2 0.0 collective-permute-done.7.refs_4_
  30.3 0.8 %middle_products.1 = (f32[29,128,128]{2,1,0:T(8,128)S(1)}, f32[14,128,128]{2,1,0:T(8,128)S(1)}, f32[14,128,128]{2,1,0:T(8,128)S(1)}) custom-call(s32[5,128]{1,0:T(8,128)S(1)} %list_products.1.pairs, f32[29,128,128]{2,1,0:T(8,128)S(1)} %second_products.1.total, bf16[28,128,128]{2,1,0:T(8,128)(2,1)S(1)} %bitcast.10, ...), custom_call_target="tpu_custom_call", output_to_operand_aliasing={{0}: (1, {})} | custom-call | flops 352321536 | bytes 5505024 | tf_op jit(solution)/shard_map/middle_products/pallas_call | solution.py:406
  31.1 4.6 %collective-permute-start.9 = (f32[14,128,128]{2,1,0:T(8,128)S(1)}, f32[14,128,128]{2,1,0:T(8,128)S(1)}, u32[]{:S(2)}, u32[]{:S(2)}) collective-permute-start(f32[14,128,128]{2,1,0:T(8,128)S(1)} %get-tuple-element.8), channel_id=1, source_target_pairs={{0,1},{1,0},{2,3},{3,2},{4,5},{5,4},{6,7},{7,6},{8,9},{9,8},{10,11... | collective-permute-start | bytes 2752520 | tf_op jit(solution)/shard_map/ppermute | solution.py:416
  35.7 0.0 collective-permute-done.10.refs_5_
  35.7 3.7 %collective-permute-start.11 = (bf16[14,128,128]{2,1,0:T(8,128)(2,1)S(1)}, bf16[14,128,128]{2,1,0:T(8,128)(2,1)S(1)}, u32[]{:S(2)}, u32[]{:S(2)}) collective-permute-start(bf16[14,128,128]{2,1,0:T(8,128)(2,1)S(1)} %collective-permute-done.10.refs_5_), channel_id=1, source_target_pairs={{0,1},{1,0},{2,3},{3,2},{4,5},{5,4},{6,7},{7,6},{8,9},{9,8},{10,11... | collective-permute-start | bytes 1376264 | tf_op jit(solution)/shard_map/ppermute | solution.py:417
  39.5 1.4 %collective-permute-done.11.refs_6_ = bf16[14,128,128]{2,1,0:T(8,128)(2,1)S(1)} collective-permute-done((bf16[14,128,128]{2,1,0:T(8,128)(2,1)S(1)}, bf16[14,128,128]{2,1,0:T(8,128)(2,1)S(1)}, u32[]{:S(2)}, u32[]{:S(2)}) %collective-permute-start.11) | collective-permute-done | bytes 458784 | tf_op jit(solution)/shard_map/ppermute | solution.py:417
  40.9 0.0 collective-permute-done.9.received
  40.9 1.9 %last_products.1 = bf16[14,128,128]{2,1,0:T(8,128)(2,1)} custom-call(s32[5,128]{1,0:T(8,128)S(1)} %list_products.1.pairs, f32[14,128,128]{2,1,0:T(8,128)S(1)} %get-tuple-element.7.mine, f32[14,128,128]{2,1,0:T(8,128)S(1)} %collective-permute-done.9.received, bf16[28,128,128]{2,1,0:T(8,128)(2,1)S(1)} %bitcast.12, ...), custom_call_target="tpu_custom_call" | custom-call | flops 58720256 | bytes 3670016 | tf_op jit(solution)/shard_map/last_products/pallas_call | solution.py:418
  (7 shorter events, 0.1 us)
Async XLA Ops:
  0.0 27.8 %copy-start = (bf16[1,1,28,128,128]{4,3,2,1,0:T(8,128)(2,1)S(1)}, bf16[1,1,28,128,128]{4,3,2,1,0:T(8,128)(2,1)}, u32[]{:S(2)}) copy-start(bf16[1,1,28,128,128]{4,3,2,1,0:T(8,128)(2,1)} %param.3) | copy-start | bytes 2752516
  0.0 26.1 %copy-start.1 = (s32[4,4,28]{2,1,0:T(4,128)S(1)}, s32[4,4,28]{2,1,0:T(4,128)}, u32[]{:S(2)}) copy-start(s32[4,4,28]{2,1,0:T(4,128)} %param.4) | copy-start | bytes 5380
  0.0 26.1 %copy-start.2 = (s32[4,4,28]{2,1,0:T(4,128)S(1)}, s32[4,4,28]{2,1,0:T(4,128)}, u32[]{:S(2)}) copy-start(s32[4,4,28]{2,1,0:T(4,128)} %param.5) | copy-start | bytes 5380
  0.0 14.6 %collective-permute-start = (bf16[28,128,128]{2,1,0:T(8,128)(2,1)}, bf16[28,128,128]{2,1,0:T(8,128)(2,1)S(1)}, u32[]{:S(2)}, u32[]{:S(2)}) collective-permute-start(bf16[28,128,128]{2,1,0:T(8,128)(2,1)} %bitcast.4), channel_id=1, source_target_pairs={{0,8},{1,17},{2,10},{3,19},{4,12},{5,21},{6,14},{7,23},{8,0},{9,25... | collective-permute-start | bytes 2752520 | tf_op jit(solution)/shard_map/ppermute | solution.py:366
  4.1 10.5 %collective-permute-start.1 = (bf16[14,128,128]{2,1,0:T(8,128)(2,1)S(1)}, bf16[14,128,128]{2,1,0:T(8,128)(2,1)S(1)}, u32[]{:S(2)}, u32[]{:S(2)}) collective-permute-start(bf16[14,128,128]{2,1,0:T(8,128)(2,1)S(1)} %slice_bitcast_fusion), channel_id=1, source_target_pairs={{0,2},{2,4},{3,1},{4,6},{5,3},{7,5},{8,10},{10,12},{11,9},{12,14},... | collective-permute-start | bytes 1376264 | tf_op jit(solution)/shard_map/ppermute | solution.py:358
  8.7 9.8 %collective-permute-start.2 = (bf16[14,128,128]{2,1,0:T(8,128)(2,1)S(1)}, bf16[14,128,128]{2,1,0:T(8,128)(2,1)S(1)}, u32[]{:S(2)}, u32[]{:S(2)}) collective-permute-start(bf16[14,128,128]{2,1,0:T(8,128)(2,1)S(1)} %slice.12), channel_id=1, source_target_pairs={{0,2},{2,4},{3,1},{4,6},{5,3},{7,5},{8,10},{10,12},{11,9},{12,14},... | collective-permute-start | bytes 1376264 | tf_op jit(solution)/shard_map/ppermute | solution.py:358
  14.6 14.9 %collective-permute-start.5 = (bf16[28,128,128]{2,1,0:T(8,128)(2,1)S(1)}, bf16[28,128,128]{2,1,0:T(8,128)(2,1)S(1)}, u32[]{:S(2)}, u32[]{:S(2)}) collective-permute-start(bf16[28,128,128]{2,1,0:T(8,128)(2,1)S(1)} %collective-permute-done.refs_1_.tile), channel_id=1, source_target_pairs={{0,1},{1,0},{2,3},{3,2},{4,5},{5,4},{6,7},{7,6},{8,9},{9,8},{10,11... | collective-permute-start | bytes 2752520 | tf_op jit(solution)/shard_map/ppermute | solution.py:367
  14.6 4.6 %collective-permute-start.3 = (bf16[14,128,128]{2,1,0:T(8,128)(2,1)S(1)}, bf16[14,128,128]{2,1,0:T(8,128)(2,1)S(1)}, u32[]{:S(2)}, u32[]{:S(2)}) collective-permute-start(bf16[14,128,128]{2,1,0:T(8,128)(2,1)S(1)} %collective-permute-done.1.refs_3_.refs_4_.refs_6_), channel_id=1, source_target_pairs={{2,4},{3,1},{4,6},{5,3},{10,12},{11,9},{12,14},{13,11},{18,20},{19... | collective-permute-start | bytes 1376264 | tf_op jit(solution)/shard_map/ppermute | solution.py:358
  15.4 8.6 %collective-permute-start.6 = (bf16[14,128,128]{2,1,0:T(8,128)(2,1)S(1)}, bf16[14,128,128]{2,1,0:T(8,128)(2,1)S(1)}, u32[]{:S(2)}, u32[]{:S(2)}) collective-permute-start(bf16[14,128,128]{2,1,0:T(8,128)(2,1)S(1)} %pick_half.1), channel_id=1, source_target_pairs={{8,24},{17,25},{10,26},{19,27},{12,28},{21,29},{14,30},{23,31},{0,... | collective-permute-start | bytes 1376264 | tf_op jit(solution)/shard_map/ppermute | solution.py:377
  18.5 8.6 %collective-permute-start.4 = (bf16[14,128,128]{2,1,0:T(8,128)(2,1)S(1)}, bf16[14,128,128]{2,1,0:T(8,128)(2,1)S(1)}, u32[]{:S(2)}, u32[]{:S(2)}) collective-permute-start(bf16[14,128,128]{2,1,0:T(8,128)(2,1)S(1)} %collective-permute-done.2.refs_4_.refs_5_.refs_7_), channel_id=1, source_target_pairs={{2,4},{3,1},{4,6},{5,3},{10,12},{11,9},{12,14},{13,11},{18,20},{19... | collective-permute-start | bytes 1376264 | tf_op jit(solution)/shard_map/ppermute | solution.py:358
  19.2 11.0 %collective-permute-start.8 = (bf16[14,128,128]{2,1,0:T(8,128)(2,1)S(1)}, bf16[14,128,128]{2,1,0:T(8,128)(2,1)S(1)}, u32[]{:S(2)}, u32[]{:S(2)}) collective-permute-start(bf16[14,128,128]{2,1,0:T(8,128)(2,1)S(1)} %collective-permute-done.3.refs_5_.refs_6_.refs_8_), channel_id=1, source_target_pairs={{3,1},{4,6},{11,9},{12,14},{19,17},{20,22},{27,25},{28,30}} | collective-permute-start | bytes 1376264 | tf_op jit(solution)/shard_map/ppermute | solution.py:358
  23.9 6.3 %collective-permute-start.7 = (bf16[14,128,128]{2,1,0:T(8,128)(2,1)S(1)}, bf16[14,128,128]{2,1,0:T(8,128)(2,1)S(1)}, u32[]{:S(2)}, u32[]{:S(2)}) collective-permute-start(bf16[14,128,128]{2,1,0:T(8,128)(2,1)S(1)} %collective-permute-done.6.refs_3_), channel_id=1, source_target_pairs={{0,1},{1,0},{2,3},{3,2},{4,5},{5,4},{6,7},{7,6},{8,9},{9,8},{10,11... | collective-permute-start | bytes 1376264 | tf_op jit(solution)/shard_map/ppermute | solution.py:378
  27.1 8.6 %collective-permute-start.10 = (bf16[14,128,128]{2,1,0:T(8,128)(2,1)S(1)}, bf16[14,128,128]{2,1,0:T(8,128)(2,1)S(1)}, u32[]{:S(2)}, u32[]{:S(2)}) collective-permute-start(bf16[14,128,128]{2,1,0:T(8,128)(2,1)S(1)} %collective-permute-done.4.refs_6_.refs_7_.refs_9_), channel_id=1, source_target_pairs={{3,1},{4,6},{11,9},{12,14},{19,17},{20,22},{27,25},{28,30}} | collective-permute-start | bytes 1376264 | tf_op jit(solution)/shard_map/ppermute | solution.py:358
  31.1 9.8 %collective-permute-start.9 = (f32[14,128,128]{2,1,0:T(8,128)S(1)}, f32[14,128,128]{2,1,0:T(8,128)S(1)}, u32[]{:S(2)}, u32[]{:S(2)}) collective-permute-start(f32[14,128,128]{2,1,0:T(8,128)S(1)} %get-tuple-element.8), channel_id=1, source_target_pairs={{0,1},{1,0},{2,3},{3,2},{4,5},{5,4},{6,7},{7,6},{8,9},{9,8},{10,11... | collective-permute-start | bytes 2752520 | tf_op jit(solution)/shard_map/ppermute | solution.py:416
  35.7 5.2 %collective-permute-start.11 = (bf16[14,128,128]{2,1,0:T(8,128)(2,1)S(1)}, bf16[14,128,128]{2,1,0:T(8,128)(2,1)S(1)}, u32[]{:S(2)}, u32[]{:S(2)}) collective-permute-start(bf16[14,128,128]{2,1,0:T(8,128)(2,1)S(1)} %collective-permute-done.10.refs_5_), channel_id=1, source_target_pairs={{0,1},{1,0},{2,3},{3,2},{4,5},{5,4},{6,7},{7,6},{8,9},{9,8},{10,11... | collective-permute-start | bytes 1376264 | tf_op jit(solution)/shard_map/ppermute | solution.py:417

commit v8 on v7

--- a/solution.py
+++ b/solution.py
@@ -67,6 +67,16 @@
                                 for p in (r ^ by, r ^ far)
                             )
                         )
+        return pairs
+
+    def last_pairs(self):
+        pairs = []
+        for a in range(self.grid):
+            for l in (a - self.stages, a + self.stages):
+                if self.whole and not 0 <= l < self.grid:
+                    continue
+                if self.shift(a, l % self.grid) == l - a:
+                    pairs += [(a * 2, a * 2 + 1), (a * 2 + 1, a * 2)]
         return pairs
 
     def taken(self, a, layer, stage):
@@ -414,7 +424,7 @@
         name="middle_products",
     )(lists, total, *lefts, *before, first)
     received = lax.ppermute(other, "layer", swap)
-    second_swapped = lax.ppermute(second, "layer", swap)
+    second_swapped = lax.ppermute(second, ("col", "layer"), plan.last_pairs())
     square = pl.pallas_call(
         functools.partial(last_kernel, plan, len(lefts), bounds[1]),
         out_shape=jax.ShapeDtypeStruct((share, size, size), jnp.bfloat16),

time: 43.6 us -> 45.5 us (1.044)
  starting transfers between devices: 25.4 us -> 27.3 us
    ppermute x1, starting transfers between devices: 3.74 us -> 5.64 us  [on_device(): second_swapped = lax.ppermute(second, ('col', 'layer'), plan.last_pairs())]
where the time goes in v8:
time: 45.5 us; the launch traced here: 44.7 us
  starting transfers between devices  27.3 us (60%)
  waiting for transfers between devices  8.93 us (20%)
  Pallas kernels  6.11 us (13%)
  local copies, waits for them, and re-layouts  2.15 us (5%)
    ppermute x6, starting transfers between devices, on_device(): arrived.append(lax.ppermute(part, ('col', 'layer'), pairs))  9.73 us
    ppermute x1, starting transfers between devices, on_device(): second_swapped = lax.ppermute(second, ('col', 'layer'), plan.last_pairs())  5.64 us
    ppermute x1, starting transfers between devices, on_device(): received = lax.ppermute(other, 'layer', swap)  4.64 us
    ppermute x1, waiting for transfers between devices, on_device(): far = lax.ppermute(sent, everywhere, plan.far_pairs())  4.03 us
    ppermute x1, starting transfers between devices, on_device(): near.append(lax.ppermute(own, everywhere, plan.near_pairs(bys)))  3.03 us
    ppermute x1, waiting for transfers between devices, on_device(): near.append(lax.ppermute(own, everywhere, plan.near_pairs(bys)))  2.43 us
    ppermute x1, starting transfers between devices, on_device(): far_swapped = lax.ppermute(far, 'layer', swap)  2.15 us
    slice x2, local copies, waits for them, and re-layouts, on_device(): (lax.optimization_barrier(own) if i else own)[i:j]  2.13 us
  transfers between devices with their start and end apart: 12, of which 4 were waited for; matrix products, arithmetic and copies ran while one was open for 5% of the time, Pallas kernels for 10%

profile of v8, /device:TPU:0, one launch (start us, length us, event | category | flops | bytes accessed | tf_op | source)
XLA Modules:
  0.0 44.7 jit_solution(6207089929410305056)
XLA Ops:
  0.0 3.0 %collective-permute-start = (bf16[28,128,128]{2,1,0:T(8,128)(2,1)}, bf16[28,128,128]{2,1,0:T(8,128)(2,1)S(1)}, u32[]{:S(2)}, u32[]{:S(2)}) collective-permute-start(bf16[28,128,128]{2,1,0:T(8,128)(2,1)} %bitcast.4), channel_id=1, source_target_pairs={{0,8},{1,17},{2,10},{3,19},{4,12},{5,21},{6,14},{7,23},{8,0},{9,25... | collective-permute-start | bytes 2752520 | tf_op jit(solution)/shard_map/ppermute | solution.py:376
  3.0 1.1 %slice_bitcast_fusion = bf16[14,128,128]{2,1,0:T(8,128)(2,1)S(1)} fusion(bf16[1,1,28,128,128]{4,3,2,1,0:T(8,128)(2,1)} %param.3), kind=kLoop, calls=%fused_computation | loop fusion | bytes 917504 | tf_op jit(solution)/shard_map/slice | solution.py:338
  4.1 3.5 %collective-permute-start.1 = (bf16[14,128,128]{2,1,0:T(8,128)(2,1)S(1)}, bf16[14,128,128]{2,1,0:T(8,128)(2,1)S(1)}, u32[]{:S(2)}, u32[]{:S(2)}) collective-permute-start(bf16[14,128,128]{2,1,0:T(8,128)(2,1)S(1)} %slice_bitcast_fusion), channel_id=1, source_target_pairs={{0,2},{2,4},{3,1},{4,6},{5,3},{7,5},{8,10},{10,12},{11,9},{12,14},... | collective-permute-start | bytes 1376264 | tf_op jit(solution)/shard_map/ppermute | solution.py:368
  7.6 1.1 %slice.12 = bf16[14,128,128]{2,1,0:T(8,128)(2,1)S(1)} slice(bf16[28,128,128]{2,1,0:T(8,128)(2,1)} %bitcast.5), slice={[14:28], [0:128], [0:128]} | slice | bytes 917504 | tf_op jit(solution)/shard_map/slice | solution.py:338
  8.7 3.5 %collective-permute-start.2 = (bf16[14,128,128]{2,1,0:T(8,128)(2,1)S(1)}, bf16[14,128,128]{2,1,0:T(8,128)(2,1)S(1)}, u32[]{:S(2)}, u32[]{:S(2)}) collective-permute-start(bf16[14,128,128]{2,1,0:T(8,128)(2,1)S(1)} %slice.12), channel_id=1, source_target_pairs={{0,2},{2,4},{3,1},{4,6},{5,3},{7,5},{8,10},{10,12},{11,9},{12,14},... | collective-permute-start | bytes 1376264 | tf_op jit(solution)/shard_map/ppermute | solution.py:368
  12.2 2.4 %collective-permute-done.refs_1_.tile = bf16[28,128,128]{2,1,0:T(8,128)(2,1)S(1)} collective-permute-done((bf16[28,128,128]{2,1,0:T(8,128)(2,1)}, bf16[28,128,128]{2,1,0:T(8,128)(2,1)S(1)}, u32[]{:S(2)}, u32[]{:S(2)}) %collective-permute-start) | collective-permute-done | bytes 917536 | tf_op jit(solution)/shard_map/ppermute | solution.py:376
  14.6 0.0 collective-permute-start.5
  14.6 0.0 collective-permute-done.1.refs_3_.refs_4_.refs_6_
  14.6 0.7 %collective-permute-start.3 = (bf16[14,128,128]{2,1,0:T(8,128)(2,1)S(1)}, bf16[14,128,128]{2,1,0:T(8,128)(2,1)S(1)}, u32[]{:S(2)}, u32[]{:S(2)}) collective-permute-start(bf16[14,128,128]{2,1,0:T(8,128)(2,1)S(1)} %collective-permute-done.1.refs_3_.refs_4_.refs_6_), channel_id=1, source_target_pairs={{2,4},{3,1},{4,6},{5,3},{10,12},{11,9},{12,14},{13,11},{18,20},{19... | collective-permute-start | bytes 1376264 | tf_op jit(solution)/shard_map/ppermute | solution.py:368
  15.4 2.1 %collective-permute-start.6 = (bf16[14,128,128]{2,1,0:T(8,128)(2,1)S(1)}, bf16[14,128,128]{2,1,0:T(8,128)(2,1)S(1)}, u32[]{:S(2)}, u32[]{:S(2)}) collective-permute-start(bf16[14,128,128]{2,1,0:T(8,128)(2,1)S(1)} %pick_half.1), channel_id=1, source_target_pairs={{8,24},{17,25},{10,26},{19,27},{12,28},{21,29},{14,30},{23,31},{0,... | collective-permute-start | bytes 1376264 | tf_op jit(solution)/shard_map/ppermute | solution.py:387
  17.5 1.0 %collective-permute-done.2.refs_4_.refs_5_.refs_7_ = bf16[14,128,128]{2,1,0:T(8,128)(2,1)S(1)} collective-permute-done((bf16[14,128,128]{2,1,0:T(8,128)(2,1)S(1)}, bf16[14,128,128]{2,1,0:T(8,128)(2,1)S(1)}, u32[]{:S(2)}, u32[]{:S(2)}) %collective-permute-start.2) | collective-permute-done | bytes 458784 | tf_op jit(solution)/shard_map/ppermute | solution.py:368
  18.5 0.7 %collective-permute-start.4 = (bf16[14,128,128]{2,1,0:T(8,128)(2,1)S(1)}, bf16[14,128,128]{2,1,0:T(8,128)(2,1)S(1)}, u32[]{:S(2)}, u32[]{:S(2)}) collective-permute-start(bf16[14,128,128]{2,1,0:T(8,128)(2,1)S(1)} %collective-permute-done.2.refs_4_.refs_5_.refs_7_), channel_id=1, source_target_pairs={{2,4},{3,1},{4,6},{5,3},{10,12},{11,9},{12,14},{13,11},{18,20},{19... | collective-permute-start | bytes 1376264 | tf_op jit(solution)/shard_map/ppermute | solution.py:368
  19.2 0.0 collective-permute-done.3.refs_5_.refs_6_.refs_8_
  19.2 0.7 %collective-permute-start.8 = (bf16[14,128,128]{2,1,0:T(8,128)(2,1)S(1)}, bf16[14,128,128]{2,1,0:T(8,128)(2,1)S(1)}, u32[]{:S(2)}, u32[]{:S(2)}) collective-permute-start(bf16[14,128,128]{2,1,0:T(8,128)(2,1)S(1)} %collective-permute-done.3.refs_5_.refs_6_.refs_8_), channel_id=1, source_target_pairs={{3,1},{4,6},{11,9},{12,14},{19,17},{20,22},{27,25},{28,30}} | collective-permute-start | bytes 1376264 | tf_op jit(solution)/shard_map/ppermute | solution.py:368
  19.9 4.0 %collective-permute-done.6.refs_3_ = bf16[14,128,128]{2,1,0:T(8,128)(2,1)S(1)} collective-permute-done((bf16[14,128,128]{2,1,0:T(8,128)(2,1)S(1)}, bf16[14,128,128]{2,1,0:T(8,128)(2,1)S(1)}, u32[]{:S(2)}, u32[]{:S(2)}) %collective-permute-start.6) | collective-permute-done | bytes 458784 | tf_op jit(solution)/shard_map/ppermute | solution.py:387
  23.9 2.1 %collective-permute-start.7 = (bf16[14,128,128]{2,1,0:T(8,128)(2,1)S(1)}, bf16[14,128,128]{2,1,0:T(8,128)(2,1)S(1)}, u32[]{:S(2)}, u32[]{:S(2)}) collective-permute-start(bf16[14,128,128]{2,1,0:T(8,128)(2,1)S(1)} %collective-permute-done.6.refs_3_), channel_id=1, source_target_pairs={{0,1},{1,0},{2,3},{3,2},{4,5},{5,4},{6,7},{7,6},{8,9},{9,8},{10,11... | collective-permute-start | bytes 1376264 | tf_op jit(solution)/shard_map/ppermute | solution.py:388
  26.1 0.0 copy-done.2
  26.1 1.0 %list_products.1.pairs = s32[5,128]{1,0:T(8,128)S(1)} custom-call(s32[4,4,28]{2,1,0:T(4,128)S(1)} %convert_add_fusion.slot_keys), custom_call_target="tpu_custom_call" | custom-call | bytes 1835008 | tf_op jit(solution)/shard_map/list_products/pallas_call | solution.py:353
  27.1 0.0 collective-permute-done.4.refs_6_.refs_7_.refs_9_
  27.1 0.7 %collective-permute-start.10 = (bf16[14,128,128]{2,1,0:T(8,128)(2,1)S(1)}, bf16[14,128,128]{2,1,0:T(8,128)(2,1)S(1)}, u32[]{:S(2)}, u32[]{:S(2)}) collective-permute-start(bf16[14,128,128]{2,1,0:T(8,128)(2,1)S(1)} %collective-permute-done.4.refs_6_.refs_7_.refs_9_), channel_id=1, source_target_pairs={{3,1},{4,6},{11,9},{12,14},{19,17},{20,22},{27,25},{28,30}} | collective-permute-start | bytes 1376264 | tf_op jit(solution)/shard_map/ppermute | solution.py:368
  27.8 1.8 %early_products.1.total = f32[29,128,128]{2,1,0:T(8,128)S(1)} custom-call(s32[5,128]{1,0:T(8,128)S(1)} %list_products.1.pairs, bf16[28,128,128]{2,1,0:T(8,128)(2,1)S(1)} %bitcast.6, bf16[28,128,128]{2,1,0:T(8,128)(2,1)S(1)} %collective-permute-done.refs_1_.tile, bf16[28,128,128]{2,1,0:T(8,128)(2,1)S(1)} %bitcast.7, ...), custom_call_target="tpu_custom_call" | custom-call | flops 352321536 | bytes 5505024 | tf_op jit(solution)/shard_map/early_products/pallas_call | solution.py:394
  29.6 0.0 collective-permute-done.5.refs_2_
  29.6 0.7 %second_products.1.total = f32[29,128,128]{2,1,0:T(8,128)S(1)} custom-call(s32[5,128]{1,0:T(8,128)S(1)} %list_products.1.pairs, f32[29,128,128]{2,1,0:T(8,128)S(1)} %early_products.1.total, bf16[28,128,128]{2,1,0:T(8,128)(2,1)S(1)} %bitcast.8, bf16[28,128,128]{2,1,0:T(8,128)(2,1)S(1)} %collective-permute-done.refs_1_.tile, ...), custom_call_target="tpu_custom_call", output_to_operand_aliasing={{}: (1, {})} | custom-call | flops 117440512 | bytes 1835008 | tf_op jit(solution)/shard_map/second_products/pallas_call | solution.py:403
  30.2 0.0 collective-permute-done.8.refs_10_
  30.2 0.0 collective-permute-done.7.refs_4_
  30.3 0.8 %middle_products.1 = (f32[29,128,128]{2,1,0:T(8,128)S(1)}, f32[14,128,128]{2,1,0:T(8,128)S(1)}, f32[14,128,128]{2,1,0:T(8,128)S(1)}) custom-call(s32[5,128]{1,0:T(8,128)S(1)} %list_products.1.pairs, f32[29,128,128]{2,1,0:T(8,128)S(1)} %second_products.1.total, bf16[28,128,128]{2,1,0:T(8,128)(2,1)S(1)} %bitcast.10, ...), custom_call_target="tpu_custom_call", output_to_operand_aliasing={{0}: (1, {})} | custom-call | flops 352321536 | bytes 5505024 | tf_op jit(solution)/shard_map/middle_products/pallas_call | solution.py:416
  31.1 4.6 %collective-permute-start.9 = (f32[14,128,128]{2,1,0:T(8,128)S(1)}, f32[14,128,128]{2,1,0:T(8,128)S(1)}, u32[]{:S(2)}, u32[]{:S(2)}) collective-permute-start(f32[14,128,128]{2,1,0:T(8,128)S(1)} %get-tuple-element.8), channel_id=1, source_target_pairs={{0,1},{1,0},{2,3},{3,2},{4,5},{5,4},{6,7},{7,6},{8,9},{9,8},{10,11... | collective-permute-start | bytes 2752520 | tf_op jit(solution)/shard_map/ppermute | solution.py:426
  35.7 0.0 collective-permute-done.10.refs_5_
  35.7 5.6 %collective-permute-start.11 = (bf16[14,128,128]{2,1,0:T(8,128)(2,1)S(1)}, bf16[14,128,128]{2,1,0:T(8,128)(2,1)S(1)}, u32[]{:S(2)}, u32[]{:S(2)}) collective-permute-start(bf16[14,128,128]{2,1,0:T(8,128)(2,1)S(1)} %collective-permute-done.10.refs_5_), channel_id=1, source_target_pairs={{0,1},{1,0},{6,7},{7,6},{8,9},{9,8},{14,15},{15,14},{16,17},{17,16... | collective-permute-start | bytes 1376264 | tf_op jit(solution)/shard_map/ppermute | solution.py:427
  41.4 1.4 %collective-permute-done.11.refs_6_ = bf16[14,128,128]{2,1,0:T(8,128)(2,1)S(1)} collective-permute-done((bf16[14,128,128]{2,1,0:T(8,128)(2,1)S(1)}, bf16[14,128,128]{2,1,0:T(8,128)(2,1)S(1)}, u32[]{:S(2)}, u32[]{:S(2)}) %collective-permute-start.11) | collective-permute-done | bytes 458784 | tf_op jit(solution)/shard_map/ppermute | solution.py:427
  42.8 0.0 collective-permute-done.9.received
  42.8 1.9 %last_products.1 = bf16[14,128,128]{2,1,0:T(8,128)(2,1)} custom-call(s32[5,128]{1,0:T(8,128)S(1)} %list_products.1.pairs, f32[14,128,128]{2,1,0:T(8,128)S(1)} %get-tuple-element.7.mine, f32[14,128,128]{2,1,0:T(8,128)S(1)} %collective-permute-done.9.received, bf16[28,128,128]{2,1,0:T(8,128)(2,1)S(1)} %bitcast.12, ...), custom_call_target="tpu_custom_call" | custom-call | flops 58720256 | bytes 3670016 | tf_op jit(solution)/shard_map/last_products/pallas_call | solution.py:428
  (7 shorter events, 0.1 us)
Async XLA Ops:
  0.0 27.8 %copy-start = (bf16[1,1,28,128,128]{4,3,2,1,0:T(8,128)(2,1)S(1)}, bf16[1,1,28,128,128]{4,3,2,1,0:T(8,128)(2,1)}, u32[]{:S(2)}) copy-start(bf16[1,1,28,128,128]{4,3,2,1,0:T(8,128)(2,1)} %param.3) | copy-start | bytes 2752516
  0.0 26.1 %copy-start.1 = (s32[4,4,28]{2,1,0:T(4,128)S(1)}, s32[4,4,28]{2,1,0:T(4,128)}, u32[]{:S(2)}) copy-start(s32[4,4,28]{2,1,0:T(4,128)} %param.4) | copy-start | bytes 5380
  0.0 26.1 %copy-start.2 = (s32[4,4,28]{2,1,0:T(4,128)S(1)}, s32[4,4,28]{2,1,0:T(4,128)}, u32[]{:S(2)}) copy-start(s32[4,4,28]{2,1,0:T(4,128)} %param.5) | copy-start | bytes 5380
  0.0 14.6 %collective-permute-start = (bf16[28,128,128]{2,1,0:T(8,128)(2,1)}, bf16[28,128,128]{2,1,0:T(8,128)(2,1)S(1)}, u32[]{:S(2)}, u32[]{:S(2)}) collective-permute-start(bf16[28,128,128]{2,1,0:T(8,128)(2,1)} %bitcast.4), channel_id=1, source_target_pairs={{0,8},{1,17},{2,10},{3,19},{4,12},{5,21},{6,14},{7,23},{8,0},{9,25... | collective-permute-start | bytes 2752520 | tf_op jit(solution)/shard_map/ppermute | solution.py:376
  4.1 10.5 %collective-permute-start.1 = (bf16[14,128,128]{2,1,0:T(8,128)(2,1)S(1)}, bf16[14,128,128]{2,1,0:T(8,128)(2,1)S(1)}, u32[]{:S(2)}, u32[]{:S(2)}) collective-permute-start(bf16[14,128,128]{2,1,0:T(8,128)(2,1)S(1)} %slice_bitcast_fusion), channel_id=1, source_target_pairs={{0,2},{2,4},{3,1},{4,6},{5,3},{7,5},{8,10},{10,12},{11,9},{12,14},... | collective-permute-start | bytes 1376264 | tf_op jit(solution)/shard_map/ppermute | solution.py:368
  8.7 9.8 %collective-permute-start.2 = (bf16[14,128,128]{2,1,0:T(8,128)(2,1)S(1)}, bf16[14,128,128]{2,1,0:T(8,128)(2,1)S(1)}, u32[]{:S(2)}, u32[]{:S(2)}) collective-permute-start(bf16[14,128,128]{2,1,0:T(8,128)(2,1)S(1)} %slice.12), channel_id=1, source_target_pairs={{0,2},{2,4},{3,1},{4,6},{5,3},{7,5},{8,10},{10,12},{11,9},{12,14},... | collective-permute-start | bytes 1376264 | tf_op jit(solution)/shard_map/ppermute | solution.py:368
  14.6 14.9 %collective-permute-start.5 = (bf16[28,128,128]{2,1,0:T(8,128)(2,1)S(1)}, bf16[28,128,128]{2,1,0:T(8,128)(2,1)S(1)}, u32[]{:S(2)}, u32[]{:S(2)}) collective-permute-start(bf16[28,128,128]{2,1,0:T(8,128)(2,1)S(1)} %collective-permute-done.refs_1_.tile), channel_id=1, source_target_pairs={{0,1},{1,0},{2,3},{3,2},{4,5},{5,4},{6,7},{7,6},{8,9},{9,8},{10,11... | collective-permute-start | bytes 2752520 | tf_op jit(solution)/shard_map/ppermute | solution.py:377
  14.6 4.6 %collective-permute-start.3 = (bf16[14,128,128]{2,1,0:T(8,128)(2,1)S(1)}, bf16[14,128,128]{2,1,0:T(8,128)(2,1)S(1)}, u32[]{:S(2)}, u32[]{:S(2)}) collective-permute-start(bf16[14,128,128]{2,1,0:T(8,128)(2,1)S(1)} %collective-permute-done.1.refs_3_.refs_4_.refs_6_), channel_id=1, source_target_pairs={{2,4},{3,1},{4,6},{5,3},{10,12},{11,9},{12,14},{13,11},{18,20},{19... | collective-permute-start | bytes 1376264 | tf_op jit(solution)/shard_map/ppermute | solution.py:368
  15.4 8.6 %collective-permute-start.6 = (bf16[14,128,128]{2,1,0:T(8,128)(2,1)S(1)}, bf16[14,128,128]{2,1,0:T(8,128)(2,1)S(1)}, u32[]{:S(2)}, u32[]{:S(2)}) collective-permute-start(bf16[14,128,128]{2,1,0:T(8,128)(2,1)S(1)} %pick_half.1), channel_id=1, source_target_pairs={{8,24},{17,25},{10,26},{19,27},{12,28},{21,29},{14,30},{23,31},{0,... | collective-permute-start | bytes 1376264 | tf_op jit(solution)/shard_map/ppermute | solution.py:387
  18.5 8.6 %collective-permute-start.4 = (bf16[14,128,128]{2,1,0:T(8,128)(2,1)S(1)}, bf16[14,128,128]{2,1,0:T(8,128)(2,1)S(1)}, u32[]{:S(2)}, u32[]{:S(2)}) collective-permute-start(bf16[14,128,128]{2,1,0:T(8,128)(2,1)S(1)} %collective-permute-done.2.refs_4_.refs_5_.refs_7_), channel_id=1, source_target_pairs={{2,4},{3,1},{4,6},{5,3},{10,12},{11,9},{12,14},{13,11},{18,20},{19... | collective-permute-start | bytes 1376264 | tf_op jit(solution)/shard_map/ppermute | solution.py:368
  19.2 11.0 %collective-permute-start.8 = (bf16[14,128,128]{2,1,0:T(8,128)(2,1)S(1)}, bf16[14,128,128]{2,1,0:T(8,128)(2,1)S(1)}, u32[]{:S(2)}, u32[]{:S(2)}) collective-permute-start(bf16[14,128,128]{2,1,0:T(8,128)(2,1)S(1)} %collective-permute-done.3.refs_5_.refs_6_.refs_8_), channel_id=1, source_target_pairs={{3,1},{4,6},{11,9},{12,14},{19,17},{20,22},{27,25},{28,30}} | collective-permute-start | bytes 1376264 | tf_op jit(solution)/shard_map/ppermute | solution.py:368
  23.9 6.3 %collective-permute-start.7 = (bf16[14,128,128]{2,1,0:T(8,128)(2,1)S(1)}, bf16[14,128,128]{2,1,0:T(8,128)(2,1)S(1)}, u32[]{:S(2)}, u32[]{:S(2)}) collective-permute-start(bf16[14,128,128]{2,1,0:T(8,128)(2,1)S(1)} %collective-permute-done.6.refs_3_), channel_id=1, source_target_pairs={{0,1},{1,0},{2,3},{3,2},{4,5},{5,4},{6,7},{7,6},{8,9},{9,8},{10,11... | collective-permute-start | bytes 1376264 | tf_op jit(solution)/shard_map/ppermute | solution.py:388
  27.1 8.6 %collective-permute-start.10 = (bf16[14,128,128]{2,1,0:T(8,128)(2,1)S(1)}, bf16[14,128,128]{2,1,0:T(8,128)(2,1)S(1)}, u32[]{:S(2)}, u32[]{:S(2)}) collective-permute-start(bf16[14,128,128]{2,1,0:T(8,128)(2,1)S(1)} %collective-permute-done.4.refs_6_.refs_7_.refs_9_), channel_id=1, source_target_pairs={{3,1},{4,6},{11,9},{12,14},{19,17},{20,22},{27,25},{28,30}} | collective-permute-start | bytes 1376264 | tf_op jit(solution)/shard_map/ppermute | solution.py:368
  31.1 11.7 %collective-permute-start.9 = (f32[14,128,128]{2,1,0:T(8,128)S(1)}, f32[14,128,128]{2,1,0:T(8,128)S(1)}, u32[]{:S(2)}, u32[]{:S(2)}) collective-permute-start(f32[14,128,128]{2,1,0:T(8,128)S(1)} %get-tuple-element.8), channel_id=1, source_target_pairs={{0,1},{1,0},{2,3},{3,2},{4,5},{5,4},{6,7},{7,6},{8,9},{9,8},{10,11... | collective-permute-start | bytes 2752520 | tf_op jit(solution)/shard_map/ppermute | solution.py:426
  35.7 7.1 %collective-permute-start.11 = (bf16[14,128,128]{2,1,0:T(8,128)(2,1)S(1)}, bf16[14,128,128]{2,1,0:T(8,128)(2,1)S(1)}, u32[]{:S(2)}, u32[]{:S(2)}) collective-permute-start(bf16[14,128,128]{2,1,0:T(8,128)(2,1)S(1)} %collective-permute-done.10.refs_5_), channel_id=1, source_target_pairs={{0,1},{1,0},{6,7},{7,6},{8,9},{9,8},{14,15},{15,14},{16,17},{17,16... | collective-permute-start | bytes 1376264 | tf_op jit(solution)/shard_map/ppermute | solution.py:427

commit v9 on v7

--- a/solution.py
+++ b/solution.py
@@ -194,9 +194,9 @@
     def __init__(self, plan, refs):
         near = plan.grid // 2 - 1
         self.far = plan.grid - 1
-        self.own, self.near = refs[0], refs[1 : 1 + near]
-        self.swapped = refs[1 + near : 1 + 2 * near]
-        self.halves = refs[1 + 2 * near :]
+        self.own, refs = refs[:CHUNKS], refs[CHUNKS:]
+        self.near, refs = refs[:near], refs[near:]
+        self.swapped, self.halves = refs[:near], refs[near:]
 
     def all(self, by, layer):
         yield from self.direct(by, layer)
@@ -204,7 +204,7 @@
         yield from self.opposite(by, layer)
 
     def direct(self, by, layer):
-        yield by == 0, blocks_of([self.own])
+        yield by == 0, blocks_of(self.own)
         for k, tile in enumerate(self.near):
             yield by == 2 * k + 1 + layer, blocks_of([tile])
 
@@ -242,7 +242,7 @@
 
 def early_kernel(plan, n, parts, pairs, *refs):
     lefts = Lefts(plan, refs[:n])
-    rights, (acc,) = stages_of(parts[:-1], refs[n:])
+    rights, (acc,) = stages_of(parts[:-2], refs[n:])
     a, b, layer = place()
     acc[...] = jnp.zeros_like(acc)
     for stage, right in enumerate(rights):
@@ -260,8 +260,24 @@
     for stage, right in enumerate(rights):
         by = b ^ plan.taken(a, layer, stage)[0]
         count = pairs[stage, pairs.shape[1] - 1]
-        cases = lefts.indirect(by, layer)
+        cases = list(lefts.indirect(by, layer))
+        if stage == plan.stages - 1:
+            cases += lefts.direct(by, layer)
         run_jobs(cases, count, pairs, stage, blocks_of(right), acc)
+
+
+def split_kernel(tile, first, second, sem):
+    size = first.shape[0]
+    copies = [
+        pltpu.make_async_copy(tile.at[pl.ds(0, size)], first, sem.at[0]),
+        pltpu.make_async_copy(
+            tile.at[pl.ds(size, second.shape[0])], second, sem.at[1]
+        ),
+    ]
+    for copy in copies:
+        copy.start()
+    for copy in copies:
+        copy.wait()
 
 
 def pick_kernel(tile, half):
@@ -324,10 +340,6 @@
     slots, size = own.shape[0], own.shape[1]
     share = slots // 2
     bounds = [slots * i // CHUNKS for i in range(CHUNKS + 1)]
-    held = [
-        (lax.optimization_barrier(own) if i else own)[i:j]
-        for i, j in zip(bounds[:-1], bounds[1:])
-    ]
     scalars = pl.BlockSpec(memory_space=pltpu.SMEM)
     vmem = pl.BlockSpec(memory_space=pltpu.VMEM)
     compiler_params = pltpu.CompilerParams(vmem_limit_bytes=GRANT)
@@ -340,6 +352,19 @@
             transcendentals=0,
         )
 
+    held = pl.pallas_call(
+        split_kernel,
+        out_shape=[
+            jax.ShapeDtypeStruct((j - i, size, size), own.dtype)
+            for i, j in zip(bounds[:-1], bounds[1:])
+        ],
+        in_specs=[pl.BlockSpec(memory_space=pl.ANY)],
+        out_specs=[vmem] * CHUNKS,
+        scratch_shapes=[pltpu.SemaphoreType.DMA((CHUNKS,))],
+        compiler_params=compiler_params,
+        cost_estimate=cost(0, 2),
+        name="split_tile",
+    )(own)
     lists = pl.pallas_call(
         functools.partial(list_kernel, plan, bounds),
         out_shape=jax.ShapeDtypeStruct((plan.stages + CHUNKS, LANES), jnp.int32),
@@ -350,7 +375,8 @@
         cost_estimate=cost(0, 2),
         name="list_products",
     )(2 * slot_rows + (slot_cols != slot_rows))
-    rights = [[own]]
+    own_parts = list(held)
+    rights = [own_parts]
     for stage in range(1, plan.stages + 1):
         pairs = plan.hop_pairs(stage)
         arrived = []
@@ -376,7 +402,7 @@
     )(near[0])
     far = lax.ppermute(sent, everywhere, plan.far_pairs())
     far_swapped = lax.ppermute(far, "layer", swap)
-    direct = [own, *near]
+    direct = [*own_parts, *near]
     lefts = [*direct, *swapped, far, far_swapped]
     parts = [len(r) for r in rights]
     running = jax.ShapeDtypeStruct((slots + 1, size, size), jnp.float32)
@@ -384,12 +410,12 @@
     total = pl.pallas_call(
         functools.partial(early_kernel, plan, len(direct), parts),
         out_shape=running,
-        in_specs=[scalars] + [vmem] * (len(direct) + len(before)),
+        in_specs=[scalars] + [vmem] * (len(direct) + len(before) - parts[-2]),
         out_specs=vmem,
         compiler_params=compiler_params,
         cost_estimate=cost(slots * plan.stages, 2 * plan.stages),
         name="early_products",
-    )(lists, *direct, *before)
+    )(lists, *direct, *before[: -parts[-2]])
     total = pl.pallas_call(
         functools.partial(second_kernel, plan, len(direct) + len(swapped), parts),
         out_shape=running,

time: 43.6 us -> 43.5 us (level)
  local copies, waits for them, and re-layouts: 2.15 us -> 1.22 us
  Pallas kernels: 6.11 us -> 6.9 us
    slice x2 -> x0, local copies, waits for them, and re-layouts: 2.13 us -> none  [on_device(): (lax.optimization_barrier(own) if i else own)[i:j]]
    unnamed x6, local copies, waits for them, and re-layouts: 0.01 us -> 1.22 us
    ppermute x6, waiting for transfers between devices: 1.04 us -> 1.74 us  [on_device(): arrived.append(lax.ppermute(part, ('col', 'layer'), pairs))]
    ppermute x1, waiting for transfers between devices: 4.03 us -> 3.34 us  [on_device(): far = lax.ppermute(sent, everywhere, plan.far_pairs())]
    pallas_call x0 -> x1, Pallas kernels: none -> 0.56 us  [on_device(): pl.pallas_call(split_kernel, out_shape=[jax.ShapeDtypeStruct((j - i, size...]
  transfers between devices with their start and end apart: 12 -> 12, of which waited for: 4 -> 4; matrix products, arithmetic and copies ran while one was open for 5% -> 0% of each run, Pallas kernels for 10% -> 12%
where the time goes in v9:
time: 43.5 us; the launch traced here: 42.7 us
  starting transfers between devices  25.1 us (58%)
  waiting for transfers between devices  9.32 us (21%)
  Pallas kernels  6.9 us (16%)
  local copies, waits for them, and re-layouts  1.22 us (3%)
    ppermute x6, starting transfers between devices, on_device(): arrived.append(lax.ppermute(part, ('col', 'layer'), pairs))  9.73 us
    ppermute x1, starting transfers between devices, on_device(): received = lax.ppermute(other, 'layer', swap)  4.43 us
    ppermute x1, starting transfers between devices, on_device(): second_swapped = lax.ppermute(second, 'layer', swap)  3.74 us
    ppermute x1, waiting for transfers between devices, on_device(): far = lax.ppermute(sent, everywhere, plan.far_pairs())  3.34 us
    ppermute x1, starting transfers between devices, on_device(): near.append(lax.ppermute(own, everywhere, plan.near_pairs(bys)))  2.97 us
    ppermute x1, waiting for transfers between devices, on_device(): near.append(lax.ppermute(own, everywhere, plan.near_pairs(bys)))  2.79 us
    ppermute x1, starting transfers between devices, on_device(): far_swapped = lax.ppermute(far, 'layer', swap)  2.15 us
    ppermute x1, starting transfers between devices, on_device(): far = lax.ppermute(sent, everywhere, plan.far_pairs())  2.12 us
  transfers between devices with their start and end apart: 12, of which 4 were waited for; matrix products, arithmetic and copies ran while one was open for 0% of the time, Pallas kernels for 12%

profile of v9, /device:TPU:0, one launch (start us, length us, event | category | flops | bytes accessed | tf_op | source)
XLA Modules:
  0.0 42.7 jit_solution(14295159177447742664)
XLA Ops:
  0.0 3.0 %collective-permute-start = (bf16[28,128,128]{2,1,0:T(8,128)(2,1)}, bf16[28,128,128]{2,1,0:T(8,128)(2,1)S(1)}, u32[]{:S(2)}, u32[]{:S(2)}) collective-permute-start(bf16[28,128,128]{2,1,0:T(8,128)(2,1)} %bitcast.2), channel_id=1, source_target_pairs={{0,8},{1,17},{2,10},{3,19},{4,12},{5,21},{6,14},{7,23},{8,0},{9,25... | collective-permute-start | bytes 2752520 | tf_op jit(solution)/shard_map/ppermute | solution.py:392
  3.0 1.2 %copy-done = bf16[1,1,28,128,128]{4,3,2,1,0:T(8,128)(2,1)S(1)} copy-done((bf16[1,1,28,128,128]{4,3,2,1,0:T(8,128)(2,1)S(1)}, bf16[1,1,28,128,128]{4,3,2,1,0:T(8,128)(2,1)}, u32[]{:S(2)}) %copy-start) | copy-done | bytes 917528
  4.2 0.6 %split_tile.1 = (bf16[14,128,128]{2,1,0:T(8,128)(2,1)S(1)}, bf16[14,128,128]{2,1,0:T(8,128)(2,1)S(1)}) custom-call(bf16[28,128,128]{2,1,0:T(8,128)(2,1)S(1)} %bitcast.3), custom_call_target="tpu_custom_call" | custom-call | bytes 1835008 | tf_op jit(solution)/shard_map/split_tile/pallas_call | solution.py:355
  4.8 3.5 %collective-permute-start.1 = (bf16[14,128,128]{2,1,0:T(8,128)(2,1)S(1)}, bf16[14,128,128]{2,1,0:T(8,128)(2,1)S(1)}, u32[]{:S(2)}, u32[]{:S(2)}) collective-permute-start(bf16[14,128,128]{2,1,0:T(8,128)(2,1)S(1)} %get-tuple-element.9.refs_0_.refs_3_.refs_4_.refs_6_), channel_id=1, source_target_pairs={{0,2},{2,4},{3,1},{4,6},{5,3},{7,5},{8,10},{10,12},{11,9},{12,14},... | collective-permute-start | bytes 1376264 | tf_op jit(solution)/shard_map/ppermute | solution.py:384
  8.3 3.5 %collective-permute-start.2 = (bf16[14,128,128]{2,1,0:T(8,128)(2,1)S(1)}, bf16[14,128,128]{2,1,0:T(8,128)(2,1)S(1)}, u32[]{:S(2)}, u32[]{:S(2)}) collective-permute-start(bf16[14,128,128]{2,1,0:T(8,128)(2,1)S(1)} %get-tuple-element.10.refs_1_.refs_4_.refs_5_.refs_7_), channel_id=1, source_target_pairs={{0,2},{2,4},{3,1},{4,6},{5,3},{7,5},{8,10},{10,12},{11,9},{12,14},... | collective-permute-start | bytes 1376264 | tf_op jit(solution)/shard_map/ppermute | solution.py:384
  11.8 2.8 %collective-permute-done.refs_2_.tile = bf16[28,128,128]{2,1,0:T(8,128)(2,1)S(1)} collective-permute-done((bf16[28,128,128]{2,1,0:T(8,128)(2,1)}, bf16[28,128,128]{2,1,0:T(8,128)(2,1)S(1)}, u32[]{:S(2)}, u32[]{:S(2)}) %collective-permute-start) | collective-permute-done | bytes 917536 | tf_op jit(solution)/shard_map/ppermute | solution.py:392
  14.5 0.0 collective-permute-start.3
  14.6 0.0 collective-permute-done.1.refs_5_.refs_6_.refs_8_
  14.6 0.7 %collective-permute-start.4 = (bf16[14,128,128]{2,1,0:T(8,128)(2,1)S(1)}, bf16[14,128,128]{2,1,0:T(8,128)(2,1)S(1)}, u32[]{:S(2)}, u32[]{:S(2)}) collective-permute-start(bf16[14,128,128]{2,1,0:T(8,128)(2,1)S(1)} %collective-permute-done.1.refs_5_.refs_6_.refs_8_), channel_id=1, source_target_pairs={{2,4},{3,1},{4,6},{5,3},{10,12},{11,9},{12,14},{13,11},{18,20},{19... | collective-permute-start | bytes 1376264 | tf_op jit(solution)/shard_map/ppermute | solution.py:384
  15.3 2.1 %collective-permute-start.6 = (bf16[14,128,128]{2,1,0:T(8,128)(2,1)S(1)}, bf16[14,128,128]{2,1,0:T(8,128)(2,1)S(1)}, u32[]{:S(2)}, u32[]{:S(2)}) collective-permute-start(bf16[14,128,128]{2,1,0:T(8,128)(2,1)S(1)} %pick_half.1), channel_id=1, source_target_pairs={{8,24},{17,25},{10,26},{19,27},{12,28},{21,29},{14,30},{23,31},{0,... | collective-permute-start | bytes 1376264 | tf_op jit(solution)/shard_map/ppermute | solution.py:403
  17.4 1.7 %collective-permute-done.2.refs_6_.refs_7_.refs_9_ = bf16[14,128,128]{2,1,0:T(8,128)(2,1)S(1)} collective-permute-done((bf16[14,128,128]{2,1,0:T(8,128)(2,1)S(1)}, bf16[14,128,128]{2,1,0:T(8,128)(2,1)S(1)}, u32[]{:S(2)}, u32[]{:S(2)}) %collective-permute-start.2) | collective-permute-done | bytes 458784 | tf_op jit(solution)/shard_map/ppermute | solution.py:384
  19.1 0.7 %collective-permute-start.5 = (bf16[14,128,128]{2,1,0:T(8,128)(2,1)S(1)}, bf16[14,128,128]{2,1,0:T(8,128)(2,1)S(1)}, u32[]{:S(2)}, u32[]{:S(2)}) collective-permute-start(bf16[14,128,128]{2,1,0:T(8,128)(2,1)S(1)} %collective-permute-done.2.refs_6_.refs_7_.refs_9_), channel_id=1, source_target_pairs={{2,4},{3,1},{4,6},{5,3},{10,12},{11,9},{12,14},{13,11},{18,20},{19... | collective-permute-start | bytes 1376264 | tf_op jit(solution)/shard_map/ppermute | solution.py:384
  19.8 0.0 collective-permute-done.4.refs_8_.refs_10_
  19.8 0.7 %collective-permute-start.8 = (bf16[14,128,128]{2,1,0:T(8,128)(2,1)S(1)}, bf16[14,128,128]{2,1,0:T(8,128)(2,1)S(1)}, u32[]{:S(2)}, u32[]{:S(2)}) collective-permute-start(bf16[14,128,128]{2,1,0:T(8,128)(2,1)S(1)} %collective-permute-done.4.refs_8_.refs_10_), channel_id=1, source_target_pairs={{3,1},{4,6},{11,9},{12,14},{19,17},{20,22},{27,25},{28,30}} | collective-permute-start | bytes 1376264 | tf_op jit(solution)/shard_map/ppermute | solution.py:384
  20.5 3.3 %collective-permute-done.6.refs_4_ = bf16[14,128,128]{2,1,0:T(8,128)(2,1)S(1)} collective-permute-done((bf16[14,128,128]{2,1,0:T(8,128)(2,1)S(1)}, bf16[14,128,128]{2,1,0:T(8,128)(2,1)S(1)}, u32[]{:S(2)}, u32[]{:S(2)}) %collective-permute-start.6) | collective-permute-done | bytes 458784 | tf_op jit(solution)/shard_map/ppermute | solution.py:403
  23.9 2.1 %collective-permute-start.7 = (bf16[14,128,128]{2,1,0:T(8,128)(2,1)S(1)}, bf16[14,128,128]{2,1,0:T(8,128)(2,1)S(1)}, u32[]{:S(2)}, u32[]{:S(2)}) collective-permute-start(bf16[14,128,128]{2,1,0:T(8,128)(2,1)S(1)} %collective-permute-done.6.refs_4_), channel_id=1, source_target_pairs={{0,1},{1,0},{2,3},{3,2},{4,5},{5,4},{6,7},{7,6},{8,9},{9,8},{10,11... | collective-permute-start | bytes 1376264 | tf_op jit(solution)/shard_map/ppermute | solution.py:404
  26.0 0.0 copy-done.1
  26.0 1.0 %list_products.1.pairs = s32[5,128]{1,0:T(8,128)S(1)} custom-call(s32[4,4,28]{2,1,0:T(4,128)S(1)} %convert_add_fusion.slot_keys), custom_call_target="tpu_custom_call" | custom-call | bytes 1835008 | tf_op jit(solution)/shard_map/list_products/pallas_call | solution.py:368
  27.0 0.0 collective-permute-done.5.refs_9_.refs_11_
  27.0 0.7 %collective-permute-start.10 = (bf16[14,128,128]{2,1,0:T(8,128)(2,1)S(1)}, bf16[14,128,128]{2,1,0:T(8,128)(2,1)S(1)}, u32[]{:S(2)}, u32[]{:S(2)}) collective-permute-start(bf16[14,128,128]{2,1,0:T(8,128)(2,1)S(1)} %collective-permute-done.5.refs_9_.refs_11_), channel_id=1, source_target_pairs={{3,1},{4,6},{11,9},{12,14},{19,17},{20,22},{27,25},{28,30}} | collective-permute-start | bytes 1376264 | tf_op jit(solution)/shard_map/ppermute | solution.py:384
  27.7 2.0 %early_products.1.total = f32[29,128,128]{2,1,0:T(8,128)S(1)} custom-call(s32[5,128]{1,0:T(8,128)S(1)} %list_products.1.pairs, bf16[14,128,128]{2,1,0:T(8,128)(2,1)S(1)} %get-tuple-element.9.refs_0_.refs_3_.refs_4_.refs_6_, bf16[14,128,128]{2,1,0:T(8,128)(2,1)S(1)} %get-tuple-element.10.refs_1_.refs_4_.refs_5_.refs_7_, ...), custom_call_target="tpu_custom_call" | custom-call | flops 352321536 | bytes 5505024 | tf_op jit(solution)/shard_map/early_products/pallas_call | solution.py:410
  29.7 0.0 collective-permute-done.3.refs_3_
  29.7 0.7 %second_products.1.total = f32[29,128,128]{2,1,0:T(8,128)S(1)} custom-call(s32[5,128]{1,0:T(8,128)S(1)} %list_products.1.pairs, f32[29,128,128]{2,1,0:T(8,128)S(1)} %early_products.1.total, bf16[14,128,128]{2,1,0:T(8,128)(2,1)S(1)} %get-tuple-element.9.refs_0_.refs_3_.refs_4_.refs_6_, ...), custom_call_target="tpu_custom_call", output_to_operand_aliasing={{}: (1, {})} | custom-call | flops 117440512 | bytes 1835008 | tf_op jit(solution)/shard_map/second_products/pallas_call | solution.py:419
  30.4 0.0 collective-permute-done.8.refs_12_
  30.4 0.0 collective-permute-done.7.refs_5_
  30.4 0.8 %middle_products.1 = (f32[29,128,128]{2,1,0:T(8,128)S(1)}, f32[14,128,128]{2,1,0:T(8,128)S(1)}, f32[14,128,128]{2,1,0:T(8,128)S(1)}) custom-call(s32[5,128]{1,0:T(8,128)S(1)} %list_products.1.pairs, f32[29,128,128]{2,1,0:T(8,128)S(1)} %second_products.1.total, ...), custom_call_target="tpu_custom_call", output_to_operand_aliasing={{0}: (1, {})} | custom-call | flops 352321536 | bytes 5505024 | tf_op jit(solution)/shard_map/middle_products/pallas_call | solution.py:432
  31.2 4.4 %collective-permute-start.9 = (f32[14,128,128]{2,1,0:T(8,128)S(1)}, f32[14,128,128]{2,1,0:T(8,128)S(1)}, u32[]{:S(2)}, u32[]{:S(2)}) collective-permute-start(f32[14,128,128]{2,1,0:T(8,128)S(1)} %get-tuple-element.12), channel_id=1, source_target_pairs={{0,1},{1,0},{2,3},{3,2},{4,5},{5,4},{6,7},{7,6},{8,9},{9,8},{10,11... | collective-permute-start | bytes 2752520 | tf_op jit(solution)/shard_map/ppermute | solution.py:442
  35.7 0.0 collective-permute-done.10.refs_6_
  35.7 3.7 %collective-permute-start.11 = (bf16[14,128,128]{2,1,0:T(8,128)(2,1)S(1)}, bf16[14,128,128]{2,1,0:T(8,128)(2,1)S(1)}, u32[]{:S(2)}, u32[]{:S(2)}) collective-permute-start(bf16[14,128,128]{2,1,0:T(8,128)(2,1)S(1)} %collective-permute-done.10.refs_6_), channel_id=1, source_target_pairs={{0,1},{1,0},{2,3},{3,2},{4,5},{5,4},{6,7},{7,6},{8,9},{9,8},{10,11... | collective-permute-start | bytes 1376264 | tf_op jit(solution)/shard_map/ppermute | solution.py:443
  39.4 1.4 %collective-permute-done.11.refs_7_ = bf16[14,128,128]{2,1,0:T(8,128)(2,1)S(1)} collective-permute-done((bf16[14,128,128]{2,1,0:T(8,128)(2,1)S(1)}, bf16[14,128,128]{2,1,0:T(8,128)(2,1)S(1)}, u32[]{:S(2)}, u32[]{:S(2)}) %collective-permute-start.11) | collective-permute-done | bytes 458784 | tf_op jit(solution)/shard_map/ppermute | solution.py:443
  40.8 0.0 collective-permute-done.9.received
  40.8 1.9 %last_products.1 = bf16[14,128,128]{2,1,0:T(8,128)(2,1)} custom-call(s32[5,128]{1,0:T(8,128)S(1)} %list_products.1.pairs, f32[14,128,128]{2,1,0:T(8,128)S(1)} %get-tuple-element.11.mine, f32[14,128,128]{2,1,0:T(8,128)S(1)} %collective-permute-done.9.received, bf16[14,128,128]{2,1,0:T(8,128)(2,1)S(1)} %get-tuple-element.9.refs_0_.refs_3_.refs_4_.refs_6_, ...), custom_call_target="tpu_custom_call" | custom-call | flops 58720256 | bytes 3670016 | tf_op jit(solution)/shard_map/last_products/pallas_call | solution.py:444
  (6 shorter events, 0.1 us)
Async XLA Ops:
  0.0 14.5 %collective-permute-start = (bf16[28,128,128]{2,1,0:T(8,128)(2,1)}, bf16[28,128,128]{2,1,0:T(8,128)(2,1)S(1)}, u32[]{:S(2)}, u32[]{:S(2)}) collective-permute-start(bf16[28,128,128]{2,1,0:T(8,128)(2,1)} %bitcast.2), channel_id=1, source_target_pairs={{0,8},{1,17},{2,10},{3,19},{4,12},{5,21},{6,14},{7,23},{8,0},{9,25... | collective-permute-start | bytes 2752520 | tf_op jit(solution)/shard_map/ppermute | solution.py:392
  3.0 1.2 %copy-start = (bf16[1,1,28,128,128]{4,3,2,1,0:T(8,128)(2,1)S(1)}, bf16[1,1,28,128,128]{4,3,2,1,0:T(8,128)(2,1)}, u32[]{:S(2)}) copy-start(bf16[1,1,28,128,128]{4,3,2,1,0:T(8,128)(2,1)} %param.3) | copy-start | bytes 2752516
  4.2 21.8 %copy-start.1 = (s32[4,4,28]{2,1,0:T(4,128)S(1)}, s32[4,4,28]{2,1,0:T(4,128)}, u32[]{:S(2)}) copy-start(s32[4,4,28]{2,1,0:T(4,128)} %param.4) | copy-start | bytes 5380
  4.2 21.8 %copy-start.2 = (s32[4,4,28]{2,1,0:T(4,128)S(1)}, s32[4,4,28]{2,1,0:T(4,128)}, u32[]{:S(2)}) copy-start(s32[4,4,28]{2,1,0:T(4,128)} %param.5) | copy-start | bytes 5380
  4.8 9.8 %collective-permute-start.1 = (bf16[14,128,128]{2,1,0:T(8,128)(2,1)S(1)}, bf16[14,128,128]{2,1,0:T(8,128)(2,1)S(1)}, u32[]{:S(2)}, u32[]{:S(2)}) collective-permute-start(bf16[14,128,128]{2,1,0:T(8,128)(2,1)S(1)} %get-tuple-element.9.refs_0_.refs_3_.refs_4_.refs_6_), channel_id=1, source_target_pairs={{0,2},{2,4},{3,1},{4,6},{5,3},{7,5},{8,10},{10,12},{11,9},{12,14},... | collective-permute-start | bytes 1376264 | tf_op jit(solution)/shard_map/ppermute | solution.py:384
  8.3 10.9 %collective-permute-start.2 = (bf16[14,128,128]{2,1,0:T(8,128)(2,1)S(1)}, bf16[14,128,128]{2,1,0:T(8,128)(2,1)S(1)}, u32[]{:S(2)}, u32[]{:S(2)}) collective-permute-start(bf16[14,128,128]{2,1,0:T(8,128)(2,1)S(1)} %get-tuple-element.10.refs_1_.refs_4_.refs_5_.refs_7_), channel_id=1, source_target_pairs={{0,2},{2,4},{3,1},{4,6},{5,3},{7,5},{8,10},{10,12},{11,9},{12,14},... | collective-permute-start | bytes 1376264 | tf_op jit(solution)/shard_map/ppermute | solution.py:384
  14.5 15.1 %collective-permute-start.3 = (bf16[28,128,128]{2,1,0:T(8,128)(2,1)S(1)}, bf16[28,128,128]{2,1,0:T(8,128)(2,1)S(1)}, u32[]{:S(2)}, u32[]{:S(2)}) collective-permute-start(bf16[28,128,128]{2,1,0:T(8,128)(2,1)S(1)} %collective-permute-done.refs_2_.tile), channel_id=1, source_target_pairs={{0,1},{1,0},{2,3},{3,2},{4,5},{5,4},{6,7},{7,6},{8,9},{9,8},{10,11... | collective-permute-start | bytes 2752520 | tf_op jit(solution)/shard_map/ppermute | solution.py:393
  14.6 5.3 %collective-permute-start.4 = (bf16[14,128,128]{2,1,0:T(8,128)(2,1)S(1)}, bf16[14,128,128]{2,1,0:T(8,128)(2,1)S(1)}, u32[]{:S(2)}, u32[]{:S(2)}) collective-permute-start(bf16[14,128,128]{2,1,0:T(8,128)(2,1)S(1)} %collective-permute-done.1.refs_5_.refs_6_.refs_8_), channel_id=1, source_target_pairs={{2,4},{3,1},{4,6},{5,3},{10,12},{11,9},{12,14},{13,11},{18,20},{19... | collective-permute-start | bytes 1376264 | tf_op jit(solution)/shard_map/ppermute | solution.py:384
  15.3 8.6 %collective-permute-start.6 = (bf16[14,128,128]{2,1,0:T(8,128)(2,1)S(1)}, bf16[14,128,128]{2,1,0:T(8,128)(2,1)S(1)}, u32[]{:S(2)}, u32[]{:S(2)}) collective-permute-start(bf16[14,128,128]{2,1,0:T(8,128)(2,1)S(1)} %pick_half.1), channel_id=1, source_target_pairs={{8,24},{17,25},{10,26},{19,27},{12,28},{21,29},{14,30},{23,31},{0,... | collective-permute-start | bytes 1376264 | tf_op jit(solution)/shard_map/ppermute | solution.py:403
  19.1 7.9 %collective-permute-start.5 = (bf16[14,128,128]{2,1,0:T(8,128)(2,1)S(1)}, bf16[14,128,128]{2,1,0:T(8,128)(2,1)S(1)}, u32[]{:S(2)}, u32[]{:S(2)}) collective-permute-start(bf16[14,128,128]{2,1,0:T(8,128)(2,1)S(1)} %collective-permute-done.2.refs_6_.refs_7_.refs_9_), channel_id=1, source_target_pairs={{2,4},{3,1},{4,6},{5,3},{10,12},{11,9},{12,14},{13,11},{18,20},{19... | collective-permute-start | bytes 1376264 | tf_op jit(solution)/shard_map/ppermute | solution.py:384
  19.8 10.5 %collective-permute-start.8 = (bf16[14,128,128]{2,1,0:T(8,128)(2,1)S(1)}, bf16[14,128,128]{2,1,0:T(8,128)(2,1)S(1)}, u32[]{:S(2)}, u32[]{:S(2)}) collective-permute-start(bf16[14,128,128]{2,1,0:T(8,128)(2,1)S(1)} %collective-permute-done.4.refs_8_.refs_10_), channel_id=1, source_target_pairs={{3,1},{4,6},{11,9},{12,14},{19,17},{20,22},{27,25},{28,30}} | collective-permute-start | bytes 1376264 | tf_op jit(solution)/shard_map/ppermute | solution.py:384
  23.9 6.5 %collective-permute-start.7 = (bf16[14,128,128]{2,1,0:T(8,128)(2,1)S(1)}, bf16[14,128,128]{2,1,0:T(8,128)(2,1)S(1)}, u32[]{:S(2)}, u32[]{:S(2)}) collective-permute-start(bf16[14,128,128]{2,1,0:T(8,128)(2,1)S(1)} %collective-permute-done.6.refs_4_), channel_id=1, source_target_pairs={{0,1},{1,0},{2,3},{3,2},{4,5},{5,4},{6,7},{7,6},{8,9},{9,8},{10,11... | collective-permute-start | bytes 1376264 | tf_op jit(solution)/shard_map/ppermute | solution.py:404
  27.0 8.6 %collective-permute-start.10 = (bf16[14,128,128]{2,1,0:T(8,128)(2,1)S(1)}, bf16[14,128,128]{2,1,0:T(8,128)(2,1)S(1)}, u32[]{:S(2)}, u32[]{:S(2)}) collective-permute-start(bf16[14,128,128]{2,1,0:T(8,128)(2,1)S(1)} %collective-permute-done.5.refs_9_.refs_11_), channel_id=1, source_target_pairs={{3,1},{4,6},{11,9},{12,14},{19,17},{20,22},{27,25},{28,30}} | collective-permute-start | bytes 1376264 | tf_op jit(solution)/shard_map/ppermute | solution.py:384
  31.2 9.6 %collective-permute-start.9 = (f32[14,128,128]{2,1,0:T(8,128)S(1)}, f32[14,128,128]{2,1,0:T(8,128)S(1)}, u32[]{:S(2)}, u32[]{:S(2)}) collective-permute-start(f32[14,128,128]{2,1,0:T(8,128)S(1)} %get-tuple-element.12), channel_id=1, source_target_pairs={{0,1},{1,0},{2,3},{3,2},{4,5},{5,4},{6,7},{7,6},{8,9},{9,8},{10,11... | collective-permute-start | bytes 2752520 | tf_op jit(solution)/shard_map/ppermute | solution.py:442
  35.7 5.2 %collective-permute-start.11 = (bf16[14,128,128]{2,1,0:T(8,128)(2,1)S(1)}, bf16[14,128,128]{2,1,0:T(8,128)(2,1)S(1)}, u32[]{:S(2)}, u32[]{:S(2)}) collective-permute-start(bf16[14,128,128]{2,1,0:T(8,128)(2,1)S(1)} %collective-permute-done.10.refs_6_), channel_id=1, source_target_pairs={{0,1},{1,0},{2,3},{3,2},{4,5},{5,4},{6,7},{7,6},{8,9},{9,8},{10,11... | collective-permute-start | bytes 1376264 | tf_op jit(solution)/shard_map/ppermute | solution.py:443

commit v10 on v9

--- a/solution.py
+++ b/solution.py
@@ -10,6 +10,7 @@
 TB = 28
 GROUP = 8
 LANES = 128
+WRITTEN = 2
 GRANT = 8 << 20
 CHUNKS = 2
 
@@ -266,13 +267,15 @@
         run_jobs(cases, count, pairs, stage, blocks_of(right), acc)
 
 
-def split_kernel(tile, first, second, sem):
-    size = first.shape[0]
+def split_kernel(low, tile, part, sem):
+    size = part.shape[0]
     copies = [
-        pltpu.make_async_copy(tile.at[pl.ds(0, size)], first, sem.at[0]),
         pltpu.make_async_copy(
-            tile.at[pl.ds(size, second.shape[0])], second, sem.at[1]
-        ),
+            tile.at[pl.ds(low + start, end - start)],
+            part.at[pl.ds(start, end - start)],
+            sem.at[j],
+        )
+        for j, (start, end) in enumerate(((0, size // 2), (size // 2, size)))
     ]
     for copy in copies:
         copy.start()
@@ -326,8 +329,8 @@
         lambda slot: jnp.minimum(slot - layer * share, share),
     )
     copies = []
-    for j, (start, end) in enumerate(((0, share // 2), (share // 2, share))):
-        here = pl.ds(start, end - start)
+    for j, start in enumerate(range(0, share, WRITTEN)):
+        here = pl.ds(start, min(WRITTEN, share - start))
         rounded[here] = acc[here].astype(rounded.dtype)
         copies.append(pltpu.make_async_copy(rounded.at[here], out.at[here], sem.at[j]))
         copies[-1].start()
@@ -352,19 +355,19 @@
             transcendentals=0,
         )
 
-    held = pl.pallas_call(
-        split_kernel,
-        out_shape=[
-            jax.ShapeDtypeStruct((j - i, size, size), own.dtype)
-            for i, j in zip(bounds[:-1], bounds[1:])
-        ],
-        in_specs=[pl.BlockSpec(memory_space=pl.ANY)],
-        out_specs=[vmem] * CHUNKS,
-        scratch_shapes=[pltpu.SemaphoreType.DMA((CHUNKS,))],
-        compiler_params=compiler_params,
-        cost_estimate=cost(0, 2),
-        name="split_tile",
-    )(own)
+    held = [
+        pl.pallas_call(
+            functools.partial(split_kernel, i),
+            out_shape=jax.ShapeDtypeStruct((j - i, size, size), own.dtype),
+            in_specs=[pl.BlockSpec(memory_space=pl.ANY)],
+            out_specs=vmem,
+            scratch_shapes=[pltpu.SemaphoreType.DMA((2,))],
+            compiler_params=compiler_params,
+            cost_estimate=cost(0, 1),
+            name="split_tile",
+        )(own)
+        for i, j in zip(bounds[:-1], bounds[1:])
+    ]
     lists = pl.pallas_call(
         functools.partial(list_kernel, plan, bounds),
         out_shape=jax.ShapeDtypeStruct((plan.stages + CHUNKS, LANES), jnp.int32),
@@ -449,7 +452,7 @@
         scratch_shapes=[
             pltpu.VMEM((share + 1, size, size), jnp.float32),
             pltpu.VMEM((share, size, size), jnp.bfloat16),
-            pltpu.SemaphoreType.DMA((2,)),
+            pltpu.SemaphoreType.DMA((pl.cdiv(share, WRITTEN),)),
         ],
         compiler_params=compiler_params,
         cost_estimate=cost(slots // 2, 4),

time: 43.5 us -> 43.6 us (level)
  Pallas kernels: 6.9 us -> 7.57 us
  waiting for transfers between devices: 9.32 us -> 8.66 us
    ppermute x1, waiting for transfers between devices: 2.79 us -> 2.13 us  [on_device(): near.append(lax.ppermute(own, everywhere, plan.near_pairs(bys)))]
    pallas_call x1 -> x2, Pallas kernels: 0.56 us -> 1.21 us  [on_device(): pl.pallas_call(functools.partial(split_kernel, i), out_shape=jax.ShapeDty...]
  transfers between devices with their start and end apart: 12 -> 12, of which waited for: 4 -> 4; matrix products, arithmetic and copies ran while one was open for 0% -> 0% of each run, Pallas kernels for 12% -> 13%
where the time goes in v10:
time: 43.6 us; the launch traced here: 42.7 us
  starting transfers between devices  25.1 us (58%)
  waiting for transfers between devices  8.66 us (20%)
  Pallas kernels  7.57 us (17%)
  local copies, waits for them, and re-layouts  1.22 us (3%)
    ppermute x6, starting transfers between devices, on_device(): arrived.append(lax.ppermute(part, ('col', 'layer'), pairs))  9.73 us
    ppermute x1, starting transfers between devices, on_device(): received = lax.ppermute(other, 'layer', swap)  4.43 us
    ppermute x1, starting transfers between devices, on_device(): second_swapped = lax.ppermute(second, 'layer', swap)  3.74 us
    ppermute x1, waiting for transfers between devices, on_device(): far = lax.ppermute(sent, everywhere, plan.far_pairs())  3.3 us
    ppermute x1, starting transfers between devices, on_device(): near.append(lax.ppermute(own, everywhere, plan.near_pairs(bys)))  2.97 us
    ppermute x1, starting transfers between devices, on_device(): far_swapped = lax.ppermute(far, 'layer', swap)  2.15 us
    ppermute x1, waiting for transfers between devices, on_device(): near.append(lax.ppermute(own, everywhere, plan.near_pairs(bys)))  2.13 us
    ppermute x1, starting transfers between devices, on_device(): far = lax.ppermute(sent, everywhere, plan.far_pairs())  2.12 us
  transfers between devices with their start and end apart: 12, of which 4 were waited for; matrix products, arithmetic and copies ran while one was open for 0% of the time, Pallas kernels for 13%

profile of v10, /device:TPU:0, one launch (start us, length us, event | category | flops | bytes accessed | tf_op | source)
XLA Modules:
  0.0 42.7 jit_solution(6484145975326168749)
XLA Ops:
  0.0 3.0 %collective-permute-start = (bf16[28,128,128]{2,1,0:T(8,128)(2,1)}, bf16[28,128,128]{2,1,0:T(8,128)(2,1)S(1)}, u32[]{:S(2)}, u32[]{:S(2)}) collective-permute-start(bf16[28,128,128]{2,1,0:T(8,128)(2,1)} %bitcast.2), channel_id=1, source_target_pairs={{0,8},{1,17},{2,10},{3,19},{4,12},{5,21},{6,14},{7,23},{8,0},{9,25... | collective-permute-start | bytes 2752520 | tf_op jit(solution)/shard_map/ppermute | solution.py:395
  3.0 1.2 %copy-done = bf16[1,1,28,128,128]{4,3,2,1,0:T(8,128)(2,1)S(1)} copy-done((bf16[1,1,28,128,128]{4,3,2,1,0:T(8,128)(2,1)S(1)}, bf16[1,1,28,128,128]{4,3,2,1,0:T(8,128)(2,1)}, u32[]{:S(2)}) %copy-start) | copy-done | bytes 917528
  4.2 0.6 %split_tile.2.refs_0_.refs_3_.refs_4_.refs_6_ = bf16[14,128,128]{2,1,0:T(8,128)(2,1)S(1)} custom-call(bf16[28,128,128]{2,1,0:T(8,128)(2,1)S(1)} %bitcast.3), custom_call_target="tpu_custom_call" | custom-call | bytes 917504 | tf_op jit(solution)/shard_map/split_tile/pallas_call | solution.py:359
  4.8 3.5 %collective-permute-start.1 = (bf16[14,128,128]{2,1,0:T(8,128)(2,1)S(1)}, bf16[14,128,128]{2,1,0:T(8,128)(2,1)S(1)}, u32[]{:S(2)}, u32[]{:S(2)}) collective-permute-start(bf16[14,128,128]{2,1,0:T(8,128)(2,1)S(1)} %split_tile.2.refs_0_.refs_3_.refs_4_.refs_6_), channel_id=1, source_target_pairs={{0,2},{2,4},{3,1},{4,6},{5,3},{7,5},{8,10},{10,12},{11,9},{12,14},... | collective-permute-start | bytes 1376264 | tf_op jit(solution)/shard_map/ppermute | solution.py:387
  8.3 0.6 %split_tile.3.refs_1_.refs_4_.refs_5_.refs_7_ = bf16[14,128,128]{2,1,0:T(8,128)(2,1)S(1)} custom-call(bf16[28,128,128]{2,1,0:T(8,128)(2,1)S(1)} %bitcast.4), custom_call_target="tpu_custom_call" | custom-call | bytes 917504 | tf_op jit(solution)/shard_map/split_tile/pallas_call | solution.py:359
  8.9 3.5 %collective-permute-start.2 = (bf16[14,128,128]{2,1,0:T(8,128)(2,1)S(1)}, bf16[14,128,128]{2,1,0:T(8,128)(2,1)S(1)}, u32[]{:S(2)}, u32[]{:S(2)}) collective-permute-start(bf16[14,128,128]{2,1,0:T(8,128)(2,1)S(1)} %split_tile.3.refs_1_.refs_4_.refs_5_.refs_7_), channel_id=1, source_target_pairs={{0,2},{2,4},{3,1},{4,6},{5,3},{7,5},{8,10},{10,12},{11,9},{12,14},... | collective-permute-start | bytes 1376264 | tf_op jit(solution)/shard_map/ppermute | solution.py:387
  12.4 2.1 %collective-permute-done.refs_2_.tile = bf16[28,128,128]{2,1,0:T(8,128)(2,1)S(1)} collective-permute-done((bf16[28,128,128]{2,1,0:T(8,128)(2,1)}, bf16[28,128,128]{2,1,0:T(8,128)(2,1)S(1)}, u32[]{:S(2)}, u32[]{:S(2)}) %collective-permute-start) | collective-permute-done | bytes 917536 | tf_op jit(solution)/shard_map/ppermute | solution.py:395
  14.5 0.0 collective-permute-start.3
  14.6 0.0 collective-permute-done.1.refs_5_.refs_6_.refs_8_
  14.6 0.7 %collective-permute-start.4 = (bf16[14,128,128]{2,1,0:T(8,128)(2,1)S(1)}, bf16[14,128,128]{2,1,0:T(8,128)(2,1)S(1)}, u32[]{:S(2)}, u32[]{:S(2)}) collective-permute-start(bf16[14,128,128]{2,1,0:T(8,128)(2,1)S(1)} %collective-permute-done.1.refs_5_.refs_6_.refs_8_), channel_id=1, source_target_pairs={{2,4},{3,1},{4,6},{5,3},{10,12},{11,9},{12,14},{13,11},{18,20},{19... | collective-permute-start | bytes 1376264 | tf_op jit(solution)/shard_map/ppermute | solution.py:387
  15.3 2.1 %collective-permute-start.6 = (bf16[14,128,128]{2,1,0:T(8,128)(2,1)S(1)}, bf16[14,128,128]{2,1,0:T(8,128)(2,1)S(1)}, u32[]{:S(2)}, u32[]{:S(2)}) collective-permute-start(bf16[14,128,128]{2,1,0:T(8,128)(2,1)S(1)} %pick_half.1), channel_id=1, source_target_pairs={{8,24},{17,25},{10,26},{19,27},{12,28},{21,29},{14,30},{23,31},{0,... | collective-permute-start | bytes 1376264 | tf_op jit(solution)/shard_map/ppermute | solution.py:406
  17.4 1.8 %collective-permute-done.2.refs_6_.refs_7_.refs_9_ = bf16[14,128,128]{2,1,0:T(8,128)(2,1)S(1)} collective-permute-done((bf16[14,128,128]{2,1,0:T(8,128)(2,1)S(1)}, bf16[14,128,128]{2,1,0:T(8,128)(2,1)S(1)}, u32[]{:S(2)}, u32[]{:S(2)}) %collective-permute-start.2) | collective-permute-done | bytes 458784 | tf_op jit(solution)/shard_map/ppermute | solution.py:387
  19.2 0.7 %collective-permute-start.5 = (bf16[14,128,128]{2,1,0:T(8,128)(2,1)S(1)}, bf16[14,128,128]{2,1,0:T(8,128)(2,1)S(1)}, u32[]{:S(2)}, u32[]{:S(2)}) collective-permute-start(bf16[14,128,128]{2,1,0:T(8,128)(2,1)S(1)} %collective-permute-done.2.refs_6_.refs_7_.refs_9_), channel_id=1, source_target_pairs={{2,4},{3,1},{4,6},{5,3},{10,12},{11,9},{12,14},{13,11},{18,20},{19... | collective-permute-start | bytes 1376264 | tf_op jit(solution)/shard_map/ppermute | solution.py:387
  19.9 0.0 collective-permute-done.4.refs_8_.refs_10_
  19.9 0.7 %collective-permute-start.8 = (bf16[14,128,128]{2,1,0:T(8,128)(2,1)S(1)}, bf16[14,128,128]{2,1,0:T(8,128)(2,1)S(1)}, u32[]{:S(2)}, u32[]{:S(2)}) collective-permute-start(bf16[14,128,128]{2,1,0:T(8,128)(2,1)S(1)} %collective-permute-done.4.refs_8_.refs_10_), channel_id=1, source_target_pairs={{3,1},{4,6},{11,9},{12,14},{19,17},{20,22},{27,25},{28,30}} | collective-permute-start | bytes 1376264 | tf_op jit(solution)/shard_map/ppermute | solution.py:387
  20.6 3.3 %collective-permute-done.6.refs_4_ = bf16[14,128,128]{2,1,0:T(8,128)(2,1)S(1)} collective-permute-done((bf16[14,128,128]{2,1,0:T(8,128)(2,1)S(1)}, bf16[14,128,128]{2,1,0:T(8,128)(2,1)S(1)}, u32[]{:S(2)}, u32[]{:S(2)}) %collective-permute-start.6) | collective-permute-done | bytes 458784 | tf_op jit(solution)/shard_map/ppermute | solution.py:406
  23.9 2.1 %collective-permute-start.7 = (bf16[14,128,128]{2,1,0:T(8,128)(2,1)S(1)}, bf16[14,128,128]{2,1,0:T(8,128)(2,1)S(1)}, u32[]{:S(2)}, u32[]{:S(2)}) collective-permute-start(bf16[14,128,128]{2,1,0:T(8,128)(2,1)S(1)} %collective-permute-done.6.refs_4_), channel_id=1, source_target_pairs={{0,1},{1,0},{2,3},{3,2},{4,5},{5,4},{6,7},{7,6},{8,9},{9,8},{10,11... | collective-permute-start | bytes 1376264 | tf_op jit(solution)/shard_map/ppermute | solution.py:407
  26.0 1.0 %list_products.1.pairs = s32[5,128]{1,0:T(8,128)S(1)} custom-call(s32[4,4,28]{2,1,0:T(4,128)S(1)} %convert_add_fusion.slot_keys), custom_call_target="tpu_custom_call" | custom-call | bytes 1835008 | tf_op jit(solution)/shard_map/list_products/pallas_call | solution.py:371
  27.0 0.0 collective-permute-done.5.refs_9_.refs_11_
  27.0 0.7 %collective-permute-start.10 = (bf16[14,128,128]{2,1,0:T(8,128)(2,1)S(1)}, bf16[14,128,128]{2,1,0:T(8,128)(2,1)S(1)}, u32[]{:S(2)}, u32[]{:S(2)}) collective-permute-start(bf16[14,128,128]{2,1,0:T(8,128)(2,1)S(1)} %collective-permute-done.5.refs_9_.refs_11_), channel_id=1, source_target_pairs={{3,1},{4,6},{11,9},{12,14},{19,17},{20,22},{27,25},{28,30}} | collective-permute-start | bytes 1376264 | tf_op jit(solution)/shard_map/ppermute | solution.py:387
  27.7 2.0 %early_products.1.total = f32[29,128,128]{2,1,0:T(8,128)S(1)} custom-call(s32[5,128]{1,0:T(8,128)S(1)} %list_products.1.pairs, bf16[14,128,128]{2,1,0:T(8,128)(2,1)S(1)} %split_tile.2.refs_0_.refs_3_.refs_4_.refs_6_, bf16[14,128,128]{2,1,0:T(8,128)(2,1)S(1)} %split_tile.3.refs_1_.refs_4_.refs_5_.refs_7_, ...), custom_call_target="tpu_custom_call" | custom-call | flops 352321536 | bytes 5505024 | tf_op jit(solution)/shard_map/early_products/pallas_call | solution.py:413
  29.7 0.0 collective-permute-done.3.refs_3_
  29.7 0.7 %second_products.1.total = f32[29,128,128]{2,1,0:T(8,128)S(1)} custom-call(s32[5,128]{1,0:T(8,128)S(1)} %list_products.1.pairs, f32[29,128,128]{2,1,0:T(8,128)S(1)} %early_products.1.total, bf16[14,128,128]{2,1,0:T(8,128)(2,1)S(1)} %split_tile.2.refs_0_.refs_3_.refs_4_.refs_6_, ...), custom_call_target="tpu_custom_call", output_to_operand_aliasing={{}: (1, {})} | custom-call | flops 117440512 | bytes 1835008 | tf_op jit(solution)/shard_map/second_products/pallas_call | solution.py:422
  30.4 0.0 collective-permute-done.8.refs_12_
  30.4 0.0 collective-permute-done.7.refs_5_
  30.4 0.8 %middle_products.1 = (f32[29,128,128]{2,1,0:T(8,128)S(1)}, f32[14,128,128]{2,1,0:T(8,128)S(1)}, f32[14,128,128]{2,1,0:T(8,128)S(1)}) custom-call(s32[5,128]{1,0:T(8,128)S(1)} %list_products.1.pairs, f32[29,128,128]{2,1,0:T(8,128)S(1)} %second_products.1.total, ...), custom_call_target="tpu_custom_call", output_to_operand_aliasing={{0}: (1, {})} | custom-call | flops 352321536 | bytes 5505024 | tf_op jit(solution)/shard_map/middle_products/pallas_call | solution.py:435
  31.2 4.4 %collective-permute-start.9 = (f32[14,128,128]{2,1,0:T(8,128)S(1)}, f32[14,128,128]{2,1,0:T(8,128)S(1)}, u32[]{:S(2)}, u32[]{:S(2)}) collective-permute-start(f32[14,128,128]{2,1,0:T(8,128)S(1)} %get-tuple-element.8), channel_id=1, source_target_pairs={{0,1},{1,0},{2,3},{3,2},{4,5},{5,4},{6,7},{7,6},{8,9},{9,8},{10,11... | collective-permute-start | bytes 2752520 | tf_op jit(solution)/shard_map/ppermute | solution.py:445
  35.7 0.0 collective-permute-done.10.refs_6_
  35.7 3.7 %collective-permute-start.11 = (bf16[14,128,128]{2,1,0:T(8,128)(2,1)S(1)}, bf16[14,128,128]{2,1,0:T(8,128)(2,1)S(1)}, u32[]{:S(2)}, u32[]{:S(2)}) collective-permute-start(bf16[14,128,128]{2,1,0:T(8,128)(2,1)S(1)} %collective-permute-done.10.refs_6_), channel_id=1, source_target_pairs={{0,1},{1,0},{2,3},{3,2},{4,5},{5,4},{6,7},{7,6},{8,9},{9,8},{10,11... | collective-permute-start | bytes 1376264 | tf_op jit(solution)/shard_map/ppermute | solution.py:446
  39.4 1.4 %collective-permute-done.11.refs_7_ = bf16[14,128,128]{2,1,0:T(8,128)(2,1)S(1)} collective-permute-done((bf16[14,128,128]{2,1,0:T(8,128)(2,1)S(1)}, bf16[14,128,128]{2,1,0:T(8,128)(2,1)S(1)}, u32[]{:S(2)}, u32[]{:S(2)}) %collective-permute-start.11) | collective-permute-done | bytes 458784 | tf_op jit(solution)/shard_map/ppermute | solution.py:446
  40.8 0.0 collective-permute-done.9.received
  40.8 1.9 %last_products.1 = bf16[14,128,128]{2,1,0:T(8,128)(2,1)} custom-call(s32[5,128]{1,0:T(8,128)S(1)} %list_products.1.pairs, f32[14,128,128]{2,1,0:T(8,128)S(1)} %get-tuple-element.7.mine, f32[14,128,128]{2,1,0:T(8,128)S(1)} %collective-permute-done.9.received, bf16[14,128,128]{2,1,0:T(8,128)(2,1)S(1)} %split_tile.2.refs_0_.refs_3_.refs_4_.refs_6_, ...), custom_call_target="tpu_custom_call" | custom-call | flops 58720256 | bytes 3670016 | tf_op jit(solution)/shard_map/last_products/pallas_call | solution.py:447
  (7 shorter events, 0.1 us)
Async XLA Ops:
  0.0 14.5 %collective-permute-start = (bf16[28,128,128]{2,1,0:T(8,128)(2,1)}, bf16[28,128,128]{2,1,0:T(8,128)(2,1)S(1)}, u32[]{:S(2)}, u32[]{:S(2)}) collective-permute-start(bf16[28,128,128]{2,1,0:T(8,128)(2,1)} %bitcast.2), channel_id=1, source_target_pairs={{0,8},{1,17},{2,10},{3,19},{4,12},{5,21},{6,14},{7,23},{8,0},{9,25... | collective-permute-start | bytes 2752520 | tf_op jit(solution)/shard_map/ppermute | solution.py:395
  3.0 1.2 %copy-start = (bf16[1,1,28,128,128]{4,3,2,1,0:T(8,128)(2,1)S(1)}, bf16[1,1,28,128,128]{4,3,2,1,0:T(8,128)(2,1)}, u32[]{:S(2)}) copy-start(bf16[1,1,28,128,128]{4,3,2,1,0:T(8,128)(2,1)} %param.3) | copy-start | bytes 2752516
  4.2 21.8 %copy-start.1 = (s32[4,4,28]{2,1,0:T(4,128)S(1)}, s32[4,4,28]{2,1,0:T(4,128)}, u32[]{:S(2)}) copy-start(s32[4,4,28]{2,1,0:T(4,128)} %param.4) | copy-start | bytes 5380
  4.2 21.8 %copy-start.2 = (s32[4,4,28]{2,1,0:T(4,128)S(1)}, s32[4,4,28]{2,1,0:T(4,128)}, u32[]{:S(2)}) copy-start(s32[4,4,28]{2,1,0:T(4,128)} %param.5) | copy-start | bytes 5380
  4.8 9.8 %collective-permute-start.1 = (bf16[14,128,128]{2,1,0:T(8,128)(2,1)S(1)}, bf16[14,128,128]{2,1,0:T(8,128)(2,1)S(1)}, u32[]{:S(2)}, u32[]{:S(2)}) collective-permute-start(bf16[14,128,128]{2,1,0:T(8,128)(2,1)S(1)} %split_tile.2.refs_0_.refs_3_.refs_4_.refs_6_), channel_id=1, source_target_pairs={{0,2},{2,4},{3,1},{4,6},{5,3},{7,5},{8,10},{10,12},{11,9},{12,14},... | collective-permute-start | bytes 1376264 | tf_op jit(solution)/shard_map/ppermute | solution.py:387
  8.9 10.2 %collective-permute-start.2 = (bf16[14,128,128]{2,1,0:T(8,128)(2,1)S(1)}, bf16[14,128,128]{2,1,0:T(8,128)(2,1)S(1)}, u32[]{:S(2)}, u32[]{:S(2)}) collective-permute-start(bf16[14,128,128]{2,1,0:T(8,128)(2,1)S(1)} %split_tile.3.refs_1_.refs_4_.refs_5_.refs_7_), channel_id=1, source_target_pairs={{0,2},{2,4},{3,1},{4,6},{5,3},{7,5},{8,10},{10,12},{11,9},{12,14},... | collective-permute-start | bytes 1376264 | tf_op jit(solution)/shard_map/ppermute | solution.py:387
  14.5 15.1 %collective-permute-start.3 = (bf16[28,128,128]{2,1,0:T(8,128)(2,1)S(1)}, bf16[28,128,128]{2,1,0:T(8,128)(2,1)S(1)}, u32[]{:S(2)}, u32[]{:S(2)}) collective-permute-start(bf16[28,128,128]{2,1,0:T(8,128)(2,1)S(1)} %collective-permute-done.refs_2_.tile), channel_id=1, source_target_pairs={{0,1},{1,0},{2,3},{3,2},{4,5},{5,4},{6,7},{7,6},{8,9},{9,8},{10,11... | collective-permute-start | bytes 2752520 | tf_op jit(solution)/shard_map/ppermute | solution.py:396
  14.6 5.3 %collective-permute-start.4 = (bf16[14,128,128]{2,1,0:T(8,128)(2,1)S(1)}, bf16[14,128,128]{2,1,0:T(8,128)(2,1)S(1)}, u32[]{:S(2)}, u32[]{:S(2)}) collective-permute-start(bf16[14,128,128]{2,1,0:T(8,128)(2,1)S(1)} %collective-permute-done.1.refs_5_.refs_6_.refs_8_), channel_id=1, source_target_pairs={{2,4},{3,1},{4,6},{5,3},{10,12},{11,9},{12,14},{13,11},{18,20},{19... | collective-permute-start | bytes 1376264 | tf_op jit(solution)/shard_map/ppermute | solution.py:387
  15.3 8.6 %collective-permute-start.6 = (bf16[14,128,128]{2,1,0:T(8,128)(2,1)S(1)}, bf16[14,128,128]{2,1,0:T(8,128)(2,1)S(1)}, u32[]{:S(2)}, u32[]{:S(2)}) collective-permute-start(bf16[14,128,128]{2,1,0:T(8,128)(2,1)S(1)} %pick_half.1), channel_id=1, source_target_pairs={{8,24},{17,25},{10,26},{19,27},{12,28},{21,29},{14,30},{23,31},{0,... | collective-permute-start | bytes 1376264 | tf_op jit(solution)/shard_map/ppermute | solution.py:406
  19.2 7.8 %collective-permute-start.5 = (bf16[14,128,128]{2,1,0:T(8,128)(2,1)S(1)}, bf16[14,128,128]{2,1,0:T(8,128)(2,1)S(1)}, u32[]{:S(2)}, u32[]{:S(2)}) collective-permute-start(bf16[14,128,128]{2,1,0:T(8,128)(2,1)S(1)} %collective-permute-done.2.refs_6_.refs_7_.refs_9_), channel_id=1, source_target_pairs={{2,4},{3,1},{4,6},{5,3},{10,12},{11,9},{12,14},{13,11},{18,20},{19... | collective-permute-start | bytes 1376264 | tf_op jit(solution)/shard_map/ppermute | solution.py:387
  19.9 10.5 %collective-permute-start.8 = (bf16[14,128,128]{2,1,0:T(8,128)(2,1)S(1)}, bf16[14,128,128]{2,1,0:T(8,128)(2,1)S(1)}, u32[]{:S(2)}, u32[]{:S(2)}) collective-permute-start(bf16[14,128,128]{2,1,0:T(8,128)(2,1)S(1)} %collective-permute-done.4.refs_8_.refs_10_), channel_id=1, source_target_pairs={{3,1},{4,6},{11,9},{12,14},{19,17},{20,22},{27,25},{28,30}} | collective-permute-start | bytes 1376264 | tf_op jit(solution)/shard_map/ppermute | solution.py:387
  23.9 6.5 %collective-permute-start.7 = (bf16[14,128,128]{2,1,0:T(8,128)(2,1)S(1)}, bf16[14,128,128]{2,1,0:T(8,128)(2,1)S(1)}, u32[]{:S(2)}, u32[]{:S(2)}) collective-permute-start(bf16[14,128,128]{2,1,0:T(8,128)(2,1)S(1)} %collective-permute-done.6.refs_4_), channel_id=1, source_target_pairs={{0,1},{1,0},{2,3},{3,2},{4,5},{5,4},{6,7},{7,6},{8,9},{9,8},{10,11... | collective-permute-start | bytes 1376264 | tf_op jit(solution)/shard_map/ppermute | solution.py:407
  27.0 8.6 %collective-permute-start.10 = (bf16[14,128,128]{2,1,0:T(8,128)(2,1)S(1)}, bf16[14,128,128]{2,1,0:T(8,128)(2,1)S(1)}, u32[]{:S(2)}, u32[]{:S(2)}) collective-permute-start(bf16[14,128,128]{2,1,0:T(8,128)(2,1)S(1)} %collective-permute-done.5.refs_9_.refs_11_), channel_id=1, source_target_pairs={{3,1},{4,6},{11,9},{12,14},{19,17},{20,22},{27,25},{28,30}} | collective-permute-start | bytes 1376264 | tf_op jit(solution)/shard_map/ppermute | solution.py:387
  31.2 9.6 %collective-permute-start.9 = (f32[14,128,128]{2,1,0:T(8,128)S(1)}, f32[14,128,128]{2,1,0:T(8,128)S(1)}, u32[]{:S(2)}, u32[]{:S(2)}) collective-permute-start(f32[14,128,128]{2,1,0:T(8,128)S(1)} %get-tuple-element.8), channel_id=1, source_target_pairs={{0,1},{1,0},{2,3},{3,2},{4,5},{5,4},{6,7},{7,6},{8,9},{9,8},{10,11... | collective-permute-start | bytes 2752520 | tf_op jit(solution)/shard_map/ppermute | solution.py:445
  35.7 5.2 %collective-permute-start.11 = (bf16[14,128,128]{2,1,0:T(8,128)(2,1)S(1)}, bf16[14,128,128]{2,1,0:T(8,128)(2,1)S(1)}, u32[]{:S(2)}, u32[]{:S(2)}) collective-permute-start(bf16[14,128,128]{2,1,0:T(8,128)(2,1)S(1)} %collective-permute-done.10.refs_6_), channel_id=1, source_target_pairs={{0,1},{1,0},{2,3},{3,2},{4,5},{5,4},{6,7},{7,6},{8,9},{9,8},{10,11... | collective-permute-start | bytes 1376264 | tf_op jit(solution)/shard_map/ppermute | solution.py:446

commit v11 on v9

--- a/solution.py
+++ b/solution.py
@@ -156,9 +156,9 @@
         pairs[pl.ds(stage, 1), :] = jnp.where(lane == LANES - 1, count, entry)
 
 
-def add_products(count, pairs, row, left, right, acc, at):
+def add_products(count, pairs, row, left, right, acc, at, group):
     def step(i, carry):
-        codes = [pairs[row, i * GROUP + j] for j in range(GROUP)]
+        codes = [pairs[row, i * group + j] for j in range(group)]
         products = [
             jnp.dot(
                 left(code // 4096),
@@ -171,7 +171,7 @@
             acc[at(code % 64)] += product
         return carry
 
-    lax.fori_loop(0, (count + GROUP - 1) // GROUP, step, 0)
+    lax.fori_loop(0, (count + group - 1) // group, step, 0)
 
 
 def blocks_of(parts):
@@ -224,12 +224,14 @@
         yield by == self.far, block
 
 
-def run_jobs(cases, count, pairs, row, right, acc, at=lambda slot: slot):
+def run_jobs(
+    cases, count, pairs, row, right, acc, at=lambda slot: slot, group=GROUP
+):
     for here, left in cases:
 
         @pl.when(here & (count > 0))
         def _(left=left):
-            add_products(count, pairs, row, left, right, acc, at)
+            add_products(count, pairs, row, left, right, acc, at, group)
 
 
 def stages_of(parts, refs):
@@ -324,6 +326,7 @@
         right,
         acc,
         lambda slot: jnp.minimum(slot - layer * share, share),
+        GROUP // 2,
     )
     copies = []
     for j, (start, end) in enumerate(((0, share // 2), (share // 2, share))):

time: 43.5 us -> 43.4 us (level)
  no operation moved by 1% of the time
where the time goes in v11:
time: 43.4 us; the launch traced here: 42.6 us
  starting transfers between devices  25.1 us (58%)
  waiting for transfers between devices  9.32 us (21%)
  Pallas kernels  6.79 us (16%)
  local copies, waits for them, and re-layouts  1.22 us (3%)
    ppermute x6, starting transfers between devices, on_device(): arrived.append(lax.ppermute(part, ('col', 'layer'), pairs))  9.73 us
    ppermute x1, starting transfers between devices, on_device(): received = lax.ppermute(other, 'layer', swap)  4.43 us
    ppermute x1, starting transfers between devices, on_device(): second_swapped = lax.ppermute(second, 'layer', swap)  3.74 us
    ppermute x1, waiting for transfers between devices, on_device(): far = lax.ppermute(sent, everywhere, plan.far_pairs())  3.34 us
    ppermute x1, starting transfers between devices, on_device(): near.append(lax.ppermute(own, everywhere, plan.near_pairs(bys)))  2.97 us
    ppermute x1, waiting for transfers between devices, on_device(): near.append(lax.ppermute(own, everywhere, plan.near_pairs(bys)))  2.79 us
    ppermute x1, starting transfers between devices, on_device(): far_swapped = lax.ppermute(far, 'layer', swap)  2.15 us
    ppermute x1, starting transfers between devices, on_device(): far = lax.ppermute(sent, everywhere, plan.far_pairs())  2.12 us
  transfers between devices with their start and end apart: 12, of which 4 were waited for; matrix products, arithmetic and copies ran while one was open for 0% of the time, Pallas kernels for 12%

profile of v11, /device:TPU:0, one launch (start us, length us, event | category | flops | bytes accessed | tf_op | source)
XLA Modules:
  0.0 42.6 jit_solution(16729711377010532661)
XLA Ops:
  0.0 3.0 %collective-permute-start = (bf16[28,128,128]{2,1,0:T(8,128)(2,1)}, bf16[28,128,128]{2,1,0:T(8,128)(2,1)S(1)}, u32[]{:S(2)}, u32[]{:S(2)}) collective-permute-start(bf16[28,128,128]{2,1,0:T(8,128)(2,1)} %bitcast.2), channel_id=1, source_target_pairs={{0,8},{1,17},{2,10},{3,19},{4,12},{5,21},{6,14},{7,23},{8,0},{9,25... | collective-permute-start | bytes 2752520 | tf_op jit(solution)/shard_map/ppermute | solution.py:395
  3.0 1.2 %copy-done = bf16[1,1,28,128,128]{4,3,2,1,0:T(8,128)(2,1)S(1)} copy-done((bf16[1,1,28,128,128]{4,3,2,1,0:T(8,128)(2,1)S(1)}, bf16[1,1,28,128,128]{4,3,2,1,0:T(8,128)(2,1)}, u32[]{:S(2)}) %copy-start) | copy-done | bytes 917528
  4.2 0.6 %split_tile.1 = (bf16[14,128,128]{2,1,0:T(8,128)(2,1)S(1)}, bf16[14,128,128]{2,1,0:T(8,128)(2,1)S(1)}) custom-call(bf16[28,128,128]{2,1,0:T(8,128)(2,1)S(1)} %bitcast.3), custom_call_target="tpu_custom_call" | custom-call | bytes 1835008 | tf_op jit(solution)/shard_map/split_tile/pallas_call | solution.py:358
  4.8 3.5 %collective-permute-start.1 = (bf16[14,128,128]{2,1,0:T(8,128)(2,1)S(1)}, bf16[14,128,128]{2,1,0:T(8,128)(2,1)S(1)}, u32[]{:S(2)}, u32[]{:S(2)}) collective-permute-start(bf16[14,128,128]{2,1,0:T(8,128)(2,1)S(1)} %get-tuple-element.9.refs_0_.refs_3_.refs_4_.refs_6_), channel_id=1, source_target_pairs={{0,2},{2,4},{3,1},{4,6},{5,3},{7,5},{8,10},{10,12},{11,9},{12,14},... | collective-permute-start | bytes 1376264 | tf_op jit(solution)/shard_map/ppermute | solution.py:387
  8.3 3.5 %collective-permute-start.2 = (bf16[14,128,128]{2,1,0:T(8,128)(2,1)S(1)}, bf16[14,128,128]{2,1,0:T(8,128)(2,1)S(1)}, u32[]{:S(2)}, u32[]{:S(2)}) collective-permute-start(bf16[14,128,128]{2,1,0:T(8,128)(2,1)S(1)} %get-tuple-element.10.refs_1_.refs_4_.refs_5_.refs_7_), channel_id=1, source_target_pairs={{0,2},{2,4},{3,1},{4,6},{5,3},{7,5},{8,10},{10,12},{11,9},{12,14},... | collective-permute-start | bytes 1376264 | tf_op jit(solution)/shard_map/ppermute | solution.py:387
  11.8 2.8 %collective-permute-done.refs_2_.tile = bf16[28,128,128]{2,1,0:T(8,128)(2,1)S(1)} collective-permute-done((bf16[28,128,128]{2,1,0:T(8,128)(2,1)}, bf16[28,128,128]{2,1,0:T(8,128)(2,1)S(1)}, u32[]{:S(2)}, u32[]{:S(2)}) %collective-permute-start) | collective-permute-done | bytes 917536 | tf_op jit(solution)/shard_map/ppermute | solution.py:395
  14.5 0.0 collective-permute-start.3
  14.6 0.0 collective-permute-done.1.refs_5_.refs_6_.refs_8_
  14.6 0.7 %collective-permute-start.4 = (bf16[14,128,128]{2,1,0:T(8,128)(2,1)S(1)}, bf16[14,128,128]{2,1,0:T(8,128)(2,1)S(1)}, u32[]{:S(2)}, u32[]{:S(2)}) collective-permute-start(bf16[14,128,128]{2,1,0:T(8,128)(2,1)S(1)} %collective-permute-done.1.refs_5_.refs_6_.refs_8_), channel_id=1, source_target_pairs={{2,4},{3,1},{4,6},{5,3},{10,12},{11,9},{12,14},{13,11},{18,20},{19... | collective-permute-start | bytes 1376264 | tf_op jit(solution)/shard_map/ppermute | solution.py:387
  15.3 2.1 %collective-permute-start.6 = (bf16[14,128,128]{2,1,0:T(8,128)(2,1)S(1)}, bf16[14,128,128]{2,1,0:T(8,128)(2,1)S(1)}, u32[]{:S(2)}, u32[]{:S(2)}) collective-permute-start(bf16[14,128,128]{2,1,0:T(8,128)(2,1)S(1)} %pick_half.1), channel_id=1, source_target_pairs={{8,24},{17,25},{10,26},{19,27},{12,28},{21,29},{14,30},{23,31},{0,... | collective-permute-start | bytes 1376264 | tf_op jit(solution)/shard_map/ppermute | solution.py:406
  17.4 1.7 %collective-permute-done.2.refs_6_.refs_7_.refs_9_ = bf16[14,128,128]{2,1,0:T(8,128)(2,1)S(1)} collective-permute-done((bf16[14,128,128]{2,1,0:T(8,128)(2,1)S(1)}, bf16[14,128,128]{2,1,0:T(8,128)(2,1)S(1)}, u32[]{:S(2)}, u32[]{:S(2)}) %collective-permute-start.2) | collective-permute-done | bytes 458784 | tf_op jit(solution)/shard_map/ppermute | solution.py:387
  19.1 0.7 %collective-permute-start.5 = (bf16[14,128,128]{2,1,0:T(8,128)(2,1)S(1)}, bf16[14,128,128]{2,1,0:T(8,128)(2,1)S(1)}, u32[]{:S(2)}, u32[]{:S(2)}) collective-permute-start(bf16[14,128,128]{2,1,0:T(8,128)(2,1)S(1)} %collective-permute-done.2.refs_6_.refs_7_.refs_9_), channel_id=1, source_target_pairs={{2,4},{3,1},{4,6},{5,3},{10,12},{11,9},{12,14},{13,11},{18,20},{19... | collective-permute-start | bytes 1376264 | tf_op jit(solution)/shard_map/ppermute | solution.py:387
  19.8 0.0 collective-permute-done.4.refs_8_.refs_10_
  19.8 0.7 %collective-permute-start.8 = (bf16[14,128,128]{2,1,0:T(8,128)(2,1)S(1)}, bf16[14,128,128]{2,1,0:T(8,128)(2,1)S(1)}, u32[]{:S(2)}, u32[]{:S(2)}) collective-permute-start(bf16[14,128,128]{2,1,0:T(8,128)(2,1)S(1)} %collective-permute-done.4.refs_8_.refs_10_), channel_id=1, source_target_pairs={{3,1},{4,6},{11,9},{12,14},{19,17},{20,22},{27,25},{28,30}} | collective-permute-start | bytes 1376264 | tf_op jit(solution)/shard_map/ppermute | solution.py:387
  20.5 3.3 %collective-permute-done.6.refs_4_ = bf16[14,128,128]{2,1,0:T(8,128)(2,1)S(1)} collective-permute-done((bf16[14,128,128]{2,1,0:T(8,128)(2,1)S(1)}, bf16[14,128,128]{2,1,0:T(8,128)(2,1)S(1)}, u32[]{:S(2)}, u32[]{:S(2)}) %collective-permute-start.6) | collective-permute-done | bytes 458784 | tf_op jit(solution)/shard_map/ppermute | solution.py:406
  23.9 2.1 %collective-permute-start.7 = (bf16[14,128,128]{2,1,0:T(8,128)(2,1)S(1)}, bf16[14,128,128]{2,1,0:T(8,128)(2,1)S(1)}, u32[]{:S(2)}, u32[]{:S(2)}) collective-permute-start(bf16[14,128,128]{2,1,0:T(8,128)(2,1)S(1)} %collective-permute-done.6.refs_4_), channel_id=1, source_target_pairs={{0,1},{1,0},{2,3},{3,2},{4,5},{5,4},{6,7},{7,6},{8,9},{9,8},{10,11... | collective-permute-start | bytes 1376264 | tf_op jit(solution)/shard_map/ppermute | solution.py:407
  26.0 0.0 copy-done.1
  26.0 1.0 %list_products.1.pairs = s32[5,128]{1,0:T(8,128)S(1)} custom-call(s32[4,4,28]{2,1,0:T(4,128)S(1)} %convert_add_fusion.slot_keys), custom_call_target="tpu_custom_call" | custom-call | bytes 1835008 | tf_op jit(solution)/shard_map/list_products/pallas_call | solution.py:371
  27.0 0.0 collective-permute-done.5.refs_9_.refs_11_
  27.0 0.7 %collective-permute-start.10 = (bf16[14,128,128]{2,1,0:T(8,128)(2,1)S(1)}, bf16[14,128,128]{2,1,0:T(8,128)(2,1)S(1)}, u32[]{:S(2)}, u32[]{:S(2)}) collective-permute-start(bf16[14,128,128]{2,1,0:T(8,128)(2,1)S(1)} %collective-permute-done.5.refs_9_.refs_11_), channel_id=1, source_target_pairs={{3,1},{4,6},{11,9},{12,14},{19,17},{20,22},{27,25},{28,30}} | collective-permute-start | bytes 1376264 | tf_op jit(solution)/shard_map/ppermute | solution.py:387
  27.7 2.0 %early_products.1.total = f32[29,128,128]{2,1,0:T(8,128)S(1)} custom-call(s32[5,128]{1,0:T(8,128)S(1)} %list_products.1.pairs, bf16[14,128,128]{2,1,0:T(8,128)(2,1)S(1)} %get-tuple-element.9.refs_0_.refs_3_.refs_4_.refs_6_, bf16[14,128,128]{2,1,0:T(8,128)(2,1)S(1)} %get-tuple-element.10.refs_1_.refs_4_.refs_5_.refs_7_, ...), custom_call_target="tpu_custom_call" | custom-call | flops 352321536 | bytes 5505024 | tf_op jit(solution)/shard_map/early_products/pallas_call | solution.py:413
  29.7 0.0 collective-permute-done.3.refs_3_
  29.7 0.7 %second_products.1.total = f32[29,128,128]{2,1,0:T(8,128)S(1)} custom-call(s32[5,128]{1,0:T(8,128)S(1)} %list_products.1.pairs, f32[29,128,128]{2,1,0:T(8,128)S(1)} %early_products.1.total, bf16[14,128,128]{2,1,0:T(8,128)(2,1)S(1)} %get-tuple-element.9.refs_0_.refs_3_.refs_4_.refs_6_, ...), custom_call_target="tpu_custom_call", output_to_operand_aliasing={{}: (1, {})} | custom-call | flops 117440512 | bytes 1835008 | tf_op jit(solution)/shard_map/second_products/pallas_call | solution.py:422
  30.4 0.0 collective-permute-done.8.refs_12_
  30.4 0.0 collective-permute-done.7.refs_5_
  30.4 0.8 %middle_products.1 = (f32[29,128,128]{2,1,0:T(8,128)S(1)}, f32[14,128,128]{2,1,0:T(8,128)S(1)}, f32[14,128,128]{2,1,0:T(8,128)S(1)}) custom-call(s32[5,128]{1,0:T(8,128)S(1)} %list_products.1.pairs, f32[29,128,128]{2,1,0:T(8,128)S(1)} %second_products.1.total, ...), custom_call_target="tpu_custom_call", output_to_operand_aliasing={{0}: (1, {})} | custom-call | flops 352321536 | bytes 5505024 | tf_op jit(solution)/shard_map/middle_products/pallas_call | solution.py:435
  31.2 4.4 %collective-permute-start.9 = (f32[14,128,128]{2,1,0:T(8,128)S(1)}, f32[14,128,128]{2,1,0:T(8,128)S(1)}, u32[]{:S(2)}, u32[]{:S(2)}) collective-permute-start(f32[14,128,128]{2,1,0:T(8,128)S(1)} %get-tuple-element.12), channel_id=1, source_target_pairs={{0,1},{1,0},{2,3},{3,2},{4,5},{5,4},{6,7},{7,6},{8,9},{9,8},{10,11... | collective-permute-start | bytes 2752520 | tf_op jit(solution)/shard_map/ppermute | solution.py:445
  35.7 0.0 collective-permute-done.10.refs_6_
  35.7 3.7 %collective-permute-start.11 = (bf16[14,128,128]{2,1,0:T(8,128)(2,1)S(1)}, bf16[14,128,128]{2,1,0:T(8,128)(2,1)S(1)}, u32[]{:S(2)}, u32[]{:S(2)}) collective-permute-start(bf16[14,128,128]{2,1,0:T(8,128)(2,1)S(1)} %collective-permute-done.10.refs_6_), channel_id=1, source_target_pairs={{0,1},{1,0},{2,3},{3,2},{4,5},{5,4},{6,7},{7,6},{8,9},{9,8},{10,11... | collective-permute-start | bytes 1376264 | tf_op jit(solution)/shard_map/ppermute | solution.py:446
  39.4 1.4 %collective-permute-done.11.refs_7_ = bf16[14,128,128]{2,1,0:T(8,128)(2,1)S(1)} collective-permute-done((bf16[14,128,128]{2,1,0:T(8,128)(2,1)S(1)}, bf16[14,128,128]{2,1,0:T(8,128)(2,1)S(1)}, u32[]{:S(2)}, u32[]{:S(2)}) %collective-permute-start.11) | collective-permute-done | bytes 458784 | tf_op jit(solution)/shard_map/ppermute | solution.py:446
  40.8 0.0 collective-permute-done.9.received
  40.8 1.7 %last_products.1 = bf16[14,128,128]{2,1,0:T(8,128)(2,1)} custom-call(s32[5,128]{1,0:T(8,128)S(1)} %list_products.1.pairs, f32[14,128,128]{2,1,0:T(8,128)S(1)} %get-tuple-element.11.mine, f32[14,128,128]{2,1,0:T(8,128)S(1)} %collective-permute-done.9.received, bf16[14,128,128]{2,1,0:T(8,128)(2,1)S(1)} %get-tuple-element.9.refs_0_.refs_3_.refs_4_.refs_6_, ...), custom_call_target="tpu_custom_call" | custom-call | flops 58720256 | bytes 3670016 | tf_op jit(solution)/shard_map/last_products/pallas_call | solution.py:447
  (6 shorter events, 0.1 us)
Async XLA Ops:
  0.0 14.5 %collective-permute-start = (bf16[28,128,128]{2,1,0:T(8,128)(2,1)}, bf16[28,128,128]{2,1,0:T(8,128)(2,1)S(1)}, u32[]{:S(2)}, u32[]{:S(2)}) collective-permute-start(bf16[28,128,128]{2,1,0:T(8,128)(2,1)} %bitcast.2), channel_id=1, source_target_pairs={{0,8},{1,17},{2,10},{3,19},{4,12},{5,21},{6,14},{7,23},{8,0},{9,25... | collective-permute-start | bytes 2752520 | tf_op jit(solution)/shard_map/ppermute | solution.py:395
  3.0 1.2 %copy-start = (bf16[1,1,28,128,128]{4,3,2,1,0:T(8,128)(2,1)S(1)}, bf16[1,1,28,128,128]{4,3,2,1,0:T(8,128)(2,1)}, u32[]{:S(2)}) copy-start(bf16[1,1,28,128,128]{4,3,2,1,0:T(8,128)(2,1)} %param.3) | copy-start | bytes 2752516
  4.2 21.8 %copy-start.1 = (s32[4,4,28]{2,1,0:T(4,128)S(1)}, s32[4,4,28]{2,1,0:T(4,128)}, u32[]{:S(2)}) copy-start(s32[4,4,28]{2,1,0:T(4,128)} %param.4) | copy-start | bytes 5380
  4.2 21.8 %copy-start.2 = (s32[4,4,28]{2,1,0:T(4,128)S(1)}, s32[4,4,28]{2,1,0:T(4,128)}, u32[]{:S(2)}) copy-start(s32[4,4,28]{2,1,0:T(4,128)} %param.5) | copy-start | bytes 5380
  4.8 9.8 %collective-permute-start.1 = (bf16[14,128,128]{2,1,0:T(8,128)(2,1)S(1)}, bf16[14,128,128]{2,1,0:T(8,128)(2,1)S(1)}, u32[]{:S(2)}, u32[]{:S(2)}) collective-permute-start(bf16[14,128,128]{2,1,0:T(8,128)(2,1)S(1)} %get-tuple-element.9.refs_0_.refs_3_.refs_4_.refs_6_), channel_id=1, source_target_pairs={{0,2},{2,4},{3,1},{4,6},{5,3},{7,5},{8,10},{10,12},{11,9},{12,14},... | collective-permute-start | bytes 1376264 | tf_op jit(solution)/shard_map/ppermute | solution.py:387
  8.3 10.9 %collective-permute-start.2 = (bf16[14,128,128]{2,1,0:T(8,128)(2,1)S(1)}, bf16[14,128,128]{2,1,0:T(8,128)(2,1)S(1)}, u32[]{:S(2)}, u32[]{:S(2)}) collective-permute-start(bf16[14,128,128]{2,1,0:T(8,128)(2,1)S(1)} %get-tuple-element.10.refs_1_.refs_4_.refs_5_.refs_7_), channel_id=1, source_target_pairs={{0,2},{2,4},{3,1},{4,6},{5,3},{7,5},{8,10},{10,12},{11,9},{12,14},... | collective-permute-start | bytes 1376264 | tf_op jit(solution)/shard_map/ppermute | solution.py:387
  14.5 15.1 %collective-permute-start.3 = (bf16[28,128,128]{2,1,0:T(8,128)(2,1)S(1)}, bf16[28,128,128]{2,1,0:T(8,128)(2,1)S(1)}, u32[]{:S(2)}, u32[]{:S(2)}) collective-permute-start(bf16[28,128,128]{2,1,0:T(8,128)(2,1)S(1)} %collective-permute-done.refs_2_.tile), channel_id=1, source_target_pairs={{0,1},{1,0},{2,3},{3,2},{4,5},{5,4},{6,7},{7,6},{8,9},{9,8},{10,11... | collective-permute-start | bytes 2752520 | tf_op jit(solution)/shard_map/ppermute | solution.py:396
  14.6 5.3 %collective-permute-start.4 = (bf16[14,128,128]{2,1,0:T(8,128)(2,1)S(1)}, bf16[14,128,128]{2,1,0:T(8,128)(2,1)S(1)}, u32[]{:S(2)}, u32[]{:S(2)}) collective-permute-start(bf16[14,128,128]{2,1,0:T(8,128)(2,1)S(1)} %collective-permute-done.1.refs_5_.refs_6_.refs_8_), channel_id=1, source_target_pairs={{2,4},{3,1},{4,6},{5,3},{10,12},{11,9},{12,14},{13,11},{18,20},{19... | collective-permute-start | bytes 1376264 | tf_op jit(solution)/shard_map/ppermute | solution.py:387
  15.3 8.6 %collective-permute-start.6 = (bf16[14,128,128]{2,1,0:T(8,128)(2,1)S(1)}, bf16[14,128,128]{2,1,0:T(8,128)(2,1)S(1)}, u32[]{:S(2)}, u32[]{:S(2)}) collective-permute-start(bf16[14,128,128]{2,1,0:T(8,128)(2,1)S(1)} %pick_half.1), channel_id=1, source_target_pairs={{8,24},{17,25},{10,26},{19,27},{12,28},{21,29},{14,30},{23,31},{0,... | collective-permute-start | bytes 1376264 | tf_op jit(solution)/shard_map/ppermute | solution.py:406
  19.1 7.9 %collective-permute-start.5 = (bf16[14,128,128]{2,1,0:T(8,128)(2,1)S(1)}, bf16[14,128,128]{2,1,0:T(8,128)(2,1)S(1)}, u32[]{:S(2)}, u32[]{:S(2)}) collective-permute-start(bf16[14,128,128]{2,1,0:T(8,128)(2,1)S(1)} %collective-permute-done.2.refs_6_.refs_7_.refs_9_), channel_id=1, source_target_pairs={{2,4},{3,1},{4,6},{5,3},{10,12},{11,9},{12,14},{13,11},{18,20},{19... | collective-permute-start | bytes 1376264 | tf_op jit(solution)/shard_map/ppermute | solution.py:387
  19.8 10.5 %collective-permute-start.8 = (bf16[14,128,128]{2,1,0:T(8,128)(2,1)S(1)}, bf16[14,128,128]{2,1,0:T(8,128)(2,1)S(1)}, u32[]{:S(2)}, u32[]{:S(2)}) collective-permute-start(bf16[14,128,128]{2,1,0:T(8,128)(2,1)S(1)} %collective-permute-done.4.refs_8_.refs_10_), channel_id=1, source_target_pairs={{3,1},{4,6},{11,9},{12,14},{19,17},{20,22},{27,25},{28,30}} | collective-permute-start | bytes 1376264 | tf_op jit(solution)/shard_map/ppermute | solution.py:387
  23.9 6.5 %collective-permute-start.7 = (bf16[14,128,128]{2,1,0:T(8,128)(2,1)S(1)}, bf16[14,128,128]{2,1,0:T(8,128)(2,1)S(1)}, u32[]{:S(2)}, u32[]{:S(2)}) collective-permute-start(bf16[14,128,128]{2,1,0:T(8,128)(2,1)S(1)} %collective-permute-done.6.refs_4_), channel_id=1, source_target_pairs={{0,1},{1,0},{2,3},{3,2},{4,5},{5,4},{6,7},{7,6},{8,9},{9,8},{10,11... | collective-permute-start | bytes 1376264 | tf_op jit(solution)/shard_map/ppermute | solution.py:407
  27.0 8.6 %collective-permute-start.10 = (bf16[14,128,128]{2,1,0:T(8,128)(2,1)S(1)}, bf16[14,128,128]{2,1,0:T(8,128)(2,1)S(1)}, u32[]{:S(2)}, u32[]{:S(2)}) collective-permute-start(bf16[14,128,128]{2,1,0:T(8,128)(2,1)S(1)} %collective-permute-done.5.refs_9_.refs_11_), channel_id=1, source_target_pairs={{3,1},{4,6},{11,9},{12,14},{19,17},{20,22},{27,25},{28,30}} | collective-permute-start | bytes 1376264 | tf_op jit(solution)/shard_map/ppermute | solution.py:387
  31.2 9.6 %collective-permute-start.9 = (f32[14,128,128]{2,1,0:T(8,128)S(1)}, f32[14,128,128]{2,1,0:T(8,128)S(1)}, u32[]{:S(2)}, u32[]{:S(2)}) collective-permute-start(f32[14,128,128]{2,1,0:T(8,128)S(1)} %get-tuple-element.12), channel_id=1, source_target_pairs={{0,1},{1,0},{2,3},{3,2},{4,5},{5,4},{6,7},{7,6},{8,9},{9,8},{10,11... | collective-permute-start | bytes 2752520 | tf_op jit(solution)/shard_map/ppermute | solution.py:445
  35.7 5.2 %collective-permute-start.11 = (bf16[14,128,128]{2,1,0:T(8,128)(2,1)S(1)}, bf16[14,128,128]{2,1,0:T(8,128)(2,1)S(1)}, u32[]{:S(2)}, u32[]{:S(2)}) collective-permute-start(bf16[14,128,128]{2,1,0:T(8,128)(2,1)S(1)} %collective-permute-done.10.refs_6_), channel_id=1, source_target_pairs={{0,1},{1,0},{2,3},{3,2},{4,5},{5,4},{6,7},{7,6},{8,9},{9,8},{10,11... | collective-permute-start | bytes 1376264 | tf_op jit(solution)/shard_map/ppermute | solution.py:446

commit v12 on v11

--- a/solution.py
+++ b/solution.py
@@ -311,23 +311,22 @@
     late, l, _ = late_core(plan, a)
     by = b ^ l
     row = plan.stages + 1
-    cases = lefts.all(by, layer)
-
-    def right(slot):
-        slot = jnp.maximum(slot - low, 0)
-        return lax.select(late == layer, part[slot], part_swapped[slot])
-
     count = pairs[row, pairs.shape[1] - 1]
-    run_jobs(
-        cases,
-        count,
-        pairs,
-        row,
-        right,
-        acc,
-        lambda slot: jnp.minimum(slot - layer * share, share),
-        GROUP // 2,
-    )
+    for mine_is_late, source in ((True, part), (False, part_swapped)):
+
+        def right(slot, source=source):
+            return source[jnp.maximum(slot - low, 0)]
+
+        run_jobs(
+            lefts.all(by, layer),
+            jnp.where((late == layer) == mine_is_late, count, 0),
+            pairs,
+            row,
+            right,
+            acc,
+            lambda slot: jnp.minimum(slot - layer * share, share),
+            GROUP // 2,
+        )
     copies = []
     for j, (start, end) in enumerate(((0, share // 2), (share // 2, share))):
         here = pl.ds(start, end - start)

time: 43.4 us -> 43.4 us (level)
  no operation moved by 1% of the time
where the time goes in v12:
time: 43.4 us; the launch traced here: 42.6 us
  starting transfers between devices  25.1 us (58%)
  waiting for transfers between devices  9.32 us (21%)
  Pallas kernels  6.8 us (16%)
  local copies, waits for them, and re-layouts  1.22 us (3%)
    ppermute x6, starting transfers between devices, on_device(): arrived.append(lax.ppermute(part, ('col', 'layer'), pairs))  9.73 us
    ppermute x1, starting transfers between devices, on_device(): received = lax.ppermute(other, 'layer', swap)  4.43 us
    ppermute x1, starting transfers between devices, on_device(): second_swapped = lax.ppermute(second, 'layer', swap)  3.74 us
    ppermute x1, waiting for transfers between devices, on_device(): far = lax.ppermute(sent, everywhere, plan.far_pairs())  3.34 us
    ppermute x1, starting transfers between devices, on_device(): near.append(lax.ppermute(own, everywhere, plan.near_pairs(bys)))  2.97 us
    ppermute x1, waiting for transfers between devices, on_device(): near.append(lax.ppermute(own, everywhere, plan.near_pairs(bys)))  2.79 us
    ppermute x1, starting transfers between devices, on_device(): far_swapped = lax.ppermute(far, 'layer', swap)  2.15 us
    ppermute x1, starting transfers between devices, on_device(): far = lax.ppermute(sent, everywhere, plan.far_pairs())  2.12 us
  transfers between devices with their start and end apart: 12, of which 4 were waited for; matrix products, arithmetic and copies ran while one was open for 0% of the time, Pallas kernels for 12%

profile of v12, /device:TPU:0, one launch (start us, length us, event | category | flops | bytes accessed | tf_op | source)
XLA Modules:
  0.0 42.6 jit_solution(8543214189926859103)
XLA Ops:
  0.0 3.0 %collective-permute-start = (bf16[28,128,128]{2,1,0:T(8,128)(2,1)}, bf16[28,128,128]{2,1,0:T(8,128)(2,1)S(1)}, u32[]{:S(2)}, u32[]{:S(2)}) collective-permute-start(bf16[28,128,128]{2,1,0:T(8,128)(2,1)} %bitcast.2), channel_id=1, source_target_pairs={{0,8},{1,17},{2,10},{3,19},{4,12},{5,21},{6,14},{7,23},{8,0},{9,25... | collective-permute-start | bytes 2752520 | tf_op jit(solution)/shard_map/ppermute | solution.py:394
  3.0 1.2 %copy-done = bf16[1,1,28,128,128]{4,3,2,1,0:T(8,128)(2,1)S(1)} copy-done((bf16[1,1,28,128,128]{4,3,2,1,0:T(8,128)(2,1)S(1)}, bf16[1,1,28,128,128]{4,3,2,1,0:T(8,128)(2,1)}, u32[]{:S(2)}) %copy-start) | copy-done | bytes 917528
  4.2 0.6 %split_tile.1 = (bf16[14,128,128]{2,1,0:T(8,128)(2,1)S(1)}, bf16[14,128,128]{2,1,0:T(8,128)(2,1)S(1)}) custom-call(bf16[28,128,128]{2,1,0:T(8,128)(2,1)S(1)} %bitcast.3), custom_call_target="tpu_custom_call" | custom-call | bytes 1835008 | tf_op jit(solution)/shard_map/split_tile/pallas_call | solution.py:357
  4.8 3.5 %collective-permute-start.1 = (bf16[14,128,128]{2,1,0:T(8,128)(2,1)S(1)}, bf16[14,128,128]{2,1,0:T(8,128)(2,1)S(1)}, u32[]{:S(2)}, u32[]{:S(2)}) collective-permute-start(bf16[14,128,128]{2,1,0:T(8,128)(2,1)S(1)} %get-tuple-element.9.refs_0_.refs_3_.refs_4_.refs_6_), channel_id=1, source_target_pairs={{0,2},{2,4},{3,1},{4,6},{5,3},{7,5},{8,10},{10,12},{11,9},{12,14},... | collective-permute-start | bytes 1376264 | tf_op jit(solution)/shard_map/ppermute | solution.py:386
  8.3 3.5 %collective-permute-start.2 = (bf16[14,128,128]{2,1,0:T(8,128)(2,1)S(1)}, bf16[14,128,128]{2,1,0:T(8,128)(2,1)S(1)}, u32[]{:S(2)}, u32[]{:S(2)}) collective-permute-start(bf16[14,128,128]{2,1,0:T(8,128)(2,1)S(1)} %get-tuple-element.10.refs_1_.refs_4_.refs_5_.refs_7_), channel_id=1, source_target_pairs={{0,2},{2,4},{3,1},{4,6},{5,3},{7,5},{8,10},{10,12},{11,9},{12,14},... | collective-permute-start | bytes 1376264 | tf_op jit(solution)/shard_map/ppermute | solution.py:386
  11.8 2.8 %collective-permute-done.refs_2_.tile = bf16[28,128,128]{2,1,0:T(8,128)(2,1)S(1)} collective-permute-done((bf16[28,128,128]{2,1,0:T(8,128)(2,1)}, bf16[28,128,128]{2,1,0:T(8,128)(2,1)S(1)}, u32[]{:S(2)}, u32[]{:S(2)}) %collective-permute-start) | collective-permute-done | bytes 917536 | tf_op jit(solution)/shard_map/ppermute | solution.py:394
  14.5 0.0 collective-permute-start.3
  14.6 0.0 collective-permute-done.1.refs_5_.refs_6_.refs_8_
  14.6 0.7 %collective-permute-start.4 = (bf16[14,128,128]{2,1,0:T(8,128)(2,1)S(1)}, bf16[14,128,128]{2,1,0:T(8,128)(2,1)S(1)}, u32[]{:S(2)}, u32[]{:S(2)}) collective-permute-start(bf16[14,128,128]{2,1,0:T(8,128)(2,1)S(1)} %collective-permute-done.1.refs_5_.refs_6_.refs_8_), channel_id=1, source_target_pairs={{2,4},{3,1},{4,6},{5,3},{10,12},{11,9},{12,14},{13,11},{18,20},{19... | collective-permute-start | bytes 1376264 | tf_op jit(solution)/shard_map/ppermute | solution.py:386
  15.3 2.1 %collective-permute-start.6 = (bf16[14,128,128]{2,1,0:T(8,128)(2,1)S(1)}, bf16[14,128,128]{2,1,0:T(8,128)(2,1)S(1)}, u32[]{:S(2)}, u32[]{:S(2)}) collective-permute-start(bf16[14,128,128]{2,1,0:T(8,128)(2,1)S(1)} %pick_half.1), channel_id=1, source_target_pairs={{8,24},{17,25},{10,26},{19,27},{12,28},{21,29},{14,30},{23,31},{0,... | collective-permute-start | bytes 1376264 | tf_op jit(solution)/shard_map/ppermute | solution.py:405
  17.4 1.7 %collective-permute-done.2.refs_6_.refs_7_.refs_9_ = bf16[14,128,128]{2,1,0:T(8,128)(2,1)S(1)} collective-permute-done((bf16[14,128,128]{2,1,0:T(8,128)(2,1)S(1)}, bf16[14,128,128]{2,1,0:T(8,128)(2,1)S(1)}, u32[]{:S(2)}, u32[]{:S(2)}) %collective-permute-start.2) | collective-permute-done | bytes 458784 | tf_op jit(solution)/shard_map/ppermute | solution.py:386
  19.1 0.7 %collective-permute-start.5 = (bf16[14,128,128]{2,1,0:T(8,128)(2,1)S(1)}, bf16[14,128,128]{2,1,0:T(8,128)(2,1)S(1)}, u32[]{:S(2)}, u32[]{:S(2)}) collective-permute-start(bf16[14,128,128]{2,1,0:T(8,128)(2,1)S(1)} %collective-permute-done.2.refs_6_.refs_7_.refs_9_), channel_id=1, source_target_pairs={{2,4},{3,1},{4,6},{5,3},{10,12},{11,9},{12,14},{13,11},{18,20},{19... | collective-permute-start | bytes 1376264 | tf_op jit(solution)/shard_map/ppermute | solution.py:386
  19.8 0.0 collective-permute-done.4.refs_8_.refs_10_
  19.8 0.7 %collective-permute-start.8 = (bf16[14,128,128]{2,1,0:T(8,128)(2,1)S(1)}, bf16[14,128,128]{2,1,0:T(8,128)(2,1)S(1)}, u32[]{:S(2)}, u32[]{:S(2)}) collective-permute-start(bf16[14,128,128]{2,1,0:T(8,128)(2,1)S(1)} %collective-permute-done.4.refs_8_.refs_10_), channel_id=1, source_target_pairs={{3,1},{4,6},{11,9},{12,14},{19,17},{20,22},{27,25},{28,30}} | collective-permute-start | bytes 1376264 | tf_op jit(solution)/shard_map/ppermute | solution.py:386
  20.5 3.3 %collective-permute-done.6.refs_4_ = bf16[14,128,128]{2,1,0:T(8,128)(2,1)S(1)} collective-permute-done((bf16[14,128,128]{2,1,0:T(8,128)(2,1)S(1)}, bf16[14,128,128]{2,1,0:T(8,128)(2,1)S(1)}, u32[]{:S(2)}, u32[]{:S(2)}) %collective-permute-start.6) | collective-permute-done | bytes 458784 | tf_op jit(solution)/shard_map/ppermute | solution.py:405
  23.9 2.1 %collective-permute-start.7 = (bf16[14,128,128]{2,1,0:T(8,128)(2,1)S(1)}, bf16[14,128,128]{2,1,0:T(8,128)(2,1)S(1)}, u32[]{:S(2)}, u32[]{:S(2)}) collective-permute-start(bf16[14,128,128]{2,1,0:T(8,128)(2,1)S(1)} %collective-permute-done.6.refs_4_), channel_id=1, source_target_pairs={{0,1},{1,0},{2,3},{3,2},{4,5},{5,4},{6,7},{7,6},{8,9},{9,8},{10,11... | collective-permute-start | bytes 1376264 | tf_op jit(solution)/shard_map/ppermute | solution.py:406
  26.0 0.0 copy-done.1
  26.0 1.0 %list_products.1.pairs = s32[5,128]{1,0:T(8,128)S(1)} custom-call(s32[4,4,28]{2,1,0:T(4,128)S(1)} %convert_add_fusion.slot_keys), custom_call_target="tpu_custom_call" | custom-call | bytes 1835008 | tf_op jit(solution)/shard_map/list_products/pallas_call | solution.py:370
  27.0 0.0 collective-permute-done.5.refs_9_.refs_11_
  27.0 0.7 %collective-permute-start.10 = (bf16[14,128,128]{2,1,0:T(8,128)(2,1)S(1)}, bf16[14,128,128]{2,1,0:T(8,128)(2,1)S(1)}, u32[]{:S(2)}, u32[]{:S(2)}) collective-permute-start(bf16[14,128,128]{2,1,0:T(8,128)(2,1)S(1)} %collective-permute-done.5.refs_9_.refs_11_), channel_id=1, source_target_pairs={{3,1},{4,6},{11,9},{12,14},{19,17},{20,22},{27,25},{28,30}} | collective-permute-start | bytes 1376264 | tf_op jit(solution)/shard_map/ppermute | solution.py:386
  27.7 2.0 %early_products.1.total = f32[29,128,128]{2,1,0:T(8,128)S(1)} custom-call(s32[5,128]{1,0:T(8,128)S(1)} %list_products.1.pairs, bf16[14,128,128]{2,1,0:T(8,128)(2,1)S(1)} %get-tuple-element.9.refs_0_.refs_3_.refs_4_.refs_6_, bf16[14,128,128]{2,1,0:T(8,128)(2,1)S(1)} %get-tuple-element.10.refs_1_.refs_4_.refs_5_.refs_7_, ...), custom_call_target="tpu_custom_call" | custom-call | flops 352321536 | bytes 5505024 | tf_op jit(solution)/shard_map/early_products/pallas_call | solution.py:412
  29.7 0.0 collective-permute-done.3.refs_3_
  29.7 0.7 %second_products.1.total = f32[29,128,128]{2,1,0:T(8,128)S(1)} custom-call(s32[5,128]{1,0:T(8,128)S(1)} %list_products.1.pairs, f32[29,128,128]{2,1,0:T(8,128)S(1)} %early_products.1.total, bf16[14,128,128]{2,1,0:T(8,128)(2,1)S(1)} %get-tuple-element.9.refs_0_.refs_3_.refs_4_.refs_6_, ...), custom_call_target="tpu_custom_call", output_to_operand_aliasing={{}: (1, {})} | custom-call | flops 117440512 | bytes 1835008 | tf_op jit(solution)/shard_map/second_products/pallas_call | solution.py:421
  30.4 0.0 collective-permute-done.8.refs_12_
  30.4 0.0 collective-permute-done.7.refs_5_
  30.4 0.8 %middle_products.1 = (f32[29,128,128]{2,1,0:T(8,128)S(1)}, f32[14,128,128]{2,1,0:T(8,128)S(1)}, f32[14,128,128]{2,1,0:T(8,128)S(1)}) custom-call(s32[5,128]{1,0:T(8,128)S(1)} %list_products.1.pairs, f32[29,128,128]{2,1,0:T(8,128)S(1)} %second_products.1.total, ...), custom_call_target="tpu_custom_call", output_to_operand_aliasing={{0}: (1, {})} | custom-call | flops 352321536 | bytes 5505024 | tf_op jit(solution)/shard_map/middle_products/pallas_call | solution.py:434
  31.2 4.4 %collective-permute-start.9 = (f32[14,128,128]{2,1,0:T(8,128)S(1)}, f32[14,128,128]{2,1,0:T(8,128)S(1)}, u32[]{:S(2)}, u32[]{:S(2)}) collective-permute-start(f32[14,128,128]{2,1,0:T(8,128)S(1)} %get-tuple-element.12), channel_id=1, source_target_pairs={{0,1},{1,0},{2,3},{3,2},{4,5},{5,4},{6,7},{7,6},{8,9},{9,8},{10,11... | collective-permute-start | bytes 2752520 | tf_op jit(solution)/shard_map/ppermute | solution.py:444
  35.7 0.0 collective-permute-done.10.refs_6_
  35.7 3.7 %collective-permute-start.11 = (bf16[14,128,128]{2,1,0:T(8,128)(2,1)S(1)}, bf16[14,128,128]{2,1,0:T(8,128)(2,1)S(1)}, u32[]{:S(2)}, u32[]{:S(2)}) collective-permute-start(bf16[14,128,128]{2,1,0:T(8,128)(2,1)S(1)} %collective-permute-done.10.refs_6_), channel_id=1, source_target_pairs={{0,1},{1,0},{2,3},{3,2},{4,5},{5,4},{6,7},{7,6},{8,9},{9,8},{10,11... | collective-permute-start | bytes 1376264 | tf_op jit(solution)/shard_map/ppermute | solution.py:445
  39.4 1.4 %collective-permute-done.11.refs_7_ = bf16[14,128,128]{2,1,0:T(8,128)(2,1)S(1)} collective-permute-done((bf16[14,128,128]{2,1,0:T(8,128)(2,1)S(1)}, bf16[14,128,128]{2,1,0:T(8,128)(2,1)S(1)}, u32[]{:S(2)}, u32[]{:S(2)}) %collective-permute-start.11) | collective-permute-done | bytes 458784 | tf_op jit(solution)/shard_map/ppermute | solution.py:445
  40.8 0.0 collective-permute-done.9.received
  40.8 1.8 %last_products.1 = bf16[14,128,128]{2,1,0:T(8,128)(2,1)} custom-call(s32[5,128]{1,0:T(8,128)S(1)} %list_products.1.pairs, f32[14,128,128]{2,1,0:T(8,128)S(1)} %get-tuple-element.11.mine, f32[14,128,128]{2,1,0:T(8,128)S(1)} %collective-permute-done.9.received, bf16[14,128,128]{2,1,0:T(8,128)(2,1)S(1)} %get-tuple-element.9.refs_0_.refs_3_.refs_4_.refs_6_, ...), custom_call_target="tpu_custom_call" | custom-call | flops 58720256 | bytes 3670016 | tf_op jit(solution)/shard_map/last_products/pallas_call | solution.py:446
  (6 shorter events, 0.1 us)
Async XLA Ops:
  0.0 14.5 %collective-permute-start = (bf16[28,128,128]{2,1,0:T(8,128)(2,1)}, bf16[28,128,128]{2,1,0:T(8,128)(2,1)S(1)}, u32[]{:S(2)}, u32[]{:S(2)}) collective-permute-start(bf16[28,128,128]{2,1,0:T(8,128)(2,1)} %bitcast.2), channel_id=1, source_target_pairs={{0,8},{1,17},{2,10},{3,19},{4,12},{5,21},{6,14},{7,23},{8,0},{9,25... | collective-permute-start | bytes 2752520 | tf_op jit(solution)/shard_map/ppermute | solution.py:394
  3.0 1.2 %copy-start = (bf16[1,1,28,128,128]{4,3,2,1,0:T(8,128)(2,1)S(1)}, bf16[1,1,28,128,128]{4,3,2,1,0:T(8,128)(2,1)}, u32[]{:S(2)}) copy-start(bf16[1,1,28,128,128]{4,3,2,1,0:T(8,128)(2,1)} %param.3) | copy-start | bytes 2752516
  4.2 21.8 %copy-start.1 = (s32[4,4,28]{2,1,0:T(4,128)S(1)}, s32[4,4,28]{2,1,0:T(4,128)}, u32[]{:S(2)}) copy-start(s32[4,4,28]{2,1,0:T(4,128)} %param.4) | copy-start | bytes 5380
  4.2 21.8 %copy-start.2 = (s32[4,4,28]{2,1,0:T(4,128)S(1)}, s32[4,4,28]{2,1,0:T(4,128)}, u32[]{:S(2)}) copy-start(s32[4,4,28]{2,1,0:T(4,128)} %param.5) | copy-start | bytes 5380
  4.8 9.8 %collective-permute-start.1 = (bf16[14,128,128]{2,1,0:T(8,128)(2,1)S(1)}, bf16[14,128,128]{2,1,0:T(8,128)(2,1)S(1)}, u32[]{:S(2)}, u32[]{:S(2)}) collective-permute-start(bf16[14,128,128]{2,1,0:T(8,128)(2,1)S(1)} %get-tuple-element.9.refs_0_.refs_3_.refs_4_.refs_6_), channel_id=1, source_target_pairs={{0,2},{2,4},{3,1},{4,6},{5,3},{7,5},{8,10},{10,12},{11,9},{12,14},... | collective-permute-start | bytes 1376264 | tf_op jit(solution)/shard_map/ppermute | solution.py:386
  8.3 10.9 %collective-permute-start.2 = (bf16[14,128,128]{2,1,0:T(8,128)(2,1)S(1)}, bf16[14,128,128]{2,1,0:T(8,128)(2,1)S(1)}, u32[]{:S(2)}, u32[]{:S(2)}) collective-permute-start(bf16[14,128,128]{2,1,0:T(8,128)(2,1)S(1)} %get-tuple-element.10.refs_1_.refs_4_.refs_5_.refs_7_), channel_id=1, source_target_pairs={{0,2},{2,4},{3,1},{4,6},{5,3},{7,5},{8,10},{10,12},{11,9},{12,14},... | collective-permute-start | bytes 1376264 | tf_op jit(solution)/shard_map/ppermute | solution.py:386
  14.5 15.1 %collective-permute-start.3 = (bf16[28,128,128]{2,1,0:T(8,128)(2,1)S(1)}, bf16[28,128,128]{2,1,0:T(8,128)(2,1)S(1)}, u32[]{:S(2)}, u32[]{:S(2)}) collective-permute-start(bf16[28,128,128]{2,1,0:T(8,128)(2,1)S(1)} %collective-permute-done.refs_2_.tile), channel_id=1, source_target_pairs={{0,1},{1,0},{2,3},{3,2},{4,5},{5,4},{6,7},{7,6},{8,9},{9,8},{10,11... | collective-permute-start | bytes 2752520 | tf_op jit(solution)/shard_map/ppermute | solution.py:395
  14.6 5.3 %collective-permute-start.4 = (bf16[14,128,128]{2,1,0:T(8,128)(2,1)S(1)}, bf16[14,128,128]{2,1,0:T(8,128)(2,1)S(1)}, u32[]{:S(2)}, u32[]{:S(2)}) collective-permute-start(bf16[14,128,128]{2,1,0:T(8,128)(2,1)S(1)} %collective-permute-done.1.refs_5_.refs_6_.refs_8_), channel_id=1, source_target_pairs={{2,4},{3,1},{4,6},{5,3},{10,12},{11,9},{12,14},{13,11},{18,20},{19... | collective-permute-start | bytes 1376264 | tf_op jit(solution)/shard_map/ppermute | solution.py:386
  15.3 8.6 %collective-permute-start.6 = (bf16[14,128,128]{2,1,0:T(8,128)(2,1)S(1)}, bf16[14,128,128]{2,1,0:T(8,128)(2,1)S(1)}, u32[]{:S(2)}, u32[]{:S(2)}) collective-permute-start(bf16[14,128,128]{2,1,0:T(8,128)(2,1)S(1)} %pick_half.1), channel_id=1, source_target_pairs={{8,24},{17,25},{10,26},{19,27},{12,28},{21,29},{14,30},{23,31},{0,... | collective-permute-start | bytes 1376264 | tf_op jit(solution)/shard_map/ppermute | solution.py:405
  19.1 7.9 %collective-permute-start.5 = (bf16[14,128,128]{2,1,0:T(8,128)(2,1)S(1)}, bf16[14,128,128]{2,1,0:T(8,128)(2,1)S(1)}, u32[]{:S(2)}, u32[]{:S(2)}) collective-permute-start(bf16[14,128,128]{2,1,0:T(8,128)(2,1)S(1)} %collective-permute-done.2.refs_6_.refs_7_.refs_9_), channel_id=1, source_target_pairs={{2,4},{3,1},{4,6},{5,3},{10,12},{11,9},{12,14},{13,11},{18,20},{19... | collective-permute-start | bytes 1376264 | tf_op jit(solution)/shard_map/ppermute | solution.py:386
  19.8 10.5 %collective-permute-start.8 = (bf16[14,128,128]{2,1,0:T(8,128)(2,1)S(1)}, bf16[14,128,128]{2,1,0:T(8,128)(2,1)S(1)}, u32[]{:S(2)}, u32[]{:S(2)}) collective-permute-start(bf16[14,128,128]{2,1,0:T(8,128)(2,1)S(1)} %collective-permute-done.4.refs_8_.refs_10_), channel_id=1, source_target_pairs={{3,1},{4,6},{11,9},{12,14},{19,17},{20,22},{27,25},{28,30}} | collective-permute-start | bytes 1376264 | tf_op jit(solution)/shard_map/ppermute | solution.py:386
  23.9 6.5 %collective-permute-start.7 = (bf16[14,128,128]{2,1,0:T(8,128)(2,1)S(1)}, bf16[14,128,128]{2,1,0:T(8,128)(2,1)S(1)}, u32[]{:S(2)}, u32[]{:S(2)}) collective-permute-start(bf16[14,128,128]{2,1,0:T(8,128)(2,1)S(1)} %collective-permute-done.6.refs_4_), channel_id=1, source_target_pairs={{0,1},{1,0},{2,3},{3,2},{4,5},{5,4},{6,7},{7,6},{8,9},{9,8},{10,11... | collective-permute-start | bytes 1376264 | tf_op jit(solution)/shard_map/ppermute | solution.py:406
  27.0 8.6 %collective-permute-start.10 = (bf16[14,128,128]{2,1,0:T(8,128)(2,1)S(1)}, bf16[14,128,128]{2,1,0:T(8,128)(2,1)S(1)}, u32[]{:S(2)}, u32[]{:S(2)}) collective-permute-start(bf16[14,128,128]{2,1,0:T(8,128)(2,1)S(1)} %collective-permute-done.5.refs_9_.refs_11_), channel_id=1, source_target_pairs={{3,1},{4,6},{11,9},{12,14},{19,17},{20,22},{27,25},{28,30}} | collective-permute-start | bytes 1376264 | tf_op jit(solution)/shard_map/ppermute | solution.py:386
  31.2 9.6 %collective-permute-start.9 = (f32[14,128,128]{2,1,0:T(8,128)S(1)}, f32[14,128,128]{2,1,0:T(8,128)S(1)}, u32[]{:S(2)}, u32[]{:S(2)}) collective-permute-start(f32[14,128,128]{2,1,0:T(8,128)S(1)} %get-tuple-element.12), channel_id=1, source_target_pairs={{0,1},{1,0},{2,3},{3,2},{4,5},{5,4},{6,7},{7,6},{8,9},{9,8},{10,11... | collective-permute-start | bytes 2752520 | tf_op jit(solution)/shard_map/ppermute | solution.py:444
  35.7 5.2 %collective-permute-start.11 = (bf16[14,128,128]{2,1,0:T(8,128)(2,1)S(1)}, bf16[14,128,128]{2,1,0:T(8,128)(2,1)S(1)}, u32[]{:S(2)}, u32[]{:S(2)}) collective-permute-start(bf16[14,128,128]{2,1,0:T(8,128)(2,1)S(1)} %collective-permute-done.10.refs_6_), channel_id=1, source_target_pairs={{0,1},{1,0},{2,3},{3,2},{4,5},{5,4},{6,7},{7,6},{8,9},{9,8},{10,11... | collective-permute-start | bytes 1376264 | tf_op jit(solution)/shard_map/ppermute | solution.py:445
